TPU v7x, 32 devices: a whole 2x2x4 slice. The times are simulated.
32 devices in a mesh: fsdp: 8 (over z, y), seq: 4 (over x, core).
Axes of the slice: x: 2, y: 2, z: 4, core: 2. Of those that a mesh axis runs over, the one named last changes fastest.
Arguments:
- activations: bfloat16 [8, 2560, 1024], P('fsdp', 'seq'), may hold values from -6 to 6
- cotangent: bfloat16 [8, 2560, 1024], P('fsdp', 'seq'), may hold values from -6 to 6
- gain_attn: bfloat16 [1024], P('fsdp'), may hold values from 0.25 to 1.75
- w_qkv: bfloat16 [1024, 3072], P('fsdp'), may hold values from -0.25 to 0.25
- w_attn_out: bfloat16 [1024, 1024], P('fsdp'), may hold values from -0.75 to 0.75
- gain_mlp: bfloat16 [1024], P('fsdp'), may hold values from 0.25 to 1.75
- w_in: bfloat16 [1024, 5248], P('fsdp'), may hold values from -0.1875 to 0.1875
- w_mlp_out: bfloat16 [2624, 1024], P('fsdp'), may hold values from -0.125 to 0.125
Outputs:
- output: bfloat16 [8, 2560, 1024], P('fsdp', 'seq')
- d_input: bfloat16 [8, 2560, 1024], P('fsdp', 'seq')
- grad_gain_attn: float32 [1024], P('fsdp')
- grad_gain_mlp: float32 [1024], P('fsdp')
- grad_w_qkv: float32 [1024, 3072], P('fsdp')
- grad_w_attn_out: float32 [1024, 1024], P('fsdp')
- grad_w_in: float32 [1024, 5248], P('fsdp')
- grad_w_mlp_out: float32 [2624, 1024], P('fsdp')
All inputs are finite; a program needn't handle non-finite values.
Results may differ from a plain program's by a relative error of at most 0.023.
Values may be sent and summed in bfloat16 or wider, within the bound.
No kernel may reach another device: no remote copies, remote signals or barrier semaphores. Data moves between devices by JAX's collectives and lax.ppermute only.
A program may use at most 192 MiB of HBM per device.

v0:
```python
import math

import jax
import jax.numpy as jnp
from jax import lax
from jax.sharding import PartitionSpec as P

HEADS = 16
HEAD = 64
FF = 2624
LENGTH = 2560
QB = 512


eps = 1e-05
rope_base = 160000.0


def layer_norm(values, gain_vec):
    average = jnp.mean(values, -1, keepdims=True)
    centred = values - average
    variance = jnp.mean(centred * centred, -1, keepdims=True)
    return centred * lax.rsqrt(variance + eps) * gain_vec


def gelu_exact(values):
    return 0.5 * values * (1.0 + lax.erf(values * 2.0 ** (-0.5)))


def rope_tables(positions):
    half_size = HEAD // 2
    freq_index = jnp.arange(half_size).astype(positions.dtype)
    inverse = jnp.exp(freq_index * (-2.0 * math.log(rope_base) / HEAD))
    angles = positions[:, None] * inverse[None, :]
    angles = jnp.concatenate([angles, angles], 1)
    return (jnp.cos(angles), jnp.sin(angles))


def rotate(tensor, cosine, sine_table):
    half_size = HEAD // 2
    first = tensor[..., :half_size]
    second = tensor[..., half_size:]
    turned = jnp.concatenate([-second, first], -1)
    return tensor * cosine + turned * sine_table


def contract_rows(left, right):
    return lax.dot_general(
        left, right, (((0,), (0,)), ((), ())), preferred_element_type=jnp.float32
    )


def times_transpose(left, right):
    return lax.dot_general(
        left, right, (((1,), (1,)), ((), ())), preferred_element_type=jnp.float32
    )


def split_heads(packed_heads):
    local_heads = packed_heads.shape[2] // HEAD
    queries = packed_heads[:, 0].reshape(LENGTH // QB, QB, local_heads, HEAD)
    key_rows = packed_heads[:, 1].reshape(LENGTH, local_heads, HEAD)
    value_rows = packed_heads[:, 2].reshape(LENGTH, local_heads, HEAD)
    return (local_heads, queries, key_rows, value_rows)


def attend_sequence(packed_heads):
    local_heads, queries, key_rows, value_rows = split_heads(packed_heads)
    factor = float(HEAD) ** (-0.5)

    def one_block(q_block):
        scores = (
            jnp.einsum("qhd,khd->hqk", q_block, key_rows, preferred_element_type=jnp.float32)
            * factor
        )
        row_peak = jnp.max(scores, -1, keepdims=True)
        exponent = jnp.exp(scores - row_peak)
        row_total = jnp.sum(exponent, -1, keepdims=True)
        probs = (exponent / row_total).astype(jnp.bfloat16)
        attended = jnp.einsum("hqk,khd->qhd", probs, value_rows, preferred_element_type=jnp.float32)
        attended = attended.astype(jnp.bfloat16).reshape(QB, local_heads * HEAD)
        return (attended, (row_peak + jnp.log(row_total))[..., 0])

    attended, log_sums = lax.map(one_block, queries)
    return (attended.reshape(LENGTH, local_heads * HEAD), log_sums)


def attend_backward(pieces):
    packed_heads, log_sums, grad_heads = pieces
    local_heads, queries, key_rows, value_rows = split_heads(packed_heads)
    factor = float(HEAD) ** (-0.5)
    grad_blocks = grad_heads.reshape(LENGTH // QB, QB, local_heads, HEAD)

    def one_block(carry, block_pieces):
        key_grad, value_grad = carry
        q_block, lse_block, g_block = block_pieces
        scores = (
            jnp.einsum("qhd,khd->hqk", q_block, key_rows, preferred_element_type=jnp.float32)
            * factor
        )
        probs = jnp.exp(scores - lse_block[..., None])
        value_grad = value_grad + jnp.einsum(
            "hqk,qhd->khd", probs.astype(jnp.bfloat16), g_block, preferred_element_type=jnp.float32
        )
        prob_grad = jnp.einsum(
            "qhd,khd->hqk", g_block, value_rows, preferred_element_type=jnp.float32
        )
        inner = jnp.sum(probs * prob_grad, -1, keepdims=True)
        score_grad = (probs * (prob_grad - inner)).astype(jnp.bfloat16)
        query_grad = (
            jnp.einsum("hqk,khd->qhd", score_grad, key_rows, preferred_element_type=jnp.float32)
            * factor
        )
        key_grad = (
            key_grad
            + jnp.einsum("hqk,qhd->khd", score_grad, q_block, preferred_element_type=jnp.float32)
            * factor
        )
        return ((key_grad, value_grad), query_grad)

    zeros_state = jnp.zeros((LENGTH, local_heads, HEAD), jnp.float32)
    (key_grad, value_grad), query_grad = lax.scan(
        one_block, (zeros_state, zeros_state), (queries, log_sums, grad_blocks)
    )
    width_local = local_heads * HEAD
    stacked = jnp.stack(
        [
            query_grad.reshape(LENGTH, width_local),
            key_grad.reshape(LENGTH, width_local),
            value_grad.reshape(LENGTH, width_local),
        ],
        1,
    )
    return stacked.astype(jnp.bfloat16)


def local(activations, cotangent, gain_attn, w_qkv, w_attn_out, gain_mlp, w_in, w_mlp_out):
    local_seqs, positions, width = activations.shape
    row_count = local_seqs * positions
    gathered = (
        lax.all_gather(gain_attn, "fsdp", axis=0, tiled=True),
        lax.all_gather(w_qkv, "fsdp", axis=0, tiled=True),
        lax.all_gather(w_attn_out, "fsdp", axis=0, tiled=True),
        lax.all_gather(gain_mlp, "fsdp", axis=0, tiled=True),
        lax.all_gather(w_in, "fsdp", axis=0, tiled=True),
        lax.all_gather(w_mlp_out, "fsdp", axis=0, tiled=True),
    )
    full_gain_attn, full_qkv, full_attn_out, full_gain_mlp, full_in, full_mlp_out = gathered
    tokens = activations.astype(jnp.float32).reshape(row_count, width)
    normed, first_back = jax.vjp(layer_norm, tokens, full_gain_attn.astype(jnp.float32))
    normed_low = normed.astype(jnp.bfloat16)
    packed = jnp.dot(normed_low, full_qkv, preferred_element_type=jnp.float32)
    packed = packed.reshape(local_seqs, positions, 3, HEADS, HEAD)
    starting = (lax.axis_index("seq") * positions).astype(jnp.float32)
    places = starting + jnp.arange(positions).astype(jnp.float32)
    cosine, sine_table = rope_tables(places)

    def turn_pair(pair_values):
        return rotate(pair_values, cosine[:, None, None, :], sine_table[:, None, None, :])

    turned, turn_back = jax.vjp(turn_pair, packed[:, :, :2])
    rotated = jnp.concatenate([turned, packed[:, :, 2:]], 2).astype(jnp.bfloat16)
    rotated = rotated.reshape(local_seqs, positions, 3, width)
    heads_layout = lax.all_to_all(rotated, "seq", split_axis=3, concat_axis=1, tiled=True)
    attended_heads, log_sums = lax.map(attend_sequence, heads_layout)
    attended = lax.all_to_all(attended_heads, "seq", split_axis=1, concat_axis=2, tiled=True)
    attended_rows = attended.reshape(row_count, width)
    mixed = tokens + jnp.dot(attended_rows, full_attn_out, preferred_element_type=jnp.float32)
    normed_mlp, norm_back = jax.vjp(layer_norm, mixed, full_gain_mlp.astype(jnp.float32))
    normed_mlp_low = normed_mlp.astype(jnp.bfloat16)
    gate_up = jnp.dot(normed_mlp_low, full_in, preferred_element_type=jnp.float32)

    def gated(gate_part, up_part):
        return gelu_exact(gate_part) * up_part

    hidden, gated_back = jax.vjp(gated, gate_up[:, :FF], gate_up[:, FF:])
    hidden_low = hidden.astype(jnp.bfloat16)
    result = mixed + jnp.dot(hidden_low, full_mlp_out, preferred_element_type=jnp.float32)
    output = result.astype(jnp.bfloat16).reshape(activations.shape)
    again = (
        lax.all_gather(w_qkv, "fsdp", axis=0, tiled=True),
        lax.all_gather(w_attn_out, "fsdp", axis=0, tiled=True),
        lax.all_gather(w_in, "fsdp", axis=0, tiled=True),
        lax.all_gather(w_mlp_out, "fsdp", axis=0, tiled=True),
    )
    again_qkv, again_attn_out, again_in, again_mlp_out = again
    out_grad = cotangent.reshape(row_count, width)
    grad_mlp_out = contract_rows(hidden_low, out_grad)
    hidden_grad = times_transpose(out_grad, again_mlp_out)
    gate_grad, up_grad = gated_back(hidden_grad)
    gate_up_grad = jnp.concatenate([gate_grad, up_grad], 1).astype(jnp.bfloat16)
    grad_in = contract_rows(normed_mlp_low, gate_up_grad)
    normed_mlp_grad = times_transpose(gate_up_grad, again_in)
    mixed_grad_norm, grad_gain_mlp = norm_back(normed_mlp_grad)
    mixed_grad = out_grad.astype(jnp.float32) + mixed_grad_norm
    mixed_low = mixed_grad.astype(jnp.bfloat16)
    grad_attn_out = contract_rows(attended_rows, mixed_low)
    attended_grad = times_transpose(mixed_low, again_attn_out).astype(jnp.bfloat16)
    attended_grad = attended_grad.reshape(local_seqs, positions, width)
    grad_heads = lax.all_to_all(attended_grad, "seq", split_axis=2, concat_axis=1, tiled=True)
    rotated_grad = lax.map(attend_backward, (heads_layout, log_sums, grad_heads))
    position_grad = lax.all_to_all(rotated_grad, "seq", split_axis=1, concat_axis=3, tiled=True)
    position_grad = position_grad.astype(jnp.float32).reshape(local_seqs, positions, 3, HEADS, HEAD)
    (pair_grad,) = turn_back(position_grad[:, :, :2])
    packed_grad = jnp.concatenate([pair_grad, position_grad[:, :, 2:]], 2).astype(jnp.bfloat16)
    packed_grad = packed_grad.reshape(row_count, 3 * width)
    grad_qkv = contract_rows(normed_low, packed_grad)
    normed_grad = times_transpose(packed_grad, again_qkv)
    token_grad_norm, grad_gain_attn = first_back(normed_grad)
    d_input = (mixed_grad + token_grad_norm).astype(jnp.bfloat16).reshape(activations.shape)
    gradients = (grad_gain_attn, grad_gain_mlp, grad_qkv, grad_attn_out, grad_in, grad_mlp_out)
    shards = (
        lax.psum_scatter(
            gradients[0].astype(jnp.bfloat16), "fsdp", scatter_dimension=0, tiled=True
        ).astype(jnp.float32),
        lax.psum_scatter(
            gradients[1].astype(jnp.bfloat16), "fsdp", scatter_dimension=0, tiled=True
        ).astype(jnp.float32),
        lax.psum_scatter(
            gradients[2].astype(jnp.bfloat16), "fsdp", scatter_dimension=0, tiled=True
        ).astype(jnp.float32),
        lax.psum_scatter(
            gradients[3].astype(jnp.bfloat16), "fsdp", scatter_dimension=0, tiled=True
        ).astype(jnp.float32),
        lax.psum_scatter(
            gradients[4].astype(jnp.bfloat16), "fsdp", scatter_dimension=0, tiled=True
        ).astype(jnp.float32),
        lax.psum_scatter(
            gradients[5].astype(jnp.bfloat16), "fsdp", scatter_dimension=0, tiled=True
        ).astype(jnp.float32),
    )
    shards = (
        lax.psum(shards[0].astype(jnp.bfloat16), "seq").astype(jnp.float32),
        lax.psum(shards[1].astype(jnp.bfloat16), "seq").astype(jnp.float32),
        lax.psum(shards[2].astype(jnp.bfloat16), "seq").astype(jnp.float32),
        lax.psum(shards[3].astype(jnp.bfloat16), "seq").astype(jnp.float32),
        lax.psum(shards[4].astype(jnp.bfloat16), "seq").astype(jnp.float32),
        lax.psum(shards[5].astype(jnp.bfloat16), "seq").astype(jnp.float32),
    )
    return (output, d_input, shards[0], shards[1], shards[2], shards[3], shards[4], shards[5])


def solution(mesh):
    in_specs = (
        P("fsdp", "seq", None),
        P("fsdp", "seq", None),
        P("fsdp"),
        P("fsdp", None),
        P("fsdp", None),
        P("fsdp"),
        P("fsdp", None),
        P("fsdp", None),
    )
    out_specs = (
        P("fsdp", "seq", None),
        P("fsdp", "seq", None),
        P("fsdp"),
        P("fsdp"),
        P("fsdp", None),
        P("fsdp", None),
        P("fsdp", None),
        P("fsdp", None),
    )
    return jax.shard_map(local, mesh=mesh, in_specs=in_specs, out_specs=out_specs, check_vma=False)
```

profile of v0, /device:TPU:1, one launch (start us, length us, event | category | flops | bytes accessed | tf_op | source)
XLA Modules:
  0.0 1312.5 jit_solution(7243004674187600519)
XLA Ops:
  9.4 18.0 %all-gather = bf16[8,1,128]{2,1,0:T(2,128)(2,1)S(1)} all-gather(bf16[1,1,128]{2,1,0:T(2,128)(2,1)} %bitcast.228), channel_id=1, replica_groups=mesh['fsdp'=8,'seq'=4] {'fsdp'}, dimensions={0}, use_global_device_ids=true | all-gather | bytes 2304 | tf_op jit(solution)/shard_map/all_gather | solution.py:141
  29.1 81.7 %all-gather.7.cloned.1.call-done = bf16[1024,3072]{1,0:T(8,128)(2,1)} async-done(((bf16[128,3072]{1,0:T(8,128)(2,1)}), bf16[1024,3072]{1,0:T(8,128)(2,1)}) %all-gather.7.cloned.1.call-update) | async-done | bytes 6291472 | tf_op jit(solution)/shard_map/all_gather | solution.py:142
  110.8 8.6 copy.50
  119.5 8.0 convolution_bitcast_fusion
  147.1 58.1 %all-to-all-done = bf16[1,640,3,1024]{1,2,0,3:T(4,128)(2,1)} async-done(((bf16[1,640,3,1024]{1,2,0,3:T(4,128)(2,1)}), bf16[1,640,3,1024]{1,2,0,3:T(4,128)(2,1)}, u32[]{:S(2)}, u32[]{:S(2)}) %all-to-all-start) | async-done | bytes 3932192 | tf_op jit(solution)/shard_map/all_to_all | solution.py:164
  205.2 8.1 copy.53
  227.8 93.1 %while.45 = (s32[]{:T(128)}, bf16[5,512,256]{2,1,0:T(8,128)(2,1)}, f32[5,4,512]{2,1,0:T(4,128)}, bf16[5,512,4,64]{1,3,2,0:T(8,128)(2,1)}, bf16[2560,4,64]{0,2,1:...) while((s32[]{:T(128)}, bf16[5,512,256]{2,1,0:T(8,128)(2,1)}, f32[5,4,512]{2,1,0:T(4,128)}, ...), condition=%wide.region_5.0_spmd, body=%wide.region_2.5_spmd.sunk | while | flops 1389492224 | bytes 67174496 | solution.py:84
  325.6 14.1 %reduce.1 = bf16[2560,256]{1,0:T(8,128)(2,1)} reduce(bf16[2560,1,256]{2,1,0:T(2,128)(2,1)S(1)} %bitcast.202, bf16[]{:T(256)} %broadcast.257), dimensions={1}, to_apply=%bitcast.158.reduce_sub_computation | reduce | bytes 2621442
  347.5 14.0 %all-gather.1 = bf16[8,1,128]{2,1,0:T(2,128)(2,1)S(1)} all-gather(bf16[1,1,128]{2,1,0:T(2,128)(2,1)S(1)} %bitcast.229), channel_id=1, replica_groups=mesh['fsdp'=8,'seq'=4] {'fsdp'}, dimensions={0}, use_global_device_ids=true | all-gather | bytes 2304 | tf_op jit(solution)/shard_map/all_gather | solution.py:144
  375.8 15.1 %fusion.73 = f32[640,5248]{1,0:T(8,128)} fusion(bf16[1024,5248]{1,0:T(8,128)(2,1)} %all-gather.11.cloned.1.call-done, f32[640,1024]{1,0:T(8,128)} %copy-done.7, f32[1024]{0:T(1024)S(1)} %bitcast.224, f32[640]{0:T(1024)S(1)} %fusion.67, f32[640]{0:T(1024)S(1)} %broadcast_multiply_fusion.1), kind=kOutput, calls=%fused_computation.125 | convolution fusion | flops 6881280000 | bytes 26813440 | tf_op jit(solution)/shard_map/dot_general | solution.py:171
  390.9 12.2 all-gather.13.cloned.1.call-done
  403.0 14.9 %add_convert_fusion = (bf16[640,2624]{1,0:T(8,128)(2,1)S(1)}, bf16[640,2624]{1,0:T(8,128)(2,1)}, bf16[640,2624]{1,0:T(8,128)(2,1)}) fusion(f32[640,5248]{1,0:T(8,128)} %fusion.73, bf16[2624,1024]{1,0:T(8,128)(2,1)} %all-gather.13.cloned.1.call-done, bf16[1,640,1024]{2,1,0:T(8,128)(2,1)} %param.13), kind=kOutput, calls=%fused_computation.48 | convolution fusion | flops 3471237120 | bytes 30195712 | tf_op jit(solution)/shard_map/dot_general | solution.py:54
  418.0 14.6 %multiply_reduce_fusion.2 = (bf16[1024]{0:T(1024)(128)(2,1)}, f32[640]{0:T(1024)S(1)}, f32[640,1024]{1,0:T(8,128)S(1)}) fusion(f32[640,1024]{1,0:T(8,128)S(1)} %copy-done.8, f32[640]{0:T(1024)S(1)} %fusion.67, f32[640]{0:T(1024)S(1)} %broadcast_multiply_fusion.1, f32[1024]{0:T(1024)S(1)} %bitcast.225, bf16[1024,5248]{1,0:T(8,128)(2,1)} %all-gather.11.cloned.1.call-done, ...), kind=kOutput, calls=%fused_computation.88 | convolution fusion | flops 6896679424 | bytes 22722048 | tf_op jit(solution)/shard_map/dot_general | solution.py:54
  447.0 9.7 reduce.2
  466.2 8.3 convolution_convert_fusion.1
  474.5 8.1 all-to-all-done.2
  489.2 323.5 %while.46 = (s32[]{:T(128)}, f32[2560,4,64]{0,2,1:T(8,128)}, f32[2560,4,64]{0,2,1:T(8,128)}, bf16[5,512,4,64]{1,3,2,0:T(8,128)(2,1)}, bf16[5,512,4,64]{1,3,2,0:T...) while((s32[]{:T(128)}, f32[2560,4,64]{0,2,1:T(8,128)}, ...), condition=%wide.region_12.13_spmd.clone, body=%wide.region_10.12_spmd.clone.sunk | while | flops 3421763584 | bytes 173334672 | solution.py:122
  490.0 11.4 fusion.130
  501.4 12.5 fusion.132
  514.0 14.7 %multiply_reduce_fusion.8 = (f32[4,512]{1,0:T(4,128)S(1)}, f32[4,512,2560]{2,1,0:T(8,128)}) fusion(f32[4,512,2560]{2,1,0:T(8,128)} %fusion.130, f32[4,512]{1,0:T(4,128)S(1)} %dynamic-slice_bitcast_fusion.2, bf16[2560,4,64]{0,2,1:T(8,128)(2,1)} %get-tuple-element.413, bf16[5,512,4,64]{1,3,2,0:T(8,128)(2,1)} %get-tuple-element.412, s32[]{:T(128)S(6)} %copy.94), kind=kOutput, calls=%fused_computation.14.clone.1 | convolution fusion | flops 692058112 | bytes 43532292 | tf_op jit(solution)/shard_map/while/body/eval_jaxpr/while/body/eval_jaxpr/qhd,khd->hqk/dot_general | solution.py:105
  528.7 15.1 %multiply_convert_fusion.7 = bf16[4,512,2560]{2,1,0:T(8,128)(2,1)S(1)} fusion(f32[4,512,2560]{2,1,0:T(8,128)} %get-tuple-element.360, f32[4,512,2560]{2,1,0:T(8,128)} %fusion.130, f32[4,512]{1,0:T(4,128)S(1)} %get-tuple-element.361, f32[4,512]{1,0:T(4,128)S(1)} %dynamic-slice_bitcast_fusion.2), kind=kLoop, calls=%fused_computation.13.clone.1 | loop fusion | flops 26214400 | bytes 52445184 | tf_op jit(solution)/shard_map/while/body/eval_jaxpr/while/body/eval_jaxpr/convert_element_type | solution.py:109
  554.3 11.5 fusion.130
  565.8 13.6 %fusion.132 = f32[2560,4,64]{0,2,1:T(8,128)} fusion(f32[4,512,2560]{2,1,0:T(8,128)} %fusion.130, f32[4,512]{1,0:T(4,128)S(1)} %dynamic-slice_bitcast_fusion.2, f32[2560,4,64]{0,2,1:T(8,128)} %get-tuple-element.396, pred[]{:T(512)S(6)} %compare.5, bf16[5,512,4,64]{1,3,2,0:T(8,128)(2,1)} %get-tuple-element.412, s32[]{:T(128)S(6)} %copy.94), kind=kOutput, calls=%fused_computation.24.clone.1 | convolution fusion | flops 688128000 | bytes 26484740 | tf_op jit(solution)/shard_map/while/body/eval_jaxpr/while/body/eval_jaxpr/hqk,qhd->khd/dot_general | solution.py:102
  579.3 14.3 %multiply_reduce_fusion.8 = (f32[4,512]{1,0:T(4,128)S(1)}, f32[4,512,2560]{2,1,0:T(8,128)}) fusion(f32[4,512,2560]{2,1,0:T(8,128)} %fusion.130, f32[4,512]{1,0:T(4,128)S(1)} %dynamic-slice_bitcast_fusion.2, bf16[2560,4,64]{0,2,1:T(8,128)(2,1)} %get-tuple-element.413, bf16[5,512,4,64]{1,3,2,0:T(8,128)(2,1)} %get-tuple-element.412, s32[]{:T(128)S(6)} %copy.94), kind=kOutput, calls=%fused_computation.14.clone.1 | convolution fusion | flops 692058112 | bytes 43532292 | tf_op jit(solution)/shard_map/while/body/eval_jaxpr/while/body/eval_jaxpr/qhd,khd->hqk/dot_general | solution.py:105
  593.6 14.7 %multiply_convert_fusion.7 = bf16[4,512,2560]{2,1,0:T(8,128)(2,1)S(1)} fusion(f32[4,512,2560]{2,1,0:T(8,128)} %get-tuple-element.360, f32[4,512,2560]{2,1,0:T(8,128)} %fusion.130, f32[4,512]{1,0:T(4,128)S(1)} %get-tuple-element.361, f32[4,512]{1,0:T(4,128)S(1)} %dynamic-slice_bitcast_fusion.2), kind=kLoop, calls=%fused_computation.13.clone.1 | loop fusion | flops 26214400 | bytes 52445184 | tf_op jit(solution)/shard_map/while/body/eval_jaxpr/while/body/eval_jaxpr/convert_element_type | solution.py:109
  619.7 11.3 fusion.130
  631.0 13.3 %fusion.132 = f32[2560,4,64]{0,2,1:T(8,128)} fusion(f32[4,512,2560]{2,1,0:T(8,128)} %fusion.130, f32[4,512]{1,0:T(4,128)S(1)} %dynamic-slice_bitcast_fusion.2, f32[2560,4,64]{0,2,1:T(8,128)} %get-tuple-element.396, pred[]{:T(512)S(6)} %compare.5, bf16[5,512,4,64]{1,3,2,0:T(8,128)(2,1)} %get-tuple-element.412, s32[]{:T(128)S(6)} %copy.94), kind=kOutput, calls=%fused_computation.24.clone.1 | convolution fusion | flops 688128000 | bytes 26484740 | tf_op jit(solution)/shard_map/while/body/eval_jaxpr/while/body/eval_jaxpr/hqk,qhd->khd/dot_general | solution.py:102
  644.3 14.2 %multiply_reduce_fusion.8 = (f32[4,512]{1,0:T(4,128)S(1)}, f32[4,512,2560]{2,1,0:T(8,128)}) fusion(f32[4,512,2560]{2,1,0:T(8,128)} %fusion.130, f32[4,512]{1,0:T(4,128)S(1)} %dynamic-slice_bitcast_fusion.2, bf16[2560,4,64]{0,2,1:T(8,128)(2,1)} %get-tuple-element.413, bf16[5,512,4,64]{1,3,2,0:T(8,128)(2,1)} %get-tuple-element.412, s32[]{:T(128)S(6)} %copy.94), kind=kOutput, calls=%fused_computation.14.clone.1 | convolution fusion | flops 692058112 | bytes 43532292 | tf_op jit(solution)/shard_map/while/body/eval_jaxpr/while/body/eval_jaxpr/qhd,khd->hqk/dot_general | solution.py:105
  658.5 14.3 %multiply_convert_fusion.7 = bf16[4,512,2560]{2,1,0:T(8,128)(2,1)S(1)} fusion(f32[4,512,2560]{2,1,0:T(8,128)} %get-tuple-element.360, f32[4,512,2560]{2,1,0:T(8,128)} %fusion.130, f32[4,512]{1,0:T(4,128)S(1)} %get-tuple-element.361, f32[4,512]{1,0:T(4,128)S(1)} %dynamic-slice_bitcast_fusion.2), kind=kLoop, calls=%fused_computation.13.clone.1 | loop fusion | flops 26214400 | bytes 52445184 | tf_op jit(solution)/shard_map/while/body/eval_jaxpr/while/body/eval_jaxpr/convert_element_type | solution.py:109
  684.2 11.3 fusion.130
  695.5 13.3 %fusion.132 = f32[2560,4,64]{0,2,1:T(8,128)} fusion(f32[4,512,2560]{2,1,0:T(8,128)} %fusion.130, f32[4,512]{1,0:T(4,128)S(1)} %dynamic-slice_bitcast_fusion.2, f32[2560,4,64]{0,2,1:T(8,128)} %get-tuple-element.396, pred[]{:T(512)S(6)} %compare.5, bf16[5,512,4,64]{1,3,2,0:T(8,128)(2,1)} %get-tuple-element.412, s32[]{:T(128)S(6)} %copy.94), kind=kOutput, calls=%fused_computation.24.clone.1 | convolution fusion | flops 688128000 | bytes 26484740 | tf_op jit(solution)/shard_map/while/body/eval_jaxpr/while/body/eval_jaxpr/hqk,qhd->khd/dot_general | solution.py:102
  708.8 14.2 %multiply_reduce_fusion.8 = (f32[4,512]{1,0:T(4,128)S(1)}, f32[4,512,2560]{2,1,0:T(8,128)}) fusion(f32[4,512,2560]{2,1,0:T(8,128)} %fusion.130, f32[4,512]{1,0:T(4,128)S(1)} %dynamic-slice_bitcast_fusion.2, bf16[2560,4,64]{0,2,1:T(8,128)(2,1)} %get-tuple-element.413, bf16[5,512,4,64]{1,3,2,0:T(8,128)(2,1)} %get-tuple-element.412, s32[]{:T(128)S(6)} %copy.94), kind=kOutput, calls=%fused_computation.14.clone.1 | convolution fusion | flops 692058112 | bytes 43532292 | tf_op jit(solution)/shard_map/while/body/eval_jaxpr/while/body/eval_jaxpr/qhd,khd->hqk/dot_general | solution.py:105
  723.0 14.3 %multiply_convert_fusion.7 = bf16[4,512,2560]{2,1,0:T(8,128)(2,1)S(1)} fusion(f32[4,512,2560]{2,1,0:T(8,128)} %get-tuple-element.360, f32[4,512,2560]{2,1,0:T(8,128)} %fusion.130, f32[4,512]{1,0:T(4,128)S(1)} %get-tuple-element.361, f32[4,512]{1,0:T(4,128)S(1)} %dynamic-slice_bitcast_fusion.2), kind=kLoop, calls=%fused_computation.13.clone.1 | loop fusion | flops 26214400 | bytes 52445184 | tf_op jit(solution)/shard_map/while/body/eval_jaxpr/while/body/eval_jaxpr/convert_element_type | solution.py:109
  748.7 11.3 fusion.130
  760.0 13.3 %fusion.132 = f32[2560,4,64]{0,2,1:T(8,128)} fusion(f32[4,512,2560]{2,1,0:T(8,128)} %fusion.130, f32[4,512]{1,0:T(4,128)S(1)} %dynamic-slice_bitcast_fusion.2, f32[2560,4,64]{0,2,1:T(8,128)} %get-tuple-element.396, pred[]{:T(512)S(6)} %compare.5, bf16[5,512,4,64]{1,3,2,0:T(8,128)(2,1)} %get-tuple-element.412, s32[]{:T(128)S(6)} %copy.94), kind=kOutput, calls=%fused_computation.24.clone.1 | convolution fusion | flops 688128000 | bytes 26484740 | tf_op jit(solution)/shard_map/while/body/eval_jaxpr/while/body/eval_jaxpr/hqk,qhd->khd/dot_general | solution.py:102
  773.3 14.2 %multiply_reduce_fusion.8 = (f32[4,512]{1,0:T(4,128)S(1)}, f32[4,512,2560]{2,1,0:T(8,128)}) fusion(f32[4,512,2560]{2,1,0:T(8,128)} %fusion.130, f32[4,512]{1,0:T(4,128)S(1)} %dynamic-slice_bitcast_fusion.2, bf16[2560,4,64]{0,2,1:T(8,128)(2,1)} %get-tuple-element.413, bf16[5,512,4,64]{1,3,2,0:T(8,128)(2,1)} %get-tuple-element.412, s32[]{:T(128)S(6)} %copy.94), kind=kOutput, calls=%fused_computation.14.clone.1 | convolution fusion | flops 692058112 | bytes 43532292 | tf_op jit(solution)/shard_map/while/body/eval_jaxpr/while/body/eval_jaxpr/qhd,khd->hqk/dot_general | solution.py:105
  787.5 14.3 %multiply_convert_fusion.7 = bf16[4,512,2560]{2,1,0:T(8,128)(2,1)S(1)} fusion(f32[4,512,2560]{2,1,0:T(8,128)} %get-tuple-element.360, f32[4,512,2560]{2,1,0:T(8,128)} %fusion.130, f32[4,512]{1,0:T(4,128)S(1)} %get-tuple-element.361, f32[4,512]{1,0:T(4,128)S(1)} %dynamic-slice_bitcast_fusion.2), kind=kLoop, calls=%fused_computation.13.clone.1 | loop fusion | flops 26214400 | bytes 52445184 | tf_op jit(solution)/shard_map/while/body/eval_jaxpr/while/body/eval_jaxpr/convert_element_type | solution.py:109
  824.8 8.6 copy.65
  833.4 63.1 %all_to_all.54 = bf16[1,2560,3,256]{3,2,0,1:T(4,128)(2,1)S(1)} all-to-all(bf16[1,2560,3,256]{3,2,0,1:T(4,128)(2,1)} %copy.65), channel_id=1, replica_groups=mesh['fsdp'=8,'seq'=4] {'seq'}, dimensions={1} | all-to-all | bytes 7864320 | tf_op jit(solution)/shard_map/all_to_all | solution.py:202
  900.9 9.2 copy.67
  928.3 15.7 %convolution_convert_fusion = bf16[1024,5248]{1,0:T(8,128)(2,1)} fusion(bf16[640,2624]{1,0:T(8,128)(2,1)} %get-tuple-element.246, bf16[640,2624]{1,0:T(8,128)(2,1)} %copy-done.41, f32[640,1024]{1,0:T(8,128)} %copy-done.7, f32[1024]{0:T(1024)S(1)} %bitcast.227, f32[640]{0:T(1024)S(1)} %copy-done.36, f32[640]{0:T(1024)S(1)} %copy-done.24), kind=kOutput, calls=%fused_computation.44 | convolution fusion | flops 6900088832 | bytes 20096000 | tf_op jit(solution)/shard_map/dot_general | solution.py:48
  945.9 9.4 fusion.57
  955.3 87.6 %reduce-scatter.5.cloned.1.call-done = bf16[128,3072]{1,0:T(8,128)(2,1)} async-done(((bf16[1024,3072]{1,0:T(8,128)(2,1)}), bf16[128,3072]{1,0:T(8,128)(2,1)}) %reduce-scatter.5.cloned.1.call-update) | async-done | bytes 786448 | tf_op jit(solution)/shard_map/reduce_scatter | solution.py:219
  1042.9 185.8 %reduce-scatter.9.cloned.1.call-done = bf16[128,5248]{1,0:T(8,128)(2,1)} async-done(((bf16[1024,5248]{1,0:T(8,128)(2,1)}), bf16[128,5248]{1,0:T(8,128)(2,1)}) %reduce-scatter.9.cloned.1.call-update) | async-done | bytes 1343504 | tf_op jit(solution)/shard_map/reduce_scatter | solution.py:225
  1228.8 8.1 fusion.49
  1238.4 16.0 %all-reduce.4 = (bf16[1024]{0:T(1024)(128)(2,1)S(1)}, bf16[1024]{0:T(1024)(128)(2,1)S(1)}) all-reduce(bf16[1024]{0:T(1024)(128)(2,1)S(1)} %get-tuple-element.199, bf16[1024]{0:T(1024)(128)(2,1)S(1)} %copy-done.37), channel_id=2, replica_groups=mesh['fsdp'=8,'seq'=4] {'fsdp'}, use_global_device_ids=true, to_apply=%region_16.17.clone | all-reduce | flops 2048 | bytes 8192
  1254.5 9.4 all-reduce.5
  1269.0 29.3 %all-reduce.9.cloned.1.call-done = (bf16[128,3072]{1,0:T(8,128)(2,1)}, bf16[128,1024]{1,0:T(8,128)(2,1)}, bf16[128,5248]{1,0:T(8,128)(2,1)}, bf16[328,1024]{1,0:T(8,128)(2,1)}) async-done(((bf16[128,3072]{1,0:T(8,128)(2,1)}, bf16[128,1024]{1,0:T(8,128)(2,1)}, bf16[128,5248]{1,0:T(8,128)(2,1)}, bf16[328,1024]{1,0:T(8,128)(2,1)}), (bf16[128,3072]{1,0:T(8,128)(2,1)}, bf16[128,1024]{1,0:T(8,128)(2,1)}, ...) | async-done | bytes 3063824 | tf_op jit(solution)/shard_map/psum | solution.py:235
  (234 shorter events, 293.5 us)
Async XLA Ops:
  7.2 20.6 %copy-start.3 = (bf16[1,640,1024]{2,1,0:T(8,128)(2,1)S(1)}, bf16[1,640,1024]{2,1,0:T(8,128)(2,1)}, u32[]{:S(2)}) copy-start(bf16[1,640,1024]{2,1,0:T(8,128)(2,1)} %param.12) | copy-start | bytes 3932164
  7.2 103.7 %all-gather.7.cloned.1.call-start = ((), (), s32[]{:S(2)}) async-start(), calls=%async_computation.8 | async-start | bytes 7077888 | tf_op jit(solution)/shard_map/all_gather | solution.py:142
  7.9 362.3 %all-gather.9.cloned.1.call-start = ((), (), s32[]{:S(2)}) async-start(), calls=%async_computation.9 | async-start | bytes 2359296 | tf_op jit(solution)/shard_map/all_gather | solution.py:143
  8.7 367.1 %all-gather.11.cloned.1.call-start = ((), (), s32[]{:S(2)}) async-start(), calls=%async_computation.10 | async-start | bytes 12091392 | tf_op jit(solution)/shard_map/all_gather | solution.py:145
  27.4 92.1 %copy-start.27 = (f32[8,1,128]{2,1,0:T(1,128)}, f32[8,1,128]{2,1,0:T(1,128)S(1)}, u32[]{:S(2)}) copy-start(f32[8,1,128]{2,1,0:T(1,128)S(1)} %convert_element_type.213) | copy-start | bytes 12292
  27.8 102.3 %copy-start.14 = (f32[640,64]{0,1:T(8,128)}, f32[640,64]{0,1:T(8,128)S(1)}, u32[]{:S(2)}) copy-start(f32[640,64]{0,1:T(8,128)S(1)} %get-tuple-element.255) | copy-start | bytes 491524
  27.8 102.3 %copy-start.16 = (f32[640,64]{0,1:T(8,128)}, f32[640,64]{0,1:T(8,128)S(1)}, u32[]{:S(2)}) copy-start(f32[640,64]{0,1:T(8,128)S(1)} %get-tuple-element.256) | copy-start | bytes 491524
  28.1 91.4 %copy-start.21 = (f32[640]{0:T(1024)}, f32[640]{0:T(1024)S(1)}, u32[]{:S(2)}) copy-start(f32[640]{0:T(1024)S(1)} %broadcast_multiply_fusion.2) | copy-start | bytes 7684
  29.1 90.4 %copy-start.29 = (f32[640]{0:T(1024)}, f32[640]{0:T(1024)S(1)}, u32[]{:S(2)}) copy-start(f32[640]{0:T(1024)S(1)} %fusion.66) | copy-start | bytes 7684
  140.4 64.8 %all-to-all-start = ((bf16[1,640,3,1024]{1,2,0,3:T(4,128)(2,1)}), bf16[1,640,3,1024]{1,2,0,3:T(4,128)(2,1)}, u32[]{:S(2)}, u32[]{:S(2)}) async-start(bf16[1,640,3,1024]{1,2,0,3:T(4,128)(2,1)} %pad_maximum_fusion.1), calls=%async_computation | async-start | bytes 10485760 | tf_op jit(solution)/shard_map/all_to_all | solution.py:164
  146.5 256.5 %all-gather.13.cloned.1.call-start = ((), (), s32[]{:S(2)}) async-start(), calls=%async_computation.11 | async-start | bytes 6045696 | tf_op jit(solution)/shard_map/all_gather | solution.py:146
  339.7 7.8 copy-start.38
  343.3 20.7 %all-to-all-start.1 = ((bf16[4,2,81920]{2,1,0:T(2,128)(2,1)}), bf16[4,2,81920]{2,1,0:T(2,128)(2,1)S(1)}, u32[]{:S(2)}, u32[]{:S(2)}) async-start(bf16[4,2,81920]{2,1,0:T(2,128)(2,1)} %reshape.443), calls=%async_computation.1 | async-start | bytes 2621440 | tf_op jit(solution)/shard_map/all_to_all | solution.py:166
  347.5 607.8 %reduce-scatter.7.cloned.1.call-start = ((), (), s32[]{:S(2)}) async-start(), calls=%async_computation.13 | async-start | bytes 2359296 | tf_op jit(solution)/shard_map/reduce_scatter | solution.py:222
  361.5 71.1 %copy-start.33 = (f32[8,1,128]{2,1,0:T(1,128)}, f32[8,1,128]{2,1,0:T(1,128)S(1)}, u32[]{:S(2)}) copy-start(f32[8,1,128]{2,1,0:T(1,128)S(1)} %convert_element_type.214) | copy-start | bytes 12292
  366.7 3.5 copy-start.4
  373.9 1.5 copy-start.7
  373.9 58.7 %copy-start.23 = (f32[640]{0:T(1024)}, f32[640]{0:T(1024)S(1)}, u32[]{:S(2)}) copy-start(f32[640]{0:T(1024)S(1)} %broadcast_multiply_fusion.1) | copy-start | bytes 7684
  375.8 56.9 %copy-start.35 = (f32[640]{0:T(1024)}, f32[640]{0:T(1024)S(1)}, u32[]{:S(2)}) copy-start(f32[640]{0:T(1024)S(1)} %fusion.67) | copy-start | bytes 7684
  390.9 27.1 %copy-start.8 = (f32[640,1024]{1,0:T(8,128)S(1)}, f32[640,1024]{1,0:T(8,128)}, u32[]{:S(2)}) copy-start(f32[640,1024]{1,0:T(8,128)} %copy-done.7) | copy-start | bytes 7864324
  418.0 14.6 %copy-start.41 = (bf16[640,2624]{1,0:T(8,128)(2,1)}, bf16[640,2624]{1,0:T(8,128)(2,1)S(1)}, u32[]{:S(2)}) copy-start(bf16[640,2624]{1,0:T(8,128)(2,1)S(1)} %get-tuple-element.245) | copy-start | bytes 10076164
  433.5 1.5 copy-start.1
  433.6 1.5 copy-start.31
  434.0 1.8 copy-start.19
  435.8 3.2 copy-start.39
  456.7 9.5 copy-start.12
  460.4 22.3 %all-to-all-start.2 = ((bf16[4,2,81920]{2,1,0:T(2,128)(2,1)}), bf16[4,2,81920]{2,1,0:T(2,128)(2,1)}, u32[]{:S(2)}, u32[]{:S(2)}) async-start(bf16[4,2,81920]{2,1,0:T(2,128)(2,1)} %reshape.445), calls=%async_computation.2 | async-start | bytes 2621440 | tf_op jit(solution)/shard_map/all_to_all | solution.py:200
  466.2 489.1 %reduce-scatter.11.cloned.1.call-start = ((), (), s32[]{:S(2)}) async-start(), calls=%async_computation.15 | async-start | bytes 6045696 | tf_op jit(solution)/shard_map/reduce_scatter | solution.py:228
  474.5 568.4 %reduce-scatter.5.cloned.1.call-start = ((), (), s32[]{:S(2)}) async-start(), calls=%async_computation.12 | async-start | bytes 7077888 | tf_op jit(solution)/shard_map/reduce_scatter | solution.py:219
  812.7 7.7 copy-start
  820.5 2.1 copy-start.10
  910.1 2.1 copy-start.17
  910.1 5.5 slice-start
  912.2 3.9 slice-start.1
  917.5 2.3 copy-start.5
  917.5 2.3 copy-start.22
  917.5 2.3 copy-start.28
  917.5 2.3 copy-start.30
  918.0 1.9 copy-start.13
  927.7 301.0 %reduce-scatter.9.cloned.1.call-start = ((), (), s32[]{:S(2)}) async-start(), calls=%async_computation.14 | async-start | bytes 12091392 | tf_op jit(solution)/shard_map/reduce_scatter | solution.py:225
  944.0 354.3 %all-reduce.9.cloned.1.call-start = ((), (), s32[]{:S(2)}) async-start(), calls=%async_computation.16 | async-start | bytes 6127616 | tf_op jit(solution)/shard_map/psum | solution.py:235
  1228.8 8.2 copy-start.26
  1228.8 8.2 copy-start.6
  1236.9 1.5 copy-start.9
  1236.9 28.1 %copy-start.2 = (f32[640,1024]{1,0:T(8,128)S(1)}, f32[640,1024]{1,0:T(8,128)}, u32[]{:S(2)}) copy-start(f32[640,1024]{1,0:T(8,128)} %copy-done.1) | copy-start | bytes 7864324
  1236.9 28.1 %copy-start.32 = (f32[640]{0:T(1024)S(1)}, f32[640]{0:T(1024)}, u32[]{:S(2)}) copy-start(f32[640]{0:T(1024)} %copy-done.31) | copy-start | bytes 7684
  1298.3 4.4 copy-start.20
  1298.3 5.6 copy-start.18
  (8 other events, 7.2 us)
Sparse Core Ops, SparseCore 0:
  10.2 100.5 all-gather.6
  113.0 46.8 all-gather.8
  162.1 153.2 all-gather.10
  317.4 85.6 all-gather.12
  439.1 65.3 reduce-scatter.6
  507.9 105.0 reduce-scatter.10
  927.8 115.0 reduce-scatter.4
  1046.9 181.7 reduce-scatter.8
  1231.4 66.8 all-reduce.8
where the time goes:
time: 1320 us; the launch traced here: 1310 us
  waiting for transfers between devices  468 us (35%)
  matrix products  413 us (31%)
  other arithmetic  163 us (12%)
  blocking collectives  120 us (9%)
  local copies, waits for them, and re-layouts  116 us (9%)
  starting transfers between devices  16.7 us (1%)
  between operations  15.6 us (1%)
    reduce_scatter x1, waiting for transfers between devices, local(): lax.psum_scatter(gradients[4].astype(jnp.bfloat16), 'fsdp', scatter_dimen...  186 us
    reduce_scatter x1, waiting for transfers between devices, local(): lax.psum_scatter(gradients[2].astype(jnp.bfloat16), 'fsdp', scatter_dimen...  87.6 us
    all_gather x1, waiting for transfers between devices, local(): lax.all_gather(w_qkv, 'fsdp', axis=0, tiled=True)  81.7 us
    dot_general x10, matrix products, one_block(): jnp.einsum('qhd,khd->hqk', q_block, key_rows, preferred_element_type=jnp....  79 us
    convert_element_type x5, other arithmetic, one_block(): score_grad = (probs * (prob_grad - inner)).astype(jnp.bfloat16)  72.9 us
    dot_general x5, matrix products, one_block(): jnp.einsum('qhd,khd->hqk', g_block, value_rows, preferred_element_type=jn...  71.5 us
    dot_general x5, matrix products, one_block(): jnp.einsum('hqk,qhd->khd', probs.astype(jnp.bfloat16), g_block, preferred...  65.9 us
    all_to_all x1, blocking collectives, local(): lax.all_to_all(rotated_grad, 'seq', split_axis=1, concat_axis=3, tiled=True)  63.1 us
  transfers between devices with their start and end apart: 12, of which 8 were waited for; matrix products, arithmetic and copies ran while one was open for 49% of the time, Pallas kernels for 0%

commit v1 on v0

v1 whole, which is shorter than its diff:
```python
import functools
import math

import jax
import jax.numpy as jnp
from jax import lax
from jax.experimental import pallas as pl
from jax.experimental.pallas import tpu as pltpu
from jax.sharding import PartitionSpec as P

HEADS = 16
HEAD = 64
HALF = HEAD // 2
ROW_TILE = 16
BF16 = jnp.bfloat16
F32 = jnp.float32

eps = 1e-05
rope_base = 160000.0
VMEM_BYTES = 60 << 20


def dot_nn(a, b):
    return lax.dot_general(a, b, (((1,), (0,)), ((), ())), preferred_element_type=F32)


def dot_nt(a, b):
    return lax.dot_general(a, b, (((1,), (1,)), ((), ())), preferred_element_type=F32)


def dot_tn(a, b):
    return lax.dot_general(a, b, (((0,), (0,)), ((), ())), preferred_element_type=F32)


def block_rows(rows, wanted):
    best = rows
    for size in range(ROW_TILE, min(rows, wanted) + 1, ROW_TILE):
        if rows % size == 0:
            best = size
    return best


def centred_stats(values):
    average = jnp.mean(values, -1, keepdims=True)
    centred = values - average
    inverse = lax.rsqrt(jnp.mean(centred * centred, -1, keepdims=True) + eps)
    return centred * inverse, inverse


def norm_backward(grad, xhat, inverse):
    return inverse * (
        grad
        - jnp.mean(grad, -1, keepdims=True)
        - xhat * jnp.mean(grad * xhat, -1, keepdims=True)
    )


def partner(values):
    width = values.shape[-1]
    if width % 128:
        return jnp.concatenate([values[:, HALF:], values[:, :HALF]], 1)
    lane = lax.broadcasted_iota(jnp.int32, values.shape, 1)
    return jnp.where(
        lane % HEAD < HALF,
        pltpu.roll(values, width - HALF, 1),
        pltpu.roll(values, HALF, 1),
    )


def widen(table, width):
    return jnp.concatenate([table] * (width // table.shape[1]), 1)


def head_of_lane(shape):
    return lax.broadcasted_iota(jnp.int32, shape, 1) // HEAD


def only_head(values, head):
    return jnp.where(head_of_lane(values.shape) == head, values, jnp.zeros_like(values))


def qkv_body(x_ref, w_ref, cos_ref, sin_ref, q_ref, k_ref, v_ref):
    width = q_ref.shape[1]
    packed = dot_nn(x_ref[...], w_ref[...])
    cosine = widen(cos_ref[...], width)
    sine = widen(sin_ref[...], width)
    for at, ref in enumerate((q_ref, k_ref)):
        part = packed[:, at * width : (at + 1) * width]
        ref[...] = (part * cosine + partner(part) * sine).astype(BF16)
    v_ref[...] = packed[:, 2 * width :].astype(BF16)


def qkv_heads(x, weights, cosine, sine):
    rows, depth = x.shape
    width = weights.shape[1] // 3
    step = block_rows(rows, 512)
    table = cosine.shape[1]
    by_row = lambda columns: pl.BlockSpec((step, columns), lambda i: (i, 0))
    return pl.pallas_call(
        qkv_body,
        grid=(rows // step,),
        in_specs=[
            by_row(depth),
            pl.BlockSpec((depth, 3 * width), lambda i: (0, 0)),
            by_row(table),
            by_row(table),
        ],
        out_specs=[by_row(width)] * 3,
        out_shape=[jax.ShapeDtypeStruct((rows, width), BF16)] * 3,
        compiler_params=pltpu.CompilerParams(vmem_limit_bytes=VMEM_BYTES),
        cost_estimate=pl.CostEstimate(
            flops=6 * rows * depth * width,
            bytes_accessed=2 * (rows * depth + 3 * depth * width + 3 * rows * width),
            transcendentals=0,
        ),
        name="qkv_rope",
    )(x, weights, cosine, sine)


def attend_body(q_ref, k_ref, v_ref, out_ref, lse_ref):
    width = q_ref.shape[1]
    queries = q_ref[...] * jnp.asarray(HEAD**-0.5, BF16)
    keys = k_ref[...]
    values = v_ref[...]
    for head in range(width // HEAD):
        scores = dot_nt(only_head(queries, head), keys)
        peak = jnp.max(scores, -1, keepdims=True)
        exponent = jnp.exp(scores - peak)
        total = jnp.sum(exponent, -1, keepdims=True)
        out = dot_nn(exponent.astype(BF16), values) / total
        lse = jnp.broadcast_to(peak + jnp.log(total), out.shape)
        if head:
            here = head_of_lane(out.shape) == head
            out = jnp.where(here, out, previous_out)
            lse = jnp.where(here, lse, previous_lse)
        previous_out, previous_lse = out, lse
    out_ref[...] = out.astype(BF16)
    lse_ref[...] = lse.T


def attend(queries, keys, values):
    rows, local_width = queries.shape
    width = min(128, local_width)
    step = block_rows(rows, 256)
    q_spec = pl.BlockSpec((step, width), lambda g, i: (i, g))
    k_spec = pl.BlockSpec((rows, width), lambda g, i: (0, g))
    return pl.pallas_call(
        attend_body,
        grid=(local_width // width, rows // step),
        in_specs=[q_spec, k_spec, k_spec],
        out_specs=[q_spec, pl.BlockSpec((width, step), lambda g, i: (g, i))],
        out_shape=[
            jax.ShapeDtypeStruct((rows, local_width), BF16),
            jax.ShapeDtypeStruct((local_width, rows), F32),
        ],
        compiler_params=pltpu.CompilerParams(vmem_limit_bytes=VMEM_BYTES),
        cost_estimate=pl.CostEstimate(
            flops=16 * rows * rows * local_width,
            bytes_accessed=8 * rows * local_width,
            transcendentals=rows * rows * local_width // HEAD,
        ),
        name="attend",
    )(queries, keys, values)


def attend_back_body(
    q_ref, k_ref, v_ref, g_ref, out_ref, lse_ref, cos_ref, sin_ref, cos_all_ref, sin_all_ref,
    dq_ref, dk_ref, dv_ref, dk_sum, dv_sum,
):
    width = q_ref.shape[1]
    step = pl.program_id(1)

    @pl.when(step == 0)
    def _():
        dk_sum[...] = jnp.zeros_like(dk_sum)
        dv_sum[...] = jnp.zeros_like(dv_sum)

    factor = HEAD**-0.5
    queries = q_ref[...] * jnp.asarray(factor, BF16)
    keys = k_ref[...]
    values = v_ref[...]
    grads = g_ref[...]
    product = (grads.astype(F32) * out_ref[...].astype(F32)).T
    dq = jnp.zeros(product.shape, F32)
    for head in range(width // HEAD):
        own_queries = only_head(queries, head)
        own_grads = only_head(grads, head)
        lse = lse_ref[head * HEAD : head * HEAD + 1, :]
        inner = jnp.sum(product[head * HEAD : (head + 1) * HEAD], 0, keepdims=True)
        probs = jnp.exp(dot_nt(keys, own_queries) - lse)
        prob_grad = dot_nt(values, own_grads)
        score_grad = (probs * (prob_grad - inner)).astype(BF16)
        dv_sum[...] += dot_nn(probs.astype(BF16), own_grads)
        dk_sum[...] += dot_nn(score_grad, own_queries)
        dq = dq + dot_tn(only_head(keys, head), score_grad)
    dq = (dq.T * factor).astype(BF16).astype(F32)
    dq_ref[...] = (dq * cos_ref[...] - partner(dq) * sin_ref[...]).astype(BF16)

    @pl.when(step == pl.num_programs(1) - 1)
    def _():
        dk = dk_sum[...].astype(BF16).astype(F32)
        dk_ref[...] = (dk * cos_all_ref[...] - partner(dk) * sin_all_ref[...]).astype(BF16)
        dv_ref[...] = dv_sum[...].astype(BF16)


def attend_back(queries, keys, values, grads, out, lse, cosine, sine):
    rows, local_width = queries.shape
    width = min(128, local_width)
    step = block_rows(rows, 512)
    q_spec = pl.BlockSpec((step, width), lambda g, i: (i, g))
    k_spec = pl.BlockSpec((rows, width), lambda g, i: (0, g))
    t_spec = pl.BlockSpec((step, width), lambda g, i: (i, 0))
    all_spec = pl.BlockSpec((rows, width), lambda g, i: (0, 0))
    return pl.pallas_call(
        attend_back_body,
        grid=(local_width // width, rows // step),
        in_specs=[
            q_spec, k_spec, k_spec, q_spec, q_spec,
            pl.BlockSpec((width, step), lambda g, i: (g, i)),
            t_spec, t_spec, all_spec, all_spec,
        ],
        out_specs=[q_spec, k_spec, k_spec],
        out_shape=[jax.ShapeDtypeStruct((rows, local_width), BF16)] * 3,
        scratch_shapes=[pltpu.VMEM((rows, width), F32)] * 2,
        compiler_params=pltpu.CompilerParams(vmem_limit_bytes=VMEM_BYTES),
        cost_estimate=pl.CostEstimate(
            flops=40 * rows * rows * local_width,
            bytes_accessed=20 * rows * local_width,
            transcendentals=rows * rows * local_width // HEAD,
        ),
        name="attend_back",
    )(queries, keys, values, grads, out, lse, cosine, sine, cosine, sine)


def mlp_body(x_ref, c_ref, wi_ref, wo_ref, hidden_ref, gate_up_ref, back_ref, out_ref):
    units = wo_ref.shape[0]
    gate_up = dot_nn(x_ref[...], wi_ref[...])
    hidden_grad = dot_nt(c_ref[...], wo_ref[...])
    gate = gate_up[:, :units]
    up = gate_up[:, units:]
    share = 0.5 * (1.0 + lax.erf(gate * 2.0**-0.5))
    activated = gate * share
    slope = share + gate * jnp.exp(-0.5 * gate * gate) * (2.0 * math.pi) ** -0.5
    hidden = (activated * up).astype(BF16)
    hidden_ref[...] = hidden
    gate_grad = (hidden_grad * up * slope).astype(BF16)
    up_grad = (hidden_grad * activated).astype(BF16)
    both = jnp.concatenate([gate_grad, up_grad], 1)
    gate_up_ref[...] = both
    back_ref[...] = dot_nt(both, wi_ref[...]).astype(BF16)
    out_ref[...] = dot_nn(hidden, wo_ref[...]).astype(BF16)


def mlp(x, cotangent, w_in, w_out):
    rows, depth = x.shape
    units = w_out.shape[0]
    step = block_rows(rows, 320)
    by_row = lambda columns: pl.BlockSpec((step, columns), lambda i: (i, 0))
    whole = lambda shape: pl.BlockSpec(shape, lambda i: (0, 0))
    return pl.pallas_call(
        mlp_body,
        grid=(rows // step,),
        in_specs=[by_row(depth), by_row(depth), whole(w_in.shape), whole(w_out.shape)],
        out_specs=[by_row(units), by_row(2 * units), by_row(depth), by_row(depth)],
        out_shape=[
            jax.ShapeDtypeStruct((rows, columns), BF16)
            for columns in (units, 2 * units, depth, depth)
        ],
        compiler_params=pltpu.CompilerParams(vmem_limit_bytes=VMEM_BYTES),
        cost_estimate=pl.CostEstimate(
            flops=12 * rows * depth * units,
            bytes_accessed=2 * rows * (4 * depth + 3 * units) + 6 * depth * units,
            transcendentals=2 * rows * units,
        ),
        name="mlp",
    )(x, cotangent, w_in, w_out)


def local(seq_size, fsdp_size, activations, cotangent, gain_attn, w_qkv, w_attn_out, gain_mlp, w_in, w_mlp_out):
    _, positions, width = activations.shape
    shard = w_qkv.shape[0]
    ff_shard = w_mlp_out.shape[0]
    local_width = width // seq_size
    length = positions * seq_size
    me = lax.axis_index("seq")
    row = lax.axis_index("fsdp")

    bits = []
    bit = seq_size // 2
    while bit:
        bits.append(bit)
        bit //= 2
    order = [0]
    for bit in bits:
        order = order + [member ^ bit for member in order]

    def swap(values, axis, size, offset):
        return lax.ppermute(values, axis, [(i, i ^ offset) for i in range(size)])

    def gather_seq(values):
        pieces = [values]
        for bit in bits:
            pieces = pieces + [swap(piece, "seq", seq_size, bit) for piece in pieces]
        return pieces

    def scatter_seq(pieces):
        for bit in reversed(bits):
            half = len(pieces) // 2
            sent = [swap(piece, "seq", seq_size, bit) for piece in pieces[half:]]
            pieces = [
                (kept.astype(F32) + got.astype(F32)).astype(BF16)
                if half > 1
                else kept.astype(F32) + got.astype(F32)
                for kept, got in zip(pieces[:half], sent)
            ]
        return pieces[0]

    def exchange_seq(pieces):
        return [
            swap(piece, "seq", seq_size, offset) if offset else piece
            for piece, offset in zip(pieces, order)
        ]

    def by_member(pieces):
        stacked = jnp.stack(pieces)
        slots = jnp.asarray([order.index(member) for member in range(seq_size)])
        return [
            lax.dynamic_index_in_dim(stacked, slots[me ^ member], 0, keepdims=False)
            for member in range(seq_size)
        ]

    def gather_fsdp(values):
        rows = values.shape[0]
        gathered = values
        at = 0
        bit = fsdp_size // 2
        while bit:
            other = swap(gathered, "fsdp", fsdp_size, bit)
            high = (row & bit) != 0
            gathered = jnp.stack(
                [jnp.where(high, other, gathered), jnp.where(high, gathered, other)], at
            )
            at += 1
            bit //= 2
        return gathered.reshape(fsdp_size * rows, values.shape[1])

    def scatter_fsdp(values):
        rows = values.shape[0] // fsdp_size
        bit = 1
        left = values.reshape(fsdp_size // 2, 2, rows, values.shape[1])
        while True:
            mine = jnp.where((row & bit) != 0, 1, 0)
            kept = lax.dynamic_index_in_dim(left, mine, 1, keepdims=False)
            sent = lax.dynamic_index_in_dim(left, 1 - mine, 1, keepdims=False)
            total = kept.astype(F32) + swap(sent, "fsdp", fsdp_size, bit).astype(F32)
            bit *= 2
            if bit == fsdp_size:
                return total[0]
            left = total.astype(BF16).reshape(fsdp_size // (2 * bit), 2, rows, values.shape[1])

    own_gain_attn = gain_attn.astype(F32)[:, None]
    own_gain_mlp = gain_mlp.astype(F32)[:, None]

    qkv_slice = jnp.concatenate(
        [
            lax.dynamic_slice(w_qkv, (0, part * width + me * local_width), (shard, local_width))
            for part in range(3)
        ],
        1,
    )
    qkv_slice = (qkv_slice.astype(F32) * own_gain_attn).astype(BF16)
    qkv_full = gather_fsdp(qkv_slice)

    tokens = activations.reshape(positions, width).astype(F32)
    xhat, inverse = centred_stats(tokens)
    x_all = jnp.concatenate(gather_seq(xhat.astype(BF16)), 0)

    out_rows = shard // seq_size
    attn_out_slice = lax.dynamic_slice(w_attn_out, (me * out_rows, 0), (out_rows, width))
    attn_out_full = lax.all_gather(attn_out_slice, ("fsdp", "seq"), axis=0, tiled=True)

    unit_share = -(-ff_shard // seq_size)
    unit_share = -(-unit_share // ROW_TILE) * ROW_TILE
    padding = unit_share * seq_size - ff_shard
    units = fsdp_size * unit_share
    mlp_out_slice = lax.dynamic_slice(
        jnp.pad(w_mlp_out, ((0, padding), (0, 0))), (me * unit_share, 0), (unit_share, width)
    )
    in_slice = jnp.pad(
        w_in.reshape(shard, 2 * fsdp_size, ff_shard), ((0, 0), (0, 0), (0, padding))
    )
    in_slice = lax.dynamic_slice(
        in_slice, (0, 0, me * unit_share), (shard, 2 * fsdp_size, unit_share)
    ).reshape(shard, 2 * units)
    in_slice = (in_slice.astype(F32) * own_gain_mlp).astype(BF16)
    in_full = lax.all_gather(in_slice, "fsdp", axis=0, tiled=True)
    mlp_out_full = lax.all_gather(mlp_out_slice, "fsdp", axis=0, tiled=True)

    table = min(128, local_width)
    lane = lax.broadcasted_iota(jnp.int32, (length, table), 1)
    at = lax.broadcasted_iota(jnp.int32, (length, table), 0)
    members = jnp.asarray(order)[:, None, None] ^ me
    place = (members * positions + at.reshape(seq_size, positions, table) % positions).reshape(
        length, table
    )
    frequency = jnp.exp((lane % HALF).astype(F32) * (-2.0 * math.log(rope_base) / HEAD))
    angles = place.astype(F32) * frequency
    cosine = jnp.cos(angles)
    sine = jnp.sin(angles) * jnp.where(lane % HEAD < HALF, -1.0, 1.0)

    queries, keys, values = qkv_heads(x_all, qkv_full, cosine, sine)
    attended_heads, lse = attend(queries, keys, values)

    def row_pieces(array):
        return [array[n * positions : (n + 1) * positions] for n in range(seq_size)]

    attended_pieces = exchange_seq(row_pieces(attended_heads))
    attended = jnp.concatenate(attended_pieces, 1)
    attn_out_ordered = jnp.concatenate(
        [
            lax.dynamic_slice(
                attn_out_full, ((me ^ member) * local_width, 0), (local_width, width)
            )
            for member in order
        ],
        0,
    )
    mixed = tokens + dot_nn(attended, attn_out_ordered)
    xhat_mlp, inverse_mlp = centred_stats(mixed)
    x_mlp_all = jnp.concatenate(gather_seq(xhat_mlp.astype(BF16)), 0)
    own_cotangent = cotangent.reshape(positions, width)
    cotangent_all = jnp.concatenate(gather_seq(own_cotangent), 0)

    hidden, gate_up_grad, back, out = mlp(x_mlp_all, cotangent_all, in_full, mlp_out_full)
    back_sum = scatter_seq(row_pieces(back))
    output = (mixed + scatter_seq(row_pieces(out))).astype(BF16).reshape(activations.shape)
    grad_in = dot_tn(x_mlp_all, gate_up_grad).astype(BF16)
    grad_mlp_out = dot_tn(hidden, cotangent_all).astype(BF16)

    mixed_grad = own_cotangent.astype(F32) + norm_backward(back_sum, xhat_mlp, inverse_mlp)
    mixed_low = mixed_grad.astype(BF16)
    attended_grad = dot_nt(mixed_low, attn_out_ordered).astype(BF16)
    grads = jnp.concatenate(
        exchange_seq(
            [attended_grad[:, n * local_width : (n + 1) * local_width] for n in range(seq_size)]
        ),
        0,
    )
    grad_attn_out = dot_tn(jnp.concatenate(by_member(attended_pieces), 1), mixed_low).astype(BF16)
    grad_attn_out = scatter_seq(
        [
            lax.dynamic_slice(grad_attn_out, (0, (me ^ member) * local_width), (width, local_width))
            for member in order
        ]
    ).astype(BF16)

    d_queries, d_keys, d_values = attend_back(
        queries, keys, values, grads, attended_heads, lse, cosine, sine
    )
    packed_grad = jnp.concatenate([d_queries, d_keys, d_values], 1)
    normed_grad = dot_nt(packed_grad, qkv_full).astype(BF16)
    grad_qkv = dot_tn(x_all, packed_grad).astype(BF16)
    normed_grad = scatter_seq(row_pieces(normed_grad))
    d_input = (mixed_grad + norm_backward(normed_grad, xhat, inverse)).astype(BF16)
    d_input = d_input.reshape(activations.shape)

    def reduce_fsdp(values):
        return lax.psum_scatter(values, "fsdp", scatter_dimension=0, tiled=True)

    sum_in = reduce_fsdp(grad_in)
    sum_mlp_out = reduce_fsdp(grad_mlp_out)
    sum_attn_out = reduce_fsdp(grad_attn_out)
    sum_qkv = scatter_fsdp(grad_qkv).astype(BF16)

    in_pieces = [
        piece.reshape(shard, 2 * fsdp_size, unit_share) for piece in by_member(gather_seq(sum_in))
    ]
    all_in = jnp.concatenate(in_pieces, 2)[:, :, :ff_shard].reshape(shard, -1).astype(F32)
    all_mlp_out = jnp.concatenate(by_member(gather_seq(sum_mlp_out)), 0)[:ff_shard].astype(F32)
    all_attn_out = jnp.concatenate(by_member(gather_seq(sum_attn_out)), 1).astype(F32)
    qkv_pieces = by_member(gather_seq(sum_qkv))
    all_qkv = jnp.concatenate(
        [
            piece[:, part * local_width : (part + 1) * local_width]
            for part in range(3)
            for piece in qkv_pieces
        ],
        1,
    ).astype(F32)
    grad_gain_attn = jnp.sum(all_qkv * w_qkv.astype(F32), 1)
    grad_gain_mlp = jnp.sum(all_in * w_in.astype(F32), 1)
    return (
        output,
        d_input,
        grad_gain_attn,
        grad_gain_mlp,
        all_qkv * own_gain_attn,
        all_attn_out,
        all_in * own_gain_mlp,
        all_mlp_out,
    )


def solution(mesh):
    in_specs = (
        P("fsdp", "seq", None),
        P("fsdp", "seq", None),
        P("fsdp"),
        P("fsdp", None),
        P("fsdp", None),
        P("fsdp"),
        P("fsdp", None),
        P("fsdp", None),
    )
    out_specs = (
        P("fsdp", "seq", None),
        P("fsdp", "seq", None),
        P("fsdp"),
        P("fsdp"),
        P("fsdp", None),
        P("fsdp", None),
        P("fsdp", None),
        P("fsdp", None),
    )
    body = functools.partial(local, mesh.shape["seq"], mesh.shape["fsdp"])
    return jax.shard_map(body, mesh=mesh, in_specs=in_specs, out_specs=out_specs, check_vma=False)
```

time: 1320 us -> 622 us (0.47)
  matrix products: 413 us -> 41.1 us
  waiting for transfers between devices: 468 us -> 216 us
  Pallas kernels: 0 us -> 161 us
  blocking collectives: 120 us -> 0 us
  local copies, waits for them, and re-layouts: 116 us -> 36.2 us
  other arithmetic: 163 us -> 84.6 us
  starting transfers between devices: 16.7 us -> 50.6 us
    dot_general x47 -> x7, matrix products: 413 us -> 41.1 us  [the longest x4 29.3 us: dot_tn(): lax.dot_general(a, b, (((0,), (0,)), ((), ())), preferred_element_type=F32)]
    reduce_scatter x4 -> x3, waiting for transfers between devices: 273 us -> 0.02 us  [reduce_fsdp(): return lax.psum_scatter(values, 'fsdp', scatter_dimension=0, tiled=True)]
    ppermute x0 -> x45, waiting for transfers between devices: none -> 216 us  [swap(): return lax.ppermute(values, axis, [(i, i ^ offset) for i in range(size)])]
    pallas_call x0 -> x4, Pallas kernels: none -> 161 us  [the longest x1 71.9 us: attend_back(): pl.pallas_call(attend_back_body, grid=(local_width // width, rows // step...]
    all_gather x4 -> x3, waiting for transfers between devices: 93.9 us -> 0.01 us  [the longest x1 0.01 us: local(): lax.all_gather(attn_out_slice, ('fsdp', 'seq'), axis=0, tiled=True)]
    all_to_all x3 -> x0, waiting for transfers between devices: 68.7 us -> none  [the longest x1 58.1 us: local(): lax.all_to_all(rotated, 'seq', split_axis=3, concat_axis=1, tiled=True)]
    convert_element_type x16 -> x17, other arithmetic: 85.9 us -> 18.7 us  [the longest x4 10.4 us: scatter_seq(): (kept.astype(F32) + got.astype(F32)).astype(BF16)]
    all_to_all x1 -> x0, blocking collectives: 63.1 us -> none  [local(): lax.all_to_all(rotated_grad, 'seq', split_axis=1, concat_axis=3, tiled=True)]
  transfers between devices with their start and end apart: 12 -> 51, of which waited for: 8 -> 18; matrix products, arithmetic and copies ran while one was open for 49% -> 23% of each run, Pallas kernels for 0% -> 21%
where the time goes in v1:
time: 622 us; the launch traced here: 613 us
  waiting for transfers between devices  216 us (35%)
  Pallas kernels  161 us (26%)
  other arithmetic  84.6 us (14%)
  starting transfers between devices  50.6 us (8%)
  matrix products  41.1 us (7%)
  local copies, waits for them, and re-layouts  36.2 us (6%)
  between operations  23.2 us (4%)
    ppermute x45, waiting for transfers between devices, swap(): return lax.ppermute(values, axis, [(i, i ^ offset) for i in range(size)])  216 us
    pallas_call x1, Pallas kernels, attend_back(): pl.pallas_call(attend_back_body, grid=(local_width // width, rows // step...  71.9 us
    ppermute x45, starting transfers between devices, swap(): return lax.ppermute(values, axis, [(i, i ^ offset) for i in range(size)])  50.2 us
    pallas_call x1, Pallas kernels, attend(): pl.pallas_call(attend_body, grid=(local_width // width, rows // step), in...  46 us
    pallas_call x1, Pallas kernels, mlp(): pl.pallas_call(mlp_body, grid=(rows // step,), in_specs=[by_row(depth), b...  33.5 us
    dot_general x4, matrix products, dot_tn(): lax.dot_general(a, b, (((0,), (0,)), ((), ())), preferred_element_type=F32)  29.3 us
    concatenate x1, other arithmetic, local(): x_mlp_all = jnp.concatenate(gather_seq(xhat_mlp.astype(BF16)), 0)  14.6 us
    unnamed x111, local copies, waits for them, and re-layouts  12.6 us
  transfers between devices with their start and end apart: 51, of which 18 were waited for; matrix products, arithmetic and copies ran while one was open for 23% of the time, Pallas kernels for 21%

profile of v1, /device:TPU:1, one launch (start us, length us, event | category | flops | bytes accessed | tf_op | source)
XLA Modules:
  0.0 612.8 jit_solution(6928148238865519670)
XLA Ops:
  17.1 2.4 collective-permute-start.3
  22.8 2.3 copy.27
  27.2 2.1 collective-permute-done.3
  30.5 9.3 %collective-permute-done.4 = bf16[2,128,768]{2,1,0:T(8,128)(2,1)S(1)} collective-permute-done((bf16[2,128,768]{2,1,0:T(8,128)(2,1)S(1)}, bf16[2,128,768]{2,1,0:T(8,128)(2,1)S(1)}, u32[]{:S(2)}, u32[]{:S(2)}) %collective-permute-start.4) | collective-permute-done | bytes 393248 | tf_op jit(solution)/shard_map/ppermute | solution.py:298
  39.9 6.1 collective-permute-done
  49.8 8.7 %select_multiply_fusion = (f32[2560,128]{1,0:T(8,128)}, f32[2560,128]{1,0:T(8,128)}) fusion(s32[128]{0:T(128)S(1)} %get-tuple-element.110, s32[128]{0:T(128)S(1)} %get-tuple-element.112, s32[128]{0:T(128)S(1)} %get-tuple-element.111, s32[128]{0:T(128)S(1)} %get-tuple-element.113, s32[2560]{0:T(1024)S(1)} %rem.32, s32[2560]{0:T(1024)S(1)} %broadcast_add_fusion, ...), kind=kLoop, calls=%fused_computation.73 | loop fusion | flops 3604480 | bytes 2657024 | tf_op jit(solution)/shard_map/mul | solution.py:409
  58.6 13.0 %collective-permute-done.5 = bf16[2,2,128,768]{3,2,0,1:T(8,128)(2,1)} collective-permute-done((bf16[2,2,128,768]{3,2,0,1:T(8,128)(2,1)}, bf16[2,2,128,768]{3,2,0,1:T(8,128)(2,1)}, u32[]{:S(2)}, u32[]{:S(2)}) %collective-permute-start.5) | collective-permute-done | bytes 786464 | tf_op jit(solution)/shard_map/ppermute | solution.py:298
  74.2 5.0 pad_maximum_fusion.x_ref
  79.2 9.6 %qkv_rope.1 = (bf16[2560,256]{1,0:T(8,128)(2,1)}, bf16[2560,256]{1,0:T(8,128)(2,1)}, bf16[2560,256]{1,0:T(8,128)(2,1)}) custom-call(bf16[2560,1024]{1,0:T(8,128)(2,1)} %pad_maximum_fusion.x_ref, bf16[1024,768]{1,0:T(8,128)(2,1)} %bitcast.140, f32[2560,128]{1,0:T(8,128)} %get-tuple-element.101.cos_ref.cos_all_ref, ...), custom_call_target="tpu_custom_call" | custom-call | flops 4026531840 | bytes 10747904 | tf_op jit(solution)/shard_map/qkv_rope/pallas_call | solution.py:99
  88.8 46.0 %attend.1 = (bf16[2560,256]{1,0:T(8,128)(2,1)}, f32[256,2560]{1,0:T(8,128)}) custom-call(bf16[2560,256]{1,0:T(8,128)(2,1)} %get-tuple-element.20.q_ref, bf16[2560,256]{1,0:T(8,128)(2,1)} %get-tuple-element.21.k_ref, bf16[2560,256]{1,0:T(8,128)(2,1)} %get-tuple-element.22.v_ref), custom_call_target="tpu_custom_call" | custom-call | flops 26843545600 | bytes 5242880 | tf_op jit(solution)/shard_map/attend/pallas_call | solution.py:147
  142.4 3.0 collective-permute-done.6
  145.4 9.6 %collective-permute-done.8 = bf16[640,256]{1,0:T(8,128)(2,1)S(1)} collective-permute-done((bf16[640,256]{1,0:T(8,128)(2,1)S(1)}, bf16[640,256]{1,0:T(8,128)(2,1)S(1)}, u32[]{:S(2)}, u32[]{:S(2)}) %collective-permute-start.8) | collective-permute-done | bytes 327712 | tf_op jit(solution)/shard_map/ppermute | solution.py:298
  155.7 3.1 fusion.48
  161.0 19.5 %collective-permute-done.12 = bf16[640,1024]{1,0:T(8,128)(2,1)} collective-permute-done((bf16[640,1024]{1,0:T(8,128)(2,1)}, bf16[640,1024]{1,0:T(8,128)(2,1)}, u32[]{:S(2)}, u32[]{:S(2)}) %collective-permute-start.12) | collective-permute-done | bytes 1310752 | tf_op jit(solution)/shard_map/ppermute | solution.py:298
  180.5 2.9 collective-permute-start.14
  183.5 25.0 %collective-permute-done.9 = bf16[640,1024]{1,0:T(8,128)(2,1)S(1)} collective-permute-done((bf16[640,1024]{1,0:T(8,128)(2,1)S(1)}, bf16[640,1024]{1,0:T(8,128)(2,1)S(1)}, u32[]{:S(2)}, u32[]{:S(2)}) %collective-permute-start.9) | collective-permute-done | bytes 1310752 | tf_op jit(solution)/shard_map/ppermute | solution.py:298
  210.2 5.3 pad_maximum_fusion.2.c_ref
  217.7 14.6 %pad_maximum_fusion.1.x_ref = bf16[2560,1024]{1,0:T(8,128)(2,1)} fusion(bf16[640,1024]{1,0:T(8,128)(2,1)S(1)} %collective-permute-done.11, bf16[640,1024]{1,0:T(8,128)(2,1)S(1)} %collective-permute-done.10, bf16[640,1024]{1,0:T(8,128)(2,1)S(1)} %collective-permute-done.9, bf16[640,1024]{1,0:T(8,128)(2,1)S(1)} %fusion.16), kind=kLoop, calls=%fused_computation.2 | loop fusion | flops 20971520 | bytes 10485760 | tf_op jit(solution)/shard_map/concatenate | solution.py:430
  232.3 33.5 %mlp.1 = (bf16[2560,768]{1,0:T(8,128)(2,1)}, bf16[2560,1536]{1,0:T(8,128)(2,1)}, bf16[2560,1024]{1,0:T(8,128)(2,1)}, bf16[2560,1024]{1,0:T(8,128)(2,1)}) custom-call(bf16[2560,1024]{1,0:T(8,128)(2,1)} %pad_maximum_fusion.1.x_ref, bf16[2560,1024]{1,0:T(8,128)(2,1)} %pad_maximum_fusion.2.c_ref, bf16[1024,1536]{1,0:T(8,128)(2,1)} %all-gather.6.cloned.1.call-done.wi_ref, ...), custom_call_target="tpu_custom_call" | custom-call | flops 24159191040 | bytes 37486592 | tf_op jit(solution)/shard_map/mlp/pallas_call | solution.py:260
  265.8 3.7 fusion.44
  282.8 3.5 add_convert_fusion.2
  287.7 3.4 add_convert_fusion.5
  291.4 7.3 %convolution_convert_fusion.3 = bf16[768,1024]{1,0:T(8,128)(2,1)} fusion(bf16[2560,768]{1,0:T(8,128)(2,1)S(1)} %copy-done.47, bf16[640,1024]{1,0:T(8,128)(2,1)S(1)} %copy-done.22, bf16[640,1024]{1,0:T(8,128)(2,1)S(1)} %copy-done.20, bf16[640,1024]{1,0:T(8,128)(2,1)} %collective-permute-done.12, bf16[640,1024]{1,0:T(8,128)(2,1)} %bitcast.8), kind=kOutput, calls=%fused_computation.43 | convolution fusion | flops 4048289792 | bytes 10747904 | tf_op jit(solution)/shard_map/dot_general | solution.py:32
  298.7 18.3 %collective-permute-done.20 = bf16[640,1024]{1,0:T(8,128)(2,1)} collective-permute-done((bf16[640,1024]{1,0:T(8,128)(2,1)}, bf16[640,1024]{1,0:T(8,128)(2,1)}, u32[]{:S(2)}, u32[]{:S(2)}) %collective-permute-start.20) | collective-permute-done | bytes 1310752 | tf_op jit(solution)/shard_map/ppermute | solution.py:298
  317.0 3.2 fusion.14
  320.2 24.8 %collective-permute-done.17 = bf16[640,1024]{1,0:T(8,128)(2,1)} collective-permute-done((bf16[640,1024]{1,0:T(8,128)(2,1)}, bf16[640,1024]{1,0:T(8,128)(2,1)}, u32[]{:S(2)}, u32[]{:S(2)}) %collective-permute-start.17) | collective-permute-done | bytes 1310752 | tf_op jit(solution)/shard_map/ppermute | solution.py:298
  345.1 5.2 multiply_add_fusion
  354.1 2.3 collective-permute-done.37
  358.0 3.9 convolution_convert_fusion.5
  365.1 4.7 collective-permute-done.38
  372.1 13.5 %convolution_convert_fusion.1 = bf16[1024,1536]{1,0:T(8,128)(2,1)} fusion(bf16[2560,1536]{1,0:T(8,128)(2,1)} %get-tuple-element.30, bf16[640,1024]{1,0:T(8,128)(2,1)} %copy-done.18, bf16[640,1024]{1,0:T(8,128)(2,1)} %copy-done.17, bf16[640,1024]{1,0:T(8,128)(2,1)S(1)} %copy-done.16, bf16[640,1024]{1,0:T(8,128)(2,1)S(1)} %copy-done.12), kind=kOutput, calls=%fused_computation.4 | convolution fusion | flops 8075608064 | bytes 16252928 | tf_op jit(solution)/shard_map/dot_general | solution.py:32
  385.6 2.3 pad_maximum_fusion.9.g_ref
  387.9 71.9 %attend_back.1 = (bf16[2560,256]{1,0:T(8,128)(2,1)}, bf16[2560,256]{1,0:T(8,128)(2,1)}, bf16[2560,256]{1,0:T(8,128)(2,1)}) custom-call(bf16[2560,256]{1,0:T(8,128)(2,1)} %get-tuple-element.20.q_ref, bf16[2560,256]{1,0:T(8,128)(2,1)} %get-tuple-element.21.k_ref, bf16[2560,256]{1,0:T(8,128)(2,1)} %get-tuple-element.22.v_ref, ...), custom_call_target="tpu_custom_call" | custom-call | flops 67108864000 | bytes 13107200 | tf_op jit(solution)/shard_map/attend_back/pallas_call | solution.py:214
  463.1 6.7 %convolution_convert_fusion.4 = bf16[1024,768]{1,0:T(8,128)(2,1)S(1)} fusion(bf16[2560,768]{1,0:T(8,128)(2,1)S(1)} %constant_dynamic-update-slice_fusion, bf16[640,1024]{1,0:T(8,128)(2,1)} %collective-permute-done.2, bf16[640,1024]{1,0:T(8,128)(2,1)} %collective-permute-done.1, bf16[640,1024]{1,0:T(8,128)(2,1)} %collective-permute-done, ...), kind=kOutput, calls=%fused_computation.44 | convolution fusion | flops 4048289792 | bytes 10747904 | tf_op jit(solution)/shard_map/dot_general | solution.py:32
  471.3 4.8 convolution_convert_fusion
  476.0 19.8 %collective-permute-done.27 = bf16[4,128,768]{2,1,0:T(8,128)(2,1)S(1)} collective-permute-done((bf16[4,128,768]{2,1,0:T(8,128)(2,1)S(1)}, bf16[4,128,768]{2,1,0:T(8,128)(2,1)S(1)}, u32[]{:S(2)}, u32[]{:S(2)}) %collective-permute-start.27) | collective-permute-done | bytes 786464 | tf_op jit(solution)/shard_map/ppermute | solution.py:298
  496.1 2.3 collective-permute-start.28
  503.6 5.2 collective-permute-done.42
  511.6 4.7 collective-permute-start.24
  517.3 12.5 %collective-permute-done.29 = bf16[1,128,768]{2,1,0:T(8,128)(2,1)S(1)} collective-permute-done((bf16[1,128,768]{2,1,0:T(8,128)(2,1)S(1)}, bf16[1,128,768]{2,1,0:T(8,128)(2,1)S(1)}, u32[]{:S(2)}, u32[]{:S(2)}) %collective-permute-start.29) | collective-permute-done | bytes 196640 | tf_op jit(solution)/shard_map/ppermute | solution.py:298
  537.3 3.3 add_convert_fusion
  543.0 29.6 %collective-permute-done.39 = bf16[128,256]{1,0:T(8,128)(2,1)S(1)} collective-permute-done((bf16[128,256]{1,0:T(8,128)(2,1)}, bf16[128,256]{1,0:T(8,128)(2,1)S(1)}, u32[]{:S(2)}, u32[]{:S(2)}) %collective-permute-start.39) | collective-permute-done | bytes 65568 | tf_op jit(solution)/shard_map/ppermute | solution.py:298
  573.4 3.1 convert_multiply_fusion.2
  577.5 2.8 fusion.15
  581.9 9.4 %collective-permute-done.33 = bf16[128,1536]{1,0:T(8,128)(2,1)S(1)} collective-permute-done((bf16[128,1536]{1,0:T(8,128)(2,1)}, bf16[128,1536]{1,0:T(8,128)(2,1)S(1)}, u32[]{:S(2)}, u32[]{:S(2)}) %collective-permute-start.33) | collective-permute-done | bytes 393248 | tf_op jit(solution)/shard_map/ppermute | solution.py:298
  592.1 4.2 fusion.20
  599.4 2.7 convert_multiply_fusion
  602.2 3.3 copy.35
  (271 shorter events, 86.2 us)
Async XLA Ops:
  7.2 133.4 %all-gather.4.cloned.1.call-start = ((), (), s32[]{:S(2)}) async-start(), calls=%async_computation.3 | async-start | bytes 2162688 | tf_op jit(solution)/shard_map/all_gather | solution.py:380
  8.8 223.5 %all-gather.8.cloned.1.call-start = ((), (), s32[]{:S(2)}) async-start(), calls=%async_computation.5 | async-start | bytes 1769472 | tf_op jit(solution)/shard_map/all_gather | solution.py:397
  10.5 221.7 %all-gather.6.cloned.1.call-start = ((), (), s32[]{:S(2)}) async-start(), calls=%async_computation.4 | async-start | bytes 3538944 | tf_op jit(solution)/shard_map/all_gather | solution.py:396
  13.0 33.0 %collective-permute-start = (bf16[640,1024]{1,0:T(8,128)(2,1)S(1)}, bf16[640,1024]{1,0:T(8,128)(2,1)}, u32[]{:S(2)}, u32[]{:S(2)}) collective-permute-start(bf16[640,1024]{1,0:T(8,128)(2,1)S(1)} %fusion.6), channel_id=1, source_target_pairs={{0,2},{1,3},{2,0},{3,1},{4,6},{5,7},{6,4},{7,5},{8,10},{9,11},{10,... | collective-permute-start | bytes 3932168 | tf_op jit(solution)/shard_map/ppermute | solution.py:298
  15.1 59.1 %collective-permute-start.1 = (bf16[640,1024]{1,0:T(8,128)(2,1)S(1)}, bf16[640,1024]{1,0:T(8,128)(2,1)}, u32[]{:S(2)}, u32[]{:S(2)}) collective-permute-start(bf16[640,1024]{1,0:T(8,128)(2,1)S(1)} %fusion.6), channel_id=1, source_target_pairs={{0,1},{1,0},{2,3},{3,2},{4,5},{5,4},{6,7},{7,6},{8,9},{9,8},{10,11... | collective-permute-start | bytes 3932168 | tf_op jit(solution)/shard_map/ppermute | solution.py:298
  17.1 12.2 %collective-permute-start.3 = (bf16[128,768]{1,0:T(8,128)(2,1)S(1)}, bf16[128,768]{1,0:T(8,128)(2,1)S(1)}, u32[]{:S(2)}, u32[]{:S(2)}) collective-permute-start(bf16[128,768]{1,0:T(8,128)(2,1)S(1)} %multiply_convert_fusion.1), channel_id=1, source_target_pairs={{0,16},{4,20},{8,24},{12,28},{16,0},{20,4},{24,8},{28,12},{1,17},{... | collective-permute-start | bytes 589832 | tf_op jit(solution)/shard_map/ppermute | solution.py:298
  27.1 475.0 %reduce-scatter.8.cloned.1.call-start = ((), (), s32[]{:S(2)}) async-start(), calls=%async_computation.8 | async-start | bytes 1769472 | tf_op jit(solution)/shard_map/reduce_scatter | solution.py:468
  29.4 10.4 %collective-permute-start.4 = (bf16[2,128,768]{2,1,0:T(8,128)(2,1)S(1)}, bf16[2,128,768]{2,1,0:T(8,128)(2,1)S(1)}, u32[]{:S(2)}, u32[]{:S(2)}) collective-permute-start(bf16[2,128,768]{2,1,0:T(8,128)(2,1)S(1)} %pad_maximum_fusion.17), channel_id=1, source_target_pairs={{0,8},{4,12},{8,0},{12,4},{16,24},{20,28},{24,16},{28,20},{1,9},{5... | collective-permute-start | bytes 1179656 | tf_op jit(solution)/shard_map/ppermute | solution.py:298
  46.0 28.2 %collective-permute-start.2 = (bf16[640,1024]{1,0:T(8,128)(2,1)}, bf16[640,1024]{1,0:T(8,128)(2,1)}, u32[]{:S(2)}, u32[]{:S(2)}) collective-permute-start(bf16[640,1024]{1,0:T(8,128)(2,1)} %collective-permute-done), channel_id=1, source_target_pairs={{0,1},{1,0},{2,3},{3,2},{4,5},{5,4},{6,7},{7,6},{8,9},{9,8},{10,11... | collective-permute-start | bytes 3932168 | tf_op jit(solution)/shard_map/ppermute | solution.py:298
  48.2 23.3 %collective-permute-start.5 = (bf16[2,2,128,768]{3,2,0,1:T(8,128)(2,1)}, bf16[2,2,128,768]{3,2,0,1:T(8,128)(2,1)}, u32[]{:S(2)}, u32[]{:S(2)}) collective-permute-start(bf16[2,2,128,768]{3,2,0,1:T(8,128)(2,1)} %pad_maximum_fusion.11), channel_id=1, source_target_pairs={{0,4},{4,0},{8,12},{12,8},{16,20},{20,16},{24,28},{28,24},{1,5},{5... | collective-permute-start | bytes 2359304 | tf_op jit(solution)/shard_map/ppermute | solution.py:298
  136.8 8.6 %collective-permute-start.6 = (bf16[640,256]{1,0:T(8,128)(2,1)S(1)}, bf16[640,256]{1,0:T(8,128)(2,1)S(1)}, u32[]{:S(2)}, u32[]{:S(2)}) collective-permute-start(bf16[640,256]{1,0:T(8,128)(2,1)S(1)} %get-tuple-element.73), channel_id=1, source_target_pairs={{0,2},{1,3},{2,0},{3,1},{4,6},{5,7},{6,4},{7,5},{8,10},{9,11},{10,... | collective-permute-start | bytes 983048 | tf_op jit(solution)/shard_map/ppermute | solution.py:298
  138.2 7.2 %collective-permute-start.7 = (bf16[640,256]{1,0:T(8,128)(2,1)S(1)}, bf16[640,256]{1,0:T(8,128)(2,1)S(1)}, u32[]{:S(2)}, u32[]{:S(2)}) collective-permute-start(bf16[640,256]{1,0:T(8,128)(2,1)S(1)} %get-tuple-element.72), channel_id=1, source_target_pairs={{0,1},{1,0},{2,3},{3,2},{4,5},{5,4},{6,7},{7,6},{8,9},{9,8},{10,11... | collective-permute-start | bytes 983048 | tf_op jit(solution)/shard_map/ppermute | solution.py:298
  139.3 15.7 %collective-permute-start.8 = (bf16[640,256]{1,0:T(8,128)(2,1)S(1)}, bf16[640,256]{1,0:T(8,128)(2,1)S(1)}, u32[]{:S(2)}, u32[]{:S(2)}) collective-permute-start(bf16[640,256]{1,0:T(8,128)(2,1)S(1)} %get-tuple-element.71), channel_id=1, source_target_pairs={{0,3},{1,2},{2,1},{3,0},{4,7},{5,6},{6,5},{7,4},{8,11},{9,10},{10,... | collective-permute-start | bytes 983048 | tf_op jit(solution)/shard_map/ppermute | solution.py:298
  139.3 41.2 %collective-permute-start.12 = (bf16[640,1024]{1,0:T(8,128)(2,1)}, bf16[640,1024]{1,0:T(8,128)(2,1)}, u32[]{:S(2)}, u32[]{:S(2)}) collective-permute-start(bf16[640,1024]{1,0:T(8,128)(2,1)} %bitcast.8), channel_id=1, source_target_pairs={{0,2},{1,3},{2,0},{3,1},{4,6},{5,7},{6,4},{7,5},{8,10},{9,11},{10,... | collective-permute-start | bytes 3932168 | tf_op jit(solution)/shard_map/ppermute | solution.py:298
  159.6 48.9 %collective-permute-start.9 = (bf16[640,1024]{1,0:T(8,128)(2,1)S(1)}, bf16[640,1024]{1,0:T(8,128)(2,1)S(1)}, u32[]{:S(2)}, u32[]{:S(2)}) collective-permute-start(bf16[640,1024]{1,0:T(8,128)(2,1)S(1)} %fusion.16), channel_id=1, source_target_pairs={{0,2},{1,3},{2,0},{3,1},{4,6},{5,7},{6,4},{7,5},{8,10},{9,11},{10,... | collective-permute-start | bytes 3932168 | tf_op jit(solution)/shard_map/ppermute | solution.py:298
  161.0 49.1 %collective-permute-start.13 = (bf16[640,1024]{1,0:T(8,128)(2,1)}, bf16[640,1024]{1,0:T(8,128)(2,1)S(1)}, u32[]{:S(2)}, u32[]{:S(2)}) collective-permute-start(bf16[640,1024]{1,0:T(8,128)(2,1)} %bitcast.8), channel_id=1, source_target_pairs={{0,1},{1,0},{2,3},{3,2},{4,5},{5,4},{6,7},{7,6},{8,9},{9,8},{10,11... | collective-permute-start | bytes 3932168 | tf_op jit(solution)/shard_map/ppermute | solution.py:298
  180.5 29.7 %collective-permute-start.14 = (bf16[640,1024]{1,0:T(8,128)(2,1)}, bf16[640,1024]{1,0:T(8,128)(2,1)S(1)}, u32[]{:S(2)}, u32[]{:S(2)}) collective-permute-start(bf16[640,1024]{1,0:T(8,128)(2,1)} %collective-permute-done.12), channel_id=1, source_target_pairs={{0,1},{1,0},{2,3},{3,2},{4,5},{5,4},{6,7},{7,6},{8,9},{9,8},{10,11... | collective-permute-start | bytes 3932168 | tf_op jit(solution)/shard_map/ppermute | solution.py:298
  183.5 32.0 %collective-permute-start.10 = (bf16[640,1024]{1,0:T(8,128)(2,1)S(1)}, bf16[640,1024]{1,0:T(8,128)(2,1)S(1)}, u32[]{:S(2)}, u32[]{:S(2)}) collective-permute-start(bf16[640,1024]{1,0:T(8,128)(2,1)S(1)} %fusion.16), channel_id=1, source_target_pairs={{0,1},{1,0},{2,3},{3,2},{4,5},{5,4},{6,7},{7,6},{8,9},{9,8},{10,11... | collective-permute-start | bytes 3932168 | tf_op jit(solution)/shard_map/ppermute | solution.py:298
  208.5 7.0 %collective-permute-start.11 = (bf16[640,1024]{1,0:T(8,128)(2,1)S(1)}, bf16[640,1024]{1,0:T(8,128)(2,1)S(1)}, u32[]{:S(2)}, u32[]{:S(2)}) collective-permute-start(bf16[640,1024]{1,0:T(8,128)(2,1)S(1)} %collective-permute-done.9), channel_id=1, source_target_pairs={{0,1},{1,0},{2,3},{3,2},{4,5},{5,4},{6,7},{7,6},{8,9},{9,8},{10,11... | collective-permute-start | bytes 3932168 | tf_op jit(solution)/shard_map/ppermute | solution.py:298
  269.4 13.3 %collective-permute-start.19 = (bf16[640,1024]{1,0:T(8,128)(2,1)}, bf16[640,1024]{1,0:T(8,128)(2,1)}, u32[]{:S(2)}, u32[]{:S(2)}) collective-permute-start(bf16[640,1024]{1,0:T(8,128)(2,1)} %get-tuple-element.47), channel_id=1, source_target_pairs={{0,1},{1,0},{2,3},{3,2},{4,5},{5,4},{6,7},{7,6},{8,9},{9,8},{10,11... | collective-permute-start | bytes 3932168 | tf_op jit(solution)/shard_map/ppermute | solution.py:298
  271.3 16.4 %collective-permute-start.16 = (bf16[640,1024]{1,0:T(8,128)(2,1)}, bf16[640,1024]{1,0:T(8,128)(2,1)}, u32[]{:S(2)}, u32[]{:S(2)}) collective-permute-start(bf16[640,1024]{1,0:T(8,128)(2,1)} %get-tuple-element.49), channel_id=1, source_target_pairs={{0,1},{1,0},{2,3},{3,2},{4,5},{5,4},{6,7},{7,6},{8,9},{9,8},{10,11... | collective-permute-start | bytes 3932168 | tf_op jit(solution)/shard_map/ppermute | solution.py:298
  282.3 16.5 %collective-permute-start.18 = (bf16[640,1024]{1,0:T(8,128)(2,1)}, bf16[640,1024]{1,0:T(8,128)(2,1)}, u32[]{:S(2)}, u32[]{:S(2)}) collective-permute-start(bf16[640,1024]{1,0:T(8,128)(2,1)} %get-tuple-element.46), channel_id=1, source_target_pairs={{0,1},{1,0},{2,3},{3,2},{4,5},{5,4},{6,7},{7,6},{8,9},{9,8},{10,11... | collective-permute-start | bytes 3932168 | tf_op jit(solution)/shard_map/ppermute | solution.py:298
  282.4 37.9 %collective-permute-start.15 = (bf16[640,1024]{1,0:T(8,128)(2,1)}, bf16[640,1024]{1,0:T(8,128)(2,1)}, u32[]{:S(2)}, u32[]{:S(2)}) collective-permute-start(bf16[640,1024]{1,0:T(8,128)(2,1)} %get-tuple-element.48), channel_id=1, source_target_pairs={{0,1},{1,0},{2,3},{3,2},{4,5},{5,4},{6,7},{7,6},{8,9},{9,8},{10,11... | collective-permute-start | bytes 3932168 | tf_op jit(solution)/shard_map/ppermute | solution.py:298
  286.3 30.7 %collective-permute-start.20 = (bf16[640,1024]{1,0:T(8,128)(2,1)}, bf16[640,1024]{1,0:T(8,128)(2,1)}, u32[]{:S(2)}, u32[]{:S(2)}) collective-permute-start(bf16[640,1024]{1,0:T(8,128)(2,1)} %add_convert_fusion.2), channel_id=1, source_target_pairs={{0,2},{1,3},{2,0},{3,1},{4,6},{5,7},{6,4},{7,5},{8,10},{9,11},{10,... | collective-permute-start | bytes 3932168 | tf_op jit(solution)/shard_map/ppermute | solution.py:298
  291.1 54.0 %collective-permute-start.17 = (bf16[640,1024]{1,0:T(8,128)(2,1)}, bf16[640,1024]{1,0:T(8,128)(2,1)}, u32[]{:S(2)}, u32[]{:S(2)}) collective-permute-start(bf16[640,1024]{1,0:T(8,128)(2,1)} %add_convert_fusion.5), channel_id=1, source_target_pairs={{0,2},{1,3},{2,0},{3,1},{4,6},{5,7},{6,4},{7,5},{8,10},{9,11},{10,... | collective-permute-start | bytes 3932168 | tf_op jit(solution)/shard_map/ppermute | solution.py:298
  298.7 243.2 %reduce-scatter.6.cloned.1.call-start = ((), (), s32[]{:S(2)}) async-start(), calls=%async_computation.7 | async-start | bytes 589824 | tf_op jit(solution)/shard_map/reduce_scatter | solution.py:468
  354.1 11.0 %collective-permute-start.36 = (bf16[1024,256]{1,0:T(8,128)(2,1)}, bf16[1024,256]{1,0:T(8,128)(2,1)S(1)}, u32[]{:S(2)}, u32[]{:S(2)}) collective-permute-start(bf16[1024,256]{1,0:T(8,128)(2,1)} %get-tuple-element.52), channel_id=1, source_target_pairs={{0,1},{1,0},{2,3},{3,2},{4,5},{5,4},{6,7},{7,6},{8,9},{9,8},{10,11... | collective-permute-start | bytes 1572872 | tf_op jit(solution)/shard_map/ppermute | solution.py:298
  356.6 13.2 %collective-permute-start.38 = (bf16[1024,256]{1,0:T(8,128)(2,1)S(1)}, bf16[1024,256]{1,0:T(8,128)(2,1)S(1)}, u32[]{:S(2)}, u32[]{:S(2)}) collective-permute-start(bf16[1024,256]{1,0:T(8,128)(2,1)S(1)} %add_convert_fusion.8), channel_id=1, source_target_pairs={{0,2},{1,3},{2,0},{3,1},{4,6},{5,7},{6,4},{7,5},{8,10},{9,11},{10,... | collective-permute-start | bytes 1572872 | tf_op jit(solution)/shard_map/ppermute | solution.py:298
  362.8 22.7 %collective-permute-start.21 = (bf16[640,256]{1,0:T(8,128)(2,1)}, bf16[640,256]{1,0:T(8,128)(2,1)}, u32[]{:S(2)}, u32[]{:S(2)}) collective-permute-start(bf16[640,256]{1,0:T(8,128)(2,1)} %get-tuple-element.78), channel_id=1, source_target_pairs={{0,2},{1,3},{2,0},{3,1},{4,6},{5,7},{6,4},{7,5},{8,10},{9,11},{10,... | collective-permute-start | bytes 983048 | tf_op jit(solution)/shard_map/ppermute | solution.py:298
  363.0 22.6 %collective-permute-start.22 = (bf16[640,256]{1,0:T(8,128)(2,1)}, bf16[640,256]{1,0:T(8,128)(2,1)}, u32[]{:S(2)}, u32[]{:S(2)}) collective-permute-start(bf16[640,256]{1,0:T(8,128)(2,1)} %get-tuple-element.77), channel_id=1, source_target_pairs={{0,1},{1,0},{2,3},{3,2},{4,5},{5,4},{6,7},{7,6},{8,9},{9,8},{10,11... | collective-permute-start | bytes 983048 | tf_op jit(solution)/shard_map/ppermute | solution.py:298
  363.9 21.7 %collective-permute-start.23 = (bf16[640,256]{1,0:T(8,128)(2,1)S(1)}, bf16[640,256]{1,0:T(8,128)(2,1)}, u32[]{:S(2)}, u32[]{:S(2)}) collective-permute-start(bf16[640,256]{1,0:T(8,128)(2,1)S(1)} %get-tuple-element.76), channel_id=1, source_target_pairs={{0,3},{1,2},{2,1},{3,0},{4,7},{5,6},{6,5},{7,4},{8,11},{9,10},{10,... | collective-permute-start | bytes 983048 | tf_op jit(solution)/shard_map/ppermute | solution.py:298
  371.8 208.5 %reduce-scatter.4.cloned.1.call-start = ((), (), s32[]{:S(2)}) async-start(), calls=%async_computation.6 | async-start | bytes 3538944 | tf_op jit(solution)/shard_map/reduce_scatter | solution.py:468
  469.9 26.0 %collective-permute-start.27 = (bf16[4,128,768]{2,1,0:T(8,128)(2,1)S(1)}, bf16[4,128,768]{2,1,0:T(8,128)(2,1)S(1)}, u32[]{:S(2)}, u32[]{:S(2)}) collective-permute-start(bf16[4,128,768]{2,1,0:T(8,128)(2,1)S(1)} %dynamic-slice_bitcast_fusion), channel_id=1, source_target_pairs={{0,4},{4,0},{8,12},{12,8},{16,20},{20,16},{24,28},{28,24},{1,5},{5... | collective-permute-start | bytes 2359304 | tf_op jit(solution)/shard_map/ppermute | solution.py:298
  496.1 13.5 %collective-permute-start.28 = (bf16[2,128,768]{2,1,0:T(8,128)(2,1)S(1)}, bf16[2,128,768]{2,1,0:T(8,128)(2,1)S(1)}, u32[]{:S(2)}, u32[]{:S(2)}) collective-permute-start(bf16[2,128,768]{2,1,0:T(8,128)(2,1)S(1)} %dynamic-slice_bitcast_fusion.1), channel_id=1, source_target_pairs={{0,8},{4,12},{8,0},{12,4},{16,24},{20,28},{24,16},{28,20},{1,9},{5... | collective-permute-start | bytes 1179656 | tf_op jit(solution)/shard_map/ppermute | solution.py:298
  500.1 37.2 %collective-permute-start.25 = (bf16[640,1024]{1,0:T(8,128)(2,1)}, bf16[640,1024]{1,0:T(8,128)(2,1)}, u32[]{:S(2)}, u32[]{:S(2)}) collective-permute-start(bf16[640,1024]{1,0:T(8,128)(2,1)} %get-tuple-element.45), channel_id=1, source_target_pairs={{0,1},{1,0},{2,3},{3,2},{4,5},{5,4},{6,7},{7,6},{8,9},{9,8},{10,11... | collective-permute-start | bytes 3932168 | tf_op jit(solution)/shard_map/ppermute | solution.py:298
  502.1 6.8 %collective-permute-start.42 = (bf16[96,1024]{1,0:T(8,128)(2,1)}, bf16[96,1024]{1,0:T(8,128)(2,1)S(1)}, u32[]{:S(2)}, u32[]{:S(2)}) collective-permute-start(bf16[96,1024]{1,0:T(8,128)(2,1)} %reduce-scatter.8.cloned.1.call-done), channel_id=1, source_target_pairs={{0,2},{1,3},{2,0},{3,1},{4,6},{5,7},{6,4},{7,5},{8,10},{9,11},{10,... | collective-permute-start | bytes 589832 | tf_op jit(solution)/shard_map/ppermute | solution.py:298
  503.3 13.0 %collective-permute-start.43 = (bf16[96,1024]{1,0:T(8,128)(2,1)}, bf16[96,1024]{1,0:T(8,128)(2,1)S(1)}, u32[]{:S(2)}, u32[]{:S(2)}) collective-permute-start(bf16[96,1024]{1,0:T(8,128)(2,1)} %reduce-scatter.8.cloned.1.call-done), channel_id=1, source_target_pairs={{0,1},{1,0},{2,3},{3,2},{4,5},{5,4},{6,7},{7,6},{8,9},{9,8},{10,11... | collective-permute-start | bytes 589832 | tf_op jit(solution)/shard_map/ppermute | solution.py:298
  508.9 7.4 %collective-permute-start.44 = (bf16[96,1024]{1,0:T(8,128)(2,1)S(1)}, bf16[96,1024]{1,0:T(8,128)(2,1)S(1)}, u32[]{:S(2)}, u32[]{:S(2)}) collective-permute-start(bf16[96,1024]{1,0:T(8,128)(2,1)S(1)} %collective-permute-done.42), channel_id=1, source_target_pairs={{0,1},{1,0},{2,3},{3,2},{4,5},{5,4},{6,7},{7,6},{8,9},{9,8},{10,11... | collective-permute-start | bytes 589832 | tf_op jit(solution)/shard_map/ppermute | solution.py:298
  509.8 20.1 %collective-permute-start.29 = (bf16[1,128,768]{2,1,0:T(8,128)(2,1)S(1)}, bf16[1,128,768]{2,1,0:T(8,128)(2,1)S(1)}, u32[]{:S(2)}, u32[]{:S(2)}) collective-permute-start(bf16[1,128,768]{2,1,0:T(8,128)(2,1)S(1)} %constant_dynamic-slice_fusion.6), channel_id=1, source_target_pairs={{0,16},{4,20},{8,24},{12,28},{16,0},{20,4},{24,8},{28,12},{1,17},{... | collective-permute-start | bytes 589832 | tf_op jit(solution)/shard_map/ppermute | solution.py:298
  511.6 65.9 %collective-permute-start.24 = (bf16[640,1024]{1,0:T(8,128)(2,1)}, bf16[640,1024]{1,0:T(8,128)(2,1)S(1)}, u32[]{:S(2)}, u32[]{:S(2)}) collective-permute-start(bf16[640,1024]{1,0:T(8,128)(2,1)} %get-tuple-element.44), channel_id=1, source_target_pairs={{0,1},{1,0},{2,3},{3,2},{4,5},{5,4},{6,7},{7,6},{8,9},{9,8},{10,11... | collective-permute-start | bytes 3932168 | tf_op jit(solution)/shard_map/ppermute | solution.py:298
  529.9 5.6 collective-permute-start.30
  532.5 9.6 %collective-permute-start.31 = (bf16[128,768]{1,0:T(8,128)(2,1)S(1)}, bf16[128,768]{1,0:T(8,128)(2,1)S(1)}, u32[]{:S(2)}, u32[]{:S(2)}) collective-permute-start(bf16[128,768]{1,0:T(8,128)(2,1)S(1)} %bitcast.149), channel_id=1, source_target_pairs={{0,1},{1,0},{2,3},{3,2},{4,5},{5,4},{6,7},{7,6},{8,9},{9,8},{10,11... | collective-permute-start | bytes 589832 | tf_op jit(solution)/shard_map/ppermute | solution.py:298
  535.5 7.2 %collective-permute-start.32 = (bf16[128,768]{1,0:T(8,128)(2,1)S(1)}, bf16[128,768]{1,0:T(8,128)(2,1)S(1)}, u32[]{:S(2)}, u32[]{:S(2)}) collective-permute-start(bf16[128,768]{1,0:T(8,128)(2,1)S(1)} %collective-permute-done.30), channel_id=1, source_target_pairs={{0,1},{1,0},{2,3},{3,2},{4,5},{5,4},{6,7},{7,6},{8,9},{9,8},{10,11... | collective-permute-start | bytes 589832 | tf_op jit(solution)/shard_map/ppermute | solution.py:298
  540.6 36.9 %collective-permute-start.26 = (bf16[640,1024]{1,0:T(8,128)(2,1)}, bf16[640,1024]{1,0:T(8,128)(2,1)}, u32[]{:S(2)}, u32[]{:S(2)}) collective-permute-start(bf16[640,1024]{1,0:T(8,128)(2,1)} %add_convert_fusion), channel_id=1, source_target_pairs={{0,2},{1,3},{2,0},{3,1},{4,6},{5,7},{6,4},{7,5},{8,10},{9,11},{10,... | collective-permute-start | bytes 3932168 | tf_op jit(solution)/shard_map/ppermute | solution.py:298
  541.8 30.8 %collective-permute-start.39 = (bf16[128,256]{1,0:T(8,128)(2,1)}, bf16[128,256]{1,0:T(8,128)(2,1)S(1)}, u32[]{:S(2)}, u32[]{:S(2)}) collective-permute-start(bf16[128,256]{1,0:T(8,128)(2,1)} %reduce-scatter.6.cloned.1.call-done), channel_id=1, source_target_pairs={{0,2},{1,3},{2,0},{3,1},{4,6},{5,7},{6,4},{7,5},{8,10},{9,11},{10,... | collective-permute-start | bytes 196616 | tf_op jit(solution)/shard_map/ppermute | solution.py:298
  542.1 34.5 %collective-permute-start.40 = (bf16[128,256]{1,0:T(8,128)(2,1)}, bf16[128,256]{1,0:T(8,128)(2,1)S(1)}, u32[]{:S(2)}, u32[]{:S(2)}) collective-permute-start(bf16[128,256]{1,0:T(8,128)(2,1)} %reduce-scatter.6.cloned.1.call-done), channel_id=1, source_target_pairs={{0,1},{1,0},{2,3},{3,2},{4,5},{5,4},{6,7},{7,6},{8,9},{9,8},{10,11... | collective-permute-start | bytes 196616 | tf_op jit(solution)/shard_map/ppermute | solution.py:298
  580.3 11.0 %collective-permute-start.33 = (bf16[128,1536]{1,0:T(8,128)(2,1)}, bf16[128,1536]{1,0:T(8,128)(2,1)S(1)}, u32[]{:S(2)}, u32[]{:S(2)}) collective-permute-start(bf16[128,1536]{1,0:T(8,128)(2,1)} %reduce-scatter.4.cloned.1.call-done), channel_id=1, source_target_pairs={{0,2},{1,3},{2,0},{3,1},{4,6},{5,7},{6,4},{7,5},{8,10},{9,11},{10,... | collective-permute-start | bytes 1179656 | tf_op jit(solution)/shard_map/ppermute | solution.py:298
  581.7 14.7 %collective-permute-start.34 = (bf16[128,1536]{1,0:T(8,128)(2,1)}, bf16[128,1536]{1,0:T(8,128)(2,1)S(1)}, u32[]{:S(2)}, u32[]{:S(2)}) collective-permute-start(bf16[128,1536]{1,0:T(8,128)(2,1)} %reduce-scatter.4.cloned.1.call-done), channel_id=1, source_target_pairs={{0,1},{1,0},{2,3},{3,2},{4,5},{5,4},{6,7},{7,6},{8,9},{9,8},{10,11... | collective-permute-start | bytes 1179656 | tf_op jit(solution)/shard_map/ppermute | solution.py:298
  (51 other events, 643.6 us)
Sparse Core Ops, SparseCore 0:
  11.5 63.5 all-gather.3
  77.2 41.9 all-gather.7
  121.5 59.0 all-gather.5
  298.8 64.9 reduce-scatter.7
  371.9 62.7 reduce-scatter.5
  438.2 92.3 reduce-scatter.3

commit v2 on v1

v2 whole, which is shorter than its diff:
```python
import functools
import math

import jax
import jax.numpy as jnp
from jax import lax
from jax.experimental import pallas as pl
from jax.experimental.pallas import tpu as pltpu
from jax.sharding import PartitionSpec as P

HEADS = 16
HEAD = 64
HALF = HEAD // 2
ROW_TILE = 16
BF16 = jnp.bfloat16
F32 = jnp.float32

eps = 1e-05
rope_base = 160000.0
VMEM_BYTES = 60 << 20


def dot_nn(a, b):
    return lax.dot_general(a, b, (((1,), (0,)), ((), ())), preferred_element_type=F32)


def dot_nt(a, b):
    return lax.dot_general(a, b, (((1,), (1,)), ((), ())), preferred_element_type=F32)


def dot_tn(a, b):
    return lax.dot_general(a, b, (((0,), (0,)), ((), ())), preferred_element_type=F32)


def block_rows(rows, wanted):
    best = rows
    for size in range(ROW_TILE, min(rows, wanted) + 1, ROW_TILE):
        if rows % size == 0:
            best = size
    return best


def centred_stats(values):
    average = jnp.mean(values, -1, keepdims=True)
    centred = values - average
    inverse = lax.rsqrt(jnp.mean(centred * centred, -1, keepdims=True) + eps)
    return centred * inverse, inverse


def norm_backward(grad, xhat, inverse):
    return inverse * (
        grad
        - jnp.mean(grad, -1, keepdims=True)
        - xhat * jnp.mean(grad * xhat, -1, keepdims=True)
    )


def partner(values):
    width = values.shape[-1]
    if width % 128:
        return jnp.concatenate([values[:, HALF:], values[:, :HALF]], 1)
    lane = lax.broadcasted_iota(jnp.int32, values.shape, 1)
    return jnp.where(
        lane % HEAD < HALF,
        pltpu.roll(values, width - HALF, 1),
        pltpu.roll(values, HALF, 1),
    )


def head_of_lane(shape):
    return lax.broadcasted_iota(jnp.int32, shape, 1) // HEAD


def only_head(values, head):
    return jnp.where(head_of_lane(values.shape) == head, values, jnp.zeros_like(values))


def take_piece(piece_refs, steps, scratch):
    for at, ref in enumerate(piece_refs):

        @pl.when(pl.program_id(0) // steps == at)
        def _(ref=ref):
            scratch[...] = ref[...]

    return scratch[...]


def piece_specs(count, steps, rows, columns):
    return [
        pl.BlockSpec(
            (rows, columns), lambda i, at=at: (jnp.clip(i - at * steps, 0, steps - 1), 0)
        )
        for at in range(count)
    ]


def qkv_body(count, steps, *refs):
    pieces, (w_ref, cos_ref, sin_ref) = refs[:count], refs[count : count + 3]
    q_ref, k_ref, v_ref, x_ref, scratch = refs[-5:]
    width = q_ref.shape[1]
    x = take_piece(pieces, steps, scratch)
    x_ref[...] = x
    packed = dot_nn(x, w_ref[...])
    cosine = cos_ref[...]
    sine = sin_ref[...]
    lanes = cosine.shape[1]
    for group in range(width // lanes):
        here = slice(group * lanes, (group + 1) * lanes)
        for at, ref in enumerate((q_ref, k_ref, v_ref)):
            start = (3 * group + at) * lanes
            part = packed[:, start : start + lanes]
            if at < 2:
                part = part * cosine + partner(part) * sine
            ref[:, here] = part.astype(BF16)


def qkv_heads(pieces, weights, cosine, sine, before):
    count = len(pieces)
    rows, depth = pieces[0].shape
    width = weights.shape[1] // 3
    step = block_rows(rows, 320)
    steps = rows // step
    length, table = cosine.shape
    first = count * steps if before else 0
    by_row = lambda columns: pl.BlockSpec((step, columns), lambda i: (i + first, 0))
    total = count * rows
    return pl.pallas_call(
        functools.partial(qkv_body, count, steps),
        grid=(count * steps,),
        in_specs=piece_specs(count, steps, step, depth)
        + [pl.BlockSpec((depth, 3 * width), lambda i: (0, 0)), by_row(table), by_row(table)]
        + [pl.BlockSpec(memory_space=pl.ANY)] * len(before),
        out_specs=[by_row(width)] * 3 + [by_row(depth)],
        out_shape=[jax.ShapeDtypeStruct((length, width), BF16)] * 3
        + [jax.ShapeDtypeStruct((length, depth), BF16)],
        scratch_shapes=[pltpu.VMEM((step, depth), BF16)],
        input_output_aliases={count + 3 + at: at for at in range(len(before))},
        compiler_params=pltpu.CompilerParams(vmem_limit_bytes=VMEM_BYTES),
        cost_estimate=pl.CostEstimate(
            flops=6 * total * depth * width,
            bytes_accessed=2 * (2 * total * depth + 3 * depth * width + 3 * total * width),
            transcendentals=0,
        ),
        name="qkv_rope",
    )(*pieces, weights, cosine, sine, *before)


def attend_body(q_ref, k_ref, v_ref, out_ref, lse_ref):
    width = q_ref.shape[1]
    queries = q_ref[...] * jnp.asarray(HEAD**-0.5, BF16)
    keys = k_ref[...]
    values = v_ref[...]
    for head in range(width // HEAD):
        scores = dot_nt(only_head(queries, head), keys)
        peak = jnp.max(scores, -1, keepdims=True)
        exponent = jnp.exp(scores - peak)
        total = jnp.sum(exponent, -1, keepdims=True)
        out = dot_nn(exponent.astype(BF16), values) / total
        lse = jnp.broadcast_to(peak + jnp.log(total), out.shape)
        if head:
            here = head_of_lane(out.shape) == head
            out = jnp.where(here, out, previous_out)
            lse = jnp.where(here, lse, previous_lse)
        previous_out, previous_lse = out, lse
    out_ref[...] = out.astype(BF16)
    lse_ref[...] = lse.T


def attend(queries, keys, values, group):
    rows, local_width = queries.shape
    width = min(128, local_width)
    step = block_rows(rows, 256)
    q_spec = pl.BlockSpec((step, width), lambda i: (i, group))
    k_spec = pl.BlockSpec((rows, width), lambda i: (0, group))
    return pl.pallas_call(
        attend_body,
        grid=(rows // step,),
        in_specs=[q_spec, k_spec, k_spec],
        out_specs=[
            pl.BlockSpec((step, width), lambda i: (i, 0)),
            pl.BlockSpec((width, step), lambda i: (0, i)),
        ],
        out_shape=[
            jax.ShapeDtypeStruct((rows, width), BF16),
            jax.ShapeDtypeStruct((width, rows), F32),
        ],
        compiler_params=pltpu.CompilerParams(vmem_limit_bytes=VMEM_BYTES),
        cost_estimate=pl.CostEstimate(
            flops=16 * rows * rows * width,
            bytes_accessed=8 * rows * width,
            transcendentals=rows * rows * width // HEAD,
        ),
        name="attend",
    )(queries, keys, values)


def attend_back_body(
    q_ref, k_ref, v_ref, g_ref, out_ref, lse_ref, cos_ref, sin_ref, packed_ref, dk_sum, dv_sum
):
    step_rows, width = q_ref.shape
    step = pl.program_id(0)

    @pl.when(step == 0)
    def _():
        dk_sum[...] = jnp.zeros_like(dk_sum)
        dv_sum[...] = jnp.zeros_like(dv_sum)

    factor = HEAD**-0.5
    queries = q_ref[...] * jnp.asarray(factor, BF16)
    keys = k_ref[...]
    values = v_ref[...]
    grads = g_ref[...]
    product = (grads.astype(F32) * out_ref[...].astype(F32)).T
    dq = jnp.zeros(product.shape, F32)
    for head in range(width // HEAD):
        own_queries = only_head(queries, head)
        own_grads = only_head(grads, head)
        lse = lse_ref[head * HEAD : head * HEAD + 1, :]
        inner = jnp.sum(product[head * HEAD : (head + 1) * HEAD], 0, keepdims=True)
        probs = jnp.exp(dot_nt(keys, own_queries) - lse)
        prob_grad = dot_nt(values, own_grads)
        score_grad = (probs * (prob_grad - inner)).astype(BF16)
        dv_sum[...] += dot_nn(probs.astype(BF16), own_grads)
        dk_sum[...] += dot_nn(score_grad, own_queries)
        dq = dq + dot_tn(only_head(keys, head), score_grad)
    dq = (dq.T * factor).astype(BF16).astype(F32)
    here = pl.ds(pl.multiple_of(step * step_rows, ROW_TILE), step_rows)
    packed_ref[here, :width] = (dq * cos_ref[here, :] - partner(dq) * sin_ref[here, :]).astype(BF16)

    @pl.when(step == pl.num_programs(0) - 1)
    def _():
        dk = dk_sum[...].astype(BF16).astype(F32)
        packed_ref[:, width : 2 * width] = (
            dk * cos_ref[...] - partner(dk) * sin_ref[...]
        ).astype(BF16)
        packed_ref[:, 2 * width :] = dv_sum[...].astype(BF16)


def attend_back(queries, keys, values, grads, out, lse, cosine, sine, group):
    rows, local_width = queries.shape
    width = min(128, local_width)
    step = block_rows(rows, 512)
    q_spec = pl.BlockSpec((step, width), lambda i: (i, group))
    k_spec = pl.BlockSpec((rows, width), lambda i: (0, group))
    own_spec = pl.BlockSpec((step, width), lambda i: (i, 0))
    all_spec = pl.BlockSpec((rows, width), lambda i: (0, 0))
    return pl.pallas_call(
        attend_back_body,
        grid=(rows // step,),
        in_specs=[
            q_spec, k_spec, k_spec, own_spec, own_spec,
            pl.BlockSpec((width, step), lambda i: (0, i)),
            all_spec, all_spec,
        ],
        out_specs=pl.BlockSpec((rows, 3 * width), lambda i: (0, 0)),
        out_shape=jax.ShapeDtypeStruct((rows, 3 * width), BF16),
        scratch_shapes=[pltpu.VMEM((rows, width), F32)] * 2,
        compiler_params=pltpu.CompilerParams(vmem_limit_bytes=VMEM_BYTES),
        cost_estimate=pl.CostEstimate(
            flops=40 * rows * rows * width,
            bytes_accessed=20 * rows * width,
            transcendentals=rows * rows * width // HEAD,
        ),
        name="attend_back",
    )(queries, keys, values, grads, out, lse, cosine, sine)


def mlp_body(count, steps, *refs):
    x_pieces, c_pieces = refs[:count], refs[count : 2 * count]
    wi_ref, wo_ref = refs[2 * count : 2 * count + 2]
    x_scratch, c_scratch = refs[-2:]
    results = refs[-2 - 4 - 2 * count : -2]
    hidden_ref, gate_up_ref, x_ref, c_ref = results[:4]
    back_refs, out_refs = results[4 : 4 + count], results[4 + count :]
    units = wo_ref.shape[0]
    x = take_piece(x_pieces, steps, x_scratch)
    cotangent = take_piece(c_pieces, steps, c_scratch)
    x_ref[...] = x
    c_ref[...] = cotangent
    gate_up = dot_nn(x, wi_ref[...])
    hidden_grad = dot_nt(cotangent, wo_ref[...])
    gate = gate_up[:, :units]
    up = gate_up[:, units:]
    share = 0.5 * (1.0 + lax.erf(gate * 2.0**-0.5))
    activated = gate * share
    slope = share + gate * jnp.exp(-0.5 * gate * gate) * (2.0 * math.pi) ** -0.5
    hidden = (activated * up).astype(BF16)
    hidden_ref[...] = hidden
    gate_grad = (hidden_grad * up * slope).astype(BF16)
    up_grad = (hidden_grad * activated).astype(BF16)
    both = jnp.concatenate([gate_grad, up_grad], 1)
    gate_up_ref[...] = both
    back = dot_nt(both, wi_ref[...]).astype(BF16)
    out = dot_nn(hidden, wo_ref[...]).astype(BF16)
    for at in range(count):

        @pl.when(pl.program_id(0) // steps == at)
        def _(at=at):
            back_refs[at][...] = back
            out_refs[at][...] = out


def mlp(x_pieces, c_pieces, w_in, w_out, length, before):
    count = len(x_pieces)
    rows, depth = x_pieces[0].shape
    units = w_out.shape[0]
    step = block_rows(rows, 320)
    steps = rows // step
    total = count * rows
    first = count * steps if before else 0
    by_row = lambda columns: pl.BlockSpec((step, columns), lambda i: (i + first, 0))
    whole = lambda shape: pl.BlockSpec(shape, lambda i: (0, 0))
    pieces = piece_specs(count, steps, step, depth)
    results = pl.pallas_call(
        functools.partial(mlp_body, count, steps),
        grid=(count * steps,),
        in_specs=pieces
        + pieces
        + [whole((depth, 2 * units)), whole(w_out.shape)]
        + [pl.BlockSpec(memory_space=pl.ANY)] * len(before),
        out_specs=[by_row(units), by_row(2 * units), by_row(depth), by_row(depth)]
        + pieces
        + pieces,
        out_shape=[
            jax.ShapeDtypeStruct((length, columns), BF16)
            for columns in (units, 2 * units, depth, depth)
        ]
        + [jax.ShapeDtypeStruct((rows, depth), BF16)] * (2 * count),
        scratch_shapes=[pltpu.VMEM((step, depth), BF16)] * 2,
        input_output_aliases={2 * count + 2 + at: at for at in range(len(before))},
        compiler_params=pltpu.CompilerParams(vmem_limit_bytes=VMEM_BYTES),
        cost_estimate=pl.CostEstimate(
            flops=12 * total * depth * units,
            bytes_accessed=2 * total * (6 * depth + 3 * units) + 6 * depth * units,
            transcendentals=2 * total * units,
        ),
        name="mlp",
    )(*x_pieces, *c_pieces, w_in, w_out, *before)
    return results[:4], results[4 : 4 + count], results[4 + count :]


def token_grad_body(groups, count, steps, *refs):
    packed = jnp.concatenate([ref[...] for ref in refs[:groups]], 1)
    results = refs[groups + 1 :]
    grad = dot_nt(packed, refs[groups][...]).astype(BF16)
    for at in range(count):

        @pl.when(pl.program_id(0) // steps == at)
        def _(at=at):
            results[at][...] = grad


def token_grad(packed, weights, count, positions, first):
    groups = len(packed)
    depth, columns = weights.shape
    step = block_rows(positions, 320)
    steps = positions // step
    total = count * positions
    return pl.pallas_call(
        functools.partial(token_grad_body, groups, count, steps),
        grid=(count * steps,),
        in_specs=[
            pl.BlockSpec((step, columns // groups), lambda i: (i + first * steps, 0))
        ] * groups
        + [pl.BlockSpec((depth, columns), lambda i: (0, 0))],
        out_specs=piece_specs(count, steps, step, depth),
        out_shape=[jax.ShapeDtypeStruct((positions, depth), BF16)] * count,
        compiler_params=pltpu.CompilerParams(vmem_limit_bytes=VMEM_BYTES),
        cost_estimate=pl.CostEstimate(
            flops=2 * total * depth * columns,
            bytes_accessed=2 * (total * depth + depth * columns + total * columns),
            transcendentals=0,
        ),
        name="token_grad",
    )(*packed, weights)


def local(seq_size, fsdp_size, activations, cotangent, gain_attn, w_qkv, w_attn_out, gain_mlp, w_in, w_mlp_out):
    _, positions, width = activations.shape
    shard = w_qkv.shape[0]
    ff_shard = w_mlp_out.shape[0]
    local_width = width // seq_size
    length = positions * seq_size
    half = seq_size // 2
    lanes = min(128, local_width)
    groups = local_width // lanes
    me = lax.axis_index("seq")
    row = lax.axis_index("fsdp")
    after = lax.optimization_barrier


    def swap(values, axis, size, offset):
        return lax.ppermute(values, axis, [(i, i ^ offset) for i in range(size)])

    def swap_seq(values, offset):
        return swap(values, "seq", seq_size, offset)

    def spread(values):
        pieces = [values]
        bit = 1
        while bit < half:
            pieces = pieces + [swap_seq(piece, bit) for piece in pieces]
            bit *= 2
        return pieces

    def gather_seq(values):
        return spread(values) + spread(swap_seq(values, half))

    def fold(pieces):
        pieces = list(pieces)
        while len(pieces) > 1:
            left = len(pieces) // 2
            got = [swap_seq(piece.astype(BF16), left) for piece in pieces[left:]]
            pieces = [kept.astype(F32) + other.astype(F32) for kept, other in zip(pieces, got)]
        return pieces[0].astype(F32)

    def far_sum(pieces):
        return swap_seq(fold(pieces).astype(BF16), half)

    def exchange_seq(pieces):
        return [pieces[0]] + [swap_seq(pieces[k], k) for k in range(1, seq_size)]

    def by_member(pieces):
        stacked = jnp.stack(pieces)
        return [
            lax.dynamic_index_in_dim(stacked, me ^ member, 0, keepdims=False)
            for member in range(seq_size)
        ]

    def gather_fsdp(values):
        rows = values.shape[0]
        gathered = values
        at = 0
        bit = fsdp_size // 2
        while bit:
            other = swap(gathered, "fsdp", fsdp_size, bit)
            high = (row & bit) != 0
            gathered = jnp.stack(
                [jnp.where(high, other, gathered), jnp.where(high, gathered, other)], at
            )
            at += 1
            bit //= 2
        return gathered.reshape(fsdp_size * rows, values.shape[1])

    def halve_fsdp(values, bit):
        rows = shard
        blocks = values.shape[0] // rows
        left = values.reshape(blocks // 2, 2, rows, values.shape[1])
        mine = jnp.where((row & bit) != 0, 1, 0)
        kept = lax.dynamic_index_in_dim(left, mine, 1, keepdims=False)
        sent = lax.dynamic_index_in_dim(left, 1 - mine, 1, keepdims=False)
        total = kept.astype(F32) + swap(sent, "fsdp", fsdp_size, bit).astype(F32)
        return total.astype(BF16).reshape(blocks // 2 * rows, values.shape[1])

    def reduce_fsdp(values):
        return lax.psum_scatter(values, "fsdp", scatter_dimension=0, tiled=True)

    own_gain_attn = gain_attn.astype(F32)[:, None]
    own_gain_mlp = gain_mlp.astype(F32)[:, None]

    qkv_slice = jnp.concatenate(
        [
            lax.dynamic_slice(
                w_qkv, (0, part * width + me * local_width + group * lanes), (shard, lanes)
            )
            for group in range(groups)
            for part in range(3)
        ],
        1,
    )
    qkv_slice = (qkv_slice.astype(F32) * own_gain_attn).astype(BF16)
    qkv_full = gather_fsdp(qkv_slice)

    tokens = activations.reshape(positions, width).astype(F32)
    xhat, inverse = centred_stats(tokens)
    own_x = xhat.astype(BF16)
    far_x = swap_seq(own_x, half)
    near_x_pieces = spread(own_x)
    far_x_pieces = spread(far_x)
    own_cotangent = cotangent.reshape(positions, width)
    near_c_pieces = spread(own_cotangent)
    far_c_pieces = spread(swap_seq(after((own_cotangent, far_x))[0], half))

    unit_share = -(-ff_shard // seq_size)
    unit_share = -(-unit_share // ROW_TILE) * ROW_TILE
    padding = unit_share * seq_size - ff_shard
    units = fsdp_size * unit_share
    attn_out_slice = lax.dynamic_slice(w_attn_out, (0, me * local_width), (shard, local_width))
    mlp_out_slice = lax.dynamic_slice(
        jnp.pad(w_mlp_out, ((0, padding), (0, 0))), (me * unit_share, 0), (unit_share, width)
    )
    in_slice = jnp.pad(
        w_in.reshape(shard, 2 * fsdp_size, ff_shard), ((0, 0), (0, 0), (0, padding))
    )
    in_slice = lax.dynamic_slice(
        in_slice, (0, 0, me * unit_share), (shard, 2 * fsdp_size, unit_share)
    ).reshape(shard, 2 * units)
    in_slice = (in_slice.astype(F32) * own_gain_mlp).astype(BF16)
    rows = math.gcd(unit_share, shard)
    tall, wide = unit_share // rows, shard // rows
    mlp_out_slice = (
        mlp_out_slice.reshape(tall, rows, wide, width // wide)
        .transpose(2, 1, 0, 3)
        .reshape(shard, tall * width // wide)
    )
    later = lax.all_gather(
        jnp.concatenate([in_slice, mlp_out_slice, attn_out_slice], 1), "fsdp", axis=0, tiled=True
    )
    mlp_out_full = (
        later[:, 2 * units : 2 * units + tall * width // wide]
        .reshape(fsdp_size, wide, rows, tall, width // wide)
        .transpose(0, 3, 2, 1, 4)
        .reshape(units, width)
    )
    lane = lax.broadcasted_iota(jnp.int32, (length, lanes), 1)
    at = lax.broadcasted_iota(jnp.int32, (length, lanes), 0)
    place = ((at // positions) ^ me) * positions + at % positions
    frequency = jnp.exp((lane % HALF).astype(F32) * (-2.0 * math.log(rope_base) / HEAD))
    angles = place.astype(F32) * frequency
    cosine = jnp.cos(angles)
    sine = jnp.sin(angles) * jnp.where(lane % HEAD < HALF, -1.0, 1.0)

    begun = qkv_heads(near_x_pieces, qkv_full, cosine, sine, [])
    queries, keys, values, x_all = qkv_heads(far_x_pieces, qkv_full, cosine, sine, begun)

    def row_pieces(array):
        return [array[k * positions : (k + 1) * positions] for k in range(seq_size)]

    heads = [attend(queries, keys, values, 0)]
    group_pieces = [exchange_seq(row_pieces(heads[0][0]))]
    sections = gather_seq(after((later, heads[0][0]))[0][:, -local_width:])
    attn_out_full = jnp.concatenate(by_member(sections), 1)
    for group in range(1, groups):
        heads.append(attend(after((queries, later))[0], keys, values, group))
        group_pieces.append(exchange_seq(row_pieces(heads[group][0])))
    attended_pieces = [jnp.concatenate(pieces, 1) for pieces in zip(*group_pieces)]
    attn_out_ordered = jnp.concatenate(
        [
            lax.dynamic_slice(
                attn_out_full, ((me ^ member) * local_width, 0), (local_width, width)
            )
            for member in range(seq_size)
        ],
        0,
    )
    attended = jnp.concatenate(attended_pieces, 1)
    mixed = tokens + dot_nn(attended, attn_out_ordered)
    xhat_mlp, inverse_mlp = centred_stats(mixed)
    own_x_mlp = xhat_mlp.astype(BF16)
    far_x_mlp_pieces = spread(swap_seq(own_x_mlp, half))
    begun, near_back, near_out = mlp(
        spread(own_x_mlp), near_c_pieces, later, mlp_out_full, length, []
    )
    (hidden, gate_up_grad, x_mlp_all, cotangent_all), far_back, far_out = mlp(
        far_x_mlp_pieces, far_c_pieces, later, mlp_out_full, length, begun
    )
    back_far = far_sum(far_back)
    back_near = fold(near_back)
    grad_mlp_out = dot_tn(hidden, cotangent_all).astype(BF16)
    grad_in = dot_tn(x_mlp_all, gate_up_grad).astype(BF16)
    back_far, grad_mlp_out, grad_in = after((back_far, grad_mlp_out, grad_in))

    mixed_grad = own_cotangent.astype(F32) + norm_backward(
        back_near + back_far.astype(F32), xhat_mlp, inverse_mlp
    )
    mixed_low = mixed_grad.astype(BF16)
    attended_grad = dot_nt(mixed_low, attn_out_ordered).astype(BF16)
    grads = []
    for group in range(groups):
        columns = [k * local_width + group * lanes for k in range(seq_size)]
        pieces = [attended_grad[:, start : start + lanes] for start in columns]
        grads.append(jnp.concatenate(exchange_seq(pieces), 0))
    grad_attn_out = dot_tn(jnp.concatenate(by_member(attended_pieces), 1), mixed_low).astype(BF16)
    grads[0], grad_attn_out = after((grads[0], grad_attn_out))
    column_pieces = [
        lax.dynamic_slice(grad_attn_out, (0, (me ^ k) * local_width), (width, local_width))
        for k in range(seq_size)
    ]
    near_attn_out = fold(column_pieces[:half])
    far_attn_out = fold(column_pieces[half:]).astype(BF16)
    sum_near_out = fold(near_out)
    sum_far_out = fold(far_out).astype(BF16)
    grads[0], sum_far_out, far_attn_out = after((grads[0], sum_far_out, far_attn_out))
    sum_far_out = swap_seq(sum_far_out, half)
    far_attn_out = swap_seq(far_attn_out, half)

    def back_of(group):
        out, lse = heads[group]
        return attend_back(queries, keys, values, grads[group], out, lse, cosine, sine, group)

    packed = [back_of(0)]
    packed[0], sum_far_out, far_attn_out = after((packed[0], sum_far_out, far_attn_out))
    output = (mixed + (sum_near_out + sum_far_out.astype(F32))).astype(BF16)
    grad_attn_out = (near_attn_out + far_attn_out.astype(F32)).astype(BF16)
    first_grads = jnp.concatenate(
        [dot_tn(x_all, packed[0]).astype(BF16), grad_attn_out], 1
    )
    sum_in = reduce_fsdp(grad_in)
    sum_mlp_out = reduce_fsdp(after((grad_mlp_out, grad_in))[0])
    reduced = [halve_fsdp(first_grads, 1)]
    for group in range(1, groups):
        grads[group], output, first_grads, sum_in = after(
            (grads[group], output, first_grads, sum_in)
        )
        packed.append(back_of(group))

    far_grads = token_grad(packed, qkv_full, half, positions, half)
    far_grads = fold(far_grads).astype(BF16)
    near_grads = token_grad(packed, qkv_full, half, positions, 0)
    if groups > 1:
        last_grads = [dot_tn(x_all, section).astype(BF16) for section in packed[1:]]
        last_grads, far_grads = after((last_grads, far_grads))
        reduced += [halve_fsdp(section, 1) for section in last_grads]
    reduced[-1], sum_mlp_out = after((reduced[-1], sum_mlp_out))
    far_grads = swap_seq(far_grads, half)
    normed_grad = far_grads.astype(F32) + fold(near_grads)
    d_input = (mixed_grad + norm_backward(normed_grad, xhat, inverse)).astype(BF16)
    reduced = jnp.concatenate(reduced, 1)
    bit = 2
    while bit < fsdp_size:
        reduced = halve_fsdp(reduced, bit)
        bit *= 2

    in_pieces = by_member(gather_seq(sum_in))
    all_in = jnp.concatenate(
        [piece.reshape(shard, 2 * fsdp_size, unit_share) for piece in in_pieces], 2
    )
    all_in = all_in[:, :, :ff_shard].reshape(shard, -1).astype(F32)
    all_mlp_out = jnp.concatenate(by_member(gather_seq(sum_mlp_out)), 0)[:ff_shard].astype(F32)
    pieces = by_member(gather_seq(reduced))
    section = 3 * lanes
    all_attn_out = jnp.concatenate(
        [piece[:, section : section + local_width] for piece in pieces], 1
    ).astype(F32)
    starts = [0] + [section * group + local_width for group in range(1, groups)]
    all_qkv = jnp.concatenate(
        [
            piece[:, start + part * lanes : start + (part + 1) * lanes]
            for part in range(3)
            for piece in pieces
            for start in starts
        ],
        1,
    ).astype(F32)
    grad_gain_attn = jnp.sum(all_qkv * w_qkv.astype(F32), 1)
    grad_gain_mlp = jnp.sum(all_in * w_in.astype(F32), 1)
    return (
        output.reshape(activations.shape),
        d_input.reshape(activations.shape),
        grad_gain_attn,
        grad_gain_mlp,
        all_qkv * own_gain_attn,
        all_attn_out,
        all_in * own_gain_mlp,
        all_mlp_out,
    )


def solution(mesh):
    in_specs = (
        P("fsdp", "seq", None),
        P("fsdp", "seq", None),
        P("fsdp"),
        P("fsdp", None),
        P("fsdp", None),
        P("fsdp"),
        P("fsdp", None),
        P("fsdp", None),
    )
    out_specs = (
        P("fsdp", "seq", None),
        P("fsdp", "seq", None),
        P("fsdp"),
        P("fsdp"),
        P("fsdp", None),
        P("fsdp", None),
        P("fsdp", None),
        P("fsdp", None),
    )
    body = functools.partial(local, mesh.shape["seq"], mesh.shape["fsdp"])
    return jax.shard_map(body, mesh=mesh, in_specs=in_specs, out_specs=out_specs, check_vma=False)
```

time: 622 us -> 585 us (0.941)
  waiting for transfers between devices: 216 us -> 158 us
  Pallas kernels: 161 us -> 193 us
  other arithmetic: 84.6 us -> 58.8 us
  local copies, waits for them, and re-layouts: 36.2 us -> 60.7 us
  between operations: 23.2 us -> 15.2 us
    ppermute x45 -> x52, waiting for transfers between devices: 216 us -> 158 us  [swap(): return lax.ppermute(values, axis, [(i, i ^ offset) for i in range(size)])]
    pallas_call x4 -> x10, Pallas kernels: 161 us -> 193 us  [the longest x2 75.3 us: attend_back(): pl.pallas_call(attend_back_body, grid=(rows // step,), in_specs=[q_spec,...]
    concatenate x5 -> x6, other arithmetic: 28.3 us -> 5.34 us  [the longest x2 2.88 us: local(): grads.append(jnp.concatenate(exchange_seq(pieces), 0))]
    unnamed x111 -> x131, local copies, waits for them, and re-layouts: 12.6 us -> 24.6 us
    reshape x0 -> x3, local copies, waits for them, and re-layouts: none -> 10.3 us  [the longest x1 5.65 us: local(): mlp_out_full = later[:, 2 * units:2 * units + tall * width // wide].resha...]
    dot_general x2 -> x1, matrix products: 8.67 us -> 1.55 us  [dot_nt(): lax.dot_general(a, b, (((1,), (1,)), ((), ())), preferred_element_type=F32)]
    dot_general x4 -> x5, matrix products: 29.3 us -> 36.3 us  [dot_tn(): lax.dot_general(a, b, (((0,), (0,)), ((), ())), preferred_element_type=F32)]
    convert_element_type x11 -> x13, other arithmetic: 14.3 us -> 20 us  [the longest x1 4.18 us: local(): output = (mixed + (sum_near_out + sum_far_out.astype(F32))).astype(BF16)]
  transfers between devices with their start and end apart: 51 -> 55, of which waited for: 18 -> 21; matrix products, arithmetic and copies ran while one was open for 23% -> 24% of each run, Pallas kernels for 21% -> 30%
where the time goes in v2:
time: 585 us; the launch traced here: 580 us
  Pallas kernels  193 us (33%)
  waiting for transfers between devices  158 us (27%)
  local copies, waits for them, and re-layouts  60.7 us (10%)
  other arithmetic  58.8 us (10%)
  starting transfers between devices  54.1 us (9%)
  matrix products  39.4 us (7%)
  between operations  15.2 us (3%)
    ppermute x52, waiting for transfers between devices, swap(): return lax.ppermute(values, axis, [(i, i ^ offset) for i in range(size)])  158 us
    pallas_call x2, Pallas kernels, attend_back(): pl.pallas_call(attend_back_body, grid=(rows // step,), in_specs=[q_spec,...  75.3 us
    ppermute x52, starting transfers between devices, swap(): return lax.ppermute(values, axis, [(i, i ^ offset) for i in range(size)])  54 us
    pallas_call x2, Pallas kernels, attend(): pl.pallas_call(attend_body, grid=(rows // step,), in_specs=[q_spec, k_spe...  47.7 us
    pallas_call x2, Pallas kernels, mlp(): pl.pallas_call(functools.partial(mlp_body, count, steps), grid=(count * s...  43.4 us
    dot_general x5, matrix products, dot_tn(): lax.dot_general(a, b, (((0,), (0,)), ((), ())), preferred_element_type=F32)  36.3 us
    unnamed x131, local copies, waits for them, and re-layouts  24.6 us
    pallas_call x2, Pallas kernels, qkv_heads(): pl.pallas_call(functools.partial(qkv_body, count, steps), grid=(count * s...  13.8 us
  transfers between devices with their start and end apart: 55, of which 21 were waited for; matrix products, arithmetic and copies ran while one was open for 24% of the time, Pallas kernels for 30%

profile of v2, /device:TPU:1, one launch (start us, length us, event | category | flops | bytes accessed | tf_op | source)
XLA Modules:
  0.0 580.0 jit_solution(98429255242099949)
XLA Ops:
  17.7 3.2 collective-permute-start.2
  24.3 11.2 %collective-permute-done.2 = bf16[128,768]{1,0:T(8,128)(2,1)S(1)} collective-permute-done((bf16[128,768]{1,0:T(8,128)(2,1)S(1)}, bf16[128,768]{1,0:T(8,128)(2,1)S(1)}, u32[]{:S(2)}, u32[]{:S(2)}) %collective-permute-start.2) | collective-permute-done | bytes 196640 | tf_op jit(solution)/shard_map/ppermute | solution.py:393
  35.7 6.1 %collective-permute-start.3 = (bf16[2,128,768]{2,1,0:T(8,128)(2,1)S(1)}, bf16[2,128,768]{2,1,0:T(8,128)(2,1)S(1)}, u32[]{:S(2)}, u32[]{:S(2)}) collective-permute-start(bf16[2,128,768]{2,1,0:T(8,128)(2,1)S(1)} %pad_maximum_fusion.19), channel_id=1, source_target_pairs={{0,8},{4,12},{8,0},{12,4},{16,24},{20,28},{24,16},{28,20},{1,9},{5... | collective-permute-start | bytes 1179656 | tf_op jit(solution)/shard_map/ppermute | solution.py:393
  41.8 17.0 %collective-permute-done.3 = bf16[2,128,768]{2,1,0:T(8,128)(2,1)S(1)} collective-permute-done((bf16[2,128,768]{2,1,0:T(8,128)(2,1)S(1)}, bf16[2,128,768]{2,1,0:T(8,128)(2,1)S(1)}, u32[]{:S(2)}, u32[]{:S(2)}) %collective-permute-start.3) | collective-permute-done | bytes 393248 | tf_op jit(solution)/shard_map/ppermute | solution.py:393
  62.0 7.5 %select_multiply_fusion = (f32[2560,128]{1,0:T(8,128)}, f32[2560,128]{1,0:T(8,128)}) fusion(s32[128]{0:T(128)S(1)} %get-tuple-element.198, s32[128]{0:T(128)S(1)} %get-tuple-element.200, s32[128]{0:T(128)S(1)} %get-tuple-element.199, s32[128]{0:T(128)S(1)} %get-tuple-element.201, s32[2560]{0:T(1024)S(1)} %get-tuple-element.195, ...), kind=kLoop, calls=%fused_computation.59 | loop fusion | flops 4587520 | bytes 2669828 | tf_op jit(solution)/shard_map/mul | solution.py:521
  69.6 22.0 %collective-permute-done.4 = bf16[2,2,128,768]{3,2,0,1:T(8,128)(2,1)} collective-permute-done((bf16[2,2,128,768]{3,2,0,1:T(8,128)(2,1)}, bf16[2,2,128,768]{3,2,0,1:T(8,128)(2,1)}, u32[]{:S(2)}, u32[]{:S(2)}) %collective-permute-start.4) | collective-permute-done | bytes 786464 | tf_op jit(solution)/shard_map/ppermute | solution.py:393
  94.2 6.9 %qkv_rope.2 = (bf16[2560,256]{1,0:T(8,128)(2,1)}, bf16[2560,256]{1,0:T(8,128)(2,1)}, bf16[2560,256]{1,0:T(8,128)(2,1)}, bf16[2560,1024]{1,0:T(8,128)(2,1)}) custom-call(bf16[640,1024]{1,0:T(8,128)(2,1)} %copy-done.16, bf16[640,1024]{1,0:T(8,128)(2,1)} %collective-permute-done.5.refs_1_, bf16[1024,768]{1,0:T(8,128)(2,1)} %bitcast.159, ...), custom_call_target="tpu_custom_call" | custom-call | flops 2013265920 | bytes 8781824 | tf_op jit(solution)/shard_map/qkv_rope/pallas_call | solution.py:127
  101.1 7.0 %qkv_rope.3 = (bf16[2560,256]{1,0:T(8,128)(2,1)}, bf16[2560,256]{1,0:T(8,128)(2,1)}, bf16[2560,256]{1,0:T(8,128)(2,1)}, bf16[2560,1024]{1,0:T(8,128)(2,1)}) custom-call(bf16[640,1024]{1,0:T(8,128)(2,1)} %collective-permute-done.refs_0_, ...), custom_call_target="tpu_custom_call", output_to_operand_aliasing={{0}: (5, {}), {1}: (6, {}), {2}: (7, {}), {3}: (8, {})} | custom-call | flops 2013265920 | bytes 8781824 | tf_op jit(solution)/shard_map/qkv_rope/pallas_call | solution.py:127
  108.1 23.9 %attend.2 = (bf16[2560,128]{1,0:T(8,128)(2,1)}, f32[128,2560]{1,0:T(8,128)}) custom-call(bf16[2560,256]{1,0:T(8,128)(2,1)} %get-tuple-element.70.q_ref, bf16[2560,256]{1,0:T(8,128)(2,1)} %get-tuple-element.67.k_ref, bf16[2560,256]{1,0:T(8,128)(2,1)} %get-tuple-element.68.v_ref), custom_call_target="tpu_custom_call" | custom-call | flops 13421772800 | bytes 2621440 | tf_op jit(solution)/shard_map/attend/pallas_call | solution.py:175
  133.9 3.4 collective-permute-start.6
  139.4 23.9 %attend.3 = (bf16[2560,128]{1,0:T(8,128)(2,1)}, f32[128,2560]{1,0:T(8,128)}) custom-call(bf16[2560,256]{1,0:T(8,128)(2,1)} %get-tuple-element.70.q_ref, bf16[2560,256]{1,0:T(8,128)(2,1)} %get-tuple-element.67.k_ref, bf16[2560,256]{1,0:T(8,128)(2,1)} %get-tuple-element.68.v_ref), custom_call_target="tpu_custom_call" | custom-call | flops 13421772800 | bytes 2621440 | tf_op jit(solution)/shard_map/attend/pallas_call | solution.py:175
  169.9 29.4 %collective-permute-done.8 = bf16[640,128]{1,0:T(8,128)(2,1)S(1)} collective-permute-done((bf16[640,128]{1,0:T(8,128)(2,1)S(1)}, bf16[640,128]{1,0:T(8,128)(2,1)S(1)}, u32[]{:S(2)}, u32[]{:S(2)}) %collective-permute-start.8) | collective-permute-done | bytes 163872 | tf_op jit(solution)/shard_map/ppermute | solution.py:393
  199.3 2.1 collective-permute-start.10
  207.4 2.8 collective-permute-done.11
  219.7 27.9 %collective-permute-done.18.refs_0_ = bf16[640,1024]{1,0:T(8,128)(2,1)} collective-permute-done((bf16[640,1024]{1,0:T(8,128)(2,1)}, bf16[640,1024]{1,0:T(8,128)(2,1)}, u32[]{:S(2)}, u32[]{:S(2)}) %collective-permute-start.18) | collective-permute-done | bytes 1310752 | tf_op jit(solution)/shard_map/ppermute | solution.py:393
  249.2 2.7 slice.192
  251.8 5.7 reshape.143
  257.5 3.1 copy.32
  262.1 21.7 %mlp.2 = (bf16[2560,768]{1,0:T(8,128)(2,1)}, bf16[2560,1536]{1,0:T(8,128)(2,1)}, bf16[2560,1024]{1,0:T(8,128)(2,1)}, bf16[2560,1024]{1,0:T(8,128)(2,1)}, bf16[64...) custom-call(bf16[640,1024]{1,0:T(8,128)(2,1)} %fusion.14.refs_0_, ...), custom_call_target="tpu_custom_call" | custom-call | flops 12079595520 | bytes 26345472 | tf_op jit(solution)/shard_map/mlp/pallas_call | solution.py:314
  283.8 21.6 %mlp.3 = (bf16[2560,768]{1,0:T(8,128)(2,1)}, bf16[2560,1536]{1,0:T(8,128)(2,1)}, bf16[2560,1024]{1,0:T(8,128)(2,1)}, bf16[2560,1024]{1,0:T(8,128)(2,1)}, bf16[64...) custom-call(bf16[640,1024]{1,0:T(8,128)(2,1)} %collective-permute-do, ...), custom_call_target="tpu_custom_call", output_to_operand_aliasing={{0}: (6, {}), {1}: (7, {}), {2}: (8, {}), {3}: (9, {})} | custom-call | flops 12079595520 | bytes 26345472 | tf_op jit(solution)/shard_map/mlp/pallas_call | solution.py:314
  305.5 3.2 collective-permute-done.22
  308.8 2.9 add_convert_fusion.3
  312.4 13.8 %convolution_convert_fusion = bf16[1024,1536]{1,0:T(8,128)(2,1)} fusion(bf16[2560,1024]{1,0:T(8,128)(2,1)} %get-tuple-element.84, bf16[2560,1536]{1,0:T(8,128)(2,1)} %get-tuple-element.85), kind=kOutput, calls=%fused_computation | convolution fusion | flops 8054636544 | bytes 16252928 | tf_op jit(solution)/shard_map/dot_general | solution.py:32
  326.3 9.1 %convolution_convert_fusion.2 = bf16[768,1024]{1,0:T(8,128)(2,1)} fusion(bf16[2560,768]{1,0:T(8,128)(2,1)} %get-tuple-element.82, bf16[2560,1024]{1,0:T(8,128)(2,1)} %get-tuple-element.83), kind=kOutput, calls=%fused_computation.36 | convolution fusion | flops 4027318272 | bytes 10747904 | tf_op jit(solution)/shard_map/dot_general | solution.py:32
  335.4 6.8 %collective-permute-done.23 = bf16[640,1024]{1,0:T(8,128)(2,1)} collective-permute-done((bf16[640,1024]{1,0:T(8,128)(2,1)}, bf16[640,1024]{1,0:T(8,128)(2,1)}, u32[]{:S(2)}, u32[]{:S(2)}) %collective-permute-start.23) | collective-permute-done | bytes 1310752 | tf_op jit(solution)/shard_map/ppermute | solution.py:393
  346.5 2.7 fusion.28
  349.2 3.0 multiply_add_fusion
  361.5 4.1 collective-permute-done.30
  377.4 37.8 %attend_back.2.refs_0_ = bf16[2560,384]{1,0:T(8,128)(2,1)} custom-call(bf16[2560,256]{1,0:T(8,128)(2,1)} %get-tuple-element.70.q_ref, bf16[2560,256]{1,0:T(8,128)(2,1)} %get-tuple-element.67.k_ref, bf16[2560,256]{1,0:T(8,128)(2,1)} %get-tuple-element.68.v_ref, bf16[2560,128]{1,0:T(8,128)(2,1)} %pad_maximum_fusion.18.g_ref, ...), custom_call_target="tpu_custom_call" | custom-call | flops 33554432000 | bytes 6553600 | tf_op jit(solution)/shard_map/attend_back/pallas_call | solution.py:247
  415.3 2.9 collective-permute-done.34
  421.3 5.4 convolution_convert_fusion.5
  427.9 4.5 reshape.147
  432.4 6.0 %constant_dynamic-slice_fusion.6 = (bf16[4,1,128,640]{2,1,0,3:T(2,128)(2,1)}, bf16[4,1,128,640]{2,1,0,3:T(2,128)(2,1)}) fusion(bf16[4,2,128,640]{2,1,0,3:T(2,128)(2,1)} %reshape.147, s32[]{:T(128)S(6)} %select_n.190, s32[]{:T(128)S(6)} %select_n.191), kind=kLoop, calls=%fused_computation.178 | loop fusion | bytes 2621448 | tf_op jit(solution)/shard_map/jit(dynamic_index_in_dim)/dynamic_slice | solution.py:450
  438.4 3.7 copy.43
  442.1 2.5 collective-permute-start.39
  444.6 4.2 add_convert_fusion.1
  448.8 37.4 %attend_back.3.refs_1_ = bf16[2560,384]{1,0:T(8,128)(2,1)} custom-call(bf16[2560,256]{1,0:T(8,128)(2,1)} %get-tuple-element.70.q_ref, bf16[2560,256]{1,0:T(8,128)(2,1)} %get-tuple-element.67.k_ref, bf16[2560,256]{1,0:T(8,128)(2,1)} %get-tuple-element.68.v_ref, bf16[2560,128]{1,0:T(8,128)(2,1)} %pad_maximum_fusion.17.g_ref, ...), custom_call_target="tpu_custom_call" | custom-call | flops 33554432000 | bytes 6553600 | tf_op jit(solution)/shard_map/attend_back/pallas_call | solution.py:247
  486.2 6.8 %token_grad.2 = (bf16[640,1024]{1,0:T(8,128)(2,1)}, bf16[640,1024]{1,0:T(8,128)(2,1)}) custom-call(bf16[2560,384]{1,0:T(8,128)(2,1)} %attend_back.2.refs_0_, bf16[2560,384]{1,0:T(8,128)(2,1)} %attend_back.3.refs_1_, bf16[1024,768]{1,0:T(8,128)(2,1)} %bitcast.161), custom_call_target="tpu_custom_call" | custom-call | flops 2013265920 | bytes 6160384 | tf_op jit(solution)/shard_map/token_grad/pallas_call | solution.py:359
  497.5 6.4 %token_grad.3 = (bf16[640,1024]{1,0:T(8,128)(2,1)}, bf16[640,1024]{1,0:T(8,128)(2,1)}) custom-call(bf16[2560,384]{1,0:T(8,128)(2,1)} %attend_back.2.refs_0_, bf16[2560,384]{1,0:T(8,128)(2,1)} %attend_back.3.refs_1_, bf16[1024,768]{1,0:T(8,128)(2,1)} %bitcast.162), custom_call_target="tpu_custom_call" | custom-call | flops 2013265920 | bytes 6160384 | tf_op jit(solution)/shard_map/token_grad/pallas_call | solution.py:359
  504.1 6.1 %convolution_convert_fusion.4 = bf16[1024,384]{1,0:T(8,128)(2,1)S(1)} fusion(bf16[2560,1024]{1,0:T(8,128)(2,1)} %get-tuple-element.98, bf16[2560,384]{1,0:T(8,128)(2,1)} %attend_back.3.refs_1_), kind=kOutput, calls=%fused_computation.42 | convolution fusion | flops 2013659136 | bytes 7995392 | tf_op jit(solution)/shard_map/dot_general | solution.py:32
  514.6 8.3 %collective-permute-done.40 = bf16[4,128,384]{2,1,0:T(8,128)(2,1)} collective-permute-done((bf16[4,128,384]{2,1,0:T(8,128)(2,1)S(1)}, bf16[4,128,384]{2,1,0:T(8,128)(2,1)}, u32[]{:S(2)}, u32[]{:S(2)}) %collective-permute-start.40) | collective-permute-done | bytes 393248 | tf_op jit(solution)/shard_map/ppermute | solution.py:393
  529.8 3.5 collective-permute-start.51
  534.6 2.2 copy.41
  539.8 3.4 collective-permute-start.42
  544.4 10.9 %collective-permute-done.42 = bf16[1,128,1024]{2,1,0:T(8,128)(2,1)S(1)} collective-permute-done((bf16[1,128,1024]{2,1,0:T(8,128)(2,1)S(1)}, bf16[1,128,1024]{2,1,0:T(8,128)(2,1)S(1)}, u32[]{:S(2)}, u32[]{:S(2)}) %collective-permute-start.42) | collective-permute-done | bytes 262176 | tf_op jit(solution)/shard_map/ppermute | solution.py:393
  558.0 3.0 fusion.29
  561.1 2.8 collective-permute-done.44
  565.5 3.5 fusion.16
  (315 shorter events, 108.7 us)
Async XLA Ops:
  7.2 130.1 %all-gather.2.cloned.1.call-start = ((), (), s32[]{:S(2)}) async-start(), calls=%async_computation.2 | async-start | bytes 5898240 | tf_op jit(solution)/shard_map/all_gather | solution.py:506
  12.8 435.9 %reduce-scatter.3.cloned.1.call-start = ((), (), s32[]{:S(2)}) async-start(), calls=%async_computation.3 | async-start | bytes 3538944 | tf_op jit(solution)/shard_map/reduce_scatter | solution.py:456
  17.7 17.8 %collective-permute-start.2 = (bf16[128,768]{1,0:T(8,128)(2,1)S(1)}, bf16[128,768]{1,0:T(8,128)(2,1)S(1)}, u32[]{:S(2)}, u32[]{:S(2)}) collective-permute-start(bf16[128,768]{1,0:T(8,128)(2,1)S(1)} %multiply_convert_fusion.1), channel_id=1, source_target_pairs={{0,16},{4,20},{8,24},{12,28},{16,0},{20,4},{24,8},{28,12},{1,17},{... | collective-permute-start | bytes 589832 | tf_op jit(solution)/shard_map/ppermute | solution.py:393
  22.0 72.2 %collective-permute-start.5 = (bf16[640,1024]{1,0:T(8,128)(2,1)S(1)}, bf16[640,1024]{1,0:T(8,128)(2,1)}, u32[]{:S(2)}, u32[]{:S(2)}) collective-permute-start(bf16[640,1024]{1,0:T(8,128)(2,1)S(1)} %fusion.6.refs_0_), channel_id=1, source_target_pairs={{0,1},{1,0},{2,3},{3,2},{4,5},{5,4},{6,7},{7,6},{8,9},{9,8},{10,11... | collective-permute-start | bytes 3932168 | tf_op jit(solution)/shard_map/ppermute | solution.py:393
  23.0 38.2 %collective-permute-start = (bf16[640,1024]{1,0:T(8,128)(2,1)S(1)}, bf16[640,1024]{1,0:T(8,128)(2,1)}, u32[]{:S(2)}, u32[]{:S(2)}) collective-permute-start(bf16[640,1024]{1,0:T(8,128)(2,1)S(1)} %fusion.6.refs_0_), channel_id=1, source_target_pairs={{0,2},{1,3},{2,0},{3,1},{4,6},{5,7},{6,4},{7,5},{8,10},{9,11},{10,... | collective-permute-start | bytes 3932168 | tf_op jit(solution)/shard_map/ppermute | solution.py:393
  35.7 23.2 %collective-permute-start.3 = (bf16[2,128,768]{2,1,0:T(8,128)(2,1)S(1)}, bf16[2,128,768]{2,1,0:T(8,128)(2,1)S(1)}, u32[]{:S(2)}, u32[]{:S(2)}) collective-permute-start(bf16[2,128,768]{2,1,0:T(8,128)(2,1)S(1)} %pad_maximum_fusion.19), channel_id=1, source_target_pairs={{0,8},{4,12},{8,0},{12,4},{16,24},{20,28},{24,16},{28,20},{1,9},{5... | collective-permute-start | bytes 1179656 | tf_op jit(solution)/shard_map/ppermute | solution.py:393
  59.9 31.7 %collective-permute-start.4 = (bf16[2,2,128,768]{3,2,0,1:T(8,128)(2,1)}, bf16[2,2,128,768]{3,2,0,1:T(8,128)(2,1)}, u32[]{:S(2)}, u32[]{:S(2)}) collective-permute-start(bf16[2,2,128,768]{3,2,0,1:T(8,128)(2,1)} %pad_maximum_fusion.11), channel_id=1, source_target_pairs={{0,4},{4,0},{8,12},{12,8},{16,20},{20,16},{24,28},{28,24},{1,5},{5... | collective-permute-start | bytes 2359304 | tf_op jit(solution)/shard_map/ppermute | solution.py:393
  61.2 39.9 %collective-permute-start.1 = (bf16[640,1024]{1,0:T(8,128)(2,1)}, bf16[640,1024]{1,0:T(8,128)(2,1)}, u32[]{:S(2)}, u32[]{:S(2)}) collective-permute-start(bf16[640,1024]{1,0:T(8,128)(2,1)} %collective-permute-done.refs_0_), channel_id=1, source_target_pairs={{0,1},{1,0},{2,3},{3,2},{4,5},{5,4},{6,7},{7,6},{8,9},{9,8},{10,11... | collective-permute-start | bytes 3932168 | tf_op jit(solution)/shard_map/ppermute | solution.py:393
  133.9 33.1 %collective-permute-start.6 = (bf16[640,128]{1,0:T(8,128)(2,1)S(1)}, bf16[640,128]{1,0:T(8,128)(2,1)S(1)}, u32[]{:S(2)}, u32[]{:S(2)}) collective-permute-start(bf16[640,128]{1,0:T(8,128)(2,1)S(1)} %get-tuple-element.178), channel_id=1, source_target_pairs={{0,1},{1,0},{2,3},{3,2},{4,5},{5,4},{6,7},{7,6},{8,9},{9,8},{10,11... | collective-permute-start | bytes 491528 | tf_op jit(solution)/shard_map/ppermute | solution.py:393
  138.4 30.5 %collective-permute-start.13 = (bf16[1024,256]{1,0:T(8,128)(2,1)S(1)}, bf16[1024,256]{1,0:T(8,128)(2,1)S(1)}, u32[]{:S(2)}, u32[]{:S(2)}) collective-permute-start(bf16[1024,256]{1,0:T(8,128)(2,1)S(1)} %get-tuple-element.129), channel_id=1, source_target_pairs={{0,2},{1,3},{2,0},{3,1},{4,6},{5,7},{6,4},{7,5},{8,10},{9,11},{10,... | collective-permute-start | bytes 1572872 | tf_op jit(solution)/shard_map/ppermute | solution.py:393
  165.5 53.7 %collective-permute-start.20 = (bf16[640,1024]{1,0:T(8,128)(2,1)}, bf16[640,1024]{1,0:T(8,128)(2,1)}, u32[]{:S(2)}, u32[]{:S(2)}) collective-permute-start(bf16[640,1024]{1,0:T(8,128)(2,1)} %bitcast.refs_2_), channel_id=1, source_target_pairs={{0,2},{1,3},{2,0},{3,1},{4,6},{5,7},{6,4},{7,5},{8,10},{9,11},{10,... | collective-permute-start | bytes 3932168 | tf_op jit(solution)/shard_map/ppermute | solution.py:393
  166.1 33.2 %collective-permute-start.8 = (bf16[640,128]{1,0:T(8,128)(2,1)S(1)}, bf16[640,128]{1,0:T(8,128)(2,1)S(1)}, u32[]{:S(2)}, u32[]{:S(2)}) collective-permute-start(bf16[640,128]{1,0:T(8,128)(2,1)S(1)} %get-tuple-element.177), channel_id=1, source_target_pairs={{0,2},{1,3},{2,0},{3,1},{4,6},{5,7},{6,4},{7,5},{8,10},{9,11},{10,... | collective-permute-start | bytes 491528 | tf_op jit(solution)/shard_map/ppermute | solution.py:393
  167.0 44.0 %collective-permute-start.12 = (bf16[1024,256]{1,0:T(8,128)(2,1)S(1)}, bf16[1024,256]{1,0:T(8,128)(2,1)S(1)}, u32[]{:S(2)}, u32[]{:S(2)}) collective-permute-start(bf16[1024,256]{1,0:T(8,128)(2,1)S(1)} %get-tuple-element.129), channel_id=1, source_target_pairs={{0,1},{1,0},{2,3},{3,2},{4,5},{5,4},{6,7},{7,6},{8,9},{9,8},{10,11... | collective-permute-start | bytes 1572872 | tf_op jit(solution)/shard_map/ppermute | solution.py:393
  168.5 34.3 %collective-permute-start.9 = (bf16[640,128]{1,0:T(8,128)(2,1)}, bf16[640,128]{1,0:T(8,128)(2,1)S(1)}, u32[]{:S(2)}, u32[]{:S(2)}) collective-permute-start(bf16[640,128]{1,0:T(8,128)(2,1)} %get-tuple-element.182), channel_id=1, source_target_pairs={{0,2},{1,3},{2,0},{3,1},{4,6},{5,7},{6,4},{7,5},{8,10},{9,11},{10,... | collective-permute-start | bytes 491528 | tf_op jit(solution)/shard_map/ppermute | solution.py:393
  168.9 42.1 %collective-permute-start.14 = (bf16[1024,256]{1,0:T(8,128)(2,1)S(1)}, bf16[1024,256]{1,0:T(8,128)(2,1)S(1)}, u32[]{:S(2)}, u32[]{:S(2)}) collective-permute-start(bf16[1024,256]{1,0:T(8,128)(2,1)S(1)} %collective-permute-done.13), channel_id=1, source_target_pairs={{0,1},{1,0},{2,3},{3,2},{4,5},{5,4},{6,7},{7,6},{8,9},{9,8},{10,11... | collective-permute-start | bytes 1572872 | tf_op jit(solution)/shard_map/ppermute | solution.py:393
  199.3 7.5 %collective-permute-start.10 = (bf16[640,128]{1,0:T(8,128)(2,1)S(1)}, bf16[640,128]{1,0:T(8,128)(2,1)S(1)}, u32[]{:S(2)}, u32[]{:S(2)}) collective-permute-start(bf16[640,128]{1,0:T(8,128)(2,1)S(1)} %get-tuple-element.176), channel_id=1, source_target_pairs={{0,3},{1,2},{2,1},{3,0},{4,7},{5,6},{6,5},{7,4},{8,11},{9,10},{10,... | collective-permute-start | bytes 491528 | tf_op jit(solution)/shard_map/ppermute | solution.py:393
  202.8 7.5 %collective-permute-start.11 = (bf16[640,128]{1,0:T(8,128)(2,1)S(1)}, bf16[640,128]{1,0:T(8,128)(2,1)S(1)}, u32[]{:S(2)}, u32[]{:S(2)}) collective-permute-start(bf16[640,128]{1,0:T(8,128)(2,1)S(1)} %get-tuple-element.181), channel_id=1, source_target_pairs={{0,3},{1,2},{2,1},{3,0},{4,7},{5,6},{6,5},{7,4},{8,11},{9,10},{10,... | collective-permute-start | bytes 491528 | tf_op jit(solution)/shard_map/ppermute | solution.py:393
  217.7 30.0 %collective-permute-start.18 = (bf16[640,1024]{1,0:T(8,128)(2,1)}, bf16[640,1024]{1,0:T(8,128)(2,1)}, u32[]{:S(2)}, u32[]{:S(2)}) collective-permute-start(bf16[640,1024]{1,0:T(8,128)(2,1)} %fusion.14.refs_0_), channel_id=1, source_target_pairs={{0,2},{1,3},{2,0},{3,1},{4,6},{5,7},{6,4},{7,5},{8,10},{9,11},{10,... | collective-permute-start | bytes 3932168 | tf_op jit(solution)/shard_map/ppermute | solution.py:393
  218.4 43.7 %collective-permute-start.16 = (bf16[640,1024]{1,0:T(8,128)(2,1)}, bf16[640,1024]{1,0:T(8,128)(2,1)}, u32[]{:S(2)}, u32[]{:S(2)}) collective-permute-start(bf16[640,1024]{1,0:T(8,128)(2,1)} %bitcast.refs_2_), channel_id=1, source_target_pairs={{0,1},{1,0},{2,3},{3,2},{4,5},{5,4},{6,7},{7,6},{8,9},{9,8},{10,11... | collective-permute-start | bytes 3932168 | tf_op jit(solution)/shard_map/ppermute | solution.py:393
  219.2 42.9 %collective-permute-start.15 = (bf16[640,1024]{1,0:T(8,128)(2,1)}, bf16[640,1024]{1,0:T(8,128)(2,1)}, u32[]{:S(2)}, u32[]{:S(2)}) collective-permute-start(bf16[640,1024]{1,0:T(8,128)(2,1)} %fusion.14.refs_0_), channel_id=1, source_target_pairs={{0,1},{1,0},{2,3},{3,2},{4,5},{5,4},{6,7},{7,6},{8,9},{9,8},{10,11... | collective-permute-start | bytes 3932168 | tf_op jit(solution)/shard_map/ppermute | solution.py:393
  219.2 64.6 %collective-permute-start.21 = (bf16[640,1024]{1,0:T(8,128)(2,1)}, bf16[640,1024]{1,0:T(8,128)(2,1)}, u32[]{:S(2)}, u32[]{:S(2)}) collective-permute-start(bf16[640,1024]{1,0:T(8,128)(2,1)} %collective-permute-done.20.refs_2_), channel_id=1, source_target_pairs={{0,1},{1,0},{2,3},{3,2},{4,5},{5,4},{6,7},{7,6},{8,9},{9,8},{10,11... | collective-permute-start | bytes 3932168 | tf_op jit(solution)/shard_map/ppermute | solution.py:393
  247.6 36.2 %collective-permute-start.19 = (bf16[640,1024]{1,0:T(8,128)(2,1)}, bf16[640,1024]{1,0:T(8,128)(2,1)}, u32[]{:S(2)}, u32[]{:S(2)}) collective-permute-start(bf16[640,1024]{1,0:T(8,128)(2,1)} %collective-permute-done.18.refs_0_), channel_id=1, source_target_pairs={{0,1},{1,0},{2,3},{3,2},{4,5},{5,4},{6,7},{7,6},{8,9},{9,8},{10,11... | collective-permute-start | bytes 3932168 | tf_op jit(solution)/shard_map/ppermute | solution.py:393
  311.7 30.6 %collective-permute-start.23 = (bf16[640,1024]{1,0:T(8,128)(2,1)}, bf16[640,1024]{1,0:T(8,128)(2,1)}, u32[]{:S(2)}, u32[]{:S(2)}) collective-permute-start(bf16[640,1024]{1,0:T(8,128)(2,1)} %add_convert_fusion.3), channel_id=1, source_target_pairs={{0,2},{1,3},{2,0},{3,1},{4,6},{5,7},{6,4},{7,5},{8,10},{9,11},{10,... | collective-permute-start | bytes 3932168 | tf_op jit(solution)/shard_map/ppermute | solution.py:393
  342.3 181.9 %reduce-scatter.5.cloned.1.call-start = ((), (), s32[]{:S(2)}) async-start(), calls=%async_computation.4 | async-start | bytes 1769472 | tf_op jit(solution)/shard_map/reduce_scatter | solution.py:456
  344.9 99.7 %collective-permute-start.27 = (bf16[640,1024]{1,0:T(8,128)(2,1)}, bf16[640,1024]{1,0:T(8,128)(2,1)}, u32[]{:S(2)}, u32[]{:S(2)}) collective-permute-start(bf16[640,1024]{1,0:T(8,128)(2,1)} %get-tuple-element.88), channel_id=1, source_target_pairs={{0,1},{1,0},{2,3},{3,2},{4,5},{5,4},{6,7},{7,6},{8,9},{9,8},{10,11... | collective-permute-start | bytes 3932168 | tf_op jit(solution)/shard_map/ppermute | solution.py:393
  346.1 21.5 %collective-permute-start.31 = (bf16[640,1024]{1,0:T(8,128)(2,1)S(1)}, bf16[640,1024]{1,0:T(8,128)(2,1)S(1)}, u32[]{:S(2)}, u32[]{:S(2)}) collective-permute-start(bf16[640,1024]{1,0:T(8,128)(2,1)S(1)} %copy-done.43), channel_id=1, source_target_pairs={{0,1},{1,0},{2,3},{3,2},{4,5},{5,4},{6,7},{7,6},{8,9},{9,8},{10,11... | collective-permute-start | bytes 3932168 | tf_op jit(solution)/shard_map/ppermute | solution.py:393
  355.1 5.7 collective-permute-start.29
  355.8 9.7 %collective-permute-start.30 = (bf16[640,128]{1,0:T(8,128)(2,1)S(1)}, bf16[640,128]{1,0:T(8,128)(2,1)S(1)}, u32[]{:S(2)}, u32[]{:S(2)}) collective-permute-start(bf16[640,128]{1,0:T(8,128)(2,1)S(1)} %get-tuple-element.155), channel_id=1, source_target_pairs={{0,3},{1,2},{2,1},{3,0},{4,7},{5,6},{6,5},{7,4},{8,11},{9,10},{10,... | collective-permute-start | bytes 491528 | tf_op jit(solution)/shard_map/ppermute | solution.py:393
  358.8 11.5 %collective-permute-start.24 = (bf16[640,128]{1,0:T(8,128)(2,1)}, bf16[640,128]{1,0:T(8,128)(2,1)}, u32[]{:S(2)}, u32[]{:S(2)}) collective-permute-start(bf16[640,128]{1,0:T(8,128)(2,1)} %get-tuple-element.160), channel_id=1, source_target_pairs={{0,1},{1,0},{2,3},{3,2},{4,5},{5,4},{6,7},{7,6},{8,9},{9,8},{10,11... | collective-permute-start | bytes 491528 | tf_op jit(solution)/shard_map/ppermute | solution.py:393
  360.8 9.7 %collective-permute-start.25 = (bf16[640,128]{1,0:T(8,128)(2,1)}, bf16[640,128]{1,0:T(8,128)(2,1)}, u32[]{:S(2)}, u32[]{:S(2)}) collective-permute-start(bf16[640,128]{1,0:T(8,128)(2,1)} %get-tuple-element.159), channel_id=1, source_target_pairs={{0,2},{1,3},{2,0},{3,1},{4,6},{5,7},{6,4},{7,5},{8,10},{9,11},{10,... | collective-permute-start | bytes 491528 | tf_op jit(solution)/shard_map/ppermute | solution.py:393
  365.6 6.4 %collective-permute-start.26 = (bf16[640,128]{1,0:T(8,128)(2,1)}, bf16[640,128]{1,0:T(8,128)(2,1)}, u32[]{:S(2)}, u32[]{:S(2)}) collective-permute-start(bf16[640,128]{1,0:T(8,128)(2,1)} %get-tuple-element.158), channel_id=1, source_target_pairs={{0,3},{1,2},{2,1},{3,0},{4,7},{5,6},{6,5},{7,4},{8,11},{9,10},{10,... | collective-permute-start | bytes 491528 | tf_op jit(solution)/shard_map/ppermute | solution.py:393
  367.6 6.4 %collective-permute-start.32 = (bf16[1024,256]{1,0:T(8,128)(2,1)}, bf16[1024,256]{1,0:T(8,128)(2,1)S(1)}, u32[]{:S(2)}, u32[]{:S(2)}) collective-permute-start(bf16[1024,256]{1,0:T(8,128)(2,1)} %get-tuple-element.131), channel_id=1, source_target_pairs={{0,1},{1,0},{2,3},{3,2},{4,5},{5,4},{6,7},{7,6},{8,9},{9,8},{10,11... | collective-permute-start | bytes 1572872 | tf_op jit(solution)/shard_map/ppermute | solution.py:393
  370.4 48.6 %collective-permute-start.35 = (bf16[1024,256]{1,0:T(8,128)(2,1)}, bf16[1024,256]{1,0:T(8,128)(2,1)S(1)}, u32[]{:S(2)}, u32[]{:S(2)}) collective-permute-start(bf16[1024,256]{1,0:T(8,128)(2,1)} %get-tuple-element.130), channel_id=1, source_target_pairs={{0,1},{1,0},{2,3},{3,2},{4,5},{5,4},{6,7},{7,6},{8,9},{9,8},{10,11... | collective-permute-start | bytes 1572872 | tf_op jit(solution)/shard_map/ppermute | solution.py:393
  375.9 42.2 %collective-permute-start.33 = (bf16[640,1024]{1,0:T(8,128)(2,1)}, bf16[640,1024]{1,0:T(8,128)(2,1)}, u32[]{:S(2)}, u32[]{:S(2)}) collective-permute-start(bf16[640,1024]{1,0:T(8,128)(2,1)} %add_convert_fusion.2), channel_id=1, source_target_pairs={{0,2},{1,3},{2,0},{3,1},{4,6},{5,7},{6,4},{7,5},{8,10},{9,11},{10,... | collective-permute-start | bytes 3932168 | tf_op jit(solution)/shard_map/ppermute | solution.py:393
  376.7 41.4 %collective-permute-start.34 = (bf16[1024,256]{1,0:T(8,128)(2,1)}, bf16[1024,256]{1,0:T(8,128)(2,1)S(1)}, u32[]{:S(2)}, u32[]{:S(2)}) collective-permute-start(bf16[1024,256]{1,0:T(8,128)(2,1)} %add_convert_fusion.5), channel_id=1, source_target_pairs={{0,2},{1,3},{2,0},{3,1},{4,6},{5,7},{6,4},{7,5},{8,10},{9,11},{10,... | collective-permute-start | bytes 1572872 | tf_op jit(solution)/shard_map/ppermute | solution.py:393
  442.1 53.2 %collective-permute-start.39 = (bf16[4,128,640]{2,1,0:T(8,128)(2,1)}, bf16[4,128,640]{2,1,0:T(8,128)(2,1)}, u32[]{:S(2)}, u32[]{:S(2)}) collective-permute-start(bf16[4,128,640]{2,1,0:T(8,128)(2,1)} %bitcast.32), channel_id=1, source_target_pairs={{0,4},{4,0},{8,12},{12,8},{16,20},{20,16},{24,28},{28,24},{1,5},{5... | collective-permute-start | bytes 1966088 | tf_op jit(solution)/shard_map/ppermute | solution.py:393
  492.9 17.7 %collective-permute-start.36 = (bf16[640,1024]{1,0:T(8,128)(2,1)}, bf16[640,1024]{1,0:T(8,128)(2,1)S(1)}, u32[]{:S(2)}, u32[]{:S(2)}) collective-permute-start(bf16[640,1024]{1,0:T(8,128)(2,1)} %get-tuple-element.106), channel_id=1, source_target_pairs={{0,1},{1,0},{2,3},{3,2},{4,5},{5,4},{6,7},{7,6},{8,9},{9,8},{10,11... | collective-permute-start | bytes 3932168 | tf_op jit(solution)/shard_map/ppermute | solution.py:393
  496.7 13.6 %collective-permute-start.47 = (bf16[128,1536]{1,0:T(8,128)(2,1)S(1)}, bf16[128,1536]{1,0:T(8,128)(2,1)S(1)}, u32[]{:S(2)}, u32[]{:S(2)}) collective-permute-start(bf16[128,1536]{1,0:T(8,128)(2,1)S(1)} %copy-done.32), channel_id=1, source_target_pairs={{0,2},{1,3},{2,0},{3,1},{4,6},{5,7},{6,4},{7,5},{8,10},{9,11},{10,... | collective-permute-start | bytes 1179656 | tf_op jit(solution)/shard_map/ppermute | solution.py:393
  497.2 15.2 %collective-permute-start.46 = (bf16[128,1536]{1,0:T(8,128)(2,1)S(1)}, bf16[128,1536]{1,0:T(8,128)(2,1)}, u32[]{:S(2)}, u32[]{:S(2)}) collective-permute-start(bf16[128,1536]{1,0:T(8,128)(2,1)S(1)} %copy-done.32), channel_id=1, source_target_pairs={{0,1},{1,0},{2,3},{3,2},{4,5},{5,4},{6,7},{7,6},{8,9},{9,8},{10,11... | collective-permute-start | bytes 1179656 | tf_op jit(solution)/shard_map/ppermute | solution.py:393
  503.9 53.1 %collective-permute-start.38 = (bf16[640,1024]{1,0:T(8,128)(2,1)}, bf16[640,1024]{1,0:T(8,128)(2,1)}, u32[]{:S(2)}, u32[]{:S(2)}) collective-permute-start(bf16[640,1024]{1,0:T(8,128)(2,1)} %get-tuple-element.109), channel_id=1, source_target_pairs={{0,1},{1,0},{2,3},{3,2},{4,5},{5,4},{6,7},{7,6},{8,9},{9,8},{10,11... | collective-permute-start | bytes 3932168 | tf_op jit(solution)/shard_map/ppermute | solution.py:393
  512.3 10.7 %collective-permute-start.40 = (bf16[4,128,384]{2,1,0:T(8,128)(2,1)S(1)}, bf16[4,128,384]{2,1,0:T(8,128)(2,1)}, u32[]{:S(2)}, u32[]{:S(2)}) collective-permute-start(bf16[4,128,384]{2,1,0:T(8,128)(2,1)S(1)} %dynamic-slice_bitcast_fusion.4), channel_id=1, source_target_pairs={{0,4},{4,0},{8,12},{12,8},{16,20},{20,16},{24,28},{28,24},{1,5},{5... | collective-permute-start | bytes 1179656 | tf_op jit(solution)/shard_map/ppermute | solution.py:393
  526.1 12.4 %collective-permute-start.41 = (bf16[2,128,1024]{2,1,0:T(8,128)(2,1)}, bf16[2,128,1024]{2,1,0:T(8,128)(2,1)}, u32[]{:S(2)}, u32[]{:S(2)}) collective-permute-start(bf16[2,128,1024]{2,1,0:T(8,128)(2,1)} %fusion.34), channel_id=1, source_target_pairs={{0,8},{4,12},{8,0},{12,4},{16,24},{20,28},{24,16},{28,20},{1,9},{5... | collective-permute-start | bytes 1572872 | tf_op jit(solution)/shard_map/ppermute | solution.py:393
  526.2 31.8 %collective-permute-start.37 = (bf16[640,1024]{1,0:T(8,128)(2,1)}, bf16[640,1024]{1,0:T(8,128)(2,1)}, u32[]{:S(2)}, u32[]{:S(2)}) collective-permute-start(bf16[640,1024]{1,0:T(8,128)(2,1)} %add_convert_fusion), channel_id=1, source_target_pairs={{0,2},{1,3},{2,0},{3,1},{4,6},{5,7},{6,4},{7,5},{8,10},{9,11},{10,... | collective-permute-start | bytes 3932168 | tf_op jit(solution)/shard_map/ppermute | solution.py:393
  527.0 9.9 %collective-permute-start.49 = (bf16[96,1024]{1,0:T(8,128)(2,1)S(1)}, bf16[96,1024]{1,0:T(8,128)(2,1)}, u32[]{:S(2)}, u32[]{:S(2)}) collective-permute-start(bf16[96,1024]{1,0:T(8,128)(2,1)S(1)} %copy-done.33), channel_id=1, source_target_pairs={{0,1},{1,0},{2,3},{3,2},{4,5},{5,4},{6,7},{7,6},{8,9},{9,8},{10,11... | collective-permute-start | bytes 589832 | tf_op jit(solution)/shard_map/ppermute | solution.py:393
  529.8 7.1 %collective-permute-start.51 = (bf16[96,1024]{1,0:T(8,128)(2,1)S(1)}, bf16[96,1024]{1,0:T(8,128)(2,1)}, u32[]{:S(2)}, u32[]{:S(2)}) collective-permute-start(bf16[96,1024]{1,0:T(8,128)(2,1)S(1)} %collective-permute-done.50), channel_id=1, source_target_pairs={{0,1},{1,0},{2,3},{3,2},{4,5},{5,4},{6,7},{7,6},{8,9},{9,8},{10,11... | collective-permute-start | bytes 589832 | tf_op jit(solution)/shard_map/ppermute | solution.py:393
  539.8 15.6 %collective-permute-start.42 = (bf16[1,128,1024]{2,1,0:T(8,128)(2,1)S(1)}, bf16[1,128,1024]{2,1,0:T(8,128)(2,1)S(1)}, u32[]{:S(2)}, u32[]{:S(2)}) collective-permute-start(bf16[1,128,1024]{2,1,0:T(8,128)(2,1)S(1)} %constant_dynamic-slice_fusion.4), channel_id=1, source_target_pairs={{0,16},{4,20},{8,24},{12,28},{16,0},{20,4},{24,8},{28,12},{1,17},{... | collective-permute-start | bytes 786440 | tf_op jit(solution)/shard_map/ppermute | solution.py:393
  555.4 8.5 %collective-permute-start.44 = (bf16[128,1024]{1,0:T(8,128)(2,1)S(1)}, bf16[128,1024]{1,0:T(8,128)(2,1)S(1)}, u32[]{:S(2)}, u32[]{:S(2)}) collective-permute-start(bf16[128,1024]{1,0:T(8,128)(2,1)S(1)} %bitcast.175), channel_id=1, source_target_pairs={{0,2},{1,3},{2,0},{3,1},{4,6},{5,7},{6,4},{7,5},{8,10},{9,11},{10,... | collective-permute-start | bytes 786440 | tf_op jit(solution)/shard_map/ppermute | solution.py:393
  556.2 12.8 %collective-permute-start.43 = (bf16[128,1024]{1,0:T(8,128)(2,1)S(1)}, bf16[128,1024]{1,0:T(8,128)(2,1)S(1)}, u32[]{:S(2)}, u32[]{:S(2)}) collective-permute-start(bf16[128,1024]{1,0:T(8,128)(2,1)S(1)} %bitcast.176), channel_id=1, source_target_pairs={{0,1},{1,0},{2,3},{3,2},{4,5},{5,4},{6,7},{7,6},{8,9},{9,8},{10,11... | collective-permute-start | bytes 786440 | tf_op jit(solution)/shard_map/ppermute | solution.py:393
  (53 other events, 315.3 us)
Sparse Core Ops, SparseCore 0:
  13.0 113.2 all-gather.1
  342.4 75.5 reduce-scatter.2
  421.4 65.2 reduce-scatter.4

commit v3 on v2

--- a/solution.py
+++ b/solution.py
@@ -94,13 +94,27 @@
     ]
 
 
-def qkv_body(count, steps, *refs):
+def bit_reversed(count):
+    order = [0]
+    while len(order) < count:
+        order = [2 * at for at in order] + [2 * at + 1 for at in order]
+    return order
+
+
+def reorder(values, blocks):
+    size = values.shape[1] // blocks
+    return jnp.concatenate(
+        [values[:, at * size : (at + 1) * size] for at in bit_reversed(blocks)], 1
+    )
+
+
+def qkv_body(blocks, count, steps, *refs):
     pieces, (w_ref, cos_ref, sin_ref) = refs[:count], refs[count : count + 3]
     q_ref, k_ref, v_ref, x_ref, scratch = refs[-5:]
     width = q_ref.shape[1]
-    x = take_piece(pieces, steps, scratch)
+    x = reorder(take_piece(pieces, steps, scratch), blocks)
     x_ref[...] = x
-    packed = dot_nn(x, w_ref[...])
+    packed = dot_nn(x, w_ref[:, : 3 * q_ref.shape[1]])
     cosine = cos_ref[...]
     sine = sin_ref[...]
     lanes = cosine.shape[1]
@@ -114,10 +128,10 @@
             ref[:, here] = part.astype(BF16)
 
 
-def qkv_heads(pieces, weights, cosine, sine, before):
+def qkv_heads(pieces, weights, cosine, sine, blocks, before):
     count = len(pieces)
     rows, depth = pieces[0].shape
-    width = weights.shape[1] // 3
+    width = weights.shape[1] // 4
     step = block_rows(rows, 320)
     steps = rows // step
     length, table = cosine.shape
@@ -125,10 +139,10 @@
     by_row = lambda columns: pl.BlockSpec((step, columns), lambda i: (i + first, 0))
     total = count * rows
     return pl.pallas_call(
-        functools.partial(qkv_body, count, steps),
+        functools.partial(qkv_body, blocks, count, steps),
         grid=(count * steps,),
         in_specs=piece_specs(count, steps, step, depth)
-        + [pl.BlockSpec((depth, 3 * width), lambda i: (0, 0)), by_row(table), by_row(table)]
+        + [pl.BlockSpec(weights.shape, lambda i: (0, 0)), by_row(table), by_row(table)]
         + [pl.BlockSpec(memory_space=pl.ANY)] * len(before),
         out_specs=[by_row(width)] * 3 + [by_row(depth)],
         out_shape=[jax.ShapeDtypeStruct((length, width), BF16)] * 3
@@ -265,14 +279,31 @@
     )(queries, keys, values, grads, out, lse, cosine, sine)
 
 
-def mlp_body(count, steps, *refs):
+def mlp_body(count, steps, blocks, units, *refs):
     x_pieces, c_pieces = refs[:count], refs[count : 2 * count]
-    wi_ref, wo_ref = refs[2 * count : 2 * count + 2]
-    x_scratch, c_scratch = refs[-2:]
-    results = refs[-2 - 4 - 2 * count : -2]
+    weights_ref = refs[2 * count]
+    x_scratch, c_scratch, wo_ref = refs[-3:]
+    results = refs[-3 - 4 - 2 * count : -3]
+    wi_ref = weights_ref.at[:, : 2 * units]
+    depth = wo_ref.shape[1]
+
+    @pl.when(pl.program_id(0) == 0)
+    def _():
+        shard, share = depth // blocks, units // blocks
+        rows = math.gcd(share, shard)
+        wide = depth * rows // shard
+        for block in range(blocks):
+            for tall in range(share // rows):
+                for at in range(shard // rows):
+                    wo_ref[
+                        pl.ds(block * share + tall * rows, rows), at * wide : (at + 1) * wide
+                    ] = weights_ref[
+                        pl.ds(block * shard + at * rows, rows),
+                        2 * units + tall * wide : 2 * units + (tall + 1) * wide,
+                    ]
+
     hidden_ref, gate_up_ref, x_ref, c_ref = results[:4]
     back_refs, out_refs = results[4 : 4 + count], results[4 + count :]
-    units = wo_ref.shape[0]
     x = take_piece(x_pieces, steps, x_scratch)
     cotangent = take_piece(c_pieces, steps, c_scratch)
     x_ref[...] = x
@@ -300,10 +331,20 @@
             out_refs[at][...] = out
 
 
-def mlp(x_pieces, c_pieces, w_in, w_out, length, before):
+def fold_rows(values, shard):
+    share, depth = values.shape
+    rows = math.gcd(share, shard)
+    tall, wide = share // rows, shard // rows
+    return (
+        values.reshape(tall, rows, wide, depth // wide)
+        .transpose(2, 1, 0, 3)
+        .reshape(shard, tall * depth // wide)
+    )
+
+
+def mlp(x_pieces, c_pieces, weights, units, blocks, length, before):
     count = len(x_pieces)
     rows, depth = x_pieces[0].shape
-    units = w_out.shape[0]
     step = block_rows(rows, 320)
     steps = rows // step
     total = count * rows
@@ -312,11 +353,11 @@
     whole = lambda shape: pl.BlockSpec(shape, lambda i: (0, 0))
     pieces = piece_specs(count, steps, step, depth)
     results = pl.pallas_call(
-        functools.partial(mlp_body, count, steps),
+        functools.partial(mlp_body, count, steps, blocks, units),
         grid=(count * steps,),
         in_specs=pieces
         + pieces
-        + [whole((depth, 2 * units)), whole(w_out.shape)]
+        + [whole(weights.shape)]
         + [pl.BlockSpec(memory_space=pl.ANY)] * len(before),
         out_specs=[by_row(units), by_row(2 * units), by_row(depth), by_row(depth)]
         + pieces
@@ -326,8 +367,8 @@
             for columns in (units, 2 * units, depth, depth)
         ]
         + [jax.ShapeDtypeStruct((rows, depth), BF16)] * (2 * count),
-        scratch_shapes=[pltpu.VMEM((step, depth), BF16)] * 2,
-        input_output_aliases={2 * count + 2 + at: at for at in range(len(before))},
+        scratch_shapes=[pltpu.VMEM((step, depth), BF16)] * 2 + [pltpu.VMEM((units, depth), BF16)],
+        input_output_aliases={2 * count + 1 + at: at for at in range(len(before))},
         compiler_params=pltpu.CompilerParams(vmem_limit_bytes=VMEM_BYTES),
         cost_estimate=pl.CostEstimate(
             flops=12 * total * depth * units,
@@ -335,14 +376,15 @@
             transcendentals=2 * total * units,
         ),
         name="mlp",
-    )(*x_pieces, *c_pieces, w_in, w_out, *before)
+    )(*x_pieces, *c_pieces, weights, *before)
     return results[:4], results[4 : 4 + count], results[4 + count :]
 
 
-def token_grad_body(groups, count, steps, *refs):
+def token_grad_body(blocks, groups, count, steps, *refs):
     packed = jnp.concatenate([ref[...] for ref in refs[:groups]], 1)
     results = refs[groups + 1 :]
-    grad = dot_nt(packed, refs[groups][...]).astype(BF16)
+    weights = refs[groups][:, : packed.shape[1]]
+    grad = reorder(dot_nt(packed, weights).astype(BF16), blocks)
     for at in range(count):
 
         @pl.when(pl.program_id(0) // steps == at)
@@ -350,19 +392,20 @@
             results[at][...] = grad
 
 
-def token_grad(packed, weights, count, positions, first):
+def token_grad(packed, weights, blocks, count, positions, first):
     groups = len(packed)
-    depth, columns = weights.shape
+    depth = weights.shape[0]
+    columns = groups * packed[0].shape[1]
     step = block_rows(positions, 320)
     steps = positions // step
     total = count * positions
     return pl.pallas_call(
-        functools.partial(token_grad_body, groups, count, steps),
+        functools.partial(token_grad_body, blocks, groups, count, steps),
         grid=(count * steps,),
         in_specs=[
             pl.BlockSpec((step, columns // groups), lambda i: (i + first * steps, 0))
         ] * groups
-        + [pl.BlockSpec((depth, columns), lambda i: (0, 0))],
+        + [pl.BlockSpec(weights.shape, lambda i: (0, 0))],
         out_specs=piece_specs(count, steps, step, depth),
         out_shape=[jax.ShapeDtypeStruct((positions, depth), BF16)] * count,
         compiler_params=pltpu.CompilerParams(vmem_limit_bytes=VMEM_BYTES),
@@ -428,29 +471,23 @@
         ]
 
     def gather_fsdp(values):
-        rows = values.shape[0]
-        gathered = values
-        at = 0
         bit = fsdp_size // 2
         while bit:
-            other = swap(gathered, "fsdp", fsdp_size, bit)
+            other = swap(values, "fsdp", fsdp_size, bit)
             high = (row & bit) != 0
-            gathered = jnp.stack(
-                [jnp.where(high, other, gathered), jnp.where(high, gathered, other)], at
+            values = jnp.concatenate(
+                [jnp.where(high, other, values), jnp.where(high, values, other)], 0
             )
-            at += 1
             bit //= 2
-        return gathered.reshape(fsdp_size * rows, values.shape[1])
+        return values
 
     def halve_fsdp(values, bit):
-        rows = shard
-        blocks = values.shape[0] // rows
-        left = values.reshape(blocks // 2, 2, rows, values.shape[1])
-        mine = jnp.where((row & bit) != 0, 1, 0)
-        kept = lax.dynamic_index_in_dim(left, mine, 1, keepdims=False)
-        sent = lax.dynamic_index_in_dim(left, 1 - mine, 1, keepdims=False)
+        size = values.shape[0] // 2
+        mine = jnp.where((row & bit) != 0, size, 0)
+        kept = lax.dynamic_slice(values, (mine, 0), (size, values.shape[1]))
+        sent = lax.dynamic_slice(values, (size - mine, 0), (size, values.shape[1]))
         total = kept.astype(F32) + swap(sent, "fsdp", fsdp_size, bit).astype(F32)
-        return total.astype(BF16).reshape(blocks // 2 * rows, values.shape[1])
+        return total.astype(BF16)
 
     def reduce_fsdp(values):
         return lax.psum_scatter(values, "fsdp", scatter_dimension=0, tiled=True)
@@ -469,7 +506,9 @@
         1,
     )
     qkv_slice = (qkv_slice.astype(F32) * own_gain_attn).astype(BF16)
-    qkv_full = gather_fsdp(qkv_slice)
+    attn_out_slice = lax.dynamic_slice(w_attn_out, (0, me * local_width), (shard, local_width))
+    attn_weights = gather_fsdp(jnp.concatenate([qkv_slice, attn_out_slice], 1))
+    packed_width = 3 * local_width
 
     tokens = activations.reshape(positions, width).astype(F32)
     xhat, inverse = centred_stats(tokens)
@@ -479,13 +518,11 @@
     far_x_pieces = spread(far_x)
     own_cotangent = cotangent.reshape(positions, width)
     near_c_pieces = spread(own_cotangent)
-    far_c_pieces = spread(swap_seq(after((own_cotangent, far_x))[0], half))
 
     unit_share = -(-ff_shard // seq_size)
     unit_share = -(-unit_share // ROW_TILE) * ROW_TILE
     padding = unit_share * seq_size - ff_shard
     units = fsdp_size * unit_share
-    attn_out_slice = lax.dynamic_slice(w_attn_out, (0, me * local_width), (shard, local_width))
     mlp_out_slice = lax.dynamic_slice(
         jnp.pad(w_mlp_out, ((0, padding), (0, 0))), (me * unit_share, 0), (unit_share, width)
     )
@@ -496,22 +533,18 @@
         in_slice, (0, 0, me * unit_share), (shard, 2 * fsdp_size, unit_share)
     ).reshape(shard, 2 * units)
     in_slice = (in_slice.astype(F32) * own_gain_mlp).astype(BF16)
-    rows = math.gcd(unit_share, shard)
-    tall, wide = unit_share // rows, shard // rows
-    mlp_out_slice = (
-        mlp_out_slice.reshape(tall, rows, wide, width // wide)
-        .transpose(2, 1, 0, 3)
-        .reshape(shard, tall * width // wide)
-    )
-    later = lax.all_gather(
-        jnp.concatenate([in_slice, mlp_out_slice, attn_out_slice], 1), "fsdp", axis=0, tiled=True
-    )
-    mlp_out_full = (
-        later[:, 2 * units : 2 * units + tall * width // wide]
-        .reshape(fsdp_size, wide, rows, tall, width // wide)
-        .transpose(0, 3, 2, 1, 4)
-        .reshape(units, width)
-    )
+    sections = jnp.concatenate(
+        [
+            attn_weights[block * shard : (block + 1) * shard, packed_width:]
+            for block in bit_reversed(fsdp_size)
+        ],
+        0,
+    )
+    mlp_slice = jnp.concatenate([in_slice, fold_rows(mlp_out_slice, shard)], 1)
+    mlp_weights = lax.all_gather(after((mlp_slice, attn_weights))[0], "fsdp", axis=0, tiled=True)
+    far_sections = swap_seq(after((sections, far_x))[0], half)
+    far_c_pieces = spread(swap_seq(after((own_cotangent, far_sections))[0], half))
+
     lane = lax.broadcasted_iota(jnp.int32, (length, lanes), 1)
     at = lax.broadcasted_iota(jnp.int32, (length, lanes), 0)
     place = ((at // positions) ^ me) * positions + at % positions
@@ -520,19 +553,20 @@
     cosine = jnp.cos(angles)
     sine = jnp.sin(angles) * jnp.where(lane % HEAD < HALF, -1.0, 1.0)
 
-    begun = qkv_heads(near_x_pieces, qkv_full, cosine, sine, [])
-    queries, keys, values, x_all = qkv_heads(far_x_pieces, qkv_full, cosine, sine, begun)
+    begun = qkv_heads(near_x_pieces, attn_weights, cosine, sine, fsdp_size, [])
+    queries, keys, values, x_all = qkv_heads(
+        far_x_pieces, attn_weights, cosine, sine, fsdp_size, begun
+    )
 
     def row_pieces(array):
         return [array[k * positions : (k + 1) * positions] for k in range(seq_size)]
 
-    heads = [attend(queries, keys, values, 0)]
+    heads = [attend(after((queries, far_sections))[0], keys, values, 0)]
     group_pieces = [exchange_seq(row_pieces(heads[0][0]))]
-    sections = gather_seq(after((later, heads[0][0]))[0][:, -local_width:])
-    attn_out_full = jnp.concatenate(by_member(sections), 1)
     for group in range(1, groups):
-        heads.append(attend(after((queries, later))[0], keys, values, group))
+        heads.append(attend(after((queries, far_c_pieces[0], heads[0]))[0], keys, values, group))
         group_pieces.append(exchange_seq(row_pieces(heads[group][0])))
+    attn_out_full = jnp.concatenate(by_member(spread(sections) + spread(far_sections)), 1)
     attended_pieces = [jnp.concatenate(pieces, 1) for pieces in zip(*group_pieces)]
     attn_out_ordered = jnp.concatenate(
         [
@@ -547,12 +581,13 @@
     mixed = tokens + dot_nn(attended, attn_out_ordered)
     xhat_mlp, inverse_mlp = centred_stats(mixed)
     own_x_mlp = xhat_mlp.astype(BF16)
-    far_x_mlp_pieces = spread(swap_seq(own_x_mlp, half))
+    far_x_mlp = swap_seq(own_x_mlp, half)
     begun, near_back, near_out = mlp(
-        spread(own_x_mlp), near_c_pieces, later, mlp_out_full, length, []
-    )
+        spread(own_x_mlp), near_c_pieces, mlp_weights, units, fsdp_size, length, []
+    )
+    far_x_mlp, begun = after((far_x_mlp, begun))
     (hidden, gate_up_grad, x_mlp_all, cotangent_all), far_back, far_out = mlp(
-        far_x_mlp_pieces, far_c_pieces, later, mlp_out_full, length, begun
+        spread(far_x_mlp), far_c_pieces, mlp_weights, units, fsdp_size, length, begun
     )
     back_far = far_sum(far_back)
     back_near = fold(near_back)
@@ -570,7 +605,8 @@
         columns = [k * local_width + group * lanes for k in range(seq_size)]
         pieces = [attended_grad[:, start : start + lanes] for start in columns]
         grads.append(jnp.concatenate(exchange_seq(pieces), 0))
-    grad_attn_out = dot_tn(jnp.concatenate(by_member(attended_pieces), 1), mixed_low).astype(BF16)
+    attended_natural = jnp.concatenate(by_member(attended_pieces), 1)
+    grad_attn_out = dot_tn(reorder(attended_natural, fsdp_size), mixed_low).astype(BF16)
     grads[0], grad_attn_out = after((grads[0], grad_attn_out))
     column_pieces = [
         lax.dynamic_slice(grad_attn_out, (0, (me ^ k) * local_width), (width, local_width))
@@ -604,9 +640,9 @@
         )
         packed.append(back_of(group))
 
-    far_grads = token_grad(packed, qkv_full, half, positions, half)
+    far_grads = token_grad(packed, attn_weights, fsdp_size, half, positions, half)
     far_grads = fold(far_grads).astype(BF16)
-    near_grads = token_grad(packed, qkv_full, half, positions, 0)
+    near_grads = token_grad(packed, attn_weights, fsdp_size, half, positions, 0)
     if groups > 1:
         last_grads = [dot_tn(x_all, section).astype(BF16) for section in packed[1:]]
         last_grads, far_grads = after((last_grads, far_grads))

time: 585 us -> 494 us (0.84)
  waiting for transfers between devices: 158 us -> 101 us
  local copies, waits for them, and re-layouts: 60.7 us -> 25.6 us
    ppermute x52, waiting for transfers between devices: 158 us -> 101 us  [swap(): return lax.ppermute(values, axis, [(i, i ^ offset) for i in range(size)])]
    unnamed x131 -> x154, local copies, waits for them, and re-layouts: 24.6 us -> 13.7 us
    reshape x3 -> x1, local copies, waits for them, and re-layouts: 10.3 us -> 0.13 us  [fold_rows(): values.reshape(tall, rows, wide, depth // wide).transpose(2, 1, 0, 3)]
  transfers between devices with their start and end apart: 55 -> 55, of which waited for: 21 -> 21; matrix products, arithmetic and copies ran while one was open for 24% -> 23% of each run, Pallas kernels for 30% -> 35%
where the time goes in v3:
time: 494 us; the launch traced here: 488 us
  Pallas kernels  195 us (39%)
  waiting for transfers between devices  101 us (20%)
  other arithmetic  62.6 us (13%)
  starting transfers between devices  50 us (10%)
  matrix products  39.2 us (8%)
  local copies, waits for them, and re-layouts  25.6 us (5%)
  between operations  15.3 us (3%)
    ppermute x52, waiting for transfers between devices, swap(): return lax.ppermute(values, axis, [(i, i ^ offset) for i in range(size)])  101 us
    pallas_call x2, Pallas kernels, attend_back(): pl.pallas_call(attend_back_body, grid=(rows // step,), in_specs=[q_spec,...  75 us
    ppermute x52, starting transfers between devices, swap(): return lax.ppermute(values, axis, [(i, i ^ offset) for i in range(size)])  49.6 us
    pallas_call x2, Pallas kernels, attend(): pl.pallas_call(attend_body, grid=(rows // step,), in_specs=[q_spec, k_spe...  47.6 us
    pallas_call x2, Pallas kernels, mlp(): pl.pallas_call(functools.partial(mlp_body, count, steps, blocks, units),...  43.8 us
    dot_general x5, matrix products, dot_tn(): lax.dot_general(a, b, (((0,), (0,)), ((), ())), preferred_element_type=F32)  36 us
    pallas_call x2, Pallas kernels, qkv_heads(): pl.pallas_call(functools.partial(qkv_body, blocks, count, steps), grid=(c...  14.6 us
    pallas_call x2, Pallas kernels, token_grad(): pl.pallas_call(functools.partial(token_grad_body, blocks, groups, count,...  13.8 us
  transfers between devices with their start and end apart: 55, of which 21 were waited for; matrix products, arithmetic and copies ran while one was open for 23% of the time, Pallas kernels for 35%

profile of v3, /device:TPU:1, one launch (start us, length us, event | category | flops | bytes accessed | tf_op | source)
XLA Modules:
  0.0 488.2 jit_solution(14951048081507485215)
XLA Ops:
  10.9 2.0 collective-permute-start
  18.7 2.4 collective-permute-start.2
  23.5 9.7 %collective-permute-done.2 = bf16[128,1024]{1,0:T(8,128)(2,1)} collective-permute-done((bf16[128,1024]{1,0:T(8,128)(2,1)S(1)}, bf16[128,1024]{1,0:T(8,128)(2,1)}, u32[]{:S(2)}, u32[]{:S(2)}) %collective-permute-start.2) | collective-permute-done | bytes 262176 | tf_op jit(solution)/shard_map/ppermute | solution.py:436
  35.6 11.5 %collective-permute-done.3 = bf16[256,1024]{1,0:T(8,128)(2,1)S(1)} collective-permute-done((bf16[256,1024]{1,0:T(8,128)(2,1)S(1)}, bf16[256,1024]{1,0:T(8,128)(2,1)S(1)}, u32[]{:S(2)}, u32[]{:S(2)}) %collective-permute-start.3) | collective-permute-done | bytes 524320 | tf_op jit(solution)/shard_map/ppermute | solution.py:436
  50.6 2.0 collective-permute-start.1
  52.6 18.9 %collective-permute-done.4 = bf16[512,1024]{1,0:T(8,128)(2,1)S(1)} collective-permute-done((bf16[512,1024]{1,0:T(8,128)(2,1)}, bf16[512,1024]{1,0:T(8,128)(2,1)S(1)}, u32[]{:S(2)}, u32[]{:S(2)}) %collective-permute-start.4) | collective-permute-done | bytes 1048608 | tf_op jit(solution)/shard_map/ppermute | solution.py:436
  75.0 7.4 %select_multiply_fusion = (f32[2560,128]{1,0:T(8,128)}, f32[2560,128]{1,0:T(8,128)}) fusion(s32[128]{0:T(128)S(1)} %get-tuple-element.208, s32[128]{0:T(128)S(1)} %get-tuple-element.210, s32[128]{0:T(128)S(1)} %get-tuple-element.209, s32[128]{0:T(128)S(1)} %get-tuple-element.211, s32[2560]{0:T(1024)S(1)} %get-tuple-element.205, ...), kind=kLoop, calls=%fused_computation.55 | loop fusion | flops 4587520 | bytes 2669828 | tf_op jit(solution)/shard_map/mul | solution.py:554
  82.4 2.7 collective-permute-start.14
  85.1 7.4 %qkv_rope.2 = (bf16[2560,256]{1,0:T(8,128)(2,1)}, bf16[2560,256]{1,0:T(8,128)(2,1)}, bf16[2560,256]{1,0:T(8,128)(2,1)}, bf16[2560,1024]{1,0:T(8,128)(2,1)}) custom-call(bf16[640,1024]{1,0:T(8,128)(2,1)} %fusion.6.refs_0_, bf16[640,1024]{1,0:T(8,128)(2,1)} %collective-permute-done.5.refs_1_, bf16[1024,1024]{1,0:T(8,128)(2,1)} %pad_maximum_fusion.refs_2_, ...), custom_call_target="tpu_custom_call" | custom-call | flops 2013265920 | bytes 8781824 | tf_op jit(solution)/shard_map/qkv_rope/pallas_call | solution.py:141
  94.6 7.2 %qkv_rope.3 = (bf16[2560,256]{1,0:T(8,128)(2,1)}, bf16[2560,256]{1,0:T(8,128)(2,1)}, bf16[2560,256]{1,0:T(8,128)(2,1)}, bf16[2560,1024]{1,0:T(8,128)(2,1)}) custom-call(bf16[640,1024]{1,0:T(8,128)(2,1)} %collective-permute-done.refs_0_, bf16[640,1024]{1,0:T(8,128)(2,1)} %copy-done.19, ...), custom_call_target="tpu_custom_call", output_to_operand_aliasing={{0}: (5, {}), {1}: (6, {}), {2}: (7, {}), {3}: (8, {})} | custom-call | flops 2013265920 | bytes 8781824 | tf_op jit(solution)/shard_map/qkv_rope/pallas_call | solution.py:141
  101.7 23.8 %attend.2 = (bf16[2560,128]{1,0:T(8,128)(2,1)}, f32[128,2560]{1,0:T(8,128)}) custom-call(bf16[2560,256]{1,0:T(8,128)(2,1)} %get-tuple-element.81.q_ref, bf16[2560,256]{1,0:T(8,128)(2,1)} %get-tuple-element.76.k_ref, bf16[2560,256]{1,0:T(8,128)(2,1)} %get-tuple-element.77.v_ref), custom_call_target="tpu_custom_call" | custom-call | flops 13421772800 | bytes 2621440 | tf_op jit(solution)/shard_map/attend/pallas_call | solution.py:189
  125.6 1.9 fusion.36
  132.2 23.8 %attend.3 = (bf16[2560,128]{1,0:T(8,128)(2,1)}, f32[128,2560]{1,0:T(8,128)}) custom-call(bf16[2560,256]{1,0:T(8,128)(2,1)} %get-tuple-element.81.q_ref, bf16[2560,256]{1,0:T(8,128)(2,1)} %get-tuple-element.76.k_ref, bf16[2560,256]{1,0:T(8,128)(2,1)} %get-tuple-element.77.v_ref), custom_call_target="tpu_custom_call" | custom-call | flops 13421772800 | bytes 2621440 | tf_op jit(solution)/shard_map/attend/pallas_call | solution.py:189
  160.6 2.8 collective-permute-done.11
  163.6 4.1 collective-permute-done.13
  175.2 22.0 %mlp.2 = (bf16[2560,768]{1,0:T(8,128)(2,1)}, bf16[2560,1536]{1,0:T(8,128)(2,1)}, bf16[2560,1024]{1,0:T(8,128)(2,1)}, bf16[2560,1024]{1,0:T(8,128)(2,1)}, bf16[64...) custom-call(bf16[640,1024]{1,0:T(8,128)(2,1)} %fusion.14.refs_0_, ...), custom_call_target="tpu_custom_call" | custom-call | flops 12079595520 | bytes 26345472 | tf_op jit(solution)/shard_map/mlp/pallas_call | solution.py:355
  197.2 4.8 collective-permute-done.19.refs_0_
  203.3 3.0 collective-permute-done.20.refs_1_
  206.3 21.8 %mlp.3 = (bf16[2560,768]{1,0:T(8,128)(2,1)}, bf16[2560,1536]{1,0:T(8,128)(2,1)}, bf16[2560,1024]{1,0:T(8,128)(2,1)}, bf16[2560,1024]{1,0:T(8,128)(2,1)}, bf16[64...) custom-call(bf16[640,1024]{1,0:T(8,128)(2,1)} %collective-permute-do, ...), custom_call_target="tpu_custom_call", output_to_operand_aliasing={{0}: (5, {}), {1}: (6, {}), {2}: (7, {}), {3}: (8, {})} | custom-call | flops 12079595520 | bytes 26345472 | tf_op jit(solution)/shard_map/mlp/pallas_call | solution.py:355
  228.5 2.9 collective-permute-done.22
  231.4 2.9 add_convert_fusion.3
  235.2 14.1 %convolution_convert_fusion = bf16[1024,1536]{1,0:T(8,128)(2,1)} fusion(bf16[2560,1024]{1,0:T(8,128)(2,1)} %get-tuple-element.99, bf16[2560,1536]{1,0:T(8,128)(2,1)} %get-tuple-element.100), kind=kOutput, calls=%fused_computation | convolution fusion | flops 8054636544 | bytes 16252928 | tf_op jit(solution)/shard_map/dot_general | solution.py:32
  249.3 9.1 %convolution_convert_fusion.2 = bf16[768,1024]{1,0:T(8,128)(2,1)} fusion(bf16[2560,768]{1,0:T(8,128)(2,1)} %get-tuple-element.97, bf16[2560,1024]{1,0:T(8,128)(2,1)} %get-tuple-element.98), kind=kOutput, calls=%fused_computation.40 | convolution fusion | flops 4027318272 | bytes 10747904 | tf_op jit(solution)/shard_map/dot_general | solution.py:32
  258.4 6.2 %collective-permute-done.23 = bf16[640,1024]{1,0:T(8,128)(2,1)} collective-permute-done((bf16[640,1024]{1,0:T(8,128)(2,1)}, bf16[640,1024]{1,0:T(8,128)(2,1)}, u32[]{:S(2)}, u32[]{:S(2)}) %collective-permute-start.23) | collective-permute-done | bytes 1310752 | tf_op jit(solution)/shard_map/ppermute | solution.py:436
  271.3 2.3 fusion.18
  273.7 3.1 multiply_add_fusion
  283.4 2.0 collective-permute-done.29
  286.5 3.5 collective-permute-done.30
  296.5 2.0 pad_maximum_fusion.16.g_ref
  298.5 2.0 add_convert_fusion.7
  301.9 37.4 %attend_back.2.refs_0_ = bf16[2560,384]{1,0:T(8,128)(2,1)} custom-call(bf16[2560,256]{1,0:T(8,128)(2,1)} %get-tuple-element.81.q_ref, bf16[2560,256]{1,0:T(8,128)(2,1)} %get-tuple-element.76.k_ref, bf16[2560,256]{1,0:T(8,128)(2,1)} %get-tuple-element.77.v_ref, bf16[2560,128]{1,0:T(8,128)(2,1)} %pad_maximum_fusion.17.g_ref, ...), custom_call_target="tpu_custom_call" | custom-call | flops 33554432000 | bytes 6553600 | tf_op jit(solution)/shard_map/attend_back/pallas_call | solution.py:261
  339.3 3.1 collective-permute-done.34
  342.4 2.0 add_convert_fusion.6
  345.7 5.5 %convolution_convert_fusion.5 = bf16[1024,384]{0,1:T(8,128)(2,1)S(1)} fusion(bf16[2560,1024]{1,0:T(8,128)(2,1)} %get-tuple-element.112, bf16[2560,384]{1,0:T(8,128)(2,1)} %attend_back.2.refs_0_), kind=kOutput, calls=%fused_computation.48 | convolution fusion | flops 2013659136 | bytes 7995392 | tf_op jit(solution)/shard_map/dot_general | solution.py:32
  353.9 3.7 add_convert_fusion.1
  357.7 37.7 %attend_back.3.refs_1_ = bf16[2560,384]{1,0:T(8,128)(2,1)} custom-call(bf16[2560,256]{1,0:T(8,128)(2,1)} %get-tuple-element.81.q_ref, bf16[2560,256]{1,0:T(8,128)(2,1)} %get-tuple-element.76.k_ref, bf16[2560,256]{1,0:T(8,128)(2,1)} %get-tuple-element.77.v_ref, bf16[2560,128]{1,0:T(8,128)(2,1)} %pad_maximum_fusion.16.g_ref, ...), custom_call_target="tpu_custom_call" | custom-call | flops 33554432000 | bytes 6553600 | tf_op jit(solution)/shard_map/attend_back/pallas_call | solution.py:261
  395.3 6.8 %token_grad.2 = (bf16[640,1024]{1,0:T(8,128)(2,1)}, bf16[640,1024]{1,0:T(8,128)(2,1)}) custom-call(bf16[2560,384]{1,0:T(8,128)(2,1)} %attend_back.2.refs_0_, bf16[2560,384]{1,0:T(8,128)(2,1)} %attend_back.3.refs_1_, bf16[1024,1024]{1,0:T(8,128)(2,1)} %pad_maximum_fusion.refs_2_), custom_call_target="tpu_custom_call" | custom-call | flops 2013265920 | bytes 6160384 | tf_op jit(solution)/shard_map/token_grad/pallas_call | solution.py:402
  404.9 7.0 %token_grad.3 = (bf16[640,1024]{1,0:T(8,128)(2,1)}, bf16[640,1024]{1,0:T(8,128)(2,1)}) custom-call(bf16[2560,384]{1,0:T(8,128)(2,1)} %attend_back.2.refs_0_, bf16[2560,384]{1,0:T(8,128)(2,1)} %attend_back.3.refs_1_, bf16[1024,1024]{1,0:T(8,128)(2,1)} %pad_maximum_fusion.refs_2_), custom_call_target="tpu_custom_call" | custom-call | flops 2013265920 | bytes 6160384 | tf_op jit(solution)/shard_map/token_grad/pallas_call | solution.py:402
  412.2 5.4 %convolution_convert_fusion.4 = bf16[1024,384]{0,1:T(8,128)(2,1)S(1)} fusion(bf16[2560,1024]{1,0:T(8,128)(2,1)} %get-tuple-element.112, bf16[2560,384]{1,0:T(8,128)(2,1)} %attend_back.3.refs_1_), kind=kOutput, calls=%fused_computation.47 | convolution fusion | flops 2013659136 | bytes 7995392 | tf_op jit(solution)/shard_map/dot_general | solution.py:32
  422.4 8.6 %collective-permute-done.40 = bf16[512,384]{0,1:T(8,128)(2,1)S(1)} collective-permute-done((bf16[512,384]{0,1:T(8,128)(2,1)}, bf16[512,384]{0,1:T(8,128)(2,1)S(1)}, u32[]{:S(2)}, u32[]{:S(2)}) %collective-permute-start.40) | collective-permute-done | bytes 393248 | tf_op jit(solution)/shard_map/ppermute | solution.py:436
  437.8 2.9 collective-permute-start.51
  442.0 2.2 copy.40
  447.6 3.3 collective-permute-start.42
  452.3 10.2 %collective-permute-done.42 = bf16[128,1024]{0,1:T(8,128)(2,1)S(1)} collective-permute-done((bf16[128,1024]{0,1:T(8,128)(2,1)S(1)}, bf16[128,1024]{0,1:T(8,128)(2,1)S(1)}, u32[]{:S(2)}, u32[]{:S(2)}) %collective-permute-start.42) | collective-permute-done | bytes 262176 | tf_op jit(solution)/shard_map/ppermute | solution.py:436
  466.3 3.0 fusion.19
  469.3 2.5 collective-permute-done.44
  473.4 3.5 fusion.16
  478.7 2.0 convert_multiply_fusion.2
  (338 shorter events, 96.8 us)
Async XLA Ops:
  7.2 168.0 %all-gather.2.cloned.1.call-start = ((), (), s32[]{:S(2)}) async-start(), calls=%async_computation.2 | async-start | bytes 5308416 | tf_op jit(solution)/shard_map/all_gather | solution.py:544
  10.9 39.7 %collective-permute-start = (bf16[640,1024]{1,0:T(8,128)(2,1)}, bf16[640,1024]{1,0:T(8,128)(2,1)}, u32[]{:S(2)}, u32[]{:S(2)}) collective-permute-start(bf16[640,1024]{1,0:T(8,128)(2,1)} %fusion.6.refs_0_), channel_id=1, source_target_pairs={{0,2},{1,3},{2,0},{3,1},{4,6},{5,7},{6,4},{7,5},{8,10},{9,11},{10,... | collective-permute-start | bytes 3932168 | tf_op jit(solution)/shard_map/ppermute | solution.py:436
  12.9 72.1 %collective-permute-start.5 = (bf16[640,1024]{1,0:T(8,128)(2,1)}, bf16[640,1024]{1,0:T(8,128)(2,1)}, u32[]{:S(2)}, u32[]{:S(2)}) collective-permute-start(bf16[640,1024]{1,0:T(8,128)(2,1)} %fusion.6.refs_0_), channel_id=1, source_target_pairs={{0,1},{1,0},{2,3},{3,2},{4,5},{5,4},{6,7},{7,6},{8,9},{9,8},{10,11... | collective-permute-start | bytes 3932168 | tf_op jit(solution)/shard_map/ppermute | solution.py:436
  18.7 14.6 %collective-permute-start.2 = (bf16[128,1024]{1,0:T(8,128)(2,1)S(1)}, bf16[128,1024]{1,0:T(8,128)(2,1)}, u32[]{:S(2)}, u32[]{:S(2)}) collective-permute-start(bf16[128,1024]{1,0:T(8,128)(2,1)S(1)} %pad_maximum_fusion.22), channel_id=1, source_target_pairs={{0,16},{4,20},{8,24},{12,28},{16,0},{20,4},{24,8},{28,12},{1,17},{... | collective-permute-start | bytes 786440 | tf_op jit(solution)/shard_map/ppermute | solution.py:436
  21.1 152.4 %collective-permute-start.17 = (bf16[640,1024]{1,0:T(8,128)(2,1)}, bf16[640,1024]{1,0:T(8,128)(2,1)}, u32[]{:S(2)}, u32[]{:S(2)}) collective-permute-start(bf16[640,1024]{1,0:T(8,128)(2,1)} %bitcast.refs_2_), channel_id=1, source_target_pairs={{0,1},{1,0},{2,3},{3,2},{4,5},{5,4},{6,7},{7,6},{8,9},{9,8},{10,11... | collective-permute-start | bytes 3932168 | tf_op jit(solution)/shard_map/ppermute | solution.py:436
  34.4 12.7 %collective-permute-start.3 = (bf16[256,1024]{1,0:T(8,128)(2,1)S(1)}, bf16[256,1024]{1,0:T(8,128)(2,1)S(1)}, u32[]{:S(2)}, u32[]{:S(2)}) collective-permute-start(bf16[256,1024]{1,0:T(8,128)(2,1)S(1)} %pad_maximum_fusion.19), channel_id=1, source_target_pairs={{0,8},{4,12},{8,0},{12,4},{16,24},{20,28},{24,16},{28,20},{1,9},{5... | collective-permute-start | bytes 1572872 | tf_op jit(solution)/shard_map/ppermute | solution.py:436
  48.4 23.2 %collective-permute-start.4 = (bf16[512,1024]{1,0:T(8,128)(2,1)}, bf16[512,1024]{1,0:T(8,128)(2,1)S(1)}, u32[]{:S(2)}, u32[]{:S(2)}) collective-permute-start(bf16[512,1024]{1,0:T(8,128)(2,1)} %pad_maximum_fusion.10), channel_id=1, source_target_pairs={{0,4},{4,0},{8,12},{12,8},{16,20},{20,16},{24,28},{28,24},{1,5},{5... | collective-permute-start | bytes 3145736 | tf_op jit(solution)/shard_map/ppermute | solution.py:436
  50.6 42.9 %collective-permute-start.1 = (bf16[640,1024]{1,0:T(8,128)(2,1)}, bf16[640,1024]{1,0:T(8,128)(2,1)S(1)}, u32[]{:S(2)}, u32[]{:S(2)}) collective-permute-start(bf16[640,1024]{1,0:T(8,128)(2,1)} %collective-permute-done.refs_0_), channel_id=1, source_target_pairs={{0,1},{1,0},{2,3},{3,2},{4,5},{5,4},{6,7},{7,6},{8,9},{9,8},{10,11... | collective-permute-start | bytes 3932168 | tf_op jit(solution)/shard_map/ppermute | solution.py:436
  72.2 20.3 %collective-permute-start.6 = (bf16[1024,256]{1,0:T(8,128)(2,1)S(1)}, bf16[1024,256]{1,0:T(8,128)(2,1)S(1)}, u32[]{:S(2)}, u32[]{:S(2)}) collective-permute-start(bf16[1024,256]{1,0:T(8,128)(2,1)S(1)} %constant_dynamic-update-slice_fusion.6), channel_id=1, source_target_pairs={{0,2},{1,3},{2,0},{3,1},{4,6},{5,7},{6,4},{7,5},{8,10},{9,11},{10,... | collective-permute-start | bytes 1572872 | tf_op jit(solution)/shard_map/ppermute | solution.py:436
  74.7 283.0 %reduce-scatter.3.cloned.1.call-start = ((), (), s32[]{:S(2)}) async-start(), calls=%async_computation.3 | async-start | bytes 3538944 | tf_op jit(solution)/shard_map/reduce_scatter | solution.py:493
  82.4 45.4 %collective-permute-start.14 = (bf16[1024,256]{1,0:T(8,128)(2,1)S(1)}, bf16[1024,256]{1,0:T(8,128)(2,1)S(1)}, u32[]{:S(2)}, u32[]{:S(2)}) collective-permute-start(bf16[1024,256]{1,0:T(8,128)(2,1)S(1)} %constant_dynamic-update-slice_fusion.6), channel_id=1, source_target_pairs={{0,1},{1,0},{2,3},{3,2},{4,5},{5,4},{6,7},{7,6},{8,9},{9,8},{10,11... | collective-permute-start | bytes 1572872 | tf_op jit(solution)/shard_map/ppermute | solution.py:436
  92.5 39.7 %collective-permute-start.7 = (bf16[640,1024]{1,0:T(8,128)(2,1)}, bf16[640,1024]{1,0:T(8,128)(2,1)}, u32[]{:S(2)}, u32[]{:S(2)}) collective-permute-start(bf16[640,1024]{1,0:T(8,128)(2,1)} %bitcast.refs_2_), channel_id=1, source_target_pairs={{0,2},{1,3},{2,0},{3,1},{4,6},{5,7},{6,4},{7,5},{8,10},{9,11},{10,... | collective-permute-start | bytes 3932168 | tf_op jit(solution)/shard_map/ppermute | solution.py:436
  93.3 35.3 %collective-permute-start.15 = (bf16[1024,256]{1,0:T(8,128)(2,1)S(1)}, bf16[1024,256]{1,0:T(8,128)(2,1)S(1)}, u32[]{:S(2)}, u32[]{:S(2)}) collective-permute-start(bf16[1024,256]{1,0:T(8,128)(2,1)S(1)} %collective-permute-done.6), channel_id=1, source_target_pairs={{0,1},{1,0},{2,3},{3,2},{4,5},{5,4},{6,7},{7,6},{8,9},{9,8},{10,11... | collective-permute-start | bytes 1572872 | tf_op jit(solution)/shard_map/ppermute | solution.py:436
  127.5 30.7 %collective-permute-start.8 = (bf16[640,128]{1,0:T(8,128)(2,1)S(1)}, bf16[640,128]{1,0:T(8,128)(2,1)S(1)}, u32[]{:S(2)}, u32[]{:S(2)}) collective-permute-start(bf16[640,128]{1,0:T(8,128)(2,1)S(1)} %get-tuple-element.188), channel_id=1, source_target_pairs={{0,1},{1,0},{2,3},{3,2},{4,5},{5,4},{6,7},{7,6},{8,9},{9,8},{10,11... | collective-permute-start | bytes 491528 | tf_op jit(solution)/shard_map/ppermute | solution.py:436
  127.8 32.8 %collective-permute-start.10 = (bf16[640,128]{1,0:T(8,128)(2,1)S(1)}, bf16[640,128]{1,0:T(8,128)(2,1)S(1)}, u32[]{:S(2)}, u32[]{:S(2)}) collective-permute-start(bf16[640,128]{1,0:T(8,128)(2,1)S(1)} %get-tuple-element.187), channel_id=1, source_target_pairs={{0,2},{1,3},{2,0},{3,1},{4,6},{5,7},{6,4},{7,5},{8,10},{9,11},{10,... | collective-permute-start | bytes 491528 | tf_op jit(solution)/shard_map/ppermute | solution.py:436
  129.4 34.2 %collective-permute-start.12 = (bf16[640,128]{1,0:T(8,128)(2,1)S(1)}, bf16[640,128]{1,0:T(8,128)(2,1)S(1)}, u32[]{:S(2)}, u32[]{:S(2)}) collective-permute-start(bf16[640,128]{1,0:T(8,128)(2,1)S(1)} %get-tuple-element.186), channel_id=1, source_target_pairs={{0,3},{1,2},{2,1},{3,0},{4,7},{5,6},{6,5},{7,4},{8,11},{9,10},{10,... | collective-permute-start | bytes 491528 | tf_op jit(solution)/shard_map/ppermute | solution.py:436
  158.2 5.3 %collective-permute-start.11 = (bf16[640,128]{1,0:T(8,128)(2,1)S(1)}, bf16[640,128]{1,0:T(8,128)(2,1)S(1)}, u32[]{:S(2)}, u32[]{:S(2)}) collective-permute-start(bf16[640,128]{1,0:T(8,128)(2,1)S(1)} %get-tuple-element.192), channel_id=1, source_target_pairs={{0,2},{1,3},{2,0},{3,1},{4,6},{5,7},{6,4},{7,5},{8,10},{9,11},{10,... | collective-permute-start | bytes 491528 | tf_op jit(solution)/shard_map/ppermute | solution.py:436
  159.8 7.9 %collective-permute-start.13 = (bf16[640,128]{1,0:T(8,128)(2,1)S(1)}, bf16[640,128]{1,0:T(8,128)(2,1)S(1)}, u32[]{:S(2)}, u32[]{:S(2)}) collective-permute-start(bf16[640,128]{1,0:T(8,128)(2,1)S(1)} %get-tuple-element.191), channel_id=1, source_target_pairs={{0,3},{1,2},{2,1},{3,0},{4,7},{5,6},{6,5},{7,4},{8,11},{9,10},{10,... | collective-permute-start | bytes 491528 | tf_op jit(solution)/shard_map/ppermute | solution.py:436
  171.8 30.1 %collective-permute-start.19 = (bf16[640,1024]{1,0:T(8,128)(2,1)}, bf16[640,1024]{1,0:T(8,128)(2,1)}, u32[]{:S(2)}, u32[]{:S(2)}) collective-permute-start(bf16[640,1024]{1,0:T(8,128)(2,1)} %fusion.14.refs_0_), channel_id=1, source_target_pairs={{0,2},{1,3},{2,0},{3,1},{4,6},{5,7},{6,4},{7,5},{8,10},{9,11},{10,... | collective-permute-start | bytes 3932168 | tf_op jit(solution)/shard_map/ppermute | solution.py:436
  172.7 30.7 %collective-permute-start.21 = (bf16[640,1024]{1,0:T(8,128)(2,1)}, bf16[640,1024]{1,0:T(8,128)(2,1)}, u32[]{:S(2)}, u32[]{:S(2)}) collective-permute-start(bf16[640,1024]{1,0:T(8,128)(2,1)} %collective-permute-done.7.refs_2_), channel_id=1, source_target_pairs={{0,1},{1,0},{2,3},{3,2},{4,5},{5,4},{6,7},{7,6},{8,9},{9,8},{10,11... | collective-permute-start | bytes 3932168 | tf_op jit(solution)/shard_map/ppermute | solution.py:436
  234.3 30.3 %collective-permute-start.23 = (bf16[640,1024]{1,0:T(8,128)(2,1)}, bf16[640,1024]{1,0:T(8,128)(2,1)}, u32[]{:S(2)}, u32[]{:S(2)}) collective-permute-start(bf16[640,1024]{1,0:T(8,128)(2,1)} %add_convert_fusion.3), channel_id=1, source_target_pairs={{0,2},{1,3},{2,0},{3,1},{4,6},{5,7},{6,4},{7,5},{8,10},{9,11},{10,... | collective-permute-start | bytes 3932168 | tf_op jit(solution)/shard_map/ppermute | solution.py:436
  264.7 167.4 %reduce-scatter.5.cloned.1.call-start = ((), (), s32[]{:S(2)}) async-start(), calls=%async_computation.4 | async-start | bytes 1769472 | tf_op jit(solution)/shard_map/reduce_scatter | solution.py:493
  269.0 84.9 %collective-permute-start.27 = (bf16[640,1024]{1,0:T(8,128)(2,1)}, bf16[640,1024]{1,0:T(8,128)(2,1)}, u32[]{:S(2)}, u32[]{:S(2)}) collective-permute-start(bf16[640,1024]{1,0:T(8,128)(2,1)} %get-tuple-element.103), channel_id=1, source_target_pairs={{0,1},{1,0},{2,3},{3,2},{4,5},{5,4},{6,7},{7,6},{8,9},{9,8},{10,11... | collective-permute-start | bytes 3932168 | tf_op jit(solution)/shard_map/ppermute | solution.py:436
  269.1 23.2 %collective-permute-start.31 = (bf16[640,1024]{1,0:T(8,128)(2,1)S(1)}, bf16[640,1024]{1,0:T(8,128)(2,1)S(1)}, u32[]{:S(2)}, u32[]{:S(2)}) collective-permute-start(bf16[640,1024]{1,0:T(8,128)(2,1)S(1)} %copy-done.48), channel_id=1, source_target_pairs={{0,1},{1,0},{2,3},{3,2},{4,5},{5,4},{6,7},{7,6},{8,9},{9,8},{10,11... | collective-permute-start | bytes 3932168 | tf_op jit(solution)/shard_map/ppermute | solution.py:436
  279.6 5.7 %collective-permute-start.29 = (bf16[640,128]{1,0:T(8,128)(2,1)S(1)}, bf16[640,128]{1,0:T(8,128)(2,1)S(1)}, u32[]{:S(2)}, u32[]{:S(2)}) collective-permute-start(bf16[640,128]{1,0:T(8,128)(2,1)S(1)} %get-tuple-element.166), channel_id=1, source_target_pairs={{0,2},{1,3},{2,0},{3,1},{4,6},{5,7},{6,4},{7,5},{8,10},{9,11},{10,... | collective-permute-start | bytes 491528 | tf_op jit(solution)/shard_map/ppermute | solution.py:436
  280.7 9.3 %collective-permute-start.30 = (bf16[640,128]{1,0:T(8,128)(2,1)S(1)}, bf16[640,128]{1,0:T(8,128)(2,1)S(1)}, u32[]{:S(2)}, u32[]{:S(2)}) collective-permute-start(bf16[640,128]{1,0:T(8,128)(2,1)S(1)} %get-tuple-element.165), channel_id=1, source_target_pairs={{0,3},{1,2},{2,1},{3,0},{4,7},{5,6},{6,5},{7,4},{8,11},{9,10},{10,... | collective-permute-start | bytes 491528 | tf_op jit(solution)/shard_map/ppermute | solution.py:436
  283.3 12.0 %collective-permute-start.24 = (bf16[640,128]{1,0:T(8,128)(2,1)}, bf16[640,128]{1,0:T(8,128)(2,1)}, u32[]{:S(2)}, u32[]{:S(2)}) collective-permute-start(bf16[640,128]{1,0:T(8,128)(2,1)} %get-tuple-element.170), channel_id=1, source_target_pairs={{0,1},{1,0},{2,3},{3,2},{4,5},{5,4},{6,7},{7,6},{8,9},{9,8},{10,11... | collective-permute-start | bytes 491528 | tf_op jit(solution)/shard_map/ppermute | solution.py:436
  285.4 10.0 %collective-permute-start.25 = (bf16[640,128]{1,0:T(8,128)(2,1)}, bf16[640,128]{1,0:T(8,128)(2,1)}, u32[]{:S(2)}, u32[]{:S(2)}) collective-permute-start(bf16[640,128]{1,0:T(8,128)(2,1)} %get-tuple-element.169), channel_id=1, source_target_pairs={{0,2},{1,3},{2,0},{3,1},{4,6},{5,7},{6,4},{7,5},{8,10},{9,11},{10,... | collective-permute-start | bytes 491528 | tf_op jit(solution)/shard_map/ppermute | solution.py:436
  290.0 6.5 %collective-permute-start.26 = (bf16[640,128]{1,0:T(8,128)(2,1)S(1)}, bf16[640,128]{1,0:T(8,128)(2,1)}, u32[]{:S(2)}, u32[]{:S(2)}) collective-permute-start(bf16[640,128]{1,0:T(8,128)(2,1)S(1)} %get-tuple-element.168), channel_id=1, source_target_pairs={{0,3},{1,2},{2,1},{3,0},{4,7},{5,6},{6,5},{7,4},{8,11},{9,10},{10,... | collective-permute-start | bytes 491528 | tf_op jit(solution)/shard_map/ppermute | solution.py:436
  292.3 6.2 %collective-permute-start.32 = (bf16[1024,256]{1,0:T(8,128)(2,1)}, bf16[1024,256]{1,0:T(8,128)(2,1)S(1)}, u32[]{:S(2)}, u32[]{:S(2)}) collective-permute-start(bf16[1024,256]{1,0:T(8,128)(2,1)} %get-tuple-element.143), channel_id=1, source_target_pairs={{0,1},{1,0},{2,3},{3,2},{4,5},{5,4},{6,7},{7,6},{8,9},{9,8},{10,11... | collective-permute-start | bytes 1572872 | tf_op jit(solution)/shard_map/ppermute | solution.py:436
  295.3 47.1 %collective-permute-start.35 = (bf16[1024,256]{1,0:T(8,128)(2,1)}, bf16[1024,256]{1,0:T(8,128)(2,1)S(1)}, u32[]{:S(2)}, u32[]{:S(2)}) collective-permute-start(bf16[1024,256]{1,0:T(8,128)(2,1)} %get-tuple-element.142), channel_id=1, source_target_pairs={{0,1},{1,0},{2,3},{3,2},{4,5},{5,4},{6,7},{7,6},{8,9},{9,8},{10,11... | collective-permute-start | bytes 1572872 | tf_op jit(solution)/shard_map/ppermute | solution.py:436
  300.5 41.9 %collective-permute-start.33 = (bf16[640,1024]{1,0:T(8,128)(2,1)}, bf16[640,1024]{1,0:T(8,128)(2,1)}, u32[]{:S(2)}, u32[]{:S(2)}) collective-permute-start(bf16[640,1024]{1,0:T(8,128)(2,1)} %add_convert_fusion.2), channel_id=1, source_target_pairs={{0,2},{1,3},{2,0},{3,1},{4,6},{5,7},{6,4},{7,5},{8,10},{9,11},{10,... | collective-permute-start | bytes 3932168 | tf_op jit(solution)/shard_map/ppermute | solution.py:436
  301.5 40.9 %collective-permute-start.34 = (bf16[1024,256]{1,0:T(8,128)(2,1)}, bf16[1024,256]{1,0:T(8,128)(2,1)S(1)}, u32[]{:S(2)}, u32[]{:S(2)}) collective-permute-start(bf16[1024,256]{1,0:T(8,128)(2,1)} %add_convert_fusion.7), channel_id=1, source_target_pairs={{0,2},{1,3},{2,0},{3,1},{4,6},{5,7},{6,4},{7,5},{8,10},{9,11},{10,... | collective-permute-start | bytes 1572872 | tf_op jit(solution)/shard_map/ppermute | solution.py:436
  352.4 50.3 %collective-permute-start.39 = (bf16[512,640]{0,1:T(8,128)(2,1)}, bf16[512,640]{0,1:T(8,128)(2,1)}, u32[]{:S(2)}, u32[]{:S(2)}) collective-permute-start(bf16[512,640]{0,1:T(8,128)(2,1)} %fusion.22), channel_id=1, source_target_pairs={{0,4},{4,0},{8,12},{12,8},{16,20},{20,16},{24,28},{28,24},{1,5},{5... | collective-permute-start | bytes 1966088 | tf_op jit(solution)/shard_map/ppermute | solution.py:436
  402.1 15.8 %collective-permute-start.36 = (bf16[640,1024]{1,0:T(8,128)(2,1)}, bf16[640,1024]{1,0:T(8,128)(2,1)S(1)}, u32[]{:S(2)}, u32[]{:S(2)}) collective-permute-start(bf16[640,1024]{1,0:T(8,128)(2,1)} %get-tuple-element.120), channel_id=1, source_target_pairs={{0,1},{1,0},{2,3},{3,2},{4,5},{5,4},{6,7},{7,6},{8,9},{9,8},{10,11... | collective-permute-start | bytes 3932168 | tf_op jit(solution)/shard_map/ppermute | solution.py:436
  404.1 13.6 %collective-permute-start.47 = (bf16[128,1536]{1,0:T(8,128)(2,1)}, bf16[128,1536]{1,0:T(8,128)(2,1)S(1)}, u32[]{:S(2)}, u32[]{:S(2)}) collective-permute-start(bf16[128,1536]{1,0:T(8,128)(2,1)} %reduce-scatter.3.cloned.1.call-done), channel_id=1, source_target_pairs={{0,2},{1,3},{2,0},{3,1},{4,6},{5,7},{6,4},{7,5},{8,10},{9,11},{10,... | collective-permute-start | bytes 1179656 | tf_op jit(solution)/shard_map/ppermute | solution.py:436
  404.6 16.6 %collective-permute-start.46 = (bf16[128,1536]{1,0:T(8,128)(2,1)}, bf16[128,1536]{1,0:T(8,128)(2,1)S(1)}, u32[]{:S(2)}, u32[]{:S(2)}) collective-permute-start(bf16[128,1536]{1,0:T(8,128)(2,1)} %reduce-scatter.3.cloned.1.call-done), channel_id=1, source_target_pairs={{0,1},{1,0},{2,3},{3,2},{4,5},{5,4},{6,7},{7,6},{8,9},{9,8},{10,11... | collective-permute-start | bytes 1179656 | tf_op jit(solution)/shard_map/ppermute | solution.py:436
  411.9 53.3 %collective-permute-start.38 = (bf16[640,1024]{1,0:T(8,128)(2,1)}, bf16[640,1024]{1,0:T(8,128)(2,1)}, u32[]{:S(2)}, u32[]{:S(2)}) collective-permute-start(bf16[640,1024]{1,0:T(8,128)(2,1)} %get-tuple-element.123), channel_id=1, source_target_pairs={{0,1},{1,0},{2,3},{3,2},{4,5},{5,4},{6,7},{7,6},{8,9},{9,8},{10,11... | collective-permute-start | bytes 3932168 | tf_op jit(solution)/shard_map/ppermute | solution.py:436
  420.3 10.6 %collective-permute-start.40 = (bf16[512,384]{0,1:T(8,128)(2,1)}, bf16[512,384]{0,1:T(8,128)(2,1)S(1)}, u32[]{:S(2)}, u32[]{:S(2)}) collective-permute-start(bf16[512,384]{0,1:T(8,128)(2,1)} %constant_dynamic-slice_fusion.9), channel_id=1, source_target_pairs={{0,4},{4,0},{8,12},{12,8},{16,20},{20,16},{24,28},{28,24},{1,5},{5... | collective-permute-start | bytes 1179656 | tf_op jit(solution)/shard_map/ppermute | solution.py:436
  432.1 5.7 %collective-permute-start.50 = (bf16[96,1024]{1,0:T(8,128)(2,1)}, bf16[96,1024]{1,0:T(8,128)(2,1)}, u32[]{:S(2)}, u32[]{:S(2)}) collective-permute-start(bf16[96,1024]{1,0:T(8,128)(2,1)} %reduce-scatter.5.cloned.1.call-done), channel_id=1, source_target_pairs={{0,2},{1,3},{2,0},{3,1},{4,6},{5,7},{6,4},{7,5},{8,10},{9,11},{10,... | collective-permute-start | bytes 589832 | tf_op jit(solution)/shard_map/ppermute | solution.py:436
  434.1 12.4 %collective-permute-start.41 = (bf16[256,1024]{0,1:T(8,128)(2,1)}, bf16[256,1024]{0,1:T(8,128)(2,1)}, u32[]{:S(2)}, u32[]{:S(2)}) collective-permute-start(bf16[256,1024]{0,1:T(8,128)(2,1)} %fusion.25), channel_id=1, source_target_pairs={{0,8},{4,12},{8,0},{12,4},{16,24},{20,28},{24,16},{28,20},{1,9},{5... | collective-permute-start | bytes 1572872 | tf_op jit(solution)/shard_map/ppermute | solution.py:436
  435.4 30.8 %collective-permute-start.37 = (bf16[640,1024]{1,0:T(8,128)(2,1)}, bf16[640,1024]{1,0:T(8,128)(2,1)}, u32[]{:S(2)}, u32[]{:S(2)}) collective-permute-start(bf16[640,1024]{1,0:T(8,128)(2,1)} %add_convert_fusion), channel_id=1, source_target_pairs={{0,2},{1,3},{2,0},{3,1},{4,6},{5,7},{6,4},{7,5},{8,10},{9,11},{10,... | collective-permute-start | bytes 3932168 | tf_op jit(solution)/shard_map/ppermute | solution.py:436
  435.5 8.7 %collective-permute-start.49 = (bf16[96,1024]{1,0:T(8,128)(2,1)S(1)}, bf16[96,1024]{1,0:T(8,128)(2,1)}, u32[]{:S(2)}, u32[]{:S(2)}) collective-permute-start(bf16[96,1024]{1,0:T(8,128)(2,1)S(1)} %copy-done.38), channel_id=1, source_target_pairs={{0,1},{1,0},{2,3},{3,2},{4,5},{5,4},{6,7},{7,6},{8,9},{9,8},{10,11... | collective-permute-start | bytes 589832 | tf_op jit(solution)/shard_map/ppermute | solution.py:436
  437.8 6.4 %collective-permute-start.51 = (bf16[96,1024]{1,0:T(8,128)(2,1)}, bf16[96,1024]{1,0:T(8,128)(2,1)}, u32[]{:S(2)}, u32[]{:S(2)}) collective-permute-start(bf16[96,1024]{1,0:T(8,128)(2,1)} %collective-permute-done.50), channel_id=1, source_target_pairs={{0,1},{1,0},{2,3},{3,2},{4,5},{5,4},{6,7},{7,6},{8,9},{9,8},{10,11... | collective-permute-start | bytes 589832 | tf_op jit(solution)/shard_map/ppermute | solution.py:436
  447.6 14.8 %collective-permute-start.42 = (bf16[128,1024]{0,1:T(8,128)(2,1)S(1)}, bf16[128,1024]{0,1:T(8,128)(2,1)S(1)}, u32[]{:S(2)}, u32[]{:S(2)}) collective-permute-start(bf16[128,1024]{0,1:T(8,128)(2,1)S(1)} %constant_dynamic-slice_fusion.8), channel_id=1, source_target_pairs={{0,16},{4,20},{8,24},{12,28},{16,0},{20,4},{24,8},{28,12},{1,17},{... | collective-permute-start | bytes 786440 | tf_op jit(solution)/shard_map/ppermute | solution.py:436
  462.5 9.2 %collective-permute-start.44 = (bf16[128,1024]{0,1:T(8,128)(2,1)S(1)}, bf16[128,1024]{0,1:T(8,128)(2,1)S(1)}, u32[]{:S(2)}, u32[]{:S(2)}) collective-permute-start(bf16[128,1024]{0,1:T(8,128)(2,1)S(1)} %add_convert_fusion.9), channel_id=1, source_target_pairs={{0,2},{1,3},{2,0},{3,1},{4,6},{5,7},{6,4},{7,5},{8,10},{9,11},{10,... | collective-permute-start | bytes 786440 | tf_op jit(solution)/shard_map/ppermute | solution.py:436
  463.4 13.5 %collective-permute-start.43 = (bf16[128,1024]{0,1:T(8,128)(2,1)S(1)}, bf16[128,1024]{0,1:T(8,128)(2,1)S(1)}, u32[]{:S(2)}, u32[]{:S(2)}) collective-permute-start(bf16[128,1024]{0,1:T(8,128)(2,1)S(1)} %add_convert_fusion.9), channel_id=1, source_target_pairs={{0,1},{1,0},{2,3},{3,2},{4,5},{5,4},{6,7},{7,6},{8,9},{9,8},{10,11... | collective-permute-start | bytes 786440 | tf_op jit(solution)/shard_map/ppermute | solution.py:436
  471.8 5.2 %collective-permute-start.45 = (bf16[128,1024]{0,1:T(8,128)(2,1)S(1)}, bf16[128,1024]{0,1:T(8,128)(2,1)S(1)}, u32[]{:S(2)}, u32[]{:S(2)}) collective-permute-start(bf16[128,1024]{0,1:T(8,128)(2,1)S(1)} %collective-permute-done.44), channel_id=1, source_target_pairs={{0,1},{1,0},{2,3},{3,2},{4,5},{5,4},{6,7},{7,6},{8,9},{9,8},{10,11... | collective-permute-start | bytes 786440 | tf_op jit(solution)/shard_map/ppermute | solution.py:436
  (59 other events, 336.1 us)
Sparse Core Ops, SparseCore 0:
  74.8 82.4 all-gather.1
  264.8 75.3 reduce-scatter.2
  344.2 63.8 reduce-scatter.4

commit v4 on v3

--- a/solution.py
+++ b/solution.py
@@ -114,7 +114,7 @@
     width = q_ref.shape[1]
     x = reorder(take_piece(pieces, steps, scratch), blocks)
     x_ref[...] = x
-    packed = dot_nn(x, w_ref[:, : 3 * q_ref.shape[1]])
+    packed = dot_nn(x, w_ref[...])
     cosine = cos_ref[...]
     sine = sin_ref[...]
     lanes = cosine.shape[1]
@@ -131,7 +131,7 @@
 def qkv_heads(pieces, weights, cosine, sine, blocks, before):
     count = len(pieces)
     rows, depth = pieces[0].shape
-    width = weights.shape[1] // 4
+    width = weights.shape[1] // 3
     step = block_rows(rows, 320)
     steps = rows // step
     length, table = cosine.shape
@@ -161,29 +161,36 @@
 
 def attend_body(q_ref, k_ref, v_ref, out_ref, lse_ref):
     width = q_ref.shape[1]
+    heads = width // HEAD
     queries = q_ref[...] * jnp.asarray(HEAD**-0.5, BF16)
     keys = k_ref[...]
     values = v_ref[...]
-    for head in range(width // HEAD):
-        scores = dot_nt(only_head(queries, head), keys)
-        peak = jnp.max(scores, -1, keepdims=True)
+    outs, totals, peaks = [], [], []
+    for head in range(heads):
+        scores = dot_nt(keys, only_head(queries, head))
+        peak = jnp.max(scores, 0, keepdims=True)
         exponent = jnp.exp(scores - peak)
-        total = jnp.sum(exponent, -1, keepdims=True)
-        out = dot_nn(exponent.astype(BF16), values) / total
-        lse = jnp.broadcast_to(peak + jnp.log(total), out.shape)
-        if head:
-            here = head_of_lane(out.shape) == head
-            out = jnp.where(here, out, previous_out)
-            lse = jnp.where(here, lse, previous_lse)
-        previous_out, previous_lse = out, lse
-    out_ref[...] = out.astype(BF16)
-    lse_ref[...] = lse.T
+        low = exponent.astype(BF16)
+        if heads == 2:
+            own = head_of_lane(values.shape) == head
+            both = dot_tn(jnp.where(own, values, jnp.ones_like(values)), low)
+            outs.append(both[head * HEAD : (head + 1) * HEAD])
+            totals.append(both[(1 - head) * HEAD : (2 - head) * HEAD])
+        else:
+            outs.append(dot_tn(values, low)[head * HEAD : (head + 1) * HEAD])
+            totals.append(
+                jnp.broadcast_to(jnp.sum(exponent, 0, keepdims=True), outs[-1].shape)
+            )
+        peaks.append(jnp.broadcast_to(peak, outs[-1].shape))
+    total = jnp.concatenate(totals, 0)
+    out_ref[...] = (jnp.concatenate(outs, 0) / total).T.astype(BF16)
+    lse_ref[...] = jnp.concatenate(peaks, 0) + jnp.log(total)
 
 
 def attend(queries, keys, values, group):
     rows, local_width = queries.shape
     width = min(128, local_width)
-    step = block_rows(rows, 256)
+    step = rows // 2
     q_spec = pl.BlockSpec((step, width), lambda i: (i, group))
     k_spec = pl.BlockSpec((rows, width), lambda i: (0, group))
     return pl.pallas_call(
@@ -383,8 +390,7 @@
 def token_grad_body(blocks, groups, count, steps, *refs):
     packed = jnp.concatenate([ref[...] for ref in refs[:groups]], 1)
     results = refs[groups + 1 :]
-    weights = refs[groups][:, : packed.shape[1]]
-    grad = reorder(dot_nt(packed, weights).astype(BF16), blocks)
+    grad = reorder(dot_nt(packed, refs[groups][...]).astype(BF16), blocks)
     for at in range(count):
 
         @pl.when(pl.program_id(0) // steps == at)
@@ -470,24 +476,20 @@
             for member in range(seq_size)
         ]
 
-    def gather_fsdp(values):
-        bit = fsdp_size // 2
-        while bit:
-            other = swap(values, "fsdp", fsdp_size, bit)
-            high = (row & bit) != 0
-            values = jnp.concatenate(
-                [jnp.where(high, other, values), jnp.where(high, values, other)], 0
-            )
-            bit //= 2
-        return values
-
-    def halve_fsdp(values, bit):
+    def double_fsdp(values, bit):
+        other = swap(values, "fsdp", fsdp_size, bit)
+        high = (row & bit) != 0
+        return jnp.concatenate(
+            [jnp.where(high, other, values), jnp.where(high, values, other)], 0
+        )
+
+    def halve_fsdp(values, bit, joined=lambda got: got):
         size = values.shape[0] // 2
         mine = jnp.where((row & bit) != 0, size, 0)
         kept = lax.dynamic_slice(values, (mine, 0), (size, values.shape[1]))
         sent = lax.dynamic_slice(values, (size - mine, 0), (size, values.shape[1]))
-        total = kept.astype(F32) + swap(sent, "fsdp", fsdp_size, bit).astype(F32)
-        return total.astype(BF16)
+        got = joined(swap(sent, "fsdp", fsdp_size, bit))
+        return (kept.astype(F32) + got.astype(F32)).astype(BF16)
 
     def reduce_fsdp(values):
         return lax.psum_scatter(values, "fsdp", scatter_dimension=0, tiled=True)
@@ -507,8 +509,6 @@
     )
     qkv_slice = (qkv_slice.astype(F32) * own_gain_attn).astype(BF16)
     attn_out_slice = lax.dynamic_slice(w_attn_out, (0, me * local_width), (shard, local_width))
-    attn_weights = gather_fsdp(jnp.concatenate([qkv_slice, attn_out_slice], 1))
-    packed_width = 3 * local_width
 
     tokens = activations.reshape(positions, width).astype(F32)
     xhat, inverse = centred_stats(tokens)
@@ -533,18 +533,6 @@
         in_slice, (0, 0, me * unit_share), (shard, 2 * fsdp_size, unit_share)
     ).reshape(shard, 2 * units)
     in_slice = (in_slice.astype(F32) * own_gain_mlp).astype(BF16)
-    sections = jnp.concatenate(
-        [
-            attn_weights[block * shard : (block + 1) * shard, packed_width:]
-            for block in bit_reversed(fsdp_size)
-        ],
-        0,
-    )
-    mlp_slice = jnp.concatenate([in_slice, fold_rows(mlp_out_slice, shard)], 1)
-    mlp_weights = lax.all_gather(after((mlp_slice, attn_weights))[0], "fsdp", axis=0, tiled=True)
-    far_sections = swap_seq(after((sections, far_x))[0], half)
-    far_c_pieces = spread(swap_seq(after((own_cotangent, far_sections))[0], half))
-
     lane = lax.broadcasted_iota(jnp.int32, (length, lanes), 1)
     at = lax.broadcasted_iota(jnp.int32, (length, lanes), 0)
     place = ((at // positions) ^ me) * positions + at % positions
@@ -553,9 +541,29 @@
     cosine = jnp.cos(angles)
     sine = jnp.sin(angles) * jnp.where(lane % HEAD < HALF, -1.0, 1.0)
 
-    begun = qkv_heads(near_x_pieces, attn_weights, cosine, sine, fsdp_size, [])
+    bit = fsdp_size // 2
+    qkv_weights, sections = qkv_slice, attn_out_slice
+    while bit:
+        if bit == 1:
+            qkv_weights, cosine, sine = after((qkv_weights, cosine, sine))
+        doubled = double_fsdp(qkv_weights, bit)
+        if bit < fsdp_size // 2:
+            sections, qkv_weights = after((sections, qkv_weights))
+            sections = double_fsdp(sections, 2 * bit)
+        qkv_weights = doubled
+        bit //= 2
+    sections = double_fsdp(after((sections, qkv_weights))[0], 1)
+    sections = jnp.concatenate(
+        [sections[block * shard : (block + 1) * shard] for block in bit_reversed(fsdp_size)], 0
+    )
+    mlp_slice = jnp.concatenate([in_slice, fold_rows(mlp_out_slice, shard)], 1)
+    mlp_weights = lax.all_gather(after((mlp_slice, qkv_weights))[0], "fsdp", axis=0, tiled=True)
+    far_sections = swap_seq(after((sections, far_x))[0], half)
+    far_c_pieces = spread(swap_seq(after((own_cotangent, far_sections))[0], half))
+
+    begun = qkv_heads(near_x_pieces, qkv_weights, cosine, sine, fsdp_size, [])
     queries, keys, values, x_all = qkv_heads(
-        far_x_pieces, attn_weights, cosine, sine, fsdp_size, begun
+        far_x_pieces, qkv_weights, cosine, sine, fsdp_size, begun
     )
 
     def row_pieces(array):
@@ -633,29 +641,52 @@
     )
     sum_in = reduce_fsdp(grad_in)
     sum_mlp_out = reduce_fsdp(after((grad_mlp_out, grad_in))[0])
-    reduced = [halve_fsdp(first_grads, 1)]
     for group in range(1, groups):
-        grads[group], output, first_grads, sum_in = after(
+        grads[group], output, _, sum_in = after(
             (grads[group], output, first_grads, sum_in)
         )
         packed.append(back_of(group))
-
-    far_grads = token_grad(packed, attn_weights, fsdp_size, half, positions, half)
-    far_grads = fold(far_grads).astype(BF16)
-    near_grads = token_grad(packed, attn_weights, fsdp_size, half, positions, 0)
-    if groups > 1:
-        last_grads = [dot_tn(x_all, section).astype(BF16) for section in packed[1:]]
-        last_grads, far_grads = after((last_grads, far_grads))
-        reduced += [halve_fsdp(section, 1) for section in last_grads]
-    reduced[-1], sum_mlp_out = after((reduced[-1], sum_mlp_out))
-    far_grads = swap_seq(far_grads, half)
-    normed_grad = far_grads.astype(F32) + fold(near_grads)
+    reduced = [halve_fsdp(first_grads, 1, lambda got: after((got, packed[-1]))[0])]
+
+    later_bits = [1 << at for at in range(1, fsdp_size.bit_length() - 1)]
+    chains = [later_bits] + [[1] + later_bits] * (groups - 1)
+    last_grads = [dot_tn(x_all, section).astype(BF16) for section in packed[1:]]
+    packed, last_grads, reduced = after((packed, last_grads, reduced))
+    reduced = reduced + last_grads
+    cuts = [0, positions // 4, positions // 2, positions]
+    near_grads, far_parts = None, None
+    for stage in range(max(len(chain) for chain in chains)):
+        if stage == 0:
+            far_grads = fold(
+                token_grad(packed, qkv_weights, fsdp_size, half, positions, half)
+            ).astype(BF16)
+        if stage == 1:
+            far_parts = [
+                swap_seq(far_grads[start:end], half) for start, end in zip(cuts, cuts[1:])
+            ]
+            near_grads = token_grad(packed, qkv_weights, fsdp_size, half, positions, 0)
+        if stage == 2:
+            near_grads = fold(near_grads)
+        reduced = [
+            halve_fsdp(section, chain[stage]) if stage < len(chain) else section
+            for section, chain in zip(reduced, chains)
+        ]
+        if stage == 0:
+            reduced, far_grads, packed = after((reduced, far_grads, packed))
+        if stage == 1:
+            reduced, near_grads, sum_mlp_out, far_parts[0] = after(
+                (reduced, near_grads, sum_mlp_out, far_parts[0])
+            )
+        if stage == 2:
+            reduced, near_grads, far_parts[1] = after((reduced, near_grads, far_parts[1]))
+    if not isinstance(near_grads, jax.Array):
+        near_grads = fold(near_grads)
+    reduced = jnp.concatenate(reduced, 1)
+    far_reduced = swap_seq(reduced, half)
+    far_reduced, far_parts = after((far_reduced, far_parts))
+    sum_mlp_out = after((sum_mlp_out, far_parts[0]))[0]
+    normed_grad = jnp.concatenate(far_parts, 0).astype(F32) + near_grads
     d_input = (mixed_grad + norm_backward(normed_grad, xhat, inverse)).astype(BF16)
-    reduced = jnp.concatenate(reduced, 1)
-    bit = 2
-    while bit < fsdp_size:
-        reduced = halve_fsdp(reduced, bit)
-        bit *= 2
 
     in_pieces = by_member(gather_seq(sum_in))
     all_in = jnp.concatenate(
@@ -663,7 +694,7 @@
     )
     all_in = all_in[:, :, :ff_shard].reshape(shard, -1).astype(F32)
     all_mlp_out = jnp.concatenate(by_member(gather_seq(sum_mlp_out)), 0)[:ff_shard].astype(F32)
-    pieces = by_member(gather_seq(reduced))
+    pieces = by_member(spread(reduced) + spread(far_reduced))
     section = 3 * lanes
     all_attn_out = jnp.concatenate(
         [piece[:, section : section + local_width] for piece in pieces], 1

time: 494 us -> 484 us (0.980)
  waiting for transfers between devices: 101 us -> 81.8 us
  Pallas kernels: 195 us -> 182 us
  starting transfers between devices: 50 us -> 60.6 us
  local copies, waits for them, and re-layouts: 25.6 us -> 32 us
    ppermute x52 -> x59, waiting for transfers between devices: 101 us -> 81.7 us  [swap(): return lax.ppermute(values, axis, [(i, i ^ offset) for i in range(size)])]
    pallas_call x2, Pallas kernels: 47.6 us -> 36.1 us  [attend(): pl.pallas_call(attend_body, grid=(rows // step,), in_specs=[q_spec, k_spe...]
    ppermute x52 -> x59, starting transfers between devices: 49.6 us -> 60.3 us  [swap(): return lax.ppermute(values, axis, [(i, i ^ offset) for i in range(size)])]
    unnamed x154 -> x165, local copies, waits for them, and re-layouts: 13.7 us -> 17 us
  transfers between devices with their start and end apart: 55 -> 62, of which waited for: 21 -> 23; matrix products, arithmetic and copies ran while one was open for 23% -> 26% of each run, Pallas kernels for 35% -> 34%
where the time goes in v4:
time: 484 us; the launch traced here: 478 us
  Pallas kernels  182 us (38%)
  waiting for transfers between devices  81.8 us (17%)
  other arithmetic  67.1 us (14%)
  starting transfers between devices  60.6 us (13%)
  matrix products  38.7 us (8%)
  local copies, waits for them, and re-layouts  32 us (7%)
  between operations  15.5 us (3%)
    ppermute x59, waiting for transfers between devices, swap(): return lax.ppermute(values, axis, [(i, i ^ offset) for i in range(size)])  81.7 us
    pallas_call x2, Pallas kernels, attend_back(): pl.pallas_call(attend_back_body, grid=(rows // step,), in_specs=[q_spec,...  75 us
    ppermute x59, starting transfers between devices, swap(): return lax.ppermute(values, axis, [(i, i ^ offset) for i in range(size)])  60.3 us
    pallas_call x2, Pallas kernels, mlp(): pl.pallas_call(functools.partial(mlp_body, count, steps, blocks, units),...  43.9 us
    pallas_call x2, Pallas kernels, attend(): pl.pallas_call(attend_body, grid=(rows // step,), in_specs=[q_spec, k_spe...  36.1 us
    dot_general x5, matrix products, dot_tn(): lax.dot_general(a, b, (((0,), (0,)), ((), ())), preferred_element_type=F32)  35.6 us
    unnamed x165, local copies, waits for them, and re-layouts  17 us
    pallas_call x2, Pallas kernels, qkv_heads(): pl.pallas_call(functools.partial(qkv_body, blocks, count, steps), grid=(c...  14 us
  transfers between devices with their start and end apart: 62, of which 23 were waited for; matrix products, arithmetic and copies ran while one was open for 26% of the time, Pallas kernels for 34%

profile of v4, /device:TPU:1, one launch (start us, length us, event | category | flops | bytes accessed | tf_op | source)
XLA Modules:
  0.0 477.8 jit_solution(13074640535807882631)
XLA Ops:
  18.6 2.4 collective-permute-start.2
  23.1 7.4 %select_multiply_fusion = (f32[2560,128]{1,0:T(8,128)}, f32[2560,128]{1,0:T(8,128)}) fusion(s32[128]{0:T(128)S(1)} %get-tuple-element.270, s32[128]{0:T(128)S(1)} %get-tuple-element.272, s32[128]{0:T(128)S(1)} %get-tuple-element.271, s32[128]{0:T(128)S(1)} %get-tuple-element.273, s32[2560]{0:T(1024)S(1)} %get-tuple-element.267, ...), kind=kLoop, calls=%fused_computation.56 | loop fusion | flops 4587520 | bytes 2669828 | tf_op jit(solution)/shard_map/mul | solution.py:542
  32.2 2.2 collective-permute-start.6
  34.8 7.0 %collective-permute-done.6 = bf16[128,256]{1,0:T(8,128)(2,1)S(1)} collective-permute-done((bf16[128,256]{1,0:T(8,128)(2,1)S(1)}, bf16[128,256]{1,0:T(8,128)(2,1)S(1)}, u32[]{:S(2)}, u32[]{:S(2)}) %collective-permute-start.6) | collective-permute-done | bytes 65568 | tf_op jit(solution)/shard_map/ppermute | solution.py:442
  44.2 2.3 collective-permute-start.7
  49.3 11.4 %collective-permute-done.4 = bf16[512,768]{1,0:T(8,128)(2,1)} collective-permute-done((bf16[512,768]{1,0:T(8,128)(2,1)S(1)}, bf16[512,768]{1,0:T(8,128)(2,1)}, u32[]{:S(2)}, u32[]{:S(2)}) %collective-permute-start.4) | collective-permute-done | bytes 786464 | tf_op jit(solution)/shard_map/ppermute | solution.py:442
  65.5 2.4 collective-permute-start.1
  69.7 3.3 collective-permute-start.20
  73.0 7.1 %qkv_rope.2 = (bf16[2560,256]{1,0:T(8,128)(2,1)}, bf16[2560,256]{1,0:T(8,128)(2,1)}, bf16[2560,256]{1,0:T(8,128)(2,1)}, bf16[2560,1024]{1,0:T(8,128)(2,1)}) custom-call(bf16[640,1024]{1,0:T(8,128)(2,1)} %fusion.6.refs_0_, bf16[640,1024]{1,0:T(8,128)(2,1)} %collective-permute-done.5.refs_1_, bf16[1024,768]{1,0:T(8,128)(2,1)} %pad_maximum_fusion.4.refs_2_, ...), custom_call_target="tpu_custom_call" | custom-call | flops 2013265920 | bytes 8781824 | tf_op jit(solution)/shard_map/qkv_rope/pallas_call | solution.py:141
  80.9 3.4 collective-permute-start.18
  85.4 6.9 %qkv_rope.3 = (bf16[2560,256]{1,0:T(8,128)(2,1)}, bf16[2560,256]{1,0:T(8,128)(2,1)}, bf16[2560,256]{1,0:T(8,128)(2,1)}, bf16[2560,1024]{1,0:T(8,128)(2,1)}) custom-call(bf16[640,1024]{1,0:T(8,128)(2,1)} %collective-permute-done.refs_0_, bf16[640,1024]{1,0:T(8,128)(2,1)} %copy-done.22, ...), custom_call_target="tpu_custom_call", output_to_operand_aliasing={{0}: (5, {}), {1}: (6, {}), {2}: (7, {}), {3}: (8, {})} | custom-call | flops 2013265920 | bytes 8781824 | tf_op jit(solution)/shard_map/qkv_rope/pallas_call | solution.py:141
  92.3 18.0 %attend.2 = (bf16[2560,128]{1,0:T(8,128)(2,1)}, f32[128,2560]{1,0:T(8,128)}) custom-call(bf16[2560,256]{1,0:T(8,128)(2,1)} %get-tuple-element.114.q_ref, bf16[2560,256]{1,0:T(8,128)(2,1)} %get-tuple-element.109.k_ref, bf16[2560,256]{1,0:T(8,128)(2,1)} %get-tuple-element.110.v_ref), custom_call_target="tpu_custom_call" | custom-call | flops 13421772800 | bytes 2621440 | tf_op jit(solution)/shard_map/attend/pallas_call | solution.py:196
  117.1 18.2 %attend.3 = (bf16[2560,128]{1,0:T(8,128)(2,1)}, f32[128,2560]{1,0:T(8,128)}) custom-call(bf16[2560,256]{1,0:T(8,128)(2,1)} %get-tuple-element.114.q_ref, bf16[2560,256]{1,0:T(8,128)(2,1)} %get-tuple-element.109.k_ref, bf16[2560,256]{1,0:T(8,128)(2,1)} %get-tuple-element.110.v_ref), custom_call_target="tpu_custom_call" | custom-call | flops 13421772800 | bytes 2621440 | tf_op jit(solution)/shard_map/attend/pallas_call | solution.py:196
  139.9 3.0 collective-permute-done.14
  143.0 4.0 collective-permute-done.16
  154.4 22.1 %mlp.2 = (bf16[2560,768]{1,0:T(8,128)(2,1)}, bf16[2560,1536]{1,0:T(8,128)(2,1)}, bf16[2560,1024]{1,0:T(8,128)(2,1)}, bf16[2560,1024]{1,0:T(8,128)(2,1)}, bf16[64...) custom-call(bf16[640,1024]{1,0:T(8,128)(2,1)} %fusion.14.refs_0_, ...), custom_call_target="tpu_custom_call" | custom-call | flops 12079595520 | bytes 26345472 | tf_op jit(solution)/shard_map/mlp/pallas_call | solution.py:362
  176.6 4.6 collective-permute-done.22.refs_0_
  182.6 3.0 collective-permute-done.23.refs_1_
  185.6 21.7 %mlp.3 = (bf16[2560,768]{1,0:T(8,128)(2,1)}, bf16[2560,1536]{1,0:T(8,128)(2,1)}, bf16[2560,1024]{1,0:T(8,128)(2,1)}, bf16[2560,1024]{1,0:T(8,128)(2,1)}, bf16[64...) custom-call(bf16[640,1024]{1,0:T(8,128)(2,1)} %collective-permute-do, ...), custom_call_target="tpu_custom_call", output_to_operand_aliasing={{0}: (5, {}), {1}: (6, {}), {2}: (7, {}), {3}: (8, {})} | custom-call | flops 12079595520 | bytes 26345472 | tf_op jit(solution)/shard_map/mlp/pallas_call | solution.py:362
  207.7 2.9 collective-permute-done.25
  210.6 2.9 add_convert_fusion.3
  214.4 13.8 %convolution_convert_fusion = bf16[1024,1536]{1,0:T(8,128)(2,1)} fusion(bf16[2560,1024]{1,0:T(8,128)(2,1)} %get-tuple-element.132, bf16[2560,1536]{1,0:T(8,128)(2,1)} %get-tuple-element.133), kind=kOutput, calls=%fused_computation | convolution fusion | flops 8054636544 | bytes 16252928 | tf_op jit(solution)/shard_map/dot_general | solution.py:32
  228.2 9.2 %convolution_convert_fusion.2 = bf16[768,1024]{1,0:T(8,128)(2,1)} fusion(bf16[2560,768]{1,0:T(8,128)(2,1)} %get-tuple-element.130, bf16[2560,1024]{1,0:T(8,128)(2,1)} %get-tuple-element.131), kind=kOutput, calls=%fused_computation.40 | convolution fusion | flops 4027318272 | bytes 10747904 | tf_op jit(solution)/shard_map/dot_general | solution.py:32
  237.4 6.4 %collective-permute-done.26 = bf16[640,1024]{1,0:T(8,128)(2,1)} collective-permute-done((bf16[640,1024]{1,0:T(8,128)(2,1)}, bf16[640,1024]{1,0:T(8,128)(2,1)}, u32[]{:S(2)}, u32[]{:S(2)}) %collective-permute-start.26) | collective-permute-done | bytes 1310752 | tf_op jit(solution)/shard_map/ppermute | solution.py:442
  250.5 2.3 fusion.18
  252.9 3.4 multiply_add_fusion
  266.1 3.6 collective-permute-done.33
  281.7 37.4 %attend_back.2.refs_0_ = bf16[2560,384]{1,0:T(8,128)(2,1)} custom-call(bf16[2560,256]{1,0:T(8,128)(2,1)} %get-tuple-element.114.q_ref, bf16[2560,256]{1,0:T(8,128)(2,1)} %get-tuple-element.109.k_ref, bf16[2560,256]{1,0:T(8,128)(2,1)} %get-tuple-element.110.v_ref, bf16[2560,128]{1,0:T(8,128)(2,1)} %pad_maximum_fusion.17.g_ref, ...), custom_call_target="tpu_custom_call" | custom-call | flops 33554432000 | bytes 6553600 | tf_op jit(solution)/shard_map/attend_back/pallas_call | solution.py:268
  319.0 3.2 collective-permute-done.37
  322.2 2.3 add_convert_fusion.5
  325.8 5.3 %convolution_convert_fusion.5 = bf16[1024,384]{0,1:T(8,128)(2,1)S(1)} fusion(bf16[2560,1024]{1,0:T(8,128)(2,1)} %get-tuple-element.145, bf16[2560,384]{1,0:T(8,128)(2,1)} %attend_back.2.refs_0_), kind=kOutput, calls=%fused_computation.49 | convolution fusion | flops 2013659136 | bytes 7995392 | tf_op jit(solution)/shard_map/dot_general | solution.py:32
  334.3 3.7 add_convert_fusion.1
  338.1 37.6 %attend_back.3.refs_1_ = bf16[2560,384]{1,0:T(8,128)(2,1)} custom-call(bf16[2560,256]{1,0:T(8,128)(2,1)} %get-tuple-element.114.q_ref, bf16[2560,256]{1,0:T(8,128)(2,1)} %get-tuple-element.109.k_ref, bf16[2560,256]{1,0:T(8,128)(2,1)} %get-tuple-element.110.v_ref, bf16[2560,128]{1,0:T(8,128)(2,1)} %pad_maximum_fusion.16.g_ref, ...), custom_call_target="tpu_custom_call" | custom-call | flops 33554432000 | bytes 6553600 | tf_op jit(solution)/shard_map/attend_back/pallas_call | solution.py:268
  375.7 5.4 %convolution_convert_fusion.4 = bf16[1024,384]{0,1:T(8,128)(2,1)S(1)} fusion(bf16[2560,1024]{1,0:T(8,128)(2,1)} %get-tuple-element.145, bf16[2560,384]{1,0:T(8,128)(2,1)} %attend_back.3.refs_1_), kind=kOutput, calls=%fused_computation.48 | convolution fusion | flops 2013659136 | bytes 7995392 | tf_op jit(solution)/shard_map/dot_general | solution.py:32
  382.7 6.5 %token_grad.2 = (bf16[640,1024]{1,0:T(8,128)(2,1)}, bf16[640,1024]{1,0:T(8,128)(2,1)}) custom-call(bf16[2560,384]{1,0:T(8,128)(2,1)} %attend_back.2.refs_0_, bf16[2560,384]{1,0:T(8,128)(2,1)} %attend_back.3.refs_1_, bf16[1024,768]{1,0:T(8,128)(2,1)} %pad_maximum_fusion.4.refs_2_), custom_call_target="tpu_custom_call" | custom-call | flops 2013265920 | bytes 6160384 | tf_op jit(solution)/shard_map/token_grad/pallas_call | solution.py:408
  390.2 2.7 collective-permute-start.40
  395.4 5.7 %collective-permute-done.40 = bf16[256,640]{0,1:T(8,128)(2,1)} collective-permute-done((bf16[256,640]{0,1:T(8,128)(2,1)S(1)}, bf16[256,640]{0,1:T(8,128)(2,1)}, u32[]{:S(2)}, u32[]{:S(2)}) %collective-permute-start.40) | collective-permute-done | bytes 327712 | tf_op jit(solution)/shard_map/ppermute | solution.py:442
  405.5 2.2 add_convert_fusion
  411.2 6.7 %token_grad.3 = (bf16[640,1024]{1,0:T(8,128)(2,1)}, bf16[640,1024]{1,0:T(8,128)(2,1)}) custom-call(bf16[2560,384]{1,0:T(8,128)(2,1)} %attend_back.2.refs_0_, bf16[2560,384]{1,0:T(8,128)(2,1)} %attend_back.3.refs_1_, bf16[1024,768]{1,0:T(8,128)(2,1)} %pad_maximum_fusion.4.refs_2_), custom_call_target="tpu_custom_call" | custom-call | flops 2013265920 | bytes 6160384 | tf_op jit(solution)/shard_map/token_grad/pallas_call | solution.py:408
  429.4 4.2 collective-permute-done.46
  433.7 3.5 convert_add_fusion.1
  437.7 2.7 convert_multiply_fusion
  440.5 3.4 copy.40
  443.9 2.2 collective-permute-start.51
  446.1 4.5 collective-permute-done.50
  450.6 5.7 %collective-permute-done.49 = bf16[128,1024]{0,1:T(8,128)(2,1)} collective-permute-done((bf16[128,1024]{0,1:T(8,128)(2,1)S(1)}, bf16[128,1024]{0,1:T(8,128)(2,1)}, u32[]{:S(2)}, u32[]{:S(2)}) %collective-permute-start.49) | collective-permute-done | bytes 262176 | tf_op jit(solution)/shard_map/ppermute | solution.py:442
  458.5 2.7 fusion.32
  461.2 2.5 fusion.16
  (375 shorter events, 117.3 us)
Async XLA Ops:
  7.2 147.2 %all-gather.2.cloned.1.call-start = ((), (), s32[]{:S(2)}) async-start(), calls=%async_computation.2 | async-start | bytes 5308416 | tf_op jit(solution)/shard_map/all_gather | solution.py:560
  10.9 54.6 %collective-permute-start = (bf16[640,1024]{1,0:T(8,128)(2,1)}, bf16[640,1024]{1,0:T(8,128)(2,1)}, u32[]{:S(2)}, u32[]{:S(2)}) collective-permute-start(bf16[640,1024]{1,0:T(8,128)(2,1)} %fusion.6.refs_0_), channel_id=1, source_target_pairs={{0,2},{1,3},{2,0},{3,1},{4,6},{5,7},{6,4},{7,5},{8,10},{9,11},{10,... | collective-permute-start | bytes 3932168 | tf_op jit(solution)/shard_map/ppermute | solution.py:442
  12.9 60.1 %collective-permute-start.5 = (bf16[640,1024]{1,0:T(8,128)(2,1)}, bf16[640,1024]{1,0:T(8,128)(2,1)}, u32[]{:S(2)}, u32[]{:S(2)}) collective-permute-start(bf16[640,1024]{1,0:T(8,128)(2,1)} %fusion.6.refs_0_), channel_id=1, source_target_pairs={{0,1},{1,0},{2,3},{3,2},{4,5},{5,4},{6,7},{7,6},{8,9},{9,8},{10,11... | collective-permute-start | bytes 3932168 | tf_op jit(solution)/shard_map/ppermute | solution.py:442
  18.6 12.0 %collective-permute-start.2 = (bf16[128,768]{1,0:T(8,128)(2,1)S(1)}, bf16[128,768]{1,0:T(8,128)(2,1)S(1)}, u32[]{:S(2)}, u32[]{:S(2)}) collective-permute-start(bf16[128,768]{1,0:T(8,128)(2,1)S(1)} %multiply_convert_fusion.1), channel_id=1, source_target_pairs={{0,16},{4,20},{8,24},{12,28},{16,0},{20,4},{24,8},{28,12},{1,17},{... | collective-permute-start | bytes 589832 | tf_op jit(solution)/shard_map/ppermute | solution.py:442
  30.9 11.7 %collective-permute-start.3 = (bf16[256,768]{1,0:T(8,128)(2,1)S(1)}, bf16[256,768]{1,0:T(8,128)(2,1)S(1)}, u32[]{:S(2)}, u32[]{:S(2)}) collective-permute-start(bf16[256,768]{1,0:T(8,128)(2,1)S(1)} %pad_maximum_fusion.19), channel_id=1, source_target_pairs={{0,8},{4,12},{8,0},{12,4},{16,24},{20,28},{24,16},{28,20},{1,9},{5... | collective-permute-start | bytes 1179656 | tf_op jit(solution)/shard_map/ppermute | solution.py:442
  32.2 9.6 %collective-permute-start.6 = (bf16[128,256]{1,0:T(8,128)(2,1)S(1)}, bf16[128,256]{1,0:T(8,128)(2,1)S(1)}, u32[]{:S(2)}, u32[]{:S(2)}) collective-permute-start(bf16[128,256]{1,0:T(8,128)(2,1)S(1)} %constant_dynamic-slice_fusion.19), channel_id=1, source_target_pairs={{0,16},{4,20},{8,24},{12,28},{16,0},{20,4},{24,8},{28,12},{1,17},{... | collective-permute-start | bytes 196616 | tf_op jit(solution)/shard_map/ppermute | solution.py:442
  42.8 17.9 %collective-permute-start.4 = (bf16[512,768]{1,0:T(8,128)(2,1)S(1)}, bf16[512,768]{1,0:T(8,128)(2,1)}, u32[]{:S(2)}, u32[]{:S(2)}) collective-permute-start(bf16[512,768]{1,0:T(8,128)(2,1)S(1)} %pad_maximum_fusion.11), channel_id=1, source_target_pairs={{0,4},{4,0},{8,12},{12,8},{16,20},{20,16},{24,28},{28,24},{1,5},{5... | collective-permute-start | bytes 2359304 | tf_op jit(solution)/shard_map/ppermute | solution.py:442
  65.5 18.9 %collective-permute-start.1 = (bf16[640,1024]{1,0:T(8,128)(2,1)}, bf16[640,1024]{1,0:T(8,128)(2,1)S(1)}, u32[]{:S(2)}, u32[]{:S(2)}) collective-permute-start(bf16[640,1024]{1,0:T(8,128)(2,1)} %collective-permute-done.refs_0_), channel_id=1, source_target_pairs={{0,1},{1,0},{2,3},{3,2},{4,5},{5,4},{6,7},{7,6},{8,9},{9,8},{10,11... | collective-permute-start | bytes 3932168 | tf_op jit(solution)/shard_map/ppermute | solution.py:442
  67.9 270.2 %reduce-scatter.3.cloned.1.call-start = ((), (), s32[]{:S(2)}) async-start(), calls=%async_computation.3 | async-start | bytes 3538944 | tf_op jit(solution)/shard_map/reduce_scatter | solution.py:495
  68.9 11.2 %collective-permute-start.9 = (bf16[1024,256]{1,0:T(8,128)(2,1)S(1)}, bf16[1024,256]{1,0:T(8,128)(2,1)S(1)}, u32[]{:S(2)}, u32[]{:S(2)}) collective-permute-start(bf16[1024,256]{1,0:T(8,128)(2,1)S(1)} %constant_dynamic-update-slice_fusion.6), channel_id=1, source_target_pairs={{0,2},{1,3},{2,0},{3,1},{4,6},{5,7},{6,4},{7,5},{8,10},{9,11},{10,... | collective-permute-start | bytes 1572872 | tf_op jit(solution)/shard_map/ppermute | solution.py:442
  69.7 83.1 %collective-permute-start.20 = (bf16[640,1024]{1,0:T(8,128)(2,1)}, bf16[640,1024]{1,0:T(8,128)(2,1)}, u32[]{:S(2)}, u32[]{:S(2)}) collective-permute-start(bf16[640,1024]{1,0:T(8,128)(2,1)} %bitcast.refs_2_), channel_id=1, source_target_pairs={{0,1},{1,0},{2,3},{3,2},{4,5},{5,4},{6,7},{7,6},{8,9},{9,8},{10,11... | collective-permute-start | bytes 3932168 | tf_op jit(solution)/shard_map/ppermute | solution.py:442
  80.0 32.3 %collective-permute-start.17 = (bf16[1024,256]{1,0:T(8,128)(2,1)S(1)}, bf16[1024,256]{1,0:T(8,128)(2,1)S(1)}, u32[]{:S(2)}, u32[]{:S(2)}) collective-permute-start(bf16[1024,256]{1,0:T(8,128)(2,1)S(1)} %constant_dynamic-update-slice_fusion.6), channel_id=1, source_target_pairs={{0,1},{1,0},{2,3},{3,2},{4,5},{5,4},{6,7},{7,6},{8,9},{9,8},{10,11... | collective-permute-start | bytes 1572872 | tf_op jit(solution)/shard_map/ppermute | solution.py:442
  80.1 37.0 %collective-permute-start.10 = (bf16[640,1024]{1,0:T(8,128)(2,1)}, bf16[640,1024]{1,0:T(8,128)(2,1)}, u32[]{:S(2)}, u32[]{:S(2)}) collective-permute-start(bf16[640,1024]{1,0:T(8,128)(2,1)} %bitcast.refs_2_), channel_id=1, source_target_pairs={{0,2},{1,3},{2,0},{3,1},{4,6},{5,7},{6,4},{7,5},{8,10},{9,11},{10,... | collective-permute-start | bytes 3932168 | tf_op jit(solution)/shard_map/ppermute | solution.py:442
  80.9 32.3 %collective-permute-start.18 = (bf16[1024,256]{1,0:T(8,128)(2,1)S(1)}, bf16[1024,256]{1,0:T(8,128)(2,1)S(1)}, u32[]{:S(2)}, u32[]{:S(2)}) collective-permute-start(bf16[1024,256]{1,0:T(8,128)(2,1)S(1)} %collective-permute-done.9), channel_id=1, source_target_pairs={{0,1},{1,0},{2,3},{3,2},{4,5},{5,4},{6,7},{7,6},{8,9},{9,8},{10,11... | collective-permute-start | bytes 1572872 | tf_op jit(solution)/shard_map/ppermute | solution.py:442
  112.4 25.1 %collective-permute-start.11 = (bf16[640,128]{1,0:T(8,128)(2,1)}, bf16[640,128]{1,0:T(8,128)(2,1)S(1)}, u32[]{:S(2)}, u32[]{:S(2)}) collective-permute-start(bf16[640,128]{1,0:T(8,128)(2,1)} %get-tuple-element.244), channel_id=1, source_target_pairs={{0,1},{1,0},{2,3},{3,2},{4,5},{5,4},{6,7},{7,6},{8,9},{9,8},{10,11... | collective-permute-start | bytes 491528 | tf_op jit(solution)/shard_map/ppermute | solution.py:442
  112.4 27.5 %collective-permute-start.13 = (bf16[640,128]{1,0:T(8,128)(2,1)}, bf16[640,128]{1,0:T(8,128)(2,1)S(1)}, u32[]{:S(2)}, u32[]{:S(2)}) collective-permute-start(bf16[640,128]{1,0:T(8,128)(2,1)} %get-tuple-element.243), channel_id=1, source_target_pairs={{0,2},{1,3},{2,0},{3,1},{4,6},{5,7},{6,4},{7,5},{8,10},{9,11},{10,... | collective-permute-start | bytes 491528 | tf_op jit(solution)/shard_map/ppermute | solution.py:442
  114.0 28.9 %collective-permute-start.15 = (bf16[640,128]{1,0:T(8,128)(2,1)}, bf16[640,128]{1,0:T(8,128)(2,1)S(1)}, u32[]{:S(2)}, u32[]{:S(2)}) collective-permute-start(bf16[640,128]{1,0:T(8,128)(2,1)} %get-tuple-element.242), channel_id=1, source_target_pairs={{0,3},{1,2},{2,1},{3,0},{4,7},{5,6},{6,5},{7,4},{8,11},{9,10},{10,... | collective-permute-start | bytes 491528 | tf_op jit(solution)/shard_map/ppermute | solution.py:442
  139.1 7.9 %collective-permute-start.16 = (bf16[640,128]{1,0:T(8,128)(2,1)S(1)}, bf16[640,128]{1,0:T(8,128)(2,1)S(1)}, u32[]{:S(2)}, u32[]{:S(2)}) collective-permute-start(bf16[640,128]{1,0:T(8,128)(2,1)S(1)} %get-tuple-element.247), channel_id=1, source_target_pairs={{0,3},{1,2},{2,1},{3,0},{4,7},{5,6},{6,5},{7,4},{8,11},{9,10},{10,... | collective-permute-start | bytes 491528 | tf_op jit(solution)/shard_map/ppermute | solution.py:442
  151.1 30.1 %collective-permute-start.22 = (bf16[640,1024]{1,0:T(8,128)(2,1)}, bf16[640,1024]{1,0:T(8,128)(2,1)}, u32[]{:S(2)}, u32[]{:S(2)}) collective-permute-start(bf16[640,1024]{1,0:T(8,128)(2,1)} %fusion.14.refs_0_), channel_id=1, source_target_pairs={{0,2},{1,3},{2,0},{3,1},{4,6},{5,7},{6,4},{7,5},{8,10},{9,11},{10,... | collective-permute-start | bytes 3932168 | tf_op jit(solution)/shard_map/ppermute | solution.py:442
  152.0 30.6 %collective-permute-start.24 = (bf16[640,1024]{1,0:T(8,128)(2,1)}, bf16[640,1024]{1,0:T(8,128)(2,1)}, u32[]{:S(2)}, u32[]{:S(2)}) collective-permute-start(bf16[640,1024]{1,0:T(8,128)(2,1)} %collective-permute-done.10.refs_2_), channel_id=1, source_target_pairs={{0,1},{1,0},{2,3},{3,2},{4,5},{5,4},{6,7},{7,6},{8,9},{9,8},{10,11... | collective-permute-start | bytes 3932168 | tf_op jit(solution)/shard_map/ppermute | solution.py:442
  213.5 30.3 %collective-permute-start.26 = (bf16[640,1024]{1,0:T(8,128)(2,1)}, bf16[640,1024]{1,0:T(8,128)(2,1)}, u32[]{:S(2)}, u32[]{:S(2)}) collective-permute-start(bf16[640,1024]{1,0:T(8,128)(2,1)} %add_convert_fusion.3), channel_id=1, source_target_pairs={{0,2},{1,3},{2,0},{3,1},{4,6},{5,7},{6,4},{7,5},{8,10},{9,11},{10,... | collective-permute-start | bytes 3932168 | tf_op jit(solution)/shard_map/ppermute | solution.py:442
  243.9 177.0 %reduce-scatter.5.cloned.1.call-start = ((), (), s32[]{:S(2)}) async-start(), calls=%async_computation.4 | async-start | bytes 1769472 | tf_op jit(solution)/shard_map/reduce_scatter | solution.py:495
  248.2 86.1 %collective-permute-start.30 = (bf16[640,1024]{1,0:T(8,128)(2,1)}, bf16[640,1024]{1,0:T(8,128)(2,1)}, u32[]{:S(2)}, u32[]{:S(2)}) collective-permute-start(bf16[640,1024]{1,0:T(8,128)(2,1)} %get-tuple-element.136), channel_id=1, source_target_pairs={{0,1},{1,0},{2,3},{3,2},{4,5},{5,4},{6,7},{7,6},{8,9},{9,8},{10,11... | collective-permute-start | bytes 3932168 | tf_op jit(solution)/shard_map/ppermute | solution.py:442
  248.3 23.5 %collective-permute-start.34 = (bf16[640,1024]{1,0:T(8,128)(2,1)S(1)}, bf16[640,1024]{1,0:T(8,128)(2,1)S(1)}, u32[]{:S(2)}, u32[]{:S(2)}) collective-permute-start(bf16[640,1024]{1,0:T(8,128)(2,1)S(1)} %copy-done.53), channel_id=1, source_target_pairs={{0,1},{1,0},{2,3},{3,2},{4,5},{5,4},{6,7},{7,6},{8,9},{9,8},{10,11... | collective-permute-start | bytes 3932168 | tf_op jit(solution)/shard_map/ppermute | solution.py:442
  260.3 9.3 %collective-permute-start.33 = (bf16[640,128]{1,0:T(8,128)(2,1)S(1)}, bf16[640,128]{1,0:T(8,128)(2,1)S(1)}, u32[]{:S(2)}, u32[]{:S(2)}) collective-permute-start(bf16[640,128]{1,0:T(8,128)(2,1)S(1)} %get-tuple-element.221), channel_id=1, source_target_pairs={{0,3},{1,2},{2,1},{3,0},{4,7},{5,6},{6,5},{7,4},{8,11},{9,10},{10,... | collective-permute-start | bytes 491528 | tf_op jit(solution)/shard_map/ppermute | solution.py:442
  262.9 11.8 %collective-permute-start.27 = (bf16[640,128]{1,0:T(8,128)(2,1)}, bf16[640,128]{1,0:T(8,128)(2,1)}, u32[]{:S(2)}, u32[]{:S(2)}) collective-permute-start(bf16[640,128]{1,0:T(8,128)(2,1)} %get-tuple-element.226), channel_id=1, source_target_pairs={{0,1},{1,0},{2,3},{3,2},{4,5},{5,4},{6,7},{7,6},{8,9},{9,8},{10,11... | collective-permute-start | bytes 491528 | tf_op jit(solution)/shard_map/ppermute | solution.py:442
  264.9 9.9 %collective-permute-start.28 = (bf16[640,128]{1,0:T(8,128)(2,1)}, bf16[640,128]{1,0:T(8,128)(2,1)}, u32[]{:S(2)}, u32[]{:S(2)}) collective-permute-start(bf16[640,128]{1,0:T(8,128)(2,1)} %get-tuple-element.225), channel_id=1, source_target_pairs={{0,2},{1,3},{2,0},{3,1},{4,6},{5,7},{6,4},{7,5},{8,10},{9,11},{10,... | collective-permute-start | bytes 491528 | tf_op jit(solution)/shard_map/ppermute | solution.py:442
  274.7 47.5 %collective-permute-start.38 = (bf16[1024,256]{1,0:T(8,128)(2,1)}, bf16[1024,256]{1,0:T(8,128)(2,1)}, u32[]{:S(2)}, u32[]{:S(2)}) collective-permute-start(bf16[1024,256]{1,0:T(8,128)(2,1)} %get-tuple-element.196), channel_id=1, source_target_pairs={{0,1},{1,0},{2,3},{3,2},{4,5},{5,4},{6,7},{7,6},{8,9},{9,8},{10,11... | collective-permute-start | bytes 1572872 | tf_op jit(solution)/shard_map/ppermute | solution.py:442
  280.2 42.0 %collective-permute-start.36 = (bf16[640,1024]{1,0:T(8,128)(2,1)S(1)}, bf16[640,1024]{1,0:T(8,128)(2,1)}, u32[]{:S(2)}, u32[]{:S(2)}) collective-permute-start(bf16[640,1024]{1,0:T(8,128)(2,1)S(1)} %copy-done.20), channel_id=1, source_target_pairs={{0,2},{1,3},{2,0},{3,1},{4,6},{5,7},{6,4},{7,5},{8,10},{9,11},{10,... | collective-permute-start | bytes 3932168 | tf_op jit(solution)/shard_map/ppermute | solution.py:442
  281.3 40.9 %collective-permute-start.37 = (bf16[1024,256]{1,0:T(8,128)(2,1)}, bf16[1024,256]{1,0:T(8,128)(2,1)}, u32[]{:S(2)}, u32[]{:S(2)}) collective-permute-start(bf16[1024,256]{1,0:T(8,128)(2,1)} %add_convert_fusion.6), channel_id=1, source_target_pairs={{0,2},{1,3},{2,0},{3,1},{4,6},{5,7},{6,4},{7,5},{8,10},{9,11},{10,... | collective-permute-start | bytes 1572872 | tf_op jit(solution)/shard_map/ppermute | solution.py:442
  333.0 48.1 %collective-permute-start.39 = (bf16[512,640]{0,1:T(8,128)(2,1)}, bf16[512,640]{0,1:T(8,128)(2,1)}, u32[]{:S(2)}, u32[]{:S(2)}) collective-permute-start(bf16[512,640]{0,1:T(8,128)(2,1)} %fusion.21), channel_id=1, source_target_pairs={{0,4},{4,0},{8,12},{12,8},{16,20},{20,16},{24,28},{28,24},{1,5},{5... | collective-permute-start | bytes 1966088 | tf_op jit(solution)/shard_map/ppermute | solution.py:442
  389.3 16.2 %collective-permute-start.42 = (bf16[640,1024]{1,0:T(8,128)(2,1)}, bf16[640,1024]{1,0:T(8,128)(2,1)}, u32[]{:S(2)}, u32[]{:S(2)}) collective-permute-start(bf16[640,1024]{1,0:T(8,128)(2,1)} %get-tuple-element.158), channel_id=1, source_target_pairs={{0,1},{1,0},{2,3},{3,2},{4,5},{5,4},{6,7},{7,6},{8,9},{9,8},{10,11... | collective-permute-start | bytes 3932168 | tf_op jit(solution)/shard_map/ppermute | solution.py:442
  390.2 10.9 %collective-permute-start.40 = (bf16[256,640]{0,1:T(8,128)(2,1)S(1)}, bf16[256,640]{0,1:T(8,128)(2,1)}, u32[]{:S(2)}, u32[]{:S(2)}) collective-permute-start(bf16[256,640]{0,1:T(8,128)(2,1)S(1)} %constant_dynamic-slice_fusion.12), channel_id=1, source_target_pairs={{0,8},{4,12},{8,0},{12,4},{16,24},{20,28},{24,16},{28,20},{1,9},{5... | collective-permute-start | bytes 983048 | tf_op jit(solution)/shard_map/ppermute | solution.py:442
  392.9 10.4 %collective-permute-start.54 = (bf16[128,1536]{1,0:T(8,128)(2,1)S(1)}, bf16[128,1536]{1,0:T(8,128)(2,1)S(1)}, u32[]{:S(2)}, u32[]{:S(2)}) collective-permute-start(bf16[128,1536]{1,0:T(8,128)(2,1)S(1)} %copy-done.41), channel_id=1, source_target_pairs={{0,2},{1,3},{2,0},{3,1},{4,6},{5,7},{6,4},{7,5},{8,10},{9,11},{10,... | collective-permute-start | bytes 1179656 | tf_op jit(solution)/shard_map/ppermute | solution.py:442
  394.2 10.3 %collective-permute-start.41 = (bf16[512,384]{0,1:T(8,128)(2,1)S(1)}, bf16[512,384]{0,1:T(8,128)(2,1)S(1)}, u32[]{:S(2)}, u32[]{:S(2)}) collective-permute-start(bf16[512,384]{0,1:T(8,128)(2,1)S(1)} %constant_dynamic-slice_fusion.11), channel_id=1, source_target_pairs={{0,4},{4,0},{8,12},{12,8},{16,20},{20,16},{24,28},{28,24},{1,5},{5... | collective-permute-start | bytes 1179656 | tf_op jit(solution)/shard_map/ppermute | solution.py:442
  394.6 27.8 %collective-permute-start.53 = (bf16[128,1536]{1,0:T(8,128)(2,1)S(1)}, bf16[128,1536]{1,0:T(8,128)(2,1)}, u32[]{:S(2)}, u32[]{:S(2)}) collective-permute-start(bf16[128,1536]{1,0:T(8,128)(2,1)S(1)} %copy-done.41), channel_id=1, source_target_pairs={{0,1},{1,0},{2,3},{3,2},{4,5},{5,4},{6,7},{7,6},{8,9},{9,8},{10,11... | collective-permute-start | bytes 1179656 | tf_op jit(solution)/shard_map/ppermute | solution.py:442
  403.3 19.1 %collective-permute-start.55 = (bf16[128,1536]{1,0:T(8,128)(2,1)S(1)}, bf16[128,1536]{1,0:T(8,128)(2,1)}, u32[]{:S(2)}, u32[]{:S(2)}) collective-permute-start(bf16[128,1536]{1,0:T(8,128)(2,1)S(1)} %collective-permute-done.54), channel_id=1, source_target_pairs={{0,1},{1,0},{2,3},{3,2},{4,5},{5,4},{6,7},{7,6},{8,9},{9,8},{10,11... | collective-permute-start | bytes 1179656 | tf_op jit(solution)/shard_map/ppermute | solution.py:442
  407.8 12.9 %collective-permute-start.44 = (bf16[256,384]{0,1:T(8,128)(2,1)S(1)}, bf16[256,384]{0,1:T(8,128)(2,1)S(1)}, u32[]{:S(2)}, u32[]{:S(2)}) collective-permute-start(bf16[256,384]{0,1:T(8,128)(2,1)S(1)} %constant_dynamic-slice_fusion.9), channel_id=1, source_target_pairs={{0,8},{4,12},{8,0},{12,4},{16,24},{20,28},{24,16},{28,20},{1,9},{5... | collective-permute-start | bytes 589832 | tf_op jit(solution)/shard_map/ppermute | solution.py:442
  409.1 11.7 %collective-permute-start.45 = (bf16[160,1024]{1,0:T(8,128)(2,1)}, bf16[160,1024]{1,0:T(8,128)(2,1)S(1)}, u32[]{:S(2)}, u32[]{:S(2)}) collective-permute-start(bf16[160,1024]{1,0:T(8,128)(2,1)} %get-tuple-element.215), channel_id=1, source_target_pairs={{0,2},{1,3},{2,0},{3,1},{4,6},{5,7},{6,4},{7,5},{8,10},{9,11},{10,... | collective-permute-start | bytes 983048 | tf_op jit(solution)/shard_map/ppermute | solution.py:442
  410.4 9.7 %collective-permute-start.43 = (bf16[128,640]{0,1:T(8,128)(2,1)S(1)}, bf16[128,640]{0,1:T(8,128)(2,1)S(1)}, u32[]{:S(2)}, u32[]{:S(2)}) collective-permute-start(bf16[128,640]{0,1:T(8,128)(2,1)S(1)} %constant_dynamic-slice_fusion.10), channel_id=1, source_target_pairs={{0,16},{4,20},{8,24},{12,28},{16,0},{20,4},{24,8},{28,12},{1,17},{... | collective-permute-start | bytes 491528 | tf_op jit(solution)/shard_map/ppermute | solution.py:442
  420.9 12.8 %collective-permute-start.47 = (bf16[640,1024]{1,0:T(8,128)(2,1)}, bf16[640,1024]{1,0:T(8,128)(2,1)}, u32[]{:S(2)}, u32[]{:S(2)}) collective-permute-start(bf16[640,1024]{1,0:T(8,128)(2,1)} %get-tuple-element.171), channel_id=1, source_target_pairs={{0,1},{1,0},{2,3},{3,2},{4,5},{5,4},{6,7},{7,6},{8,9},{9,8},{10,11... | collective-permute-start | bytes 3932168 | tf_op jit(solution)/shard_map/ppermute | solution.py:442
  426.6 7.1 %collective-permute-start.46 = (bf16[128,384]{0,1:T(8,128)(2,1)S(1)}, bf16[128,384]{0,1:T(8,128)(2,1)S(1)}, u32[]{:S(2)}, u32[]{:S(2)}) collective-permute-start(bf16[128,384]{0,1:T(8,128)(2,1)S(1)} %constant_dynamic-slice_fusion.8), channel_id=1, source_target_pairs={{0,16},{4,20},{8,24},{12,28},{16,0},{20,4},{24,8},{28,12},{1,17},{... | collective-permute-start | bytes 294920 | tf_op jit(solution)/shard_map/ppermute | solution.py:442
  427.9 9.3 %collective-permute-start.48 = (bf16[160,1024]{1,0:T(8,128)(2,1)S(1)}, bf16[160,1024]{1,0:T(8,128)(2,1)S(1)}, u32[]{:S(2)}, u32[]{:S(2)}) collective-permute-start(bf16[160,1024]{1,0:T(8,128)(2,1)S(1)} %copy-done.42), channel_id=1, source_target_pairs={{0,2},{1,3},{2,0},{3,1},{4,6},{5,7},{6,4},{7,5},{8,10},{9,11},{10,... | collective-permute-start | bytes 983048 | tf_op jit(solution)/shard_map/ppermute | solution.py:442
  428.3 22.3 %collective-permute-start.50 = (bf16[320,1024]{1,0:T(8,128)(2,1)S(1)}, bf16[320,1024]{1,0:T(8,128)(2,1)S(1)}, u32[]{:S(2)}, u32[]{:S(2)}) collective-permute-start(bf16[320,1024]{1,0:T(8,128)(2,1)S(1)} %slice.229), channel_id=1, source_target_pairs={{0,2},{1,3},{2,0},{3,1},{4,6},{5,7},{6,4},{7,5},{8,10},{9,11},{10,... | collective-permute-start | bytes 1966088 | tf_op jit(solution)/shard_map/ppermute | solution.py:442
  437.2 19.1 %collective-permute-start.49 = (bf16[128,1024]{0,1:T(8,128)(2,1)S(1)}, bf16[128,1024]{0,1:T(8,128)(2,1)}, u32[]{:S(2)}, u32[]{:S(2)}) collective-permute-start(bf16[128,1024]{0,1:T(8,128)(2,1)S(1)} %constant_dynamic-update-slice_fusion.22), channel_id=1, source_target_pairs={{0,2},{1,3},{2,0},{3,1},{4,6},{5,7},{6,4},{7,5},{8,10},{9,11},{10,... | collective-permute-start | bytes 786440 | tf_op jit(solution)/shard_map/ppermute | solution.py:442
  443.9 20.3 %collective-permute-start.51 = (bf16[128,1024]{0,1:T(8,128)(2,1)S(1)}, bf16[128,1024]{0,1:T(8,128)(2,1)S(1)}, u32[]{:S(2)}, u32[]{:S(2)}) collective-permute-start(bf16[128,1024]{0,1:T(8,128)(2,1)S(1)} %constant_dynamic-update-slice_fusion.22), channel_id=1, source_target_pairs={{0,1},{1,0},{2,3},{3,2},{4,5},{5,4},{6,7},{7,6},{8,9},{9,8},{10,11... | collective-permute-start | bytes 786440 | tf_op jit(solution)/shard_map/ppermute | solution.py:442
  456.3 7.4 %collective-permute-start.57 = (bf16[96,1024]{1,0:T(8,128)(2,1)}, bf16[96,1024]{1,0:T(8,128)(2,1)S(1)}, u32[]{:S(2)}, u32[]{:S(2)}) collective-permute-start(bf16[96,1024]{1,0:T(8,128)(2,1)} %reduce-scatter.5.cloned.1.call-done), channel_id=1, source_target_pairs={{0,2},{1,3},{2,0},{3,1},{4,6},{5,7},{6,4},{7,5},{8,10},{9,11},{10,... | collective-permute-start | bytes 589832 | tf_op jit(solution)/shard_map/ppermute | solution.py:442
  456.7 12.9 %collective-permute-start.56 = (bf16[96,1024]{1,0:T(8,128)(2,1)}, bf16[96,1024]{1,0:T(8,128)(2,1)S(1)}, u32[]{:S(2)}, u32[]{:S(2)}) collective-permute-start(bf16[96,1024]{1,0:T(8,128)(2,1)} %reduce-scatter.5.cloned.1.call-done), channel_id=1, source_target_pairs={{0,1},{1,0},{2,3},{3,2},{4,5},{5,4},{6,7},{7,6},{8,9},{9,8},{10,11... | collective-permute-start | bytes 589832 | tf_op jit(solution)/shard_map/ppermute | solution.py:442
  (71 other events, 463.9 us)
Sparse Core Ops, SparseCore 0:
  68.0 77.6 all-gather.1
  244.0 75.1 reduce-scatter.2
  322.6 64.1 reduce-scatter.4

commit v5 on v4

--- a/solution.py
+++ b/solution.py
@@ -476,8 +476,8 @@
             for member in range(seq_size)
         ]
 
-    def double_fsdp(values, bit):
-        other = swap(values, "fsdp", fsdp_size, bit)
+    def double_fsdp(values, bit, joined=lambda got: got):
+        other = joined(swap(values, "fsdp", fsdp_size, bit))
         high = (row & bit) != 0
         return jnp.concatenate(
             [jnp.where(high, other, values), jnp.where(high, values, other)], 0
@@ -533,26 +533,34 @@
         in_slice, (0, 0, me * unit_share), (shard, 2 * fsdp_size, unit_share)
     ).reshape(shard, 2 * units)
     in_slice = (in_slice.astype(F32) * own_gain_mlp).astype(BF16)
-    lane = lax.broadcasted_iota(jnp.int32, (length, lanes), 1)
-    at = lax.broadcasted_iota(jnp.int32, (length, lanes), 0)
-    place = ((at // positions) ^ me) * positions + at % positions
-    frequency = jnp.exp((lane % HALF).astype(F32) * (-2.0 * math.log(rope_base) / HEAD))
-    angles = place.astype(F32) * frequency
-    cosine = jnp.cos(angles)
-    sine = jnp.sin(angles) * jnp.where(lane % HEAD < HALF, -1.0, 1.0)
+    def rotary_tables(device):
+        lane = lax.broadcasted_iota(jnp.int32, (length, lanes), 1)
+        at = lax.broadcasted_iota(jnp.int32, (length, lanes), 0)
+        place = ((at // positions) ^ device) * positions + at % positions
+        frequency = jnp.exp((lane % HALF).astype(F32) * (-2.0 * math.log(rope_base) / HEAD))
+        angles = place.astype(F32) * frequency
+        cosine = jnp.cos(angles)
+        sine = jnp.sin(angles) * jnp.where(lane % HEAD < HALF, -1.0, 1.0)
+        return cosine, sine
 
     bit = fsdp_size // 2
     qkv_weights, sections = qkv_slice, attn_out_slice
     while bit:
+        join = lambda got: got
         if bit == 1:
-            qkv_weights, cosine, sine = after((qkv_weights, cosine, sine))
-        doubled = double_fsdp(qkv_weights, bit)
+            device, qkv_weights = after((me, qkv_weights))
+            cosine, sine = rotary_tables(device)
+            join = lambda got: after((got, cosine, sine))[0]
+        doubled = double_fsdp(qkv_weights, bit, join)
         if bit < fsdp_size // 2:
             sections, qkv_weights = after((sections, qkv_weights))
             sections = double_fsdp(sections, 2 * bit)
         qkv_weights = doubled
         bit //= 2
-    sections = double_fsdp(after((sections, qkv_weights))[0], 1)
+    begun = qkv_heads(near_x_pieces, qkv_weights, cosine, sine, fsdp_size, [])
+    sections = double_fsdp(
+        after((sections, qkv_weights))[0], 1, lambda got: after((got, begun))[0]
+    )
     sections = jnp.concatenate(
         [sections[block * shard : (block + 1) * shard] for block in bit_reversed(fsdp_size)], 0
     )
@@ -561,7 +569,6 @@
     far_sections = swap_seq(after((sections, far_x))[0], half)
     far_c_pieces = spread(swap_seq(after((own_cotangent, far_sections))[0], half))
 
-    begun = qkv_heads(near_x_pieces, qkv_weights, cosine, sine, fsdp_size, [])
     queries, keys, values, x_all = qkv_heads(
         far_x_pieces, qkv_weights, cosine, sine, fsdp_size, begun
     )
@@ -649,17 +656,13 @@
     reduced = [halve_fsdp(first_grads, 1, lambda got: after((got, packed[-1]))[0])]
 
     later_bits = [1 << at for at in range(1, fsdp_size.bit_length() - 1)]
-    chains = [later_bits] + [[1] + later_bits] * (groups - 1)
-    last_grads = [dot_tn(x_all, section).astype(BF16) for section in packed[1:]]
-    packed, last_grads, reduced = after((packed, last_grads, reduced))
-    reduced = reduced + last_grads
+    chains = [later_bits] + [[0, 1] + later_bits] * (groups - 1)
+    far_grads = fold(token_grad(packed, qkv_weights, fsdp_size, half, positions, half))
+    far_grads = far_grads.astype(BF16)
+    reduced = reduced + [dot_tn(x_all, section).astype(BF16) for section in packed[1:]]
     cuts = [0, positions // 4, positions // 2, positions]
     near_grads, far_parts = None, None
     for stage in range(max(len(chain) for chain in chains)):
-        if stage == 0:
-            far_grads = fold(
-                token_grad(packed, qkv_weights, fsdp_size, half, positions, half)
-            ).astype(BF16)
         if stage == 1:
             far_parts = [
                 swap_seq(far_grads[start:end], half) for start, end in zip(cuts, cuts[1:])
@@ -668,15 +671,17 @@
         if stage == 2:
             near_grads = fold(near_grads)
         reduced = [
-            halve_fsdp(section, chain[stage]) if stage < len(chain) else section
+            halve_fsdp(section, chain[stage])
+            if stage < len(chain) and chain[stage]
+            else section
             for section, chain in zip(reduced, chains)
         ]
         if stage == 0:
-            reduced, far_grads, packed = after((reduced, far_grads, packed))
+            reduced, far_grads, packed, sum_mlp_out = after(
+                (reduced, far_grads, packed, sum_mlp_out)
+            )
         if stage == 1:
-            reduced, near_grads, sum_mlp_out, far_parts[0] = after(
-                (reduced, near_grads, sum_mlp_out, far_parts[0])
-            )
+            reduced, near_grads, far_parts[0] = after((reduced, near_grads, far_parts[0]))
         if stage == 2:
             reduced, near_grads, far_parts[1] = after((reduced, near_grads, far_parts[1]))
     if not isinstance(near_grads, jax.Array):

time: 484 us -> 486 us (level)
  waiting for transfers between devices: 81.8 us -> 87.2 us
    ppermute x59, waiting for transfers between devices: 81.7 us -> 87.2 us  [swap(): return lax.ppermute(values, axis, [(i, i ^ offset) for i in range(size)])]
    unnamed x165 -> x152, local copies, waits for them, and re-layouts: 17 us -> 15.2 us
  transfers between devices with their start and end apart: 62 -> 62, of which waited for: 23 -> 25; matrix products, arithmetic and copies ran while one was open for 26% -> 25% of each run, Pallas kernels for 34% -> 33%
where the time goes in v5:
time: 486 us; the launch traced here: 480 us
  Pallas kernels  182 us (37%)
  waiting for transfers between devices  87.2 us (18%)
  other arithmetic  67.3 us (14%)
  starting transfers between devices  60.2 us (12%)
  matrix products  38.2 us (8%)
  local copies, waits for them, and re-layouts  29.6 us (6%)
  between operations  15.4 us (3%)
    ppermute x59, waiting for transfers between devices, swap(): return lax.ppermute(values, axis, [(i, i ^ offset) for i in range(size)])  87.2 us
    pallas_call x2, Pallas kernels, attend_back(): pl.pallas_call(attend_back_body, grid=(rows // step,), in_specs=[q_spec,...  75 us
    ppermute x59, starting transfers between devices, swap(): return lax.ppermute(values, axis, [(i, i ^ offset) for i in range(size)])  59.9 us
    pallas_call x2, Pallas kernels, mlp(): pl.pallas_call(functools.partial(mlp_body, count, steps, blocks, units),...  43.9 us
    pallas_call x2, Pallas kernels, attend(): pl.pallas_call(attend_body, grid=(rows // step,), in_specs=[q_spec, k_spe...  36.1 us
    dot_general x5, matrix products, dot_tn(): lax.dot_general(a, b, (((0,), (0,)), ((), ())), preferred_element_type=F32)  35 us
    unnamed x152, local copies, waits for them, and re-layouts  15.2 us
    pallas_call x2, Pallas kernels, qkv_heads(): pl.pallas_call(functools.partial(qkv_body, blocks, count, steps), grid=(c...  13.7 us
  transfers between devices with their start and end apart: 62, of which 25 were waited for; matrix products, arithmetic and copies ran while one was open for 25% of the time, Pallas kernels for 33%

profile of v5, /device:TPU:1, one launch (start us, length us, event | category | flops | bytes accessed | tf_op | source)
XLA Modules:
  0.0 479.8 jit_solution(1379112559346850780)
XLA Ops:
  10.9 2.7 collective-permute-start
  19.0 2.3 collective-permute-start.2
  24.7 5.9 %collective-permute-done.2 = bf16[128,768]{1,0:T(8,128)(2,1)} collective-permute-done((bf16[128,768]{1,0:T(8,128)(2,1)}, bf16[128,768]{1,0:T(8,128)(2,1)}, u32[]{:S(2)}, u32[]{:S(2)}) %collective-permute-start.2) | collective-permute-done | bytes 196640 | tf_op jit(solution)/shard_map/ppermute | solution.py:442
  32.9 3.1 collective-permute-start.6
  36.3 6.0 %collective-permute-done.6 = bf16[128,256]{1,0:T(8,128)(2,1)S(1)} collective-permute-done((bf16[128,256]{1,0:T(8,128)(2,1)S(1)}, bf16[128,256]{1,0:T(8,128)(2,1)S(1)}, u32[]{:S(2)}, u32[]{:S(2)}) %collective-permute-start.6) | collective-permute-done | bytes 65568 | tf_op jit(solution)/shard_map/ppermute | solution.py:442
  44.4 3.6 collective-permute-start.7
  48.0 7.3 %select_multiply_fusion = (f32[2560,128]{1,0:T(8,128)}, f32[2560,128]{1,0:T(8,128)}) fusion(s32[128]{0:T(128)S(1)} %get-tuple-element.266, s32[128]{0:T(128)S(1)} %get-tuple-element.268, s32[128]{0:T(128)S(1)} %get-tuple-element.267, s32[128]{0:T(128)S(1)} %get-tuple-element.269, s32[2560]{0:T(1024)S(1)} %get-tuple-element.263, ...), kind=kLoop, calls=%fused_computation.56 | loop fusion | flops 4587520 | bytes 2669828 | tf_op jit(solution)/shard_map/mul | solution.py:543
  55.4 4.8 %collective-permute-done.4 = bf16[512,768]{1,0:T(8,128)(2,1)S(1)} collective-permute-done((bf16[512,768]{1,0:T(8,128)(2,1)S(1)}, bf16[512,768]{1,0:T(8,128)(2,1)S(1)}, u32[]{:S(2)}, u32[]{:S(2)}) %collective-permute-start.4) | collective-permute-done | bytes 786464 | tf_op jit(solution)/shard_map/ppermute | solution.py:442
  63.7 3.1 collective-permute-start.1
  67.1 6.9 %qkv_rope.2 = (bf16[2560,256]{1,0:T(8,128)(2,1)}, bf16[2560,256]{1,0:T(8,128)(2,1)}, bf16[2560,256]{1,0:T(8,128)(2,1)}, bf16[2560,1024]{1,0:T(8,128)(2,1)}) custom-call(bf16[640,1024]{1,0:T(8,128)(2,1)} %fusion.6.refs_0_, bf16[640,1024]{1,0:T(8,128)(2,1)} %collective-permute-done.5.refs_1_, bf16[1024,768]{1,0:T(8,128)(2,1)} %pad_maximum_fusion.4.refs_2_, ...), custom_call_target="tpu_custom_call" | custom-call | flops 2013265920 | bytes 8781824 | tf_op jit(solution)/shard_map/qkv_rope/pallas_call | solution.py:141
  74.9 12.9 %collective-permute-done.9 = bf16[1024,256]{1,0:T(8,128)(2,1)S(1)} collective-permute-done((bf16[1024,256]{1,0:T(8,128)(2,1)S(1)}, bf16[1024,256]{1,0:T(8,128)(2,1)S(1)}, u32[]{:S(2)}, u32[]{:S(2)}) %collective-permute-start.9) | collective-permute-done | bytes 524320 | tf_op jit(solution)/shard_map/ppermute | solution.py:442
  90.1 6.9 %qkv_rope.3 = (bf16[2560,256]{1,0:T(8,128)(2,1)}, bf16[2560,256]{1,0:T(8,128)(2,1)}, bf16[2560,256]{1,0:T(8,128)(2,1)}, bf16[2560,1024]{1,0:T(8,128)(2,1)}) custom-call(bf16[640,1024]{1,0:T(8,128)(2,1)} %collective-permute-done.refs_0_, bf16[640,1024]{1,0:T(8,128)(2,1)} %copy-done.22, ...), custom_call_target="tpu_custom_call", output_to_operand_aliasing={{0}: (5, {}), {1}: (6, {}), {2}: (7, {}), {3}: (8, {})} | custom-call | flops 2013265920 | bytes 8781824 | tf_op jit(solution)/shard_map/qkv_rope/pallas_call | solution.py:141
  97.0 18.0 %attend.2 = (bf16[2560,128]{1,0:T(8,128)(2,1)}, f32[128,2560]{1,0:T(8,128)}) custom-call(bf16[2560,256]{1,0:T(8,128)(2,1)} %get-tuple-element.112.q_ref, bf16[2560,256]{1,0:T(8,128)(2,1)} %get-tuple-element.107.k_ref, bf16[2560,256]{1,0:T(8,128)(2,1)} %get-tuple-element.108.v_ref), custom_call_target="tpu_custom_call" | custom-call | flops 13421772800 | bytes 2621440 | tf_op jit(solution)/shard_map/attend/pallas_call | solution.py:196
  120.8 18.2 %attend.3 = (bf16[2560,128]{1,0:T(8,128)(2,1)}, f32[128,2560]{1,0:T(8,128)}) custom-call(bf16[2560,256]{1,0:T(8,128)(2,1)} %get-tuple-element.112.q_ref, bf16[2560,256]{1,0:T(8,128)(2,1)} %get-tuple-element.107.k_ref, bf16[2560,256]{1,0:T(8,128)(2,1)} %get-tuple-element.108.v_ref), custom_call_target="tpu_custom_call" | custom-call | flops 13421772800 | bytes 2621440 | tf_op jit(solution)/shard_map/attend/pallas_call | solution.py:196
  143.7 2.9 collective-permute-done.14
  146.7 4.0 collective-permute-done.16
  158.2 22.2 %mlp.2 = (bf16[2560,768]{1,0:T(8,128)(2,1)}, bf16[2560,1536]{1,0:T(8,128)(2,1)}, bf16[2560,1024]{1,0:T(8,128)(2,1)}, bf16[2560,1024]{1,0:T(8,128)(2,1)}, bf16[64...) custom-call(bf16[640,1024]{1,0:T(8,128)(2,1)} %fusion.14.refs_0_, ...), custom_call_target="tpu_custom_call" | custom-call | flops 12079595520 | bytes 26345472 | tf_op jit(solution)/shard_map/mlp/pallas_call | solution.py:362
  180.3 4.6 collective-permute-done.22.refs_0_
  186.3 3.0 collective-permute-done.23.refs_1_
  189.3 21.7 %mlp.3 = (bf16[2560,768]{1,0:T(8,128)(2,1)}, bf16[2560,1536]{1,0:T(8,128)(2,1)}, bf16[2560,1024]{1,0:T(8,128)(2,1)}, bf16[2560,1024]{1,0:T(8,128)(2,1)}, bf16[64...) custom-call(bf16[640,1024]{1,0:T(8,128)(2,1)} %collective-permute-do, ...), custom_call_target="tpu_custom_call", output_to_operand_aliasing={{0}: (5, {}), {1}: (6, {}), {2}: (7, {}), {3}: (8, {})} | custom-call | flops 12079595520 | bytes 26345472 | tf_op jit(solution)/shard_map/mlp/pallas_call | solution.py:362
  211.5 2.9 collective-permute-done.25
  214.3 2.9 add_convert_fusion.3
  218.5 13.8 %convolution_convert_fusion = bf16[1024,1536]{1,0:T(8,128)(2,1)} fusion(bf16[2560,1024]{1,0:T(8,128)(2,1)} %get-tuple-element.130, bf16[2560,1536]{1,0:T(8,128)(2,1)} %get-tuple-element.131), kind=kOutput, calls=%fused_computation | convolution fusion | flops 8054636544 | bytes 16252928 | tf_op jit(solution)/shard_map/dot_general | solution.py:32
  232.3 9.2 %convolution_convert_fusion.2 = bf16[768,1024]{1,0:T(8,128)(2,1)} fusion(bf16[2560,768]{1,0:T(8,128)(2,1)} %get-tuple-element.128, bf16[2560,1024]{1,0:T(8,128)(2,1)} %get-tuple-element.129), kind=kOutput, calls=%fused_computation.40 | convolution fusion | flops 4027318272 | bytes 10747904 | tf_op jit(solution)/shard_map/dot_general | solution.py:32
  241.5 6.1 %collective-permute-done.26 = bf16[640,1024]{1,0:T(8,128)(2,1)} collective-permute-done((bf16[640,1024]{1,0:T(8,128)(2,1)}, bf16[640,1024]{1,0:T(8,128)(2,1)}, u32[]{:S(2)}, u32[]{:S(2)}) %collective-permute-start.26) | collective-permute-done | bytes 1310752 | tf_op jit(solution)/shard_map/ppermute | solution.py:442
  256.6 3.5 multiply_add_fusion
  270.1 3.4 collective-permute-done.33
  285.2 37.4 %attend_back.2.refs_0_ = bf16[2560,384]{1,0:T(8,128)(2,1)} custom-call(bf16[2560,256]{1,0:T(8,128)(2,1)} %get-tuple-element.112.q_ref, bf16[2560,256]{1,0:T(8,128)(2,1)} %get-tuple-element.107.k_ref, bf16[2560,256]{1,0:T(8,128)(2,1)} %get-tuple-element.108.v_ref, bf16[2560,128]{1,0:T(8,128)(2,1)} %pad_maximum_fusion.17.g_ref, ...), custom_call_target="tpu_custom_call" | custom-call | flops 33554432000 | bytes 6553600 | tf_op jit(solution)/shard_map/attend_back/pallas_call | solution.py:268
  322.6 3.3 collective-permute-done.37
  329.1 5.3 %convolution_convert_fusion.5 = bf16[1024,384]{0,1:T(8,128)(2,1)S(1)} fusion(bf16[2560,1024]{1,0:T(8,128)(2,1)} %get-tuple-element.143, bf16[2560,384]{1,0:T(8,128)(2,1)} %attend_back.2.refs_0_), kind=kOutput, calls=%fused_computation.49 | convolution fusion | flops 2013659136 | bytes 7995392 | tf_op jit(solution)/shard_map/dot_general | solution.py:32
  337.4 3.7 add_convert_fusion.1
  341.1 37.6 %attend_back.3.refs_1_ = bf16[2560,384]{1,0:T(8,128)(2,1)} custom-call(bf16[2560,256]{1,0:T(8,128)(2,1)} %get-tuple-element.112.q_ref, bf16[2560,256]{1,0:T(8,128)(2,1)} %get-tuple-element.107.k_ref, bf16[2560,256]{1,0:T(8,128)(2,1)} %get-tuple-element.108.v_ref, bf16[2560,128]{1,0:T(8,128)(2,1)} %pad_maximum_fusion.16.g_ref, ...), custom_call_target="tpu_custom_call" | custom-call | flops 33554432000 | bytes 6553600 | tf_op jit(solution)/shard_map/attend_back/pallas_call | solution.py:268
  378.7 6.5 %token_grad.2 = (bf16[640,1024]{1,0:T(8,128)(2,1)}, bf16[640,1024]{1,0:T(8,128)(2,1)}) custom-call(bf16[2560,384]{1,0:T(8,128)(2,1)} %attend_back.2.refs_0_, bf16[2560,384]{1,0:T(8,128)(2,1)} %attend_back.3.refs_1_, bf16[1024,768]{1,0:T(8,128)(2,1)} %pad_maximum_fusion.4.refs_2_), custom_call_target="tpu_custom_call" | custom-call | flops 2013265920 | bytes 6160384 | tf_op jit(solution)/shard_map/token_grad/pallas_call | solution.py:408
  387.5 3.3 collective-permute-start.40
  391.6 4.8 %convolution_convert_fusion.4 = bf16[1024,384]{0,1:T(8,128)(2,1)S(1)} fusion(bf16[2560,1024]{1,0:T(8,128)(2,1)} %get-tuple-element.143, bf16[2560,384]{1,0:T(8,128)(2,1)S(1)} %copy-done.50), kind=kOutput, calls=%fused_computation.48 | convolution fusion | flops 2013659136 | bytes 7995392 | tf_op jit(solution)/shard_map/dot_general | solution.py:32
  396.5 2.3 collective-permute-done.40
  405.5 6.6 %token_grad.3 = (bf16[640,1024]{1,0:T(8,128)(2,1)}, bf16[640,1024]{1,0:T(8,128)(2,1)}) custom-call(bf16[2560,384]{1,0:T(8,128)(2,1)} %attend_back.2.refs_0_, bf16[2560,384]{1,0:T(8,128)(2,1)} %attend_back.3.refs_1_, bf16[1024,768]{1,0:T(8,128)(2,1)} %pad_maximum_fusion.4.refs_2_), custom_call_target="tpu_custom_call" | custom-call | flops 2013265920 | bytes 6160384 | tf_op jit(solution)/shard_map/token_grad/pallas_call | solution.py:408
  417.9 3.4 collective-permute-done.53
  425.9 2.9 collective-permute-done.45
  429.8 3.8 convert_add_fusion.1
  437.3 3.2 collective-permute-done.48
  441.8 2.7 convert_multiply_fusion
  444.5 3.4 copy.40
  448.0 2.7 collective-permute-start.51
  451.5 5.7 %collective-permute-done.49 = bf16[128,1024]{0,1:T(8,128)(2,1)} collective-permute-done((bf16[128,1024]{0,1:T(8,128)(2,1)}, bf16[128,1024]{0,1:T(8,128)(2,1)}, u32[]{:S(2)}, u32[]{:S(2)}) %collective-permute-start.49) | collective-permute-done | bytes 262176 | tf_op jit(solution)/shard_map/ppermute | solution.py:442
  457.5 2.9 collective-permute-start.56
  460.5 2.7 fusion.33
  463.1 2.5 fusion.16
  (362 shorter events, 115.9 us)
Async XLA Ops:
  7.2 151.0 %all-gather.2.cloned.1.call-start = ((), (), s32[]{:S(2)}) async-start(), calls=%async_computation.2 | async-start | bytes 5308416 | tf_op jit(solution)/shard_map/all_gather | solution.py:568
  10.9 56.2 %collective-permute-start.5 = (bf16[640,1024]{1,0:T(8,128)(2,1)}, bf16[640,1024]{1,0:T(8,128)(2,1)}, u32[]{:S(2)}, u32[]{:S(2)}) collective-permute-start(bf16[640,1024]{1,0:T(8,128)(2,1)} %fusion.6.refs_0_), channel_id=1, source_target_pairs={{0,1},{1,0},{2,3},{3,2},{4,5},{5,4},{6,7},{7,6},{8,9},{9,8},{10,11... | collective-permute-start | bytes 3932168 | tf_op jit(solution)/shard_map/ppermute | solution.py:442
  10.9 52.8 %collective-permute-start = (bf16[640,1024]{1,0:T(8,128)(2,1)}, bf16[640,1024]{1,0:T(8,128)(2,1)}, u32[]{:S(2)}, u32[]{:S(2)}) collective-permute-start(bf16[640,1024]{1,0:T(8,128)(2,1)} %fusion.6.refs_0_), channel_id=1, source_target_pairs={{0,2},{1,3},{2,0},{3,1},{4,6},{5,7},{6,4},{7,5},{8,10},{9,11},{10,... | collective-permute-start | bytes 3932168 | tf_op jit(solution)/shard_map/ppermute | solution.py:442
  19.0 11.6 %collective-permute-start.2 = (bf16[128,768]{1,0:T(8,128)(2,1)}, bf16[128,768]{1,0:T(8,128)(2,1)}, u32[]{:S(2)}, u32[]{:S(2)}) collective-permute-start(bf16[128,768]{1,0:T(8,128)(2,1)} %multiply_convert_fusion.1), channel_id=1, source_target_pairs={{0,16},{4,20},{8,24},{12,28},{16,0},{20,4},{24,8},{28,12},{1,17},{... | collective-permute-start | bytes 589832 | tf_op jit(solution)/shard_map/ppermute | solution.py:442
  31.8 11.1 %collective-permute-start.3 = (bf16[256,768]{1,0:T(8,128)(2,1)S(1)}, bf16[256,768]{1,0:T(8,128)(2,1)S(1)}, u32[]{:S(2)}, u32[]{:S(2)}) collective-permute-start(bf16[256,768]{1,0:T(8,128)(2,1)S(1)} %pad_maximum_fusion.19), channel_id=1, source_target_pairs={{0,8},{4,12},{8,0},{12,4},{16,24},{20,28},{24,16},{28,20},{1,9},{5... | collective-permute-start | bytes 1179656 | tf_op jit(solution)/shard_map/ppermute | solution.py:442
  32.9 9.4 %collective-permute-start.6 = (bf16[128,256]{1,0:T(8,128)(2,1)S(1)}, bf16[128,256]{1,0:T(8,128)(2,1)S(1)}, u32[]{:S(2)}, u32[]{:S(2)}) collective-permute-start(bf16[128,256]{1,0:T(8,128)(2,1)S(1)} %constant_dynamic-slice_fusion.19), channel_id=1, source_target_pairs={{0,16},{4,20},{8,24},{12,28},{16,0},{20,4},{24,8},{28,12},{1,17},{... | collective-permute-start | bytes 196616 | tf_op jit(solution)/shard_map/ppermute | solution.py:442
  43.1 17.2 %collective-permute-start.4 = (bf16[512,768]{1,0:T(8,128)(2,1)S(1)}, bf16[512,768]{1,0:T(8,128)(2,1)S(1)}, u32[]{:S(2)}, u32[]{:S(2)}) collective-permute-start(bf16[512,768]{1,0:T(8,128)(2,1)S(1)} %pad_maximum_fusion.11), channel_id=1, source_target_pairs={{0,4},{4,0},{8,12},{12,8},{16,20},{20,16},{24,28},{28,24},{1,5},{5... | collective-permute-start | bytes 2359304 | tf_op jit(solution)/shard_map/ppermute | solution.py:442
  44.4 11.0 %collective-permute-start.7 = (bf16[256,256]{1,0:T(8,128)(2,1)S(1)}, bf16[256,256]{1,0:T(8,128)(2,1)S(1)}, u32[]{:S(2)}, u32[]{:S(2)}) collective-permute-start(bf16[256,256]{1,0:T(8,128)(2,1)S(1)} %pad_maximum_fusion.24), channel_id=1, source_target_pairs={{0,8},{4,12},{8,0},{12,4},{16,24},{20,28},{24,16},{28,20},{1,9},{5... | collective-permute-start | bytes 393224 | tf_op jit(solution)/shard_map/ppermute | solution.py:442
  61.6 12.3 %collective-permute-start.8 = (bf16[512,256]{1,0:T(8,128)(2,1)S(1)}, bf16[512,256]{1,0:T(8,128)(2,1)S(1)}, u32[]{:S(2)}, u32[]{:S(2)}) collective-permute-start(bf16[512,256]{1,0:T(8,128)(2,1)S(1)} %pad_maximum_fusion.22), channel_id=1, source_target_pairs={{0,4},{4,0},{8,12},{12,8},{16,20},{20,16},{24,28},{28,24},{1,5},{5... | collective-permute-start | bytes 786440 | tf_op jit(solution)/shard_map/ppermute | solution.py:442
  63.7 25.4 %collective-permute-start.1 = (bf16[640,1024]{1,0:T(8,128)(2,1)}, bf16[640,1024]{1,0:T(8,128)(2,1)S(1)}, u32[]{:S(2)}, u32[]{:S(2)}) collective-permute-start(bf16[640,1024]{1,0:T(8,128)(2,1)} %collective-permute-done.refs_0_), channel_id=1, source_target_pairs={{0,1},{1,0},{2,3},{3,2},{4,5},{5,4},{6,7},{7,6},{8,9},{9,8},{10,11... | collective-permute-start | bytes 3932168 | tf_op jit(solution)/shard_map/ppermute | solution.py:442
  66.8 274.3 %reduce-scatter.3.cloned.1.call-start = ((), (), s32[]{:S(2)}) async-start(), calls=%async_computation.3 | async-start | bytes 3538944 | tf_op jit(solution)/shard_map/reduce_scatter | solution.py:495
  74.1 13.7 %collective-permute-start.9 = (bf16[1024,256]{1,0:T(8,128)(2,1)S(1)}, bf16[1024,256]{1,0:T(8,128)(2,1)S(1)}, u32[]{:S(2)}, u32[]{:S(2)}) collective-permute-start(bf16[1024,256]{1,0:T(8,128)(2,1)S(1)} %constant_dynamic-update-slice_fusion.6), channel_id=1, source_target_pairs={{0,2},{1,3},{2,0},{3,1},{4,6},{5,7},{6,4},{7,5},{8,10},{9,11},{10,... | collective-permute-start | bytes 1572872 | tf_op jit(solution)/shard_map/ppermute | solution.py:442
  74.4 82.3 %collective-permute-start.20 = (bf16[640,1024]{1,0:T(8,128)(2,1)}, bf16[640,1024]{1,0:T(8,128)(2,1)}, u32[]{:S(2)}, u32[]{:S(2)}) collective-permute-start(bf16[640,1024]{1,0:T(8,128)(2,1)} %bitcast.refs_2_), channel_id=1, source_target_pairs={{0,1},{1,0},{2,3},{3,2},{4,5},{5,4},{6,7},{7,6},{8,9},{9,8},{10,11... | collective-permute-start | bytes 3932168 | tf_op jit(solution)/shard_map/ppermute | solution.py:442
  74.7 42.2 %collective-permute-start.17 = (bf16[1024,256]{1,0:T(8,128)(2,1)S(1)}, bf16[1024,256]{1,0:T(8,128)(2,1)S(1)}, u32[]{:S(2)}, u32[]{:S(2)}) collective-permute-start(bf16[1024,256]{1,0:T(8,128)(2,1)S(1)} %constant_dynamic-update-slice_fusion.6), channel_id=1, source_target_pairs={{0,1},{1,0},{2,3},{3,2},{4,5},{5,4},{6,7},{7,6},{8,9},{9,8},{10,11... | collective-permute-start | bytes 1572872 | tf_op jit(solution)/shard_map/ppermute | solution.py:442
  87.8 33.0 %collective-permute-start.10 = (bf16[640,1024]{1,0:T(8,128)(2,1)}, bf16[640,1024]{1,0:T(8,128)(2,1)}, u32[]{:S(2)}, u32[]{:S(2)}) collective-permute-start(bf16[640,1024]{1,0:T(8,128)(2,1)} %bitcast.refs_2_), channel_id=1, source_target_pairs={{0,2},{1,3},{2,0},{3,1},{4,6},{5,7},{6,4},{7,5},{8,10},{9,11},{10,... | collective-permute-start | bytes 3932168 | tf_op jit(solution)/shard_map/ppermute | solution.py:442
  88.1 30.1 %collective-permute-start.18 = (bf16[1024,256]{1,0:T(8,128)(2,1)S(1)}, bf16[1024,256]{1,0:T(8,128)(2,1)}, u32[]{:S(2)}, u32[]{:S(2)}) collective-permute-start(bf16[1024,256]{1,0:T(8,128)(2,1)S(1)} %collective-permute-done.9), channel_id=1, source_target_pairs={{0,1},{1,0},{2,3},{3,2},{4,5},{5,4},{6,7},{7,6},{8,9},{9,8},{10,11... | collective-permute-start | bytes 1572872 | tf_op jit(solution)/shard_map/ppermute | solution.py:442
  116.9 24.3 %collective-permute-start.11 = (bf16[640,128]{1,0:T(8,128)(2,1)S(1)}, bf16[640,128]{1,0:T(8,128)(2,1)S(1)}, u32[]{:S(2)}, u32[]{:S(2)}) collective-permute-start(bf16[640,128]{1,0:T(8,128)(2,1)S(1)} %get-tuple-element.238), channel_id=1, source_target_pairs={{0,1},{1,0},{2,3},{3,2},{4,5},{5,4},{6,7},{7,6},{8,9},{9,8},{10,11... | collective-permute-start | bytes 491528 | tf_op jit(solution)/shard_map/ppermute | solution.py:442
  116.9 26.7 %collective-permute-start.13 = (bf16[640,128]{1,0:T(8,128)(2,1)}, bf16[640,128]{1,0:T(8,128)(2,1)S(1)}, u32[]{:S(2)}, u32[]{:S(2)}) collective-permute-start(bf16[640,128]{1,0:T(8,128)(2,1)} %get-tuple-element.237), channel_id=1, source_target_pairs={{0,2},{1,3},{2,0},{3,1},{4,6},{5,7},{6,4},{7,5},{8,10},{9,11},{10,... | collective-permute-start | bytes 491528 | tf_op jit(solution)/shard_map/ppermute | solution.py:442
  118.2 28.5 %collective-permute-start.15 = (bf16[640,128]{1,0:T(8,128)(2,1)S(1)}, bf16[640,128]{1,0:T(8,128)(2,1)S(1)}, u32[]{:S(2)}, u32[]{:S(2)}) collective-permute-start(bf16[640,128]{1,0:T(8,128)(2,1)S(1)} %get-tuple-element.236), channel_id=1, source_target_pairs={{0,3},{1,2},{2,1},{3,0},{4,7},{5,6},{6,5},{7,4},{8,11},{9,10},{10,... | collective-permute-start | bytes 491528 | tf_op jit(solution)/shard_map/ppermute | solution.py:442
  142.8 7.9 %collective-permute-start.16 = (bf16[640,128]{1,0:T(8,128)(2,1)S(1)}, bf16[640,128]{1,0:T(8,128)(2,1)S(1)}, u32[]{:S(2)}, u32[]{:S(2)}) collective-permute-start(bf16[640,128]{1,0:T(8,128)(2,1)S(1)} %get-tuple-element.241), channel_id=1, source_target_pairs={{0,3},{1,2},{2,1},{3,0},{4,7},{5,6},{6,5},{7,4},{8,11},{9,10},{10,... | collective-permute-start | bytes 491528 | tf_op jit(solution)/shard_map/ppermute | solution.py:442
  154.8 30.1 %collective-permute-start.22 = (bf16[640,1024]{1,0:T(8,128)(2,1)}, bf16[640,1024]{1,0:T(8,128)(2,1)}, u32[]{:S(2)}, u32[]{:S(2)}) collective-permute-start(bf16[640,1024]{1,0:T(8,128)(2,1)} %fusion.14.refs_0_), channel_id=1, source_target_pairs={{0,2},{1,3},{2,0},{3,1},{4,6},{5,7},{6,4},{7,5},{8,10},{9,11},{10,... | collective-permute-start | bytes 3932168 | tf_op jit(solution)/shard_map/ppermute | solution.py:442
  156.0 30.3 %collective-permute-start.24 = (bf16[640,1024]{1,0:T(8,128)(2,1)}, bf16[640,1024]{1,0:T(8,128)(2,1)}, u32[]{:S(2)}, u32[]{:S(2)}) collective-permute-start(bf16[640,1024]{1,0:T(8,128)(2,1)} %collective-permute-done.10.refs_2_), channel_id=1, source_target_pairs={{0,1},{1,0},{2,3},{3,2},{4,5},{5,4},{6,7},{7,6},{8,9},{9,8},{10,11... | collective-permute-start | bytes 3932168 | tf_op jit(solution)/shard_map/ppermute | solution.py:442
  217.3 30.3 %collective-permute-start.26 = (bf16[640,1024]{1,0:T(8,128)(2,1)}, bf16[640,1024]{1,0:T(8,128)(2,1)}, u32[]{:S(2)}, u32[]{:S(2)}) collective-permute-start(bf16[640,1024]{1,0:T(8,128)(2,1)} %add_convert_fusion.3), channel_id=1, source_target_pairs={{0,2},{1,3},{2,0},{3,1},{4,6},{5,7},{6,4},{7,5},{8,10},{9,11},{10,... | collective-permute-start | bytes 3932168 | tf_op jit(solution)/shard_map/ppermute | solution.py:442
  247.6 153.2 %reduce-scatter.5.cloned.1.call-start = ((), (), s32[]{:S(2)}) async-start(), calls=%async_computation.4 | async-start | bytes 1769472 | tf_op jit(solution)/shard_map/reduce_scatter | solution.py:495
  251.9 85.4 %collective-permute-start.30 = (bf16[640,1024]{1,0:T(8,128)(2,1)}, bf16[640,1024]{1,0:T(8,128)(2,1)}, u32[]{:S(2)}, u32[]{:S(2)}) collective-permute-start(bf16[640,1024]{1,0:T(8,128)(2,1)} %get-tuple-element.134), channel_id=1, source_target_pairs={{0,1},{1,0},{2,3},{3,2},{4,5},{5,4},{6,7},{7,6},{8,9},{9,8},{10,11... | collective-permute-start | bytes 3932168 | tf_op jit(solution)/shard_map/ppermute | solution.py:442
  252.0 23.8 %collective-permute-start.34 = (bf16[640,1024]{1,0:T(8,128)(2,1)S(1)}, bf16[640,1024]{1,0:T(8,128)(2,1)S(1)}, u32[]{:S(2)}, u32[]{:S(2)}) collective-permute-start(bf16[640,1024]{1,0:T(8,128)(2,1)S(1)} %copy-done.46), channel_id=1, source_target_pairs={{0,1},{1,0},{2,3},{3,2},{4,5},{5,4},{6,7},{7,6},{8,9},{9,8},{10,11... | collective-permute-start | bytes 3932168 | tf_op jit(solution)/shard_map/ppermute | solution.py:442
  264.3 9.1 %collective-permute-start.33 = (bf16[640,128]{1,0:T(8,128)(2,1)S(1)}, bf16[640,128]{1,0:T(8,128)(2,1)S(1)}, u32[]{:S(2)}, u32[]{:S(2)}) collective-permute-start(bf16[640,128]{1,0:T(8,128)(2,1)S(1)} %get-tuple-element.215), channel_id=1, source_target_pairs={{0,3},{1,2},{2,1},{3,0},{4,7},{5,6},{6,5},{7,4},{8,11},{9,10},{10,... | collective-permute-start | bytes 491528 | tf_op jit(solution)/shard_map/ppermute | solution.py:442
  266.7 12.1 %collective-permute-start.27 = (bf16[640,128]{1,0:T(8,128)(2,1)}, bf16[640,128]{1,0:T(8,128)(2,1)}, u32[]{:S(2)}, u32[]{:S(2)}) collective-permute-start(bf16[640,128]{1,0:T(8,128)(2,1)} %get-tuple-element.220), channel_id=1, source_target_pairs={{0,1},{1,0},{2,3},{3,2},{4,5},{5,4},{6,7},{7,6},{8,9},{9,8},{10,11... | collective-permute-start | bytes 491528 | tf_op jit(solution)/shard_map/ppermute | solution.py:442
  268.6 10.2 %collective-permute-start.28 = (bf16[640,128]{1,0:T(8,128)(2,1)}, bf16[640,128]{1,0:T(8,128)(2,1)}, u32[]{:S(2)}, u32[]{:S(2)}) collective-permute-start(bf16[640,128]{1,0:T(8,128)(2,1)} %get-tuple-element.219), channel_id=1, source_target_pairs={{0,2},{1,3},{2,0},{3,1},{4,6},{5,7},{6,4},{7,5},{8,10},{9,11},{10,... | collective-permute-start | bytes 491528 | tf_op jit(solution)/shard_map/ppermute | solution.py:442
  273.4 6.4 %collective-permute-start.29 = (bf16[640,128]{1,0:T(8,128)(2,1)}, bf16[640,128]{1,0:T(8,128)(2,1)}, u32[]{:S(2)}, u32[]{:S(2)}) collective-permute-start(bf16[640,128]{1,0:T(8,128)(2,1)} %get-tuple-element.218), channel_id=1, source_target_pairs={{0,3},{1,2},{2,1},{3,0},{4,7},{5,6},{6,5},{7,4},{8,11},{9,10},{10,... | collective-permute-start | bytes 491528 | tf_op jit(solution)/shard_map/ppermute | solution.py:442
  278.8 47.1 %collective-permute-start.38 = (bf16[1024,256]{1,0:T(8,128)(2,1)}, bf16[1024,256]{1,0:T(8,128)(2,1)S(1)}, u32[]{:S(2)}, u32[]{:S(2)}) collective-permute-start(bf16[1024,256]{1,0:T(8,128)(2,1)} %get-tuple-element.190), channel_id=1, source_target_pairs={{0,1},{1,0},{2,3},{3,2},{4,5},{5,4},{6,7},{7,6},{8,9},{9,8},{10,11... | collective-permute-start | bytes 1572872 | tf_op jit(solution)/shard_map/ppermute | solution.py:442
  283.8 42.1 %collective-permute-start.36 = (bf16[640,1024]{1,0:T(8,128)(2,1)}, bf16[640,1024]{1,0:T(8,128)(2,1)}, u32[]{:S(2)}, u32[]{:S(2)}) collective-permute-start(bf16[640,1024]{1,0:T(8,128)(2,1)} %add_convert_fusion.2), channel_id=1, source_target_pairs={{0,2},{1,3},{2,0},{3,1},{4,6},{5,7},{6,4},{7,5},{8,10},{9,11},{10,... | collective-permute-start | bytes 3932168 | tf_op jit(solution)/shard_map/ppermute | solution.py:442
  285.1 40.7 %collective-permute-start.37 = (bf16[1024,256]{1,0:T(8,128)(2,1)}, bf16[1024,256]{1,0:T(8,128)(2,1)S(1)}, u32[]{:S(2)}, u32[]{:S(2)}) collective-permute-start(bf16[1024,256]{1,0:T(8,128)(2,1)} %add_convert_fusion.6), channel_id=1, source_target_pairs={{0,2},{1,3},{2,0},{3,1},{4,6},{5,7},{6,4},{7,5},{8,10},{9,11},{10,... | collective-permute-start | bytes 1572872 | tf_op jit(solution)/shard_map/ppermute | solution.py:442
  336.3 49.6 %collective-permute-start.39 = (bf16[512,640]{0,1:T(8,128)(2,1)}, bf16[512,640]{0,1:T(8,128)(2,1)}, u32[]{:S(2)}, u32[]{:S(2)}) collective-permute-start(bf16[512,640]{0,1:T(8,128)(2,1)} %fusion.21), channel_id=1, source_target_pairs={{0,4},{4,0},{8,12},{12,8},{16,20},{20,16},{24,28},{28,24},{1,5},{5... | collective-permute-start | bytes 1966088 | tf_op jit(solution)/shard_map/ppermute | solution.py:442
  385.2 13.7 %collective-permute-start.41 = (bf16[640,1024]{1,0:T(8,128)(2,1)}, bf16[640,1024]{1,0:T(8,128)(2,1)}, u32[]{:S(2)}, u32[]{:S(2)}) collective-permute-start(bf16[640,1024]{1,0:T(8,128)(2,1)} %get-tuple-element.152), channel_id=1, source_target_pairs={{0,1},{1,0},{2,3},{3,2},{4,5},{5,4},{6,7},{7,6},{8,9},{9,8},{10,11... | collective-permute-start | bytes 3932168 | tf_op jit(solution)/shard_map/ppermute | solution.py:442
  387.5 11.3 %collective-permute-start.40 = (bf16[256,640]{0,1:T(8,128)(2,1)S(1)}, bf16[256,640]{0,1:T(8,128)(2,1)S(1)}, u32[]{:S(2)}, u32[]{:S(2)}) collective-permute-start(bf16[256,640]{0,1:T(8,128)(2,1)S(1)} %constant_dynamic-slice_fusion.12), channel_id=1, source_target_pairs={{0,8},{4,12},{8,0},{12,4},{16,24},{20,28},{24,16},{28,20},{1,9},{5... | collective-permute-start | bytes 983048 | tf_op jit(solution)/shard_map/ppermute | solution.py:442
  390.7 26.7 %collective-permute-start.54 = (bf16[128,1536]{1,0:T(8,128)(2,1)}, bf16[128,1536]{1,0:T(8,128)(2,1)S(1)}, u32[]{:S(2)}, u32[]{:S(2)}) collective-permute-start(bf16[128,1536]{1,0:T(8,128)(2,1)} %reduce-scatter.3.cloned.1.call-done), channel_id=1, source_target_pairs={{0,2},{1,3},{2,0},{3,1},{4,6},{5,7},{6,4},{7,5},{8,10},{9,11},{10,... | collective-permute-start | bytes 1179656 | tf_op jit(solution)/shard_map/ppermute | solution.py:442
  401.6 13.0 %collective-permute-start.43 = (bf16[512,384]{0,1:T(8,128)(2,1)}, bf16[512,384]{0,1:T(8,128)(2,1)}, u32[]{:S(2)}, u32[]{:S(2)}) collective-permute-start(bf16[512,384]{0,1:T(8,128)(2,1)} %constant_dynamic-slice_fusion.10), channel_id=1, source_target_pairs={{0,4},{4,0},{8,12},{12,8},{16,20},{20,16},{24,28},{28,24},{1,5},{5... | collective-permute-start | bytes 1179656 | tf_op jit(solution)/shard_map/ppermute | solution.py:442
  403.4 12.3 %collective-permute-start.44 = (bf16[160,1024]{1,0:T(8,128)(2,1)S(1)}, bf16[160,1024]{1,0:T(8,128)(2,1)S(1)}, u32[]{:S(2)}, u32[]{:S(2)}) collective-permute-start(bf16[160,1024]{1,0:T(8,128)(2,1)S(1)} %get-tuple-element.209), channel_id=1, source_target_pairs={{0,2},{1,3},{2,0},{3,1},{4,6},{5,7},{6,4},{7,5},{8,10},{9,11},{10,... | collective-permute-start | bytes 983048 | tf_op jit(solution)/shard_map/ppermute | solution.py:442
  404.3 9.6 %collective-permute-start.42 = (bf16[128,640]{0,1:T(8,128)(2,1)S(1)}, bf16[128,640]{0,1:T(8,128)(2,1)S(1)}, u32[]{:S(2)}, u32[]{:S(2)}) collective-permute-start(bf16[128,640]{0,1:T(8,128)(2,1)S(1)} %constant_dynamic-slice_fusion.11), channel_id=1, source_target_pairs={{0,16},{4,20},{8,24},{12,28},{16,0},{20,4},{24,8},{28,12},{1,17},{... | collective-permute-start | bytes 491528 | tf_op jit(solution)/shard_map/ppermute | solution.py:442
  415.7 14.1 %collective-permute-start.46 = (bf16[640,1024]{1,0:T(8,128)(2,1)}, bf16[640,1024]{1,0:T(8,128)(2,1)}, u32[]{:S(2)}, u32[]{:S(2)}) collective-permute-start(bf16[640,1024]{1,0:T(8,128)(2,1)} %get-tuple-element.165), channel_id=1, source_target_pairs={{0,1},{1,0},{2,3},{3,2},{4,5},{5,4},{6,7},{7,6},{8,9},{9,8},{10,11... | collective-permute-start | bytes 3932168 | tf_op jit(solution)/shard_map/ppermute | solution.py:442
  422.5 6.4 %collective-permute-start.45 = (bf16[256,384]{0,1:T(8,128)(2,1)S(1)}, bf16[256,384]{0,1:T(8,128)(2,1)}, u32[]{:S(2)}, u32[]{:S(2)}) collective-permute-start(bf16[256,384]{0,1:T(8,128)(2,1)S(1)} %constant_dynamic-slice_fusion.9), channel_id=1, source_target_pairs={{0,8},{4,12},{8,0},{12,4},{16,24},{20,28},{24,16},{28,20},{1,9},{5... | collective-permute-start | bytes 589832 | tf_op jit(solution)/shard_map/ppermute | solution.py:442
  425.3 9.3 %collective-permute-start.47 = (bf16[160,1024]{1,0:T(8,128)(2,1)}, bf16[160,1024]{1,0:T(8,128)(2,1)S(1)}, u32[]{:S(2)}, u32[]{:S(2)}) collective-permute-start(bf16[160,1024]{1,0:T(8,128)(2,1)} %get-tuple-element.208), channel_id=1, source_target_pairs={{0,2},{1,3},{2,0},{3,1},{4,6},{5,7},{6,4},{7,5},{8,10},{9,11},{10,... | collective-permute-start | bytes 983048 | tf_op jit(solution)/shard_map/ppermute | solution.py:442
  436.9 14.6 %collective-permute-start.50 = (bf16[320,1024]{1,0:T(8,128)(2,1)S(1)}, bf16[320,1024]{1,0:T(8,128)(2,1)S(1)}, u32[]{:S(2)}, u32[]{:S(2)}) collective-permute-start(bf16[320,1024]{1,0:T(8,128)(2,1)S(1)} %slice.229), channel_id=1, source_target_pairs={{0,2},{1,3},{2,0},{3,1},{4,6},{5,7},{6,4},{7,5},{8,10},{9,11},{10,... | collective-permute-start | bytes 1966088 | tf_op jit(solution)/shard_map/ppermute | solution.py:442
  441.2 16.0 %collective-permute-start.49 = (bf16[128,1024]{0,1:T(8,128)(2,1)}, bf16[128,1024]{0,1:T(8,128)(2,1)}, u32[]{:S(2)}, u32[]{:S(2)}) collective-permute-start(bf16[128,1024]{0,1:T(8,128)(2,1)} %get-tuple-element.249), channel_id=1, source_target_pairs={{0,2},{1,3},{2,0},{3,1},{4,6},{5,7},{6,4},{7,5},{8,10},{9,11},{10,... | collective-permute-start | bytes 786440 | tf_op jit(solution)/shard_map/ppermute | solution.py:442
  448.0 18.2 %collective-permute-start.51 = (bf16[128,1024]{0,1:T(8,128)(2,1)}, bf16[128,1024]{0,1:T(8,128)(2,1)S(1)}, u32[]{:S(2)}, u32[]{:S(2)}) collective-permute-start(bf16[128,1024]{0,1:T(8,128)(2,1)} %get-tuple-element.249), channel_id=1, source_target_pairs={{0,1},{1,0},{2,3},{3,2},{4,5},{5,4},{6,7},{7,6},{8,9},{9,8},{10,11... | collective-permute-start | bytes 786440 | tf_op jit(solution)/shard_map/ppermute | solution.py:442
  457.2 8.5 %collective-permute-start.57 = (bf16[96,1024]{1,0:T(8,128)(2,1)}, bf16[96,1024]{1,0:T(8,128)(2,1)S(1)}, u32[]{:S(2)}, u32[]{:S(2)}) collective-permute-start(bf16[96,1024]{1,0:T(8,128)(2,1)} %reduce-scatter.5.cloned.1.call-done), channel_id=1, source_target_pairs={{0,2},{1,3},{2,0},{3,1},{4,6},{5,7},{6,4},{7,5},{8,10},{9,11},{10,... | collective-permute-start | bytes 589832 | tf_op jit(solution)/shard_map/ppermute | solution.py:442
  457.5 14.1 %collective-permute-start.56 = (bf16[96,1024]{1,0:T(8,128)(2,1)}, bf16[96,1024]{1,0:T(8,128)(2,1)S(1)}, u32[]{:S(2)}, u32[]{:S(2)}) collective-permute-start(bf16[96,1024]{1,0:T(8,128)(2,1)} %reduce-scatter.5.cloned.1.call-done), channel_id=1, source_target_pairs={{0,1},{1,0},{2,3},{3,2},{4,5},{5,4},{6,7},{7,6},{8,9},{9,8},{10,11... | collective-permute-start | bytes 589832 | tf_op jit(solution)/shard_map/ppermute | solution.py:442
  (65 other events, 402.0 us)
Sparse Core Ops, SparseCore 0:
  67.0 78.9 all-gather.1
  247.7 75.6 reduce-scatter.2
  326.9 63.9 reduce-scatter.4

commit v6 on v5

--- a/solution.py
+++ b/solution.py
@@ -567,7 +567,7 @@
     mlp_slice = jnp.concatenate([in_slice, fold_rows(mlp_out_slice, shard)], 1)
     mlp_weights = lax.all_gather(after((mlp_slice, qkv_weights))[0], "fsdp", axis=0, tiled=True)
     far_sections = swap_seq(after((sections, far_x))[0], half)
-    far_c_pieces = spread(swap_seq(after((own_cotangent, far_sections))[0], half))
+    far_c_pieces = spread(swap_seq(after((own_cotangent, far_x))[0], half))
 
     queries, keys, values, x_all = qkv_heads(
         far_x_pieces, qkv_weights, cosine, sine, fsdp_size, begun
@@ -576,10 +576,13 @@
     def row_pieces(array):
         return [array[k * positions : (k + 1) * positions] for k in range(seq_size)]
 
-    heads = [attend(after((queries, far_sections))[0], keys, values, 0)]
+    heads = [attend(queries, keys, values, 0)]
     group_pieces = [exchange_seq(row_pieces(heads[0][0]))]
     for group in range(1, groups):
-        heads.append(attend(after((queries, far_c_pieces[0], heads[0]))[0], keys, values, group))
+        late_queries, _, far_sections, _ = after(
+            (queries, far_c_pieces[0], far_sections, heads[0])
+        )
+        heads.append(attend(late_queries, keys, values, group))
         group_pieces.append(exchange_seq(row_pieces(heads[group][0])))
     attn_out_full = jnp.concatenate(by_member(spread(sections) + spread(far_sections)), 1)
     attended_pieces = [jnp.concatenate(pieces, 1) for pieces in zip(*group_pieces)]

time: 486 us -> 485 us (level)
  waiting for transfers between devices: 87.2 us -> 81.1 us
  local copies, waits for them, and re-layouts: 29.6 us -> 35.2 us
    ppermute x59, waiting for transfers between devices: 87.2 us -> 81 us  [swap(): return lax.ppermute(values, axis, [(i, i ^ offset) for i in range(size)])]
    unnamed x152, local copies, waits for them, and re-layouts: 15.2 us -> 20.1 us
  transfers between devices with their start and end apart: 62 -> 62, of which waited for: 25 -> 27; matrix products, arithmetic and copies ran while one was open for 25% -> 26% of each run, Pallas kernels for 33% -> 33%
where the time goes in v6:
time: 485 us; the launch traced here: 480 us
  Pallas kernels  182 us (38%)
  waiting for transfers between devices  81.1 us (17%)
  other arithmetic  66.2 us (14%)
  starting transfers between devices  61.6 us (13%)
  matrix products  38.2 us (8%)
  local copies, waits for them, and re-layouts  35.2 us (7%)
  between operations  15.3 us (3%)
    ppermute x59, waiting for transfers between devices, swap(): return lax.ppermute(values, axis, [(i, i ^ offset) for i in range(size)])  81 us
    pallas_call x2, Pallas kernels, attend_back(): pl.pallas_call(attend_back_body, grid=(rows // step,), in_specs=[q_spec,...  75 us
    ppermute x59, starting transfers between devices, swap(): return lax.ppermute(values, axis, [(i, i ^ offset) for i in range(size)])  61.2 us
    pallas_call x2, Pallas kernels, mlp(): pl.pallas_call(functools.partial(mlp_body, count, steps, blocks, units),...  43.6 us
    pallas_call x2, Pallas kernels, attend(): pl.pallas_call(attend_body, grid=(rows // step,), in_specs=[q_spec, k_spe...  36.4 us
    dot_general x5, matrix products, dot_tn(): lax.dot_general(a, b, (((0,), (0,)), ((), ())), preferred_element_type=F32)  35 us
    unnamed x152, local copies, waits for them, and re-layouts  20.1 us
    pallas_call x2, Pallas kernels, qkv_heads(): pl.pallas_call(functools.partial(qkv_body, blocks, count, steps), grid=(c...  13.9 us
  transfers between devices with their start and end apart: 62, of which 27 were waited for; matrix products, arithmetic and copies ran while one was open for 26% of the time, Pallas kernels for 33%

profile of v6, /device:TPU:1, one launch (start us, length us, event | category | flops | bytes accessed | tf_op | source)
XLA Modules:
  0.0 479.8 jit_solution(10102140044625143264)
XLA Ops:
  10.9 2.7 collective-permute-start
  19.0 2.3 collective-permute-start.2
  24.7 5.9 %collective-permute-done.2 = bf16[128,768]{1,0:T(8,128)(2,1)} collective-permute-done((bf16[128,768]{1,0:T(8,128)(2,1)}, bf16[128,768]{1,0:T(8,128)(2,1)}, u32[]{:S(2)}, u32[]{:S(2)}) %collective-permute-start.2) | collective-permute-done | bytes 196640 | tf_op jit(solution)/shard_map/ppermute | solution.py:442
  32.9 3.1 collective-permute-start.7
  36.3 6.0 %collective-permute-done.7 = bf16[128,256]{1,0:T(8,128)(2,1)S(1)} collective-permute-done((bf16[128,256]{1,0:T(8,128)(2,1)S(1)}, bf16[128,256]{1,0:T(8,128)(2,1)S(1)}, u32[]{:S(2)}, u32[]{:S(2)}) %collective-permute-start.7) | collective-permute-done | bytes 65568 | tf_op jit(solution)/shard_map/ppermute | solution.py:442
  44.4 3.6 collective-permute-start.8
  48.0 7.3 %select_multiply_fusion = (f32[2560,128]{1,0:T(8,128)}, f32[2560,128]{1,0:T(8,128)}) fusion(s32[128]{0:T(128)S(1)} %get-tuple-element.266, s32[128]{0:T(128)S(1)} %get-tuple-element.268, s32[128]{0:T(128)S(1)} %get-tuple-element.267, s32[128]{0:T(128)S(1)} %get-tuple-element.269, s32[2560]{0:T(1024)S(1)} %get-tuple-element.263, ...), kind=kLoop, calls=%fused_computation.56 | loop fusion | flops 4587520 | bytes 2669828 | tf_op jit(solution)/shard_map/mul | solution.py:543
  55.4 4.8 %collective-permute-done.4 = bf16[512,768]{1,0:T(8,128)(2,1)S(1)} collective-permute-done((bf16[512,768]{1,0:T(8,128)(2,1)S(1)}, bf16[512,768]{1,0:T(8,128)(2,1)S(1)}, u32[]{:S(2)}, u32[]{:S(2)}) %collective-permute-start.4) | collective-permute-done | bytes 786464 | tf_op jit(solution)/shard_map/ppermute | solution.py:442
  64.0 3.4 collective-permute-start.1
  67.7 6.9 %qkv_rope.2 = (bf16[2560,256]{1,0:T(8,128)(2,1)}, bf16[2560,256]{1,0:T(8,128)(2,1)}, bf16[2560,256]{1,0:T(8,128)(2,1)}, bf16[2560,1024]{1,0:T(8,128)(2,1)}) custom-call(bf16[640,1024]{1,0:T(8,128)(2,1)} %fusion.6.refs_0_, bf16[640,1024]{1,0:T(8,128)(2,1)} %collective-permute-done.5.refs_1_, bf16[1024,768]{1,0:T(8,128)(2,1)} %pad_maximum_fusion.4.refs_2_, ...), custom_call_target="tpu_custom_call" | custom-call | flops 2013265920 | bytes 8781824 | tf_op jit(solution)/shard_map/qkv_rope/pallas_call | solution.py:141
  77.1 7.1 %qkv_rope.3 = (bf16[2560,256]{1,0:T(8,128)(2,1)}, bf16[2560,256]{1,0:T(8,128)(2,1)}, bf16[2560,256]{1,0:T(8,128)(2,1)}, bf16[2560,1024]{1,0:T(8,128)(2,1)}) custom-call(bf16[640,1024]{1,0:T(8,128)(2,1)} %collective-permute-done.refs_0_, bf16[640,1024]{1,0:T(8,128)(2,1)} %copy-done.22, ...), custom_call_target="tpu_custom_call", output_to_operand_aliasing={{0}: (5, {}), {1}: (6, {}), {2}: (7, {}), {3}: (8, {})} | custom-call | flops 2013265920 | bytes 8781824 | tf_op jit(solution)/shard_map/qkv_rope/pallas_call | solution.py:141
  84.2 18.0 %attend.2 = (bf16[2560,128]{1,0:T(8,128)(2,1)}, f32[128,2560]{1,0:T(8,128)}) custom-call(bf16[2560,256]{1,0:T(8,128)(2,1)} %get-tuple-element.111.q_ref, bf16[2560,256]{1,0:T(8,128)(2,1)} %get-tuple-element.101.k_ref, bf16[2560,256]{1,0:T(8,128)(2,1)} %get-tuple-element.102.v_ref), custom_call_target="tpu_custom_call" | custom-call | flops 13421772800 | bytes 2621440 | tf_op jit(solution)/shard_map/attend/pallas_call | solution.py:196
  104.3 4.0 collective-permute-start.11
  108.3 18.4 %attend.3 = (bf16[2560,128]{1,0:T(8,128)(2,1)}, f32[128,2560]{1,0:T(8,128)}) custom-call(bf16[2560,256]{1,0:T(8,128)(2,1)} %get-tuple-element.111.q_ref, bf16[2560,256]{1,0:T(8,128)(2,1)} %get-tuple-element.101.k_ref, bf16[2560,256]{1,0:T(8,128)(2,1)} %get-tuple-element.102.v_ref), custom_call_target="tpu_custom_call" | custom-call | flops 13421772800 | bytes 2621440 | tf_op jit(solution)/shard_map/attend/pallas_call | solution.py:196
  132.5 3.1 collective-permute-done.13
  143.8 2.8 collective-permute-done.16
  157.3 21.9 %mlp.2 = (bf16[2560,768]{1,0:T(8,128)(2,1)}, bf16[2560,1536]{1,0:T(8,128)(2,1)}, bf16[2560,1024]{1,0:T(8,128)(2,1)}, bf16[2560,1024]{1,0:T(8,128)(2,1)}, bf16[64...) custom-call(bf16[640,1024]{1,0:T(8,128)(2,1)} %fusion.14.refs_0_, ...), custom_call_target="tpu_custom_call" | custom-call | flops 12079595520 | bytes 26345472 | tf_op jit(solution)/shard_map/mlp/pallas_call | solution.py:362
  179.2 5.4 %collective-permute-done.22.refs_0_ = bf16[640,1024]{1,0:T(8,128)(2,1)} collective-permute-done((bf16[640,1024]{1,0:T(8,128)(2,1)}, bf16[640,1024]{1,0:T(8,128)(2,1)}, u32[]{:S(2)}, u32[]{:S(2)}) %collective-permute-start.22) | collective-permute-done | bytes 1310752 | tf_op jit(solution)/shard_map/ppermute | solution.py:442
  185.7 3.0 collective-permute-done.23.refs_1_
  188.7 21.7 %mlp.3 = (bf16[2560,768]{1,0:T(8,128)(2,1)}, bf16[2560,1536]{1,0:T(8,128)(2,1)}, bf16[2560,1024]{1,0:T(8,128)(2,1)}, bf16[2560,1024]{1,0:T(8,128)(2,1)}, bf16[64...) custom-call(bf16[640,1024]{1,0:T(8,128)(2,1)} %collective-permute-do, ...), custom_call_target="tpu_custom_call", output_to_operand_aliasing={{0}: (5, {}), {1}: (6, {}), {2}: (7, {}), {3}: (8, {})} | custom-call | flops 12079595520 | bytes 26345472 | tf_op jit(solution)/shard_map/mlp/pallas_call | solution.py:362
  210.9 2.9 collective-permute-done.25
  213.7 2.9 add_convert_fusion.3
  217.0 13.8 %convolution_convert_fusion = bf16[1024,1536]{1,0:T(8,128)(2,1)} fusion(bf16[2560,1024]{1,0:T(8,128)(2,1)} %get-tuple-element.130, bf16[2560,1536]{1,0:T(8,128)(2,1)} %get-tuple-element.131), kind=kOutput, calls=%fused_computation | convolution fusion | flops 8054636544 | bytes 16252928 | tf_op jit(solution)/shard_map/dot_general | solution.py:32
  230.8 9.2 %convolution_convert_fusion.2 = bf16[768,1024]{1,0:T(8,128)(2,1)} fusion(bf16[2560,768]{1,0:T(8,128)(2,1)} %get-tuple-element.128, bf16[2560,1024]{1,0:T(8,128)(2,1)} %get-tuple-element.129), kind=kOutput, calls=%fused_computation.40 | convolution fusion | flops 4027318272 | bytes 10747904 | tf_op jit(solution)/shard_map/dot_general | solution.py:32
  240.0 6.9 %collective-permute-done.26 = bf16[640,1024]{1,0:T(8,128)(2,1)} collective-permute-done((bf16[640,1024]{1,0:T(8,128)(2,1)}, bf16[640,1024]{1,0:T(8,128)(2,1)}, u32[]{:S(2)}, u32[]{:S(2)}) %collective-permute-start.26) | collective-permute-done | bytes 1310752 | tf_op jit(solution)/shard_map/ppermute | solution.py:442
  256.0 3.4 multiply_add_fusion
  268.6 4.2 collective-permute-done.33
  284.6 37.4 %attend_back.2.refs_0_ = bf16[2560,384]{1,0:T(8,128)(2,1)} custom-call(bf16[2560,256]{1,0:T(8,128)(2,1)} %get-tuple-element.111.q_ref, bf16[2560,256]{1,0:T(8,128)(2,1)} %get-tuple-element.101.k_ref, bf16[2560,256]{1,0:T(8,128)(2,1)} %get-tuple-element.102.v_ref, bf16[2560,128]{1,0:T(8,128)(2,1)} %pad_maximum_fusion.17.g_ref, ...), custom_call_target="tpu_custom_call" | custom-call | flops 33554432000 | bytes 6553600 | tf_op jit(solution)/shard_map/attend_back/pallas_call | solution.py:268
  322.0 3.3 collective-permute-done.37
  328.5 5.3 %convolution_convert_fusion.5 = bf16[1024,384]{0,1:T(8,128)(2,1)S(1)} fusion(bf16[2560,1024]{1,0:T(8,128)(2,1)} %get-tuple-element.143, bf16[2560,384]{1,0:T(8,128)(2,1)} %attend_back.2.refs_0_), kind=kOutput, calls=%fused_computation.49 | convolution fusion | flops 2013659136 | bytes 7995392 | tf_op jit(solution)/shard_map/dot_general | solution.py:32
  336.3 3.7 add_convert_fusion.1
  340.0 37.6 %attend_back.3.refs_1_ = bf16[2560,384]{1,0:T(8,128)(2,1)} custom-call(bf16[2560,256]{1,0:T(8,128)(2,1)} %get-tuple-element.111.q_ref, bf16[2560,256]{1,0:T(8,128)(2,1)} %get-tuple-element.101.k_ref, bf16[2560,256]{1,0:T(8,128)(2,1)} %get-tuple-element.102.v_ref, bf16[2560,128]{1,0:T(8,128)(2,1)} %pad_maximum_fusion.16.g_ref, ...), custom_call_target="tpu_custom_call" | custom-call | flops 33554432000 | bytes 6553600 | tf_op jit(solution)/shard_map/attend_back/pallas_call | solution.py:268
  377.6 6.6 %token_grad.2 = (bf16[640,1024]{1,0:T(8,128)(2,1)}, bf16[640,1024]{1,0:T(8,128)(2,1)}) custom-call(bf16[2560,384]{1,0:T(8,128)(2,1)} %attend_back.2.refs_0_, bf16[2560,384]{1,0:T(8,128)(2,1)} %attend_back.3.refs_1_, bf16[1024,768]{1,0:T(8,128)(2,1)} %pad_maximum_fusion.4.refs_2_), custom_call_target="tpu_custom_call" | custom-call | flops 2013265920 | bytes 6160384 | tf_op jit(solution)/shard_map/token_grad/pallas_call | solution.py:408
  386.3 4.7 collective-permute-start.40
  391.3 4.8 %convolution_convert_fusion.4 = bf16[1024,384]{0,1:T(8,128)(2,1)S(1)} fusion(bf16[2560,1024]{1,0:T(8,128)(2,1)} %get-tuple-element.143, bf16[2560,384]{1,0:T(8,128)(2,1)S(1)} %copy-done.50), kind=kOutput, calls=%fused_computation.48 | convolution fusion | flops 2013659136 | bytes 7995392 | tf_op jit(solution)/shard_map/dot_general | solution.py:32
  396.2 2.8 collective-permute-done.40
  404.9 6.6 %token_grad.3 = (bf16[640,1024]{1,0:T(8,128)(2,1)}, bf16[640,1024]{1,0:T(8,128)(2,1)}) custom-call(bf16[2560,384]{1,0:T(8,128)(2,1)} %attend_back.2.refs_0_, bf16[2560,384]{1,0:T(8,128)(2,1)} %attend_back.3.refs_1_, bf16[1024,768]{1,0:T(8,128)(2,1)} %pad_maximum_fusion.4.refs_2_), custom_call_target="tpu_custom_call" | custom-call | flops 2013265920 | bytes 6160384 | tf_op jit(solution)/shard_map/token_grad/pallas_call | solution.py:408
  417.6 3.4 collective-permute-done.53
  425.9 2.6 collective-permute-done.45
  429.5 3.8 convert_add_fusion.1
  437.3 2.8 collective-permute-done.48
  441.7 2.7 convert_multiply_fusion
  444.5 3.4 copy.40
  447.9 2.7 collective-permute-start.51
  450.8 5.7 %collective-permute-done.49 = bf16[128,1024]{0,1:T(8,128)(2,1)} collective-permute-done((bf16[128,1024]{0,1:T(8,128)(2,1)}, bf16[128,1024]{0,1:T(8,128)(2,1)}, u32[]{:S(2)}, u32[]{:S(2)}) %collective-permute-start.49) | collective-permute-done | bytes 262176 | tf_op jit(solution)/shard_map/ppermute | solution.py:442
  457.6 2.9 collective-permute-start.56
  460.5 2.7 fusion.33
  463.2 2.5 fusion.16
  (362 shorter events, 121.6 us)
Async XLA Ops:
  7.2 150.1 %all-gather.2.cloned.1.call-start = ((), (), s32[]{:S(2)}) async-start(), calls=%async_computation.2 | async-start | bytes 5308416 | tf_op jit(solution)/shard_map/all_gather | solution.py:568
  10.9 56.8 %collective-permute-start.5 = (bf16[640,1024]{1,0:T(8,128)(2,1)}, bf16[640,1024]{1,0:T(8,128)(2,1)}, u32[]{:S(2)}, u32[]{:S(2)}) collective-permute-start(bf16[640,1024]{1,0:T(8,128)(2,1)} %fusion.6.refs_0_), channel_id=1, source_target_pairs={{0,1},{1,0},{2,3},{3,2},{4,5},{5,4},{6,7},{7,6},{8,9},{9,8},{10,11... | collective-permute-start | bytes 3932168 | tf_op jit(solution)/shard_map/ppermute | solution.py:442
  10.9 52.8 %collective-permute-start = (bf16[640,1024]{1,0:T(8,128)(2,1)}, bf16[640,1024]{1,0:T(8,128)(2,1)}, u32[]{:S(2)}, u32[]{:S(2)}) collective-permute-start(bf16[640,1024]{1,0:T(8,128)(2,1)} %fusion.6.refs_0_), channel_id=1, source_target_pairs={{0,2},{1,3},{2,0},{3,1},{4,6},{5,7},{6,4},{7,5},{8,10},{9,11},{10,... | collective-permute-start | bytes 3932168 | tf_op jit(solution)/shard_map/ppermute | solution.py:442
  19.0 11.6 %collective-permute-start.2 = (bf16[128,768]{1,0:T(8,128)(2,1)}, bf16[128,768]{1,0:T(8,128)(2,1)}, u32[]{:S(2)}, u32[]{:S(2)}) collective-permute-start(bf16[128,768]{1,0:T(8,128)(2,1)} %multiply_convert_fusion.1), channel_id=1, source_target_pairs={{0,16},{4,20},{8,24},{12,28},{16,0},{20,4},{24,8},{28,12},{1,17},{... | collective-permute-start | bytes 589832 | tf_op jit(solution)/shard_map/ppermute | solution.py:442
  31.8 11.1 %collective-permute-start.3 = (bf16[256,768]{1,0:T(8,128)(2,1)S(1)}, bf16[256,768]{1,0:T(8,128)(2,1)S(1)}, u32[]{:S(2)}, u32[]{:S(2)}) collective-permute-start(bf16[256,768]{1,0:T(8,128)(2,1)S(1)} %pad_maximum_fusion.19), channel_id=1, source_target_pairs={{0,8},{4,12},{8,0},{12,4},{16,24},{20,28},{24,16},{28,20},{1,9},{5... | collective-permute-start | bytes 1179656 | tf_op jit(solution)/shard_map/ppermute | solution.py:442
  32.9 9.4 %collective-permute-start.7 = (bf16[128,256]{1,0:T(8,128)(2,1)S(1)}, bf16[128,256]{1,0:T(8,128)(2,1)S(1)}, u32[]{:S(2)}, u32[]{:S(2)}) collective-permute-start(bf16[128,256]{1,0:T(8,128)(2,1)S(1)} %constant_dynamic-slice_fusion.19), channel_id=1, source_target_pairs={{0,16},{4,20},{8,24},{12,28},{16,0},{20,4},{24,8},{28,12},{1,17},{... | collective-permute-start | bytes 196616 | tf_op jit(solution)/shard_map/ppermute | solution.py:442
  43.1 17.2 %collective-permute-start.4 = (bf16[512,768]{1,0:T(8,128)(2,1)S(1)}, bf16[512,768]{1,0:T(8,128)(2,1)S(1)}, u32[]{:S(2)}, u32[]{:S(2)}) collective-permute-start(bf16[512,768]{1,0:T(8,128)(2,1)S(1)} %pad_maximum_fusion.11), channel_id=1, source_target_pairs={{0,4},{4,0},{8,12},{12,8},{16,20},{20,16},{24,28},{28,24},{1,5},{5... | collective-permute-start | bytes 2359304 | tf_op jit(solution)/shard_map/ppermute | solution.py:442
  44.4 11.0 %collective-permute-start.8 = (bf16[256,256]{1,0:T(8,128)(2,1)S(1)}, bf16[256,256]{1,0:T(8,128)(2,1)S(1)}, u32[]{:S(2)}, u32[]{:S(2)}) collective-permute-start(bf16[256,256]{1,0:T(8,128)(2,1)S(1)} %pad_maximum_fusion.24), channel_id=1, source_target_pairs={{0,8},{4,12},{8,0},{12,4},{16,24},{20,28},{24,16},{28,20},{1,9},{5... | collective-permute-start | bytes 393224 | tf_op jit(solution)/shard_map/ppermute | solution.py:442
  61.6 13.0 %collective-permute-start.9 = (bf16[512,256]{1,0:T(8,128)(2,1)S(1)}, bf16[512,256]{1,0:T(8,128)(2,1)S(1)}, u32[]{:S(2)}, u32[]{:S(2)}) collective-permute-start(bf16[512,256]{1,0:T(8,128)(2,1)S(1)} %pad_maximum_fusion.22), channel_id=1, source_target_pairs={{0,4},{4,0},{8,12},{12,8},{16,20},{20,16},{24,28},{28,24},{1,5},{5... | collective-permute-start | bytes 786440 | tf_op jit(solution)/shard_map/ppermute | solution.py:442
  63.7 38.6 %collective-permute-start.6 = (bf16[640,1024]{1,0:T(8,128)(2,1)}, bf16[640,1024]{1,0:T(8,128)(2,1)}, u32[]{:S(2)}, u32[]{:S(2)}) collective-permute-start(bf16[640,1024]{1,0:T(8,128)(2,1)} %bitcast.refs_2_), channel_id=1, source_target_pairs={{0,2},{1,3},{2,0},{3,1},{4,6},{5,7},{6,4},{7,5},{8,10},{9,11},{10,... | collective-permute-start | bytes 3932168 | tf_op jit(solution)/shard_map/ppermute | solution.py:442
  64.0 12.1 %collective-permute-start.1 = (bf16[640,1024]{1,0:T(8,128)(2,1)}, bf16[640,1024]{1,0:T(8,128)(2,1)S(1)}, u32[]{:S(2)}, u32[]{:S(2)}) collective-permute-start(bf16[640,1024]{1,0:T(8,128)(2,1)} %collective-permute-done.refs_0_), channel_id=1, source_target_pairs={{0,1},{1,0},{2,3},{3,2},{4,5},{5,4},{6,7},{7,6},{8,9},{9,8},{10,11... | collective-permute-start | bytes 3932168 | tf_op jit(solution)/shard_map/ppermute | solution.py:442
  67.4 272.6 %reduce-scatter.3.cloned.1.call-start = ((), (), s32[]{:S(2)}) async-start(), calls=%async_computation.3 | async-start | bytes 3538944 | tf_op jit(solution)/shard_map/reduce_scatter | solution.py:495
  74.8 27.5 %collective-permute-start.10 = (bf16[1024,256]{1,0:T(8,128)(2,1)S(1)}, bf16[1024,256]{1,0:T(8,128)(2,1)S(1)}, u32[]{:S(2)}, u32[]{:S(2)}) collective-permute-start(bf16[1024,256]{1,0:T(8,128)(2,1)S(1)} %constant_dynamic-update-slice_fusion.6), channel_id=1, source_target_pairs={{0,2},{1,3},{2,0},{3,1},{4,6},{5,7},{6,4},{7,5},{8,10},{9,11},{10,... | collective-permute-start | bytes 1572872 | tf_op jit(solution)/shard_map/ppermute | solution.py:442
  104.3 25.5 %collective-permute-start.11 = (bf16[640,128]{1,0:T(8,128)(2,1)S(1)}, bf16[640,128]{1,0:T(8,128)(2,1)S(1)}, u32[]{:S(2)}, u32[]{:S(2)}) collective-permute-start(bf16[640,128]{1,0:T(8,128)(2,1)S(1)} %get-tuple-element.238), channel_id=1, source_target_pairs={{0,1},{1,0},{2,3},{3,2},{4,5},{5,4},{6,7},{7,6},{8,9},{9,8},{10,11... | collective-permute-start | bytes 491528 | tf_op jit(solution)/shard_map/ppermute | solution.py:442
  128.7 26.4 %collective-permute-start.20 = (bf16[640,1024]{1,0:T(8,128)(2,1)}, bf16[640,1024]{1,0:T(8,128)(2,1)}, u32[]{:S(2)}, u32[]{:S(2)}) collective-permute-start(bf16[640,1024]{1,0:T(8,128)(2,1)} %bitcast.refs_2_), channel_id=1, source_target_pairs={{0,1},{1,0},{2,3},{3,2},{4,5},{5,4},{6,7},{7,6},{8,9},{9,8},{10,11... | collective-permute-start | bytes 3932168 | tf_op jit(solution)/shard_map/ppermute | solution.py:442
  129.2 18.1 %collective-permute-start.17 = (bf16[1024,256]{1,0:T(8,128)(2,1)S(1)}, bf16[1024,256]{1,0:T(8,128)(2,1)S(1)}, u32[]{:S(2)}, u32[]{:S(2)}) collective-permute-start(bf16[1024,256]{1,0:T(8,128)(2,1)S(1)} %constant_dynamic-update-slice_fusion.6), channel_id=1, source_target_pairs={{0,1},{1,0},{2,3},{3,2},{4,5},{5,4},{6,7},{7,6},{8,9},{9,8},{10,11... | collective-permute-start | bytes 1572872 | tf_op jit(solution)/shard_map/ppermute | solution.py:442
  129.3 18.0 %collective-permute-start.18 = (bf16[1024,256]{1,0:T(8,128)(2,1)S(1)}, bf16[1024,256]{1,0:T(8,128)(2,1)S(1)}, u32[]{:S(2)}, u32[]{:S(2)}) collective-permute-start(bf16[1024,256]{1,0:T(8,128)(2,1)S(1)} %collective-permute-done.10), channel_id=1, source_target_pairs={{0,1},{1,0},{2,3},{3,2},{4,5},{5,4},{6,7},{7,6},{8,9},{9,8},{10,11... | collective-permute-start | bytes 1572872 | tf_op jit(solution)/shard_map/ppermute | solution.py:442
  130.8 8.3 %collective-permute-start.14 = (bf16[640,128]{1,0:T(8,128)(2,1)S(1)}, bf16[640,128]{1,0:T(8,128)(2,1)S(1)}, u32[]{:S(2)}, u32[]{:S(2)}) collective-permute-start(bf16[640,128]{1,0:T(8,128)(2,1)S(1)} %get-tuple-element.242), channel_id=1, source_target_pairs={{0,2},{1,3},{2,0},{3,1},{4,6},{5,7},{6,4},{7,5},{8,10},{9,11},{10,... | collective-permute-start | bytes 491528 | tf_op jit(solution)/shard_map/ppermute | solution.py:442
  135.6 7.5 %collective-permute-start.15 = (bf16[640,128]{1,0:T(8,128)(2,1)S(1)}, bf16[640,128]{1,0:T(8,128)(2,1)S(1)}, u32[]{:S(2)}, u32[]{:S(2)}) collective-permute-start(bf16[640,128]{1,0:T(8,128)(2,1)S(1)} %get-tuple-element.236), channel_id=1, source_target_pairs={{0,3},{1,2},{2,1},{3,0},{4,7},{5,6},{6,5},{7,4},{8,11},{9,10},{10,... | collective-permute-start | bytes 491528 | tf_op jit(solution)/shard_map/ppermute | solution.py:442
  139.1 7.5 %collective-permute-start.16 = (bf16[640,128]{1,0:T(8,128)(2,1)S(1)}, bf16[640,128]{1,0:T(8,128)(2,1)S(1)}, u32[]{:S(2)}, u32[]{:S(2)}) collective-permute-start(bf16[640,128]{1,0:T(8,128)(2,1)S(1)} %get-tuple-element.241), channel_id=1, source_target_pairs={{0,3},{1,2},{2,1},{3,0},{4,7},{5,6},{6,5},{7,4},{8,11},{9,10},{10,... | collective-permute-start | bytes 491528 | tf_op jit(solution)/shard_map/ppermute | solution.py:442
  154.2 30.4 %collective-permute-start.22 = (bf16[640,1024]{1,0:T(8,128)(2,1)}, bf16[640,1024]{1,0:T(8,128)(2,1)}, u32[]{:S(2)}, u32[]{:S(2)}) collective-permute-start(bf16[640,1024]{1,0:T(8,128)(2,1)} %fusion.14.refs_0_), channel_id=1, source_target_pairs={{0,2},{1,3},{2,0},{3,1},{4,6},{5,7},{6,4},{7,5},{8,10},{9,11},{10,... | collective-permute-start | bytes 3932168 | tf_op jit(solution)/shard_map/ppermute | solution.py:442
  154.5 31.2 %collective-permute-start.24 = (bf16[640,1024]{1,0:T(8,128)(2,1)}, bf16[640,1024]{1,0:T(8,128)(2,1)}, u32[]{:S(2)}, u32[]{:S(2)}) collective-permute-start(bf16[640,1024]{1,0:T(8,128)(2,1)} %collective-permute-done.6.refs_2_), channel_id=1, source_target_pairs={{0,1},{1,0},{2,3},{3,2},{4,5},{5,4},{6,7},{7,6},{8,9},{9,8},{10,11... | collective-permute-start | bytes 3932168 | tf_op jit(solution)/shard_map/ppermute | solution.py:442
  216.7 30.3 %collective-permute-start.26 = (bf16[640,1024]{1,0:T(8,128)(2,1)}, bf16[640,1024]{1,0:T(8,128)(2,1)}, u32[]{:S(2)}, u32[]{:S(2)}) collective-permute-start(bf16[640,1024]{1,0:T(8,128)(2,1)} %add_convert_fusion.3), channel_id=1, source_target_pairs={{0,2},{1,3},{2,0},{3,1},{4,6},{5,7},{6,4},{7,5},{8,10},{9,11},{10,... | collective-permute-start | bytes 3932168 | tf_op jit(solution)/shard_map/ppermute | solution.py:442
  247.0 154.0 %reduce-scatter.5.cloned.1.call-start = ((), (), s32[]{:S(2)}) async-start(), calls=%async_computation.4 | async-start | bytes 1769472 | tf_op jit(solution)/shard_map/reduce_scatter | solution.py:495
  251.3 84.6 %collective-permute-start.30 = (bf16[640,1024]{1,0:T(8,128)(2,1)}, bf16[640,1024]{1,0:T(8,128)(2,1)}, u32[]{:S(2)}, u32[]{:S(2)}) collective-permute-start(bf16[640,1024]{1,0:T(8,128)(2,1)} %get-tuple-element.134), channel_id=1, source_target_pairs={{0,1},{1,0},{2,3},{3,2},{4,5},{5,4},{6,7},{7,6},{8,9},{9,8},{10,11... | collective-permute-start | bytes 3932168 | tf_op jit(solution)/shard_map/ppermute | solution.py:442
  251.4 23.4 %collective-permute-start.34 = (bf16[640,1024]{1,0:T(8,128)(2,1)S(1)}, bf16[640,1024]{1,0:T(8,128)(2,1)S(1)}, u32[]{:S(2)}, u32[]{:S(2)}) collective-permute-start(bf16[640,1024]{1,0:T(8,128)(2,1)S(1)} %copy-done.46), channel_id=1, source_target_pairs={{0,1},{1,0},{2,3},{3,2},{4,5},{5,4},{6,7},{7,6},{8,9},{9,8},{10,11... | collective-permute-start | bytes 3932168 | tf_op jit(solution)/shard_map/ppermute | solution.py:442
  262.8 10.0 %collective-permute-start.33 = (bf16[640,128]{1,0:T(8,128)(2,1)S(1)}, bf16[640,128]{1,0:T(8,128)(2,1)S(1)}, u32[]{:S(2)}, u32[]{:S(2)}) collective-permute-start(bf16[640,128]{1,0:T(8,128)(2,1)S(1)} %get-tuple-element.215), channel_id=1, source_target_pairs={{0,3},{1,2},{2,1},{3,0},{4,7},{5,6},{6,5},{7,4},{8,11},{9,10},{10,... | collective-permute-start | bytes 491528 | tf_op jit(solution)/shard_map/ppermute | solution.py:442
  266.1 11.1 %collective-permute-start.27 = (bf16[640,128]{1,0:T(8,128)(2,1)}, bf16[640,128]{1,0:T(8,128)(2,1)}, u32[]{:S(2)}, u32[]{:S(2)}) collective-permute-start(bf16[640,128]{1,0:T(8,128)(2,1)} %get-tuple-element.220), channel_id=1, source_target_pairs={{0,1},{1,0},{2,3},{3,2},{4,5},{5,4},{6,7},{7,6},{8,9},{9,8},{10,11... | collective-permute-start | bytes 491528 | tf_op jit(solution)/shard_map/ppermute | solution.py:442
  268.0 9.2 %collective-permute-start.28 = (bf16[640,128]{1,0:T(8,128)(2,1)}, bf16[640,128]{1,0:T(8,128)(2,1)}, u32[]{:S(2)}, u32[]{:S(2)}) collective-permute-start(bf16[640,128]{1,0:T(8,128)(2,1)} %get-tuple-element.219), channel_id=1, source_target_pairs={{0,2},{1,3},{2,0},{3,1},{4,6},{5,7},{6,4},{7,5},{8,10},{9,11},{10,... | collective-permute-start | bytes 491528 | tf_op jit(solution)/shard_map/ppermute | solution.py:442
  272.8 6.4 %collective-permute-start.29 = (bf16[640,128]{1,0:T(8,128)(2,1)}, bf16[640,128]{1,0:T(8,128)(2,1)}, u32[]{:S(2)}, u32[]{:S(2)}) collective-permute-start(bf16[640,128]{1,0:T(8,128)(2,1)} %get-tuple-element.218), channel_id=1, source_target_pairs={{0,3},{1,2},{2,1},{3,0},{4,7},{5,6},{6,5},{7,4},{8,11},{9,10},{10,... | collective-permute-start | bytes 491528 | tf_op jit(solution)/shard_map/ppermute | solution.py:442
  277.1 48.1 %collective-permute-start.38 = (bf16[1024,256]{1,0:T(8,128)(2,1)}, bf16[1024,256]{1,0:T(8,128)(2,1)S(1)}, u32[]{:S(2)}, u32[]{:S(2)}) collective-permute-start(bf16[1024,256]{1,0:T(8,128)(2,1)} %get-tuple-element.190), channel_id=1, source_target_pairs={{0,1},{1,0},{2,3},{3,2},{4,5},{5,4},{6,7},{7,6},{8,9},{9,8},{10,11... | collective-permute-start | bytes 1572872 | tf_op jit(solution)/shard_map/ppermute | solution.py:442
  283.1 42.1 %collective-permute-start.36 = (bf16[640,1024]{1,0:T(8,128)(2,1)}, bf16[640,1024]{1,0:T(8,128)(2,1)}, u32[]{:S(2)}, u32[]{:S(2)}) collective-permute-start(bf16[640,1024]{1,0:T(8,128)(2,1)} %add_convert_fusion.2), channel_id=1, source_target_pairs={{0,2},{1,3},{2,0},{3,1},{4,6},{5,7},{6,4},{7,5},{8,10},{9,11},{10,... | collective-permute-start | bytes 3932168 | tf_op jit(solution)/shard_map/ppermute | solution.py:442
  283.6 41.7 %collective-permute-start.37 = (bf16[1024,256]{1,0:T(8,128)(2,1)}, bf16[1024,256]{1,0:T(8,128)(2,1)S(1)}, u32[]{:S(2)}, u32[]{:S(2)}) collective-permute-start(bf16[1024,256]{1,0:T(8,128)(2,1)} %add_convert_fusion.6), channel_id=1, source_target_pairs={{0,2},{1,3},{2,0},{3,1},{4,6},{5,7},{6,4},{7,5},{8,10},{9,11},{10,... | collective-permute-start | bytes 1572872 | tf_op jit(solution)/shard_map/ppermute | solution.py:442
  335.7 49.1 %collective-permute-start.39 = (bf16[512,640]{0,1:T(8,128)(2,1)}, bf16[512,640]{0,1:T(8,128)(2,1)}, u32[]{:S(2)}, u32[]{:S(2)}) collective-permute-start(bf16[512,640]{0,1:T(8,128)(2,1)} %fusion.21), channel_id=1, source_target_pairs={{0,4},{4,0},{8,12},{12,8},{16,20},{20,16},{24,28},{28,24},{1,5},{5... | collective-permute-start | bytes 1966088 | tf_op jit(solution)/shard_map/ppermute | solution.py:442
  384.2 14.8 %collective-permute-start.41 = (bf16[640,1024]{1,0:T(8,128)(2,1)}, bf16[640,1024]{1,0:T(8,128)(2,1)}, u32[]{:S(2)}, u32[]{:S(2)}) collective-permute-start(bf16[640,1024]{1,0:T(8,128)(2,1)} %get-tuple-element.152), channel_id=1, source_target_pairs={{0,1},{1,0},{2,3},{3,2},{4,5},{5,4},{6,7},{7,6},{8,9},{9,8},{10,11... | collective-permute-start | bytes 3932168 | tf_op jit(solution)/shard_map/ppermute | solution.py:442
  386.3 12.7 %collective-permute-start.40 = (bf16[256,640]{0,1:T(8,128)(2,1)S(1)}, bf16[256,640]{0,1:T(8,128)(2,1)S(1)}, u32[]{:S(2)}, u32[]{:S(2)}) collective-permute-start(bf16[256,640]{0,1:T(8,128)(2,1)S(1)} %constant_dynamic-slice_fusion.12), channel_id=1, source_target_pairs={{0,8},{4,12},{8,0},{12,4},{16,24},{20,28},{24,16},{28,20},{1,9},{5... | collective-permute-start | bytes 983048 | tf_op jit(solution)/shard_map/ppermute | solution.py:442
  390.9 26.2 %collective-permute-start.54 = (bf16[128,1536]{1,0:T(8,128)(2,1)}, bf16[128,1536]{1,0:T(8,128)(2,1)S(1)}, u32[]{:S(2)}, u32[]{:S(2)}) collective-permute-start(bf16[128,1536]{1,0:T(8,128)(2,1)} %reduce-scatter.3.cloned.1.call-done), channel_id=1, source_target_pairs={{0,2},{1,3},{2,0},{3,1},{4,6},{5,7},{6,4},{7,5},{8,10},{9,11},{10,... | collective-permute-start | bytes 1179656 | tf_op jit(solution)/shard_map/ppermute | solution.py:442
  401.8 12.5 %collective-permute-start.43 = (bf16[512,384]{0,1:T(8,128)(2,1)}, bf16[512,384]{0,1:T(8,128)(2,1)}, u32[]{:S(2)}, u32[]{:S(2)}) collective-permute-start(bf16[512,384]{0,1:T(8,128)(2,1)} %constant_dynamic-slice_fusion.10), channel_id=1, source_target_pairs={{0,4},{4,0},{8,12},{12,8},{16,20},{20,16},{24,28},{28,24},{1,5},{5... | collective-permute-start | bytes 1179656 | tf_op jit(solution)/shard_map/ppermute | solution.py:442
  403.4 12.0 %collective-permute-start.44 = (bf16[160,1024]{1,0:T(8,128)(2,1)S(1)}, bf16[160,1024]{1,0:T(8,128)(2,1)S(1)}, u32[]{:S(2)}, u32[]{:S(2)}) collective-permute-start(bf16[160,1024]{1,0:T(8,128)(2,1)S(1)} %get-tuple-element.209), channel_id=1, source_target_pairs={{0,2},{1,3},{2,0},{3,1},{4,6},{5,7},{6,4},{7,5},{8,10},{9,11},{10,... | collective-permute-start | bytes 983048 | tf_op jit(solution)/shard_map/ppermute | solution.py:442
  404.0 9.6 %collective-permute-start.42 = (bf16[128,640]{0,1:T(8,128)(2,1)S(1)}, bf16[128,640]{0,1:T(8,128)(2,1)S(1)}, u32[]{:S(2)}, u32[]{:S(2)}) collective-permute-start(bf16[128,640]{0,1:T(8,128)(2,1)S(1)} %constant_dynamic-slice_fusion.11), channel_id=1, source_target_pairs={{0,16},{4,20},{8,24},{12,28},{16,0},{20,4},{24,8},{28,12},{1,17},{... | collective-permute-start | bytes 491528 | tf_op jit(solution)/shard_map/ppermute | solution.py:442
  415.4 14.1 %collective-permute-start.46 = (bf16[640,1024]{1,0:T(8,128)(2,1)}, bf16[640,1024]{1,0:T(8,128)(2,1)}, u32[]{:S(2)}, u32[]{:S(2)}) collective-permute-start(bf16[640,1024]{1,0:T(8,128)(2,1)} %get-tuple-element.165), channel_id=1, source_target_pairs={{0,1},{1,0},{2,3},{3,2},{4,5},{5,4},{6,7},{7,6},{8,9},{9,8},{10,11... | collective-permute-start | bytes 3932168 | tf_op jit(solution)/shard_map/ppermute | solution.py:442
  422.1 6.4 %collective-permute-start.45 = (bf16[256,384]{0,1:T(8,128)(2,1)S(1)}, bf16[256,384]{0,1:T(8,128)(2,1)}, u32[]{:S(2)}, u32[]{:S(2)}) collective-permute-start(bf16[256,384]{0,1:T(8,128)(2,1)S(1)} %constant_dynamic-slice_fusion.9), channel_id=1, source_target_pairs={{0,8},{4,12},{8,0},{12,4},{16,24},{20,28},{24,16},{28,20},{1,9},{5... | collective-permute-start | bytes 589832 | tf_op jit(solution)/shard_map/ppermute | solution.py:442
  425.0 9.3 %collective-permute-start.47 = (bf16[160,1024]{1,0:T(8,128)(2,1)}, bf16[160,1024]{1,0:T(8,128)(2,1)S(1)}, u32[]{:S(2)}, u32[]{:S(2)}) collective-permute-start(bf16[160,1024]{1,0:T(8,128)(2,1)} %get-tuple-element.208), channel_id=1, source_target_pairs={{0,2},{1,3},{2,0},{3,1},{4,6},{5,7},{6,4},{7,5},{8,10},{9,11},{10,... | collective-permute-start | bytes 983048 | tf_op jit(solution)/shard_map/ppermute | solution.py:442
  436.2 14.6 %collective-permute-start.50 = (bf16[320,1024]{1,0:T(8,128)(2,1)S(1)}, bf16[320,1024]{1,0:T(8,128)(2,1)S(1)}, u32[]{:S(2)}, u32[]{:S(2)}) collective-permute-start(bf16[320,1024]{1,0:T(8,128)(2,1)S(1)} %slice.229), channel_id=1, source_target_pairs={{0,2},{1,3},{2,0},{3,1},{4,6},{5,7},{6,4},{7,5},{8,10},{9,11},{10,... | collective-permute-start | bytes 1966088 | tf_op jit(solution)/shard_map/ppermute | solution.py:442
  440.9 15.6 %collective-permute-start.49 = (bf16[128,1024]{0,1:T(8,128)(2,1)}, bf16[128,1024]{0,1:T(8,128)(2,1)}, u32[]{:S(2)}, u32[]{:S(2)}) collective-permute-start(bf16[128,1024]{0,1:T(8,128)(2,1)} %get-tuple-element.249), channel_id=1, source_target_pairs={{0,2},{1,3},{2,0},{3,1},{4,6},{5,7},{6,4},{7,5},{8,10},{9,11},{10,... | collective-permute-start | bytes 786440 | tf_op jit(solution)/shard_map/ppermute | solution.py:442
  447.9 18.3 %collective-permute-start.51 = (bf16[128,1024]{0,1:T(8,128)(2,1)}, bf16[128,1024]{0,1:T(8,128)(2,1)S(1)}, u32[]{:S(2)}, u32[]{:S(2)}) collective-permute-start(bf16[128,1024]{0,1:T(8,128)(2,1)} %get-tuple-element.249), channel_id=1, source_target_pairs={{0,1},{1,0},{2,3},{3,2},{4,5},{5,4},{6,7},{7,6},{8,9},{9,8},{10,11... | collective-permute-start | bytes 786440 | tf_op jit(solution)/shard_map/ppermute | solution.py:442
  456.5 9.3 %collective-permute-start.57 = (bf16[96,1024]{1,0:T(8,128)(2,1)}, bf16[96,1024]{1,0:T(8,128)(2,1)S(1)}, u32[]{:S(2)}, u32[]{:S(2)}) collective-permute-start(bf16[96,1024]{1,0:T(8,128)(2,1)} %reduce-scatter.5.cloned.1.call-done), channel_id=1, source_target_pairs={{0,2},{1,3},{2,0},{3,1},{4,6},{5,7},{6,4},{7,5},{8,10},{9,11},{10,... | collective-permute-start | bytes 589832 | tf_op jit(solution)/shard_map/ppermute | solution.py:442
  457.6 14.1 %collective-permute-start.56 = (bf16[96,1024]{1,0:T(8,128)(2,1)}, bf16[96,1024]{1,0:T(8,128)(2,1)S(1)}, u32[]{:S(2)}, u32[]{:S(2)}) collective-permute-start(bf16[96,1024]{1,0:T(8,128)(2,1)} %reduce-scatter.5.cloned.1.call-done), channel_id=1, source_target_pairs={{0,1},{1,0},{2,3},{3,2},{4,5},{5,4},{6,7},{7,6},{8,9},{9,8},{10,11... | collective-permute-start | bytes 589832 | tf_op jit(solution)/shard_map/ppermute | solution.py:442
  (65 other events, 365.4 us)
Sparse Core Ops, SparseCore 0:
  67.5 79.7 all-gather.1
  247.1 75.4 reduce-scatter.2
  326.0 64.2 reduce-scatter.4
